TPU v7x, 32 devices: a whole 2x2x4 slice. The times are simulated.
32 devices in a mesh: dp: 16 (over z, y, x), tensor: 2 (over core).
Axes of the slice: x: 2, y: 2, z: 4, core: 2. Of those that a mesh axis runs over, the one named last changes fastest.
Arguments:
- tokens: bfloat16 [16384, 768], P('dp'), may hold values from -6 to 6
- cotangent: bfloat16 [16384, 768], P('dp'), may hold values from -6 to 6
- lengths: int32 [32], P('dp'), may hold values from 113 to 512, as said below
- proj_weight: float32 [2, 768, 3, 768], P(None, 'dp', None, 'tensor'), may hold values from -0.21875 to 0.21875
- out_weight: float32 [2, 768, 768], P(None, 'dp', 'tensor'), may hold values from -0.875 to 0.875
- up_weight: float32 [2, 768, 3072], P(None, 'dp', 'tensor'), may hold values from -0.21875 to 0.21875
- down_weight: float32 [2, 768, 3072], P(None, 'dp', 'tensor'), may hold values from -0.109375 to 0.109375
- small_params: float32 [2, 8448], replicated, may hold values from -0.8 to 1.4
- proj_first: float32 [2, 768, 3, 768], P(None, 'dp', None, 'tensor'), may hold values from -0.00018310547 to 0.00018310547
- proj_second: float32 [2, 768, 3, 768], P(None, 'dp', None, 'tensor'), may hold values from 3.527916e-11 to 3.52791626e-09
- out_first: float32 [2, 768, 768], P(None, 'dp', 'tensor'), may hold values from -0.00018310547 to 0.00018310547
- out_second: float32 [2, 768, 768], P(None, 'dp', 'tensor'), may hold values from 7.0558325e-12 to 7.0558325e-10
- up_first: float32 [2, 768, 3072], P(None, 'dp', 'tensor'), may hold values from -0.00018310547 to 0.00018310547
- up_second: float32 [2, 768, 3072], P(None, 'dp', 'tensor'), may hold values from 3.527916e-11 to 3.52791626e-09
- down_first: float32 [2, 768, 3072], P(None, 'dp', 'tensor'), may hold values from -0.00018310547 to 0.00018310547
- down_second: float32 [2, 768, 3072], P(None, 'dp', 'tensor'), may hold values from 3.527916e-11 to 3.52791626e-09
- small_first: float32 [2, 8448], replicated, may hold values from -0.00018310547 to 0.00018310547
- small_second: float32 [2, 8448], replicated, may hold values from 3.527916e-11 to 5.644666e-10
Outputs:
- activations: float32 [16384, 768], P('dp')
- input_grad: float32 [16384, 768], P('dp')
- grad_norm: float32 [], replicated
- proj_first_new: float32 [2, 768, 3, 768], P(None, 'dp', None, 'tensor')
- proj_second_new: float32 [2, 768, 3, 768], P(None, 'dp', None, 'tensor')
- proj_weight_new: float32 [2, 768, 3, 768], P(None, 'dp', None, 'tensor')
- out_first_new: float32 [2, 768, 768], P(None, 'dp', 'tensor')
- out_second_new: float32 [2, 768, 768], P(None, 'dp', 'tensor')
- out_weight_new: float32 [2, 768, 768], P(None, 'dp', 'tensor')
- up_first_new: float32 [2, 768, 3072], P(None, 'dp', 'tensor')
- up_second_new: float32 [2, 768, 3072], P(None, 'dp', 'tensor')
- up_weight_new: float32 [2, 768, 3072], P(None, 'dp', 'tensor')
- down_first_new: float32 [2, 768, 3072], P(None, 'dp', 'tensor')
- down_second_new: float32 [2, 768, 3072], P(None, 'dp', 'tensor')
- down_weight_new: float32 [2, 768, 3072], P(None, 'dp', 'tensor')
- small_first_new: float32 [2, 8448], replicated
- small_second_new: float32 [2, 8448], replicated
- small_params_new: float32 [2, 8448], replicated
Inputs may be any that keep to these rules, and one draw needn't show every extreme that they name: `lengths`: each length is 512, 256 or 128, reduced by less than max(1, 16); the first sequence has length 512.
All inputs are finite; a program needn't handle non-finite values.
Results may differ from a plain program's by a relative error of at most 0.03.
The roundings to bfloat16 on the way count: a program that leaves them out, or rounds other values in their place, can miss the bound.
Values may be sent and summed in bfloat16 or wider, within the bound.
No kernel may reach another device: no remote copies, remote signals or barrier semaphores. Data moves between devices by JAX's collectives and lax.ppermute only.
A program may use at most 192 MiB of HBM per device.

v0:
```python
from functools import partial
import math

import jax
import jax.numpy as jnp
from jax import lax
from jax.sharding import PartitionSpec as P

D = 768
HEADS = 12
FF = 3072


beta_one = 0.9
beta_two = 0.999
adam_eps = 1e-06
decay_rate = 0.01
matrix_rate = 1.0
vector_rate = 0.3
clip_norm = 1.0
step_count = 10.0
norm_eps = 1e-06
masked_score = -1e30


def layer_norm(values, norm_gain, norm_shift):
    average = jnp.mean(values, axis=-1, keepdims=True)
    centered = values - average
    variance = jnp.mean(centered * centered, axis=-1, keepdims=True)
    return centered * lax.rsqrt(variance + norm_eps) * norm_gain + norm_shift


def split_vector(packed):
    bounds = [0, D, 2 * D, 2 * D + FF, 3 * D + FF, 4 * D + FF, 5 * D + FF, 6 * D + FF, 7 * D + FF]
    return [packed[bounds[place] : bounds[place + 1]] for place in range(8)]


def head_scores(query, keys, score_scale):
    return jnp.einsum("qhe,khe->hqk", query, keys, preferred_element_type=jnp.float32) * score_scale


def total_scores(pairs, score_scale):
    score_total = head_scores(pairs[0], pairs[1], score_scale)
    for place in range(2, len(pairs), 2):
        score_total = score_total + head_scores(pairs[place], pairs[place + 1], score_scale)
    return score_total


def attend_forward(block_item, score_scale):
    key_valid, value_rows = (block_item[0], block_item[1])
    score_total = total_scores(block_item[2:], score_scale)
    masked = jnp.where(key_valid[None, None, :], score_total, masked_score)
    row_max = jnp.max(masked, axis=-1, keepdims=True)
    exp_terms = jnp.exp(masked - row_max)
    row_sum = jnp.sum(exp_terms, axis=-1, keepdims=True)
    soft_low = (exp_terms / row_sum).astype(jnp.bfloat16)
    context = jnp.einsum("hqk,khe->qhe", soft_low, value_rows, preferred_element_type=jnp.float32)
    return (context.astype(jnp.bfloat16), (row_max + jnp.log(row_sum))[..., 0])


def attend_backward(block_item, score_scale, with_later, keep_total):
    key_valid, value_rows, log_norm, context_grad = (
        block_item[0],
        block_item[1],
        block_item[2],
        block_item[3],
    )
    rest = block_item[4:]
    if with_later:
        later = rest[0]
        pairs = rest[1:]
    else:
        pairs = rest
    score_total = total_scores(pairs, score_scale)
    soft = jnp.where(key_valid[None, None, :], jnp.exp(score_total - log_norm[..., None]), 0.0)
    soft_grad = jnp.einsum(
        "qhe,khe->hqk", context_grad, value_rows, preferred_element_type=jnp.float32
    )
    total_grad = soft * (soft_grad - jnp.sum(soft * soft_grad, axis=-1, keepdims=True))
    if with_later:
        total_grad = total_grad + later
    total_low = total_grad.astype(jnp.bfloat16)
    query_grad = (
        jnp.einsum("hqk,khe->qhe", total_low, pairs[1], preferred_element_type=jnp.float32)
        * score_scale
    )
    key_grad = (
        jnp.einsum("hqk,qhe->khe", total_low, pairs[0], preferred_element_type=jnp.float32)
        * score_scale
    )
    value_grad = jnp.einsum(
        "hqk,qhe->khe", soft.astype(jnp.bfloat16), context_grad, preferred_element_type=jnp.float32
    )
    results = (query_grad, key_grad, value_grad)
    if keep_total:
        results = results + (total_grad,)
    return results


def adam_parts(gradient, first, second, factor):
    clipped = gradient * factor
    first_new = beta_one * first + (1.0 - beta_one) * clipped
    second_new = beta_two * second + (1.0 - beta_two) * clipped * clipped
    first_hat = first_new / (1.0 - beta_one**step_count)
    second_hat = second_new / (1.0 - beta_two**step_count)
    return (first_new, second_new, first_hat / (jnp.sqrt(second_hat) + adam_eps))


def local(
    tokens,
    cotangent,
    lengths,
    proj_weight,
    out_weight,
    up_weight,
    down_weight,
    small_params,
    proj_first,
    proj_second,
    out_first,
    out_second,
    up_first,
    up_second,
    down_first,
    down_second,
    small_first,
    small_second,
):
    layers = proj_weight.shape[0]
    seq_count = lengths.shape[0]
    seq_len = tokens.shape[0] // seq_count
    local_width = proj_weight.shape[3]
    head_dim = D // HEADS
    local_heads = local_width // head_dim
    hidden_local = up_weight.shape[2]
    score_scale = 1.0 / math.sqrt(head_dim)
    share_scale = 1.0 / lax.axis_size("tensor")
    tensor_rank = lax.axis_index("tensor")
    proj_full, out_full, up_full, down_full = (
        lax.all_gather(proj_weight.astype(jnp.bfloat16), "dp", axis=1, tiled=True),
        lax.all_gather(out_weight.astype(jnp.bfloat16), "dp", axis=1, tiled=True),
        lax.all_gather(up_weight.astype(jnp.bfloat16), "dp", axis=1, tiled=True),
        lax.all_gather(down_weight.astype(jnp.bfloat16), "dp", axis=1, tiled=True),
    )
    positions = jnp.arange(seq_len)
    key_valid = positions[None, :] < lengths[:, None]
    row_valid = key_valid.reshape(-1, 1)

    def own_part(vector, width):
        return lax.dynamic_slice_in_dim(vector, tensor_rank * width, width)

    def place_part(local_values, full_width):
        return lax.dynamic_update_slice_in_dim(
            jnp.zeros((full_width,), jnp.float32),
            local_values,
            tensor_rank * local_values.shape[0],
            0,
        )

    def heads_view(rows):
        return rows.reshape(seq_count, seq_len, local_heads, head_dim)

    hidden = tokens.astype(jnp.float32)
    saved = []
    for layer_at in range(layers):
        bias_v, bias_o, bias_up, bias_down, gain_one, shift_one, gain_two, shift_two = split_vector(
            small_params[layer_at]
        )
        input_low = hidden.astype(jnp.bfloat16)
        projected = jnp.einsum(
            "td,dcf->tcf", input_low, proj_full[layer_at], preferred_element_type=jnp.float32
        )
        query_low = projected[:, 0].astype(jnp.bfloat16)
        key_low = projected[:, 1].astype(jnp.bfloat16)
        value_low = (projected[:, 2] + own_part(bias_v, local_width)).astype(jnp.bfloat16)
        pairs = [heads_view(query_low), heads_view(key_low)]
        for earlier in reversed(saved):
            pairs += [heads_view(earlier["query"]), heads_view(earlier["keys"])]
        context_low, log_norm = lax.map(
            partial(attend_forward, score_scale=score_scale),
            (key_valid, heads_view(value_low)) + tuple(pairs),
        )
        context_low = context_low.reshape(-1, local_width)
        attended = lax.psum(
            jnp.einsum(
                "tf,df->td", context_low, out_full[layer_at], preferred_element_type=jnp.float32
            ).astype(jnp.bfloat16),
            "tensor",
        ).astype(jnp.float32)
        first_in = hidden + attended + bias_o
        first_out = layer_norm(first_in, gain_one, shift_one)
        first_low = first_out.astype(jnp.bfloat16)
        before_act = jnp.einsum(
            "td,df->tf", first_low, up_full[layer_at], preferred_element_type=jnp.float32
        ) + own_part(bias_up, hidden_local)
        act_low = jax.nn.gelu(before_act, approximate=False).astype(jnp.bfloat16)
        returned = lax.psum(
            jnp.einsum(
                "tf,df->td", act_low, down_full[layer_at], preferred_element_type=jnp.float32
            ).astype(jnp.bfloat16),
            "tensor",
        ).astype(jnp.float32)
        second_in = first_out + returned + bias_down
        saved.append(
            {
                "layer_input": input_low,
                "query": query_low,
                "keys": key_low,
                "value_rows": value_low,
                "log_norm": log_norm,
                "context": context_low,
                "first_in": first_in,
                "first_low": first_low,
                "before_act": before_act,
                "act_low": act_low,
                "second_in": second_in,
            }
        )
        hidden = layer_norm(second_in, gain_two, shift_two)
    grad_rows = jnp.where(row_valid, cotangent.astype(jnp.float32), 0.0)
    proj_grads = [None] * layers
    out_grads = [None] * layers
    up_grads = [None] * layers
    down_grads = [None] * layers
    small_grads = [None] * layers
    later_total = None
    for layer_at in reversed(range(layers)):
        kept = saved[layer_at]
        bias_v, bias_o, bias_up, bias_down, gain_one, shift_one, gain_two, shift_two = split_vector(
            small_params[layer_at]
        )
        second_in_grad, gain_two_grad, shift_two_grad = jax.vjp(
            layer_norm, kept["second_in"], gain_two, shift_two
        )[1](grad_rows)
        down_in_low = second_in_grad.astype(jnp.bfloat16)
        down_grads[layer_at] = jnp.einsum(
            "td,tf->df", down_in_low, kept["act_low"], preferred_element_type=jnp.float32
        )
        act_grad = jnp.einsum(
            "td,df->tf", down_in_low, down_full[layer_at], preferred_element_type=jnp.float32
        )
        before_grad = jax.vjp(partial(jax.nn.gelu, approximate=False), kept["before_act"])[1](
            act_grad
        )[0]
        before_low = before_grad.astype(jnp.bfloat16)
        up_grads[layer_at] = jnp.einsum(
            "td,tf->df", kept["first_low"], before_low, preferred_element_type=jnp.float32
        )
        first_back = lax.psum(
            jnp.einsum(
                "tf,df->td", before_low, up_full[layer_at], preferred_element_type=jnp.float32
            ).astype(jnp.bfloat16),
            "tensor",
        ).astype(jnp.float32)
        first_out_grad = second_in_grad + first_back
        first_in_grad, gain_one_grad, shift_one_grad = jax.vjp(
            layer_norm, kept["first_in"], gain_one, shift_one
        )[1](first_out_grad)
        out_in_low = first_in_grad.astype(jnp.bfloat16)
        out_grads[layer_at] = jnp.einsum(
            "td,tf->df", out_in_low, kept["context"], preferred_element_type=jnp.float32
        )
        context_grad = jnp.einsum(
            "td,df->tf", out_in_low, out_full[layer_at], preferred_element_type=jnp.float32
        ).astype(jnp.bfloat16)
        pairs = [heads_view(kept["query"]), heads_view(kept["keys"])]
        for earlier in reversed(saved[:layer_at]):
            pairs += [heads_view(earlier["query"]), heads_view(earlier["keys"])]
        items = (
            key_valid,
            heads_view(kept["value_rows"]),
            kept["log_norm"],
            heads_view(context_grad),
        )
        with_later = later_total is not None
        if with_later:
            items = items + (later_total,)
        items = items + tuple(pairs)
        results = lax.map(
            partial(
                attend_backward,
                score_scale=score_scale,
                with_later=with_later,
                keep_total=layer_at > 0,
            ),
            items,
        )
        later_total = results[3] if layer_at > 0 else None
        query_grad = results[0].reshape(-1, local_width)
        key_grad = results[1].reshape(-1, local_width)
        value_grad = results[2].reshape(-1, local_width)
        proj_grad_low = jnp.stack([query_grad, key_grad, value_grad], axis=1).astype(jnp.bfloat16)
        proj_grads[layer_at] = jnp.einsum(
            "td,tcf->dcf", kept["layer_input"], proj_grad_low, preferred_element_type=jnp.float32
        )
        input_back = lax.psum(
            jnp.einsum(
                "tcf,dcf->td",
                proj_grad_low,
                proj_full[layer_at],
                preferred_element_type=jnp.float32,
            ).astype(jnp.bfloat16),
            "tensor",
        ).astype(jnp.float32)
        grad_rows = first_in_grad + input_back
        small_grads[layer_at] = jnp.concatenate(
            [
                place_part(jnp.sum(value_grad, axis=0), D),
                share_scale * jnp.sum(first_in_grad, axis=0),
                place_part(jnp.sum(before_grad, axis=0), FF),
                share_scale * jnp.sum(second_in_grad, axis=0),
                share_scale * gain_one_grad,
                share_scale * shift_one_grad,
                share_scale * gain_two_grad,
                share_scale * shift_two_grad,
            ]
        )
    big_totals = (
        jnp.stack(proj_grads),
        jnp.stack(out_grads),
        jnp.stack(up_grads),
        jnp.stack(down_grads),
    )
    small_partial = jnp.stack(small_grads)
    row_count = proj_weight.shape[1]
    summed = lax.psum((big_totals[0], big_totals[1], big_totals[2], big_totals[3]), "dp")
    row_start = lax.axis_index("dp") * row_count
    shares = tuple(
        (lax.dynamic_slice_in_dim(summed_part, row_start, row_count, 1) for summed_part in summed)
    )
    masters = (proj_weight, out_weight, up_weight, down_weight)
    firsts = (proj_first, out_first, up_first, down_first)
    seconds = (proj_second, out_second, up_second, down_second)
    square_part = jnp.sum(shares[0] * shares[0])
    for kind_at in range(1, 4):
        square_part = square_part + jnp.sum(shares[kind_at] * shares[kind_at])
    weight_square = jnp.stack(
        [jnp.sum(master * master, axis=tuple(range(1, master.ndim))) for master in masters]
    )
    square_big, weight_square, small_grad = lax.psum(
        (square_part, weight_square, small_partial), ("dp", "tensor")
    )
    grad_norm = jnp.sqrt(square_big + jnp.sum(small_grad * small_grad))
    factor = clip_norm / jnp.maximum(grad_norm, clip_norm)
    moments = []
    updates = []
    for kind_at in range(4):
        first_new, second_new, direction = adam_parts(
            shares[kind_at], firsts[kind_at], seconds[kind_at], factor
        )
        moments.append((first_new, second_new))
        updates.append(direction + decay_rate * masters[kind_at])
    update_square = jnp.stack(
        [jnp.sum(update * update, axis=tuple(range(1, update.ndim))) for update in updates]
    )
    update_square = lax.psum(update_square, ("dp", "tensor"))
    ratio = jnp.sqrt(weight_square) / jnp.sqrt(update_square)
    outputs = [hidden, grad_rows, grad_norm]
    for kind_at in range(4):
        master = masters[kind_at]
        scaled = ratio[kind_at].reshape((-1,) + (1,) * (master.ndim - 1))
        outputs += [
            moments[kind_at][0],
            moments[kind_at][1],
            master - matrix_rate * scaled * updates[kind_at],
        ]
    small_first_new, small_second_new, small_direction = adam_parts(
        small_grad, small_first, small_second, factor
    )
    outputs += [small_first_new, small_second_new, small_params - vector_rate * small_direction]
    return tuple(outputs)


def solution(mesh):
    placed = (
        P("dp", None),
        P("dp", None),
        P("dp"),
        P(None, "dp", None, "tensor"),
        P(None, "dp", "tensor"),
        P(None, "dp", "tensor"),
        P(None, "dp", "tensor"),
        P(),
        P(None, "dp", None, "tensor"),
        P(None, "dp", None, "tensor"),
        P(None, "dp", "tensor"),
        P(None, "dp", "tensor"),
        P(None, "dp", "tensor"),
        P(None, "dp", "tensor"),
        P(None, "dp", "tensor"),
        P(None, "dp", "tensor"),
        P(),
        P(),
    )
    return jax.shard_map(
        local,
        mesh=mesh,
        in_specs=placed,
        out_specs=(
            P("dp", None),
            P("dp", None),
            P(),
            P(None, "dp", None, "tensor"),
            P(None, "dp", None, "tensor"),
            P(None, "dp", None, "tensor"),
            P(None, "dp", "tensor"),
            P(None, "dp", "tensor"),
            P(None, "dp", "tensor"),
            P(None, "dp", "tensor"),
            P(None, "dp", "tensor"),
            P(None, "dp", "tensor"),
            P(None, "dp", "tensor"),
            P(None, "dp", "tensor"),
            P(None, "dp", "tensor"),
            P(),
            P(),
            P(),
        ),
        check_vma=False,
    )
```

profile of v0, /device:TPU:0, one launch (start us, length us, event | category | flops | bytes accessed | tf_op | source)
XLA Modules:
  0.0 1741.5 jit_solution(10675762374318251473)
XLA Ops:
  13.1 72.2 %all-gather.5.cloned.1.call-done = bf16[2,768,3,384]{3,1,2,0:T(8,128)(2,1)} async-done(((bf16[2,48,3,384]{3,1,2,0:T(8,128)(2,1)}), bf16[2,768,3,384]{3,1,2,0:T(8,128)(2,1)}) %all-gather.5.cloned.1.call-update) | async-done | bytes 3538960 | tf_op jit(solution)/shard_map/all_gather | solution.py:140
  85.3 5.6 fusion.209
  103.5 11.4 while.54
  116.8 26.5 %all-gather.7.cloned.1.call-done = bf16[2,768,384]{2,1,0:T(8,128)(2,1)} async-done(((bf16[2,48,384]{2,1,0:T(8,128)(2,1)}), bf16[2,768,384]{2,1,0:T(8,128)(2,1)}) %all-gather.7.cloned.1.call-update) | async-done | bytes 1179664 | tf_op jit(solution)/shard_map/all_gather | solution.py:141
  143.3 3.6 convolution_convert_fusion.1
  150.6 15.8 all-reduce.13.cloned.1.call-done
  169.4 82.1 %all-gather.9.cloned.1.call-done = bf16[2,768,1536]{2,1,0:T(8,128)(2,1)} async-done(((bf16[2,48,1536]{2,1,0:T(8,128)(2,1)}), bf16[2,768,1536]{2,1,0:T(8,128)(2,1)}) %all-gather.9.cloned.1.call-update) | async-done | bytes 4718608 | tf_op jit(solution)/shard_map/all_gather | solution.py:142
  251.5 20.8 %multiply_convert_fusion.1 = (bf16[1024,1536]{1,0:T(8,128)(2,1)}, f32[1024,1536]{1,0:T(8,128)}, f32[1024,1536]{1,0:T(8,128)}) fusion(f32[1536]{0:T(1024)S(1)} %dynamic-slice_reduce_fusion.5, bf16[2,768,1536]{2,1,0:T(8,128)(2,1)} %all-gather.9.cloned.1.call-done, f32[768]{0:T(1024)S(1)} %get-tuple-element.431, f32[768]{0:T(1024)S(1)} %get-tuple-element.432, ...), kind=kOutput, calls=%fused_computation.155 | convolution fusion | flops 2526806016 | bytes 21257216 | tf_op jit(solution)/shard_map/td,df->tf/dot_general | solution.py:193
  272.3 61.8 %all-gather.11.cloned.1.call-done = bf16[2,768,1536]{2,1,0:T(8,128)(2,1)} async-done(((bf16[2,48,1536]{2,1,0:T(8,128)(2,1)}), bf16[2,768,1536]{2,1,0:T(8,128)(2,1)}) %all-gather.11.cloned.1.call-update) | async-done | bytes 4718608 | tf_op jit(solution)/shard_map/all_gather | solution.py:143
  334.1 6.4 fusion.151
  340.6 19.1 %all-reduce.15.cloned.1.call-done = bf16[1024,768]{1,0:T(8,128)(2,1)} async-done(((bf16[1024,768]{1,0:T(8,128)(2,1)}), bf16[1024,768]{1,0:T(8,128)(2,1)}) %all-reduce.15.cloned.1.call-update) | async-done | bytes 1572880 | tf_op jit(solution)/shard_map/psum | solution.py:197
  359.7 3.5 fusion.200
  363.8 3.8 fusion.210
  380.8 14.1 while.55
  382.1 2.8 fusion.280
  389.1 2.8 fusion.280
  400.3 21.7 %all-reduce.17.cloned.1.call-done = bf16[1024,768]{1,0:T(8,128)(2,1)} async-done(((bf16[1024,768]{1,0:T(8,128)(2,1)}), bf16[1024,768]{1,0:T(8,128)(2,1)}) %all-reduce.17.cloned.1.call-update) | async-done | bytes 1572880 | tf_op jit(solution)/shard_map/psum | solution.py:184
  422.0 3.6 fusion.199
  426.4 18.9 %multiply_convert_fusion = (bf16[1024,1536]{1,0:T(8,128)(2,1)S(1)}, f32[1024,1536]{1,0:T(8,128)}, f32[1024,1536]{1,0:T(8,128)}) fusion(f32[1536]{0:T(1024)S(1)} %dynamic-slice_reduce_fusion.4, bf16[2,768,1536]{2,1,0:T(8,128)(2,1)S(1)} %bitcast.417, f32[1024,768]{1,0:T(8,128)S(1)} %get-tuple-element.545, f32[768]{0:T(1024)S(1)} %copy-done.104, ...), kind=kOutput, calls=%fused_computation.142 | convolution fusion | flops 2523660288 | bytes 21258240 | tf_op jit(solution)/shard_map/td,df->tf/dot_general | solution.py:193
  446.9 5.4 fusion.149
  452.4 21.7 %all-reduce.19.cloned.1.call-done = bf16[1024,768]{1,0:T(8,128)(2,1)} async-done(((bf16[1024,768]{1,0:T(8,128)(2,1)}), bf16[1024,768]{1,0:T(8,128)(2,1)}) %all-reduce.19.cloned.1.call-update) | async-done | bytes 1572880 | tf_op jit(solution)/shard_map/psum | solution.py:197
  474.1 3.6 fusion.197
  481.5 2.9 fusion.196
  484.5 9.5 fusion.211
  495.7 3.7 fusion.150
  503.7 8.0 convolution_bitcast_fusion.2
  511.7 9.5 all-reduce.21.cloned.1.call-done
  521.2 4.9 multiply_reduce_fusion.3
  534.5 3.3 reshape.326
  541.3 36.2 %while.56 = (s32[]{:T(128)}, bf16[2,512,6,64]{1,3,2,0:T(8,128)(2,1)}, bf16[2,512,6,64]{1,3,2,0:T(8,128)(2,1)}, f32[2,512,6,64]{1,3,2,0:T(8,128)}, f32[2,6,512,51...) while((s32[]{:T(128)}, ...), condition=%wide.region_27.28_spmd, body=%wide.region_25.27_spmd.sunk | while | flops 1227224064 | bytes 94064864 | solution.py:279
  544.7 3.4 multiply_reduce_fusion.28
  548.1 4.2 bitcast_dynamic-update-slice_fusion.8
  562.7 3.4 multiply_reduce_fusion.28
  566.0 4.3 bitcast_dynamic-update-slice_fusion.8
  577.5 2.7 fusion.206
  586.6 2.9 stack_reshape.24
  592.4 5.6 bitcast_convert_fusion.1
  598.2 7.9 convolution_bitcast_fusion
  609.0 4.3 convolution_bitcast_fusion.4
  613.3 6.5 all-reduce.23.cloned.1.call-done
  619.8 5.1 multiply_reduce_fusion.4
  627.2 9.6 fusion.212
  638.5 3.7 fusion.152
  642.3 5.6 convolution_bitcast_fusion.1
  648.0 7.4 pad_maximum_fusion.1
  655.5 4.8 convolution_bitcast_fusion.3
  660.2 3.8 all-reduce.25.cloned.1.call-done
  664.0 4.8 multiply_reduce_fusion.5
  676.8 54.5 %while.57 = (s32[]{:T(128)}, bf16[2,512,6,64]{1,3,2,0:T(8,128)(2,1)}, bf16[2,512,6,64]{1,3,2,0:T(8,128)(2,1)}, f32[2,512,6,64]{1,3,2,0:T(8,128)}, bf16[2,512,6,6...) while((s32[]{:T(128)}, ...), condition=%wide.region_36.37_spmd, body=%wide.region_34.36_spmd.sunk | while | flops 1222512128 | bytes 87736576 | solution.py:279
  676.9 5.2 exponential_select_fusion.3
  682.1 7.6 fusion.310
  689.7 7.8 fusion.311
  703.9 5.2 exponential_select_fusion.3
  709.1 7.6 fusion.310
  716.7 7.8 fusion.311
  740.2 5.2 bitcast_convert_fusion
  745.6 8.5 pad_maximum_fusion
  760.8 3.3 pad_maximum_fusion.2
  767.9 3.6 add_reduce_fusion
  772.4 736.9 %all-reduce.31.cloned.1.call-done = (f32[2,768,3,384]{3,1,2,0:T(8,128)}, f32[2,768,384]{2,1,0:T(8,128)}, f32[2,768,1536]{2,1,0:T(8,128)}, f32[2,768,1536]{2,1,0:T(8,128)}) async-done(((f32[2,768,3,384]{3,1,2,0:T(8,128)}, f32[2,768,384]{2,1,0:T(8,128)}, f32[2,768,1536]{2,1,0:T(8,128)}, f32[2,768,1536]{2,1,0:T(8,128)}), (f32[2,768,3,384]{3,1,2,0:T(8,128)}, f32[2,768,384]{2,1,0:T(8,128)}, ...) | async-done | bytes 28311568 | tf_op jit(solution)/shard_map/psum | solution.py:326
  1518.9 114.0 %all-reduce.29.cloned.1.call-done = f32[2,8448]{1,0:T(2,128)} async-done(((f32[2,8448]{1,0:T(2,128)}), f32[2,8448]{1,0:T(2,128)}) %all-reduce.29.cloned.1.call-update) | async-done | bytes 67600 | tf_op jit(solution)/shard_map/psum | solution.py:340
  1634.5 42.6 %psum.124 = f32[]{:T(128)} all-reduce(f32[]{:T(128)S(6)} %add.424), channel_id=1, replica_groups=mesh['dp'=16,'tensor'=2] {'dp','tensor'}, use_global_device_ids=true, to_apply=%region_46.47 | all-reduce | flops 1 | bytes 8 | tf_op jit(solution)/shard_map/psum | solution.py:340
  1682.4 3.2 multiply_reduce_fusion.16
  1688.1 39.3 %all-reduce = (f32[4,2]{1,0:T(4,128)S(1)}, f32[4,2]{1,0:T(4,128)S(1)}) all-reduce(f32[4,2]{1,0:T(4,128)S(1)} %pad_maximum_fusion.12, f32[4,2]{1,0:T(4,128)S(1)} %pad_maximum_fusion.11), channel_id=1, replica_groups=mesh['dp'=16,'tensor'=2] {'dp','tensor'}, use_global_device_ids=true, to_apply=%region_74.75 | all-reduce | flops 16 | bytes 128 | tf_op jit(solution)/shard_map/psum | solution.py:356
  (526 shorter events, 188.5 us)
Async XLA Ops:
  7.2 78.1 %all-gather.5.cloned.1.call-start = ((), (), s32[]{:S(2)}) async-start(), calls=%async_computation | async-start | bytes 3760128 | tf_op jit(solution)/shard_map/all_gather | solution.py:140
  9.0 134.3 %all-gather.7.cloned.1.call-start = ((), (), s32[]{:S(2)}) async-start(), calls=%async_computation.1 | async-start | bytes 1253376 | tf_op jit(solution)/shard_map/all_gather | solution.py:141
  10.6 155.7 %all-reduce.13.cloned.1.call-start = ((), (), s32[]{:S(2)}) async-start(), calls=%async_computation.2 | async-start | bytes 3145728 | tf_op jit(solution)/shard_map/psum | solution.py:184
  12.2 347.4 %copy-start.73 = (f32[768]{0:T(1024)}, f32[768]{0:T(1024)S(1)}, u32[]{:S(2)}) copy-start(f32[768]{0:T(1024)S(1)} %get-tuple-element.433) | copy-start | bytes 9220
  12.2 347.4 %copy-start.82 = (f32[768]{0:T(1024)}, f32[768]{0:T(1024)S(1)}, u32[]{:S(2)}) copy-start(f32[768]{0:T(1024)S(1)} %get-tuple-element.432) | copy-start | bytes 9220
  12.2 347.4 %copy-start.100 = (f32[768]{0:T(1024)}, f32[768]{0:T(1024)S(1)}, u32[]{:S(2)}) copy-start(f32[768]{0:T(1024)S(1)} %get-tuple-element.431) | copy-start | bytes 9220
  12.2 409.7 %copy-start.86 = (f32[768]{0:T(1024)}, f32[768]{0:T(1024)S(1)}, u32[]{:S(2)}) copy-start(f32[768]{0:T(1024)S(1)} %get-tuple-element.429) | copy-start | bytes 9220
  12.2 409.7 %copy-start.102 = (f32[768]{0:T(1024)}, f32[768]{0:T(1024)S(1)}, u32[]{:S(2)}) copy-start(f32[768]{0:T(1024)S(1)} %get-tuple-element.428) | copy-start | bytes 9220
  114.9 28.3 %copy-start.20 = (bf16[2,512,6,64]{1,3,2,0:T(8,128)(2,1)}, bf16[2,512,6,64]{1,3,2,0:T(8,128)(2,1)S(1)}, u32[]{:S(2)}) copy-start(bf16[2,512,6,64]{1,3,2,0:T(8,128)(2,1)S(1)} %get-tuple-element.1014) | copy-start | bytes 2359300
  114.9 32.0 %copy-start.69 = (f32[2,6,512]{2,1,0:T(8,128)}, f32[2,6,512]{2,1,0:T(8,128)S(1)}, u32[]{:S(2)}) copy-start(f32[2,6,512]{2,1,0:T(8,128)S(1)} %get-tuple-element.954) | copy-start | bytes 73732
  116.8 32.0 %copy-start.32 = (f32[2,48,1536]{2,1,0:T(8,128)S(1)}, f32[2,48,1536]{2,1,0:T(8,128)}, u32[]{:S(2)}) copy-start(f32[2,48,1536]{2,1,0:T(8,128)} %param.32) | copy-start | bytes 1769476
  143.3 23.1 %copy-start.10 = (bf16[1024,768]{1,0:T(8,128)(2,1)S(1)}, bf16[1024,768]{1,0:T(8,128)(2,1)}, u32[]{:S(2)}) copy-start(bf16[1024,768]{1,0:T(8,128)(2,1)} %param.26) | copy-start | bytes 4718596
  146.9 104.6 %all-gather.9.cloned.1.call-start = ((), (), s32[]{:S(2)}) async-start(), calls=%async_computation.3 | async-start | bytes 5013504 | tf_op jit(solution)/shard_map/all_gather | solution.py:142
  148.8 185.3 %all-gather.11.cloned.1.call-start = ((), (), s32[]{:S(2)}) async-start(), calls=%async_computation.4 | async-start | bytes 5013504 | tf_op jit(solution)/shard_map/all_gather | solution.py:143
  149.6 210.1 %all-reduce.15.cloned.1.call-start = ((), (), s32[]{:S(2)}) async-start(), calls=%async_computation.5 | async-start | bytes 3145728 | tf_op jit(solution)/shard_map/psum | solution.py:197
  150.5 100.9 %copy-start.116 = (f32[1536]{0:T(1024)}, f32[1536]{0:T(1024)S(1)}, u32[]{:S(2)}) copy-start(f32[1536]{0:T(1024)S(1)} %dynamic-slice_reduce_fusion.5) | copy-start | bytes 18436
  168.5 191.2 %copy-start.76 = (f32[1024]{0:T(1024)}, f32[1024]{0:T(1024)S(1)}, u32[]{:S(2)}) copy-start(f32[1024]{0:T(1024)S(1)} %broadcast_multiply_fusion.3) | copy-start | bytes 12292
  169.4 102.9 %copy-start.92 = (f32[1024]{0:T(1024)}, f32[1024]{0:T(1024)S(1)}, u32[]{:S(2)}) copy-start(f32[1024]{0:T(1024)S(1)} %multiply_reduce_fusion.13) | copy-start | bytes 12292
  169.4 190.3 %copy-start.84 = (f32[1024]{0:T(1024)}, f32[1024]{0:T(1024)S(1)}, u32[]{:S(2)}) copy-start(f32[1024]{0:T(1024)S(1)} %fusion.167) | copy-start | bytes 12292
  340.5 81.5 %all-reduce.17.cloned.1.call-start = ((), (), s32[]{:S(2)}) async-start(), calls=%async_computation.6 | async-start | bytes 3145728 | tf_op jit(solution)/shard_map/psum | solution.py:184
  363.2 58.7 %copy-start.78 = (f32[1024]{0:T(1024)}, f32[1024]{0:T(1024)S(1)}, u32[]{:S(2)}) copy-start(f32[1024]{0:T(1024)S(1)} %broadcast_multiply_fusion.2) | copy-start | bytes 12292
  363.8 58.2 %copy-start.89 = (f32[1024]{0:T(1024)}, f32[1024]{0:T(1024)S(1)}, u32[]{:S(2)}) copy-start(f32[1024]{0:T(1024)S(1)} %fusion.168) | copy-start | bytes 12292
  397.0 25.0 %copy-start.106 = (f32[768]{0:T(1024)S(1)}, f32[768]{0:T(1024)}, u32[]{:S(2)}) copy-start(f32[768]{0:T(1024)} %get-tuple-element.427) | copy-start | bytes 9220
  400.2 73.9 %all-reduce.19.cloned.1.call-start = ((), (), s32[]{:S(2)}) async-start(), calls=%async_computation.7 | async-start | bytes 3145728 | tf_op jit(solution)/shard_map/psum | solution.py:197
  425.6 19.6 %copy-start.3 = (f32[1024,768]{1,0:T(8,128)}, f32[1024,768]{1,0:T(8,128)S(1)}, u32[]{:S(2)}) copy-start(f32[1024,768]{1,0:T(8,128)S(1)} %get-tuple-element.545) | copy-start | bytes 9437188
  446.9 27.2 %copy-start.105 = (f32[768]{0:T(1024)S(1)}, f32[768]{0:T(1024)}, u32[]{:S(2)}) copy-start(f32[768]{0:T(1024)} %get-tuple-element.424) | copy-start | bytes 9220
  452.3 68.9 %all-reduce.21.cloned.1.call-start = ((), (), s32[]{:S(2)}) async-start(), calls=%async_computation.8 | async-start | bytes 3145728 | tf_op jit(solution)/shard_map/psum | solution.py:249
  474.1 10.4 slice-start.8
  481.5 14.2 slice-start.4
  484.5 9.6 copy-start.8
  484.5 11.2 slice-start.5
  499.5 120.3 %all-reduce.23.cloned.1.call-start = ((), (), s32[]{:S(2)}) async-start(), calls=%async_computation.9 | async-start | bytes 3145728 | tf_op jit(solution)/shard_map/psum | solution.py:296
  582.5 8.2 copy-start.40
  598.1 7.9 copy-start.53
  598.1 65.9 %all-reduce.25.cloned.1.call-start = ((), (), s32[]{:S(2)}) async-start(), calls=%async_computation.10 | async-start | bytes 3145728 | tf_op jit(solution)/shard_map/psum | solution.py:249
  598.1 7.9 copy-start.18
  598.1 10.3 copy-start.63
  613.3 11.6 copy-start.95
  625.4 13.1 slice-start.6
  627.2 9.6 copy-start.6
  627.2 11.2 slice-start.7
  642.2 125.6 %all-reduce.27.cloned.1.call-start = ((), (), s32[]{:S(2)}) async-start(), calls=%async_computation.11 | async-start | bytes 3145728 | tf_op jit(solution)/shard_map/psum | solution.py:296
  647.9 7.5 copy-start.11
  647.9 7.5 copy-start.14
  647.9 7.5 copy-start.74
  647.9 7.5 copy-start.77
  647.9 7.5 copy-start.83
  660.2 8.6 copy-start.93
  682.1 19.8 %slice-start = ((s8[6291456]{0:T(1024)(128)(4,1)}), s8[2097152]{0:T(1024)(128)(4,1)S(1)}, s32[]{:S(2)}) async-start(s8[6291456]{0:T(1024)(128)(4,1)} %bitcast.400), calls=%async_computation.14 | async-start | bytes 4194304 | tf_op jit(solution)/shard_map/while
  689.7 12.2 slice-start.1
  709.1 19.8 %slice-start = ((s8[6291456]{0:T(1024)(128)(4,1)}), s8[2097152]{0:T(1024)(128)(4,1)S(1)}, s32[]{:S(2)}) async-start(s8[6291456]{0:T(1024)(128)(4,1)} %bitcast.400), calls=%async_computation.14 | async-start | bytes 4194304 | tf_op jit(solution)/shard_map/while
  716.7 12.2 slice-start.1
  737.0 8.4 copy-start.57
  745.4 8.7 copy-start.26
  745.4 763.9 %all-reduce.31.cloned.1.call-start = ((), (), s32[]{:S(2)}) async-start(), calls=%async_computation.13 | async-start | bytes 56623104 | tf_op jit(solution)/shard_map/psum | solution.py:326
  745.6 8.5 copy-start.51
  764.2 868.7 %all-reduce.29.cloned.1.call-start = ((), (), s32[]{:S(2)}) async-start(), calls=%async_computation.12 | async-start | bytes 135168 | tf_op jit(solution)/shard_map/psum | solution.py:340
  767.9 910.6 %copy-start.47 = (f32[2,48,384]{2,1,0:T(8,128)S(1)}, f32[2,48,384]{2,1,0:T(8,128)}, u32[]{:S(2)}) copy-start(f32[2,48,384]{2,1,0:T(8,128)} %param.30) | copy-start | bytes 442372
  771.5 908.9 %copy-start.34 = (f32[2,48,1536]{2,1,0:T(8,128)S(1)}, f32[2,48,1536]{2,1,0:T(8,128)}, u32[]{:S(2)}) copy-start(f32[2,48,1536]{2,1,0:T(8,128)} %param.31) | copy-start | bytes 1769476
  771.5 908.9 %copy-start.66 = (f32[2,48,1536]{2,1,0:T(8,128)S(1)}, f32[2,48,1536]{2,1,0:T(8,128)}, u32[]{:S(2)}) copy-start(f32[2,48,1536]{2,1,0:T(8,128)} %param.38) | copy-start | bytes 1769476
  1509.3 173.1 %copy-start.33 = (f32[2,48,1536]{2,1,0:T(8,128)S(1)}, f32[2,48,1536]{2,1,0:T(8,128)}, u32[]{:S(2)}) copy-start(f32[2,48,1536]{2,1,0:T(8,128)} %param.32) | copy-start | bytes 1769476
  1682.4 47.4 %copy-start.42 = (f32[2,48,1536]{2,1,0:T(8,128)}, f32[2,48,1536]{2,1,0:T(8,128)S(1)}, u32[]{:S(2)}) copy-start(f32[2,48,1536]{2,1,0:T(8,128)S(1)} %get-tuple-element.528) | copy-start | bytes 1769476
  1682.4 47.4 %copy-start.43 = (f32[2,48,1536]{2,1,0:T(8,128)}, f32[2,48,1536]{2,1,0:T(8,128)S(1)}, u32[]{:S(2)}) copy-start(f32[2,48,1536]{2,1,0:T(8,128)S(1)} %get-tuple-element.529) | copy-start | bytes 1769476
  1685.6 45.4 %copy-start.44 = (f32[2,48,1536]{2,1,0:T(8,128)}, f32[2,48,1536]{2,1,0:T(8,128)S(1)}, u32[]{:S(2)}) copy-start(f32[2,48,1536]{2,1,0:T(8,128)S(1)} %get-tuple-element.530) | copy-start | bytes 1769476
  (95 other events, 298.8 us)
Sparse Core Ops, SparseCore 0:
  11.3 73.9 all-gather.4
  88.5 54.6 all-gather.6
  147.0 19.2 all-reduce.12
  169.8 81.6 all-gather.8
  255.0 79.0 all-gather.10
  340.6 19.0 all-reduce.14
  400.3 21.5 all-reduce.16
  452.5 21.5 all-reduce.18
  499.6 21.5 all-reduce.20
  598.2 21.5 all-reduce.22
  642.4 21.5 all-reduce.24
  745.5 21.5 all-reduce.26
  773.5 735.7 all-reduce.30
  1516.2 116.6 all-reduce.28
where the time goes:
time: 1750 us; the launch traced here: 1740 us
  waiting for transfers between devices  1190 us (68%)
  matrix products  238 us (14%)
  other arithmetic  121 us (7%)
  local copies, waits for them, and re-layouts  86.8 us (5%)
  blocking collectives  81.9 us (5%)
  between operations  20.9 us (1%)
    psum x1, waiting for transfers between devices, local(): lax.psum((big_totals[0], big_totals[1], big_totals[2], big_totals[3]), 'dp')  737 us
    psum x1, waiting for transfers between devices, local(): lax.psum((square_part, weight_square, small_partial), ('dp', 'tensor'))  114 us
    all_gather x1, waiting for transfers between devices, local(): lax.all_gather(up_weight.astype(jnp.bfloat16), 'dp', axis=1, tiled=True)  82.1 us
    all_gather x1, waiting for transfers between devices, local(): lax.all_gather(proj_weight.astype(jnp.bfloat16), 'dp', axis=1, tiled=True)  72.2 us
    all_gather x1, waiting for transfers between devices, local(): lax.all_gather(down_weight.astype(jnp.bfloat16), 'dp', axis=1, tiled=True)  61.8 us
    psum x1, blocking collectives, local(): lax.psum((square_part, weight_square, small_partial), ('dp', 'tensor'))  42.6 us
    psum x2, waiting for transfers between devices, local(): lax.psum(jnp.einsum('tf,df->td', act_low, down_full[layer_at], preferred_...  40.7 us
    dot_general x2, matrix products, local(): jnp.einsum('td,df->tf', first_low, up_full[layer_at], preferred_element_t...  39.6 us
  transfers between devices with their start and end apart: 14, of which 13 were waited for; matrix products, arithmetic and copies ran while one was open for 8% of the time, Pallas kernels for 0%

commit v1 on v0

v1 whole, which is shorter than its diff:
```python
from functools import partial
import math

import jax
import jax.numpy as jnp
import numpy as np
from jax import lax
from jax.experimental import pallas as pl
from jax.experimental.pallas import tpu as pltpu
from jax.sharding import PartitionSpec as P

D = 768
HEADS = 12
FF = 3072


beta_one = 0.9
beta_two = 0.999
adam_eps = 1e-06
decay_rate = 0.01
matrix_rate = 1.0
vector_rate = 0.3
clip_norm = 1.0
step_count = 10.0
norm_eps = 1e-06
masked_score = -1e30

f32 = jnp.float32
bf16 = jnp.bfloat16


def layer_norm(values, norm_gain, norm_shift):
    average = jnp.mean(values, axis=-1, keepdims=True)
    centered = values - average
    variance = jnp.mean(centered * centered, axis=-1, keepdims=True)
    return centered * lax.rsqrt(variance + norm_eps) * norm_gain + norm_shift


def split_vector(packed):
    bounds = [0, D, 2 * D, 2 * D + FF, 3 * D + FF, 4 * D + FF, 5 * D + FF, 6 * D + FF, 7 * D + FF]
    return [packed[bounds[place] : bounds[place + 1]] for place in range(8)]


class Links:
    def __init__(self, parts):
        self.parts = parts
        count = parts.bit_length() - 1
        high = list(range(count - 1, -1, -1))
        other = high[:-2] + high[-2:][::-1]
        self.orders = (other, high)
        self.masks = np.zeros((2, parts), np.int32)
        self.inverse = np.zeros((2, parts), np.int32)
        for core in range(2):
            for place in range(parts):
                mask = 0
                for stage in range(count):
                    if (place >> stage) & 1:
                        mask |= 1 << self.orders[core][stage]
                self.masks[core, place] = mask
                self.inverse[core, mask] = place
        self.stages = count

    def swap(self, value, stage):
        pairs = []
        for core in range(2):
            flip = 1 << self.orders[core][stage]
            pairs += [(2 * at + core, 2 * (at ^ flip) + core) for at in range(self.parts)]
        return lax.ppermute(value, ("dp", "tensor"), pairs)

    def sibling(self, value):
        return lax.ppermute(value, "tensor", [(0, 1), (1, 0)])

    def gather(self, share):
        held = share[None]
        for stage in range(self.stages):
            held = jnp.concatenate([held, self.swap(held, stage)], axis=0)
        return held

    def scatter(self, own, other):
        pieces = [own, self.sibling(other)]
        size = self.parts
        for stage in reversed(range(self.stages)):
            half = size // 2
            total = sum(piece[half:size].astype(f32) for piece in pieces).astype(bf16)
            pieces = [piece[:half] for piece in pieces]
            pieces.append(self.swap(total, stage))
            size = half
        return sum(piece[0].astype(f32) for piece in pieces)

    def total(self, value):
        value = value + self.sibling(value)
        for stage in range(self.stages):
            value = value + self.swap(value, stage)
        return value


def assemble_kernel(own_at, other_at, own, other, *outs, widths):
    start = 0
    for out, parts in zip(outs, widths):
        place = 0
        for width in parts:
            out[0, :, place : place + width] = own[0, :, start : start + width]
            out[0, :, place + width : place + 2 * width] = other[0, :, start : start + width]
            place += 2 * width
            start += width


def assemble(own_at, other_at, own, other, widths):
    parts, rows, cols = own.shape
    return pl.pallas_call(
        partial(assemble_kernel, widths=widths),
        out_shape=[jax.ShapeDtypeStruct((parts, rows, 2 * sum(w)), own.dtype) for w in widths],
        grid_spec=pltpu.PrefetchScalarGridSpec(
            num_scalar_prefetch=2,
            grid=(parts,),
            in_specs=[
                pl.BlockSpec((1, rows, cols), lambda i, a, b: (a[i], 0, 0)),
                pl.BlockSpec((1, rows, cols), lambda i, a, b: (b[i], 0, 0)),
            ],
            out_specs=[pl.BlockSpec((1, rows, 2 * sum(w)), lambda i, a, b: (i, 0, 0)) for w in widths],
        ),
        compiler_params=pltpu.CompilerParams(dimension_semantics=("arbitrary",)),
        name="assemble",
    )(own_at, other_at, own, other)


def outer_kernel(own_at, other_at, *refs, counts, parts, rows):
    sources = len(counts)
    own, other, turned = refs[3 * sources :]
    step = pl.program_id(0)
    start = 0
    for source, count in enumerate(counts):
        left, right_own, right_other = refs[3 * source : 3 * source + 3]

        @pl.when(step == start)
        def _():
            turned[...] = left[...].T

        @pl.when((step >= start) & (step < start + count))
        def _():
            for right, place_of, out in ((right_own, own_at, own), (right_other, other_at, other)):
                product = jnp.dot(turned[...], right[...], preferred_element_type=f32).astype(bf16)
                for block in range(parts):
                    out[place_of[block]] = product[block * rows : (block + 1) * rows]

        start += count


def outer(own_at, other_at, sources, width):
    parts = own_at.shape[0]
    rows = D // parts
    counts = [sum(spans) // width for _, _, spans in sources]
    in_specs, args = [], []
    start = 0
    for (left, right, spans), count in zip(sources, counts):
        per_span = spans[0] // width

        def column(step, half, start=start, count=count, per_span=per_span):
            at = jnp.clip(step - start, 0, count - 1)
            return (at // per_span) * (2 * per_span) + half * per_span + at % per_span

        in_specs.append(pl.BlockSpec(left.shape, lambda i, a, b: (0, 0)))
        for half in range(2):
            in_specs.append(
                pl.BlockSpec(
                    (right.shape[0], width), lambda i, a, b, half=half, column=column: (0, column(i, half))
                )
            )
        args += [left, right, right]
        start += count
    out_spec = pl.BlockSpec((parts, rows, width), lambda i, a, b: (0, 0, i))
    out_shape = jax.ShapeDtypeStruct((parts, rows, start * width), bf16)
    return pl.pallas_call(
        partial(outer_kernel, counts=counts, parts=parts, rows=rows),
        out_shape=[out_shape, out_shape],
        grid_spec=pltpu.PrefetchScalarGridSpec(
            num_scalar_prefetch=2,
            grid=(start,),
            in_specs=in_specs,
            out_specs=[out_spec, out_spec],
            scratch_shapes=[pltpu.VMEM((D, sources[0][0].shape[0]), bf16)],
        ),
        compiler_params=pltpu.CompilerParams(
            dimension_semantics=("arbitrary",), vmem_limit_bytes=48 << 20
        ),
        name="outer",
    )(own_at, other_at, *args)


def head_scores(query, keys, score_scale):
    return jnp.einsum("qhe,khe->hqk", query, keys, preferred_element_type=jnp.float32) * score_scale


def total_scores(pairs, score_scale):
    score_total = head_scores(pairs[0], pairs[1], score_scale)
    for place in range(2, len(pairs), 2):
        score_total = score_total + head_scores(pairs[place], pairs[place + 1], score_scale)
    return score_total


def attend_forward(key_valid, value_rows, pairs, score_scale):
    score_total = total_scores(pairs, score_scale)
    masked = jnp.where(key_valid[None, None, :], score_total, masked_score)
    row_max = jnp.max(masked, axis=-1, keepdims=True)
    exp_terms = jnp.exp(masked - row_max)
    row_sum = jnp.sum(exp_terms, axis=-1, keepdims=True)
    soft_low = (exp_terms / row_sum).astype(jnp.bfloat16)
    context = jnp.einsum("hqk,khe->qhe", soft_low, value_rows, preferred_element_type=jnp.float32)
    return (context.astype(jnp.bfloat16), (row_max + jnp.log(row_sum))[..., 0])


def attend_backward(key_valid, value_rows, log_norm, context_grad, later, pairs, score_scale):
    score_total = total_scores(pairs, score_scale)
    soft = jnp.where(key_valid[None, None, :], jnp.exp(score_total - log_norm[..., None]), 0.0)
    soft_grad = jnp.einsum(
        "qhe,khe->hqk", context_grad, value_rows, preferred_element_type=jnp.float32
    )
    total_grad = soft * (soft_grad - jnp.sum(soft * soft_grad, axis=-1, keepdims=True))
    if later is not None:
        total_grad = total_grad + later
    total_low = total_grad.astype(jnp.bfloat16)
    query_grad = (
        jnp.einsum("hqk,khe->qhe", total_low, pairs[1], preferred_element_type=jnp.float32)
        * score_scale
    )
    key_grad = (
        jnp.einsum("hqk,qhe->khe", total_low, pairs[0], preferred_element_type=jnp.float32)
        * score_scale
    )
    value_grad = jnp.einsum(
        "hqk,qhe->khe", soft.astype(jnp.bfloat16), context_grad, preferred_element_type=jnp.float32
    )
    return (query_grad, key_grad, value_grad, total_grad)


def adam_parts(gradient, first, second, factor):
    clipped = gradient * factor
    first_new = beta_one * first + (1.0 - beta_one) * clipped
    second_new = beta_two * second + (1.0 - beta_two) * clipped * clipped
    first_hat = first_new / (1.0 - beta_one**step_count)
    second_hat = second_new / (1.0 - beta_two**step_count)
    return (first_new, second_new, first_hat / (jnp.sqrt(second_hat) + adam_eps))


def local(
    tokens,
    cotangent,
    lengths,
    proj_weight,
    out_weight,
    up_weight,
    down_weight,
    small_params,
    proj_first,
    proj_second,
    out_first,
    out_second,
    up_first,
    up_second,
    down_first,
    down_second,
    small_first,
    small_second,
):
    layers = proj_weight.shape[0]
    seq_here = lengths.shape[0] // 2
    seq_len = tokens.shape[0] // lengths.shape[0]
    rows_here = seq_here * seq_len
    head_dim = D // HEADS
    half_d = proj_weight.shape[3]
    half_ff = up_weight.shape[2]
    row_count = proj_weight.shape[1]
    score_scale = 1.0 / math.sqrt(head_dim)
    core = lax.axis_index("tensor")
    parts = lax.axis_size("dp")
    links = Links(parts)
    at = lax.axis_index("dp")
    inverse = jnp.asarray(links.inverse)
    order = jnp.arange(parts, dtype=jnp.int32) ^ at
    own_at = inverse[core][order]
    other_at = inverse[1 - core][order]

    def shares_of(layer_at, kinds):
        table = {"proj": proj_weight, "out": out_weight, "up": up_weight, "down": down_weight}
        return jnp.concatenate(
            [table[kind][layer_at].reshape(row_count, -1).astype(bf16) for kind in kinds], axis=1
        )

    spans = {"proj": (half_d,) * 3, "out": (half_d,), "up": (half_ff,), "down": (half_ff,)}
    full = [dict() for _ in range(layers)]
    for layer_at in range(layers):
        groups = [("proj",), ("out", "up", "down")]
        for kinds in groups:
            held = links.gather(shares_of(layer_at, kinds))
            swapped = links.sibling(held)
            ready = assemble(own_at, other_at, held, swapped, [spans[kind] for kind in kinds])
            for kind, weight in zip(kinds, ready):
                full[layer_at][kind] = weight.reshape(D, -1)

    def own_first(vector):
        half = vector.shape[0] // 2
        return jnp.where(core == 0, vector, jnp.concatenate([vector[half:], vector[:half]]))

    tokens = lax.dynamic_slice_in_dim(tokens, core * rows_here, rows_here)
    cotangent = lax.dynamic_slice_in_dim(cotangent, core * rows_here, rows_here)
    lengths = lax.dynamic_slice_in_dim(lengths, core * seq_here, seq_here)
    positions = jnp.arange(seq_len)
    key_valid = positions[None, :] < lengths[:, None]
    row_valid = key_valid.reshape(-1, 1)

    def heads_view(rows):
        return rows.reshape(seq_here, seq_len, HEADS, head_dim)

    hidden = tokens.astype(jnp.float32)
    saved = []
    for layer_at in range(layers):
        bias_v, bias_o, bias_up, bias_down, gain_one, shift_one, gain_two, shift_two = split_vector(
            small_params[layer_at]
        )
        weights = full[layer_at]
        input_low = hidden.astype(jnp.bfloat16)
        projected = jnp.einsum("td,df->tf", input_low, weights["proj"], preferred_element_type=f32)
        query_low = projected[:, :D].astype(jnp.bfloat16)
        key_low = projected[:, D : 2 * D].astype(jnp.bfloat16)
        value_low = (projected[:, 2 * D :] + own_first(bias_v)).astype(jnp.bfloat16)
        pairs = [heads_view(query_low), heads_view(key_low)]
        for earlier in reversed(saved):
            pairs += [heads_view(earlier["query"]), heads_view(earlier["keys"])]
        context_low, log_norm = jax.vmap(partial(attend_forward, score_scale=score_scale))(
            key_valid, heads_view(value_low), pairs
        )
        context_low = context_low.reshape(-1, D)
        attended = jnp.einsum("tf,df->td", context_low, weights["out"], preferred_element_type=f32)
        first_in = hidden + attended + bias_o
        first_out = layer_norm(first_in, gain_one, shift_one)
        first_low = first_out.astype(jnp.bfloat16)
        before_act = jnp.einsum(
            "td,df->tf", first_low, weights["up"], preferred_element_type=f32
        ) + own_first(bias_up)
        act_low = jax.nn.gelu(before_act, approximate=False).astype(jnp.bfloat16)
        returned = jnp.einsum("tf,df->td", act_low, weights["down"], preferred_element_type=f32)
        second_in = first_out + returned + bias_down
        saved.append(
            {
                "layer_input": input_low,
                "query": query_low,
                "keys": key_low,
                "value_rows": value_low,
                "log_norm": log_norm,
                "context": context_low,
                "first_in": first_in,
                "first_low": first_low,
                "before_act": before_act,
                "act_low": act_low,
                "second_in": second_in,
            }
        )
        hidden = layer_norm(second_in, gain_two, shift_two)

    grad_rows = jnp.where(row_valid, cotangent.astype(jnp.float32), 0.0)
    shares = [None] * layers
    small_grads = [None] * layers
    later_total = None
    for layer_at in reversed(range(layers)):
        kept = saved[layer_at]
        weights = full[layer_at]
        bias_v, bias_o, bias_up, bias_down, gain_one, shift_one, gain_two, shift_two = split_vector(
            small_params[layer_at]
        )
        second_in_grad, gain_two_grad, shift_two_grad = jax.vjp(
            layer_norm, kept["second_in"], gain_two, shift_two
        )[1](grad_rows)
        down_in_low = second_in_grad.astype(jnp.bfloat16)
        act_grad = jnp.einsum("td,df->tf", down_in_low, weights["down"], preferred_element_type=f32)
        before_grad = jax.vjp(partial(jax.nn.gelu, approximate=False), kept["before_act"])[1](
            act_grad
        )[0]
        before_low = before_grad.astype(jnp.bfloat16)
        ff_share = links.scatter(
            *outer(
                own_at,
                other_at,
                [
                    (down_in_low, kept["act_low"], spans["down"]),
                    (kept["first_low"], before_low, spans["up"]),
                ],
                half_d,
            )
        )
        first_back = jnp.einsum("tf,df->td", before_low, weights["up"], preferred_element_type=f32)
        first_out_grad = second_in_grad + first_back
        first_in_grad, gain_one_grad, shift_one_grad = jax.vjp(
            layer_norm, kept["first_in"], gain_one, shift_one
        )[1](first_out_grad)
        out_in_low = first_in_grad.astype(jnp.bfloat16)
        context_grad = jnp.einsum(
            "td,df->tf", out_in_low, weights["out"], preferred_element_type=f32
        ).astype(jnp.bfloat16)
        pairs = [heads_view(kept["query"]), heads_view(kept["keys"])]
        for earlier in reversed(saved[:layer_at]):
            pairs += [heads_view(earlier["query"]), heads_view(earlier["keys"])]
        query_grad, key_grad, value_grad, later_total = jax.vmap(
            partial(attend_backward, score_scale=score_scale)
        )(
            key_valid,
            heads_view(kept["value_rows"]),
            kept["log_norm"],
            heads_view(context_grad),
            later_total,
            pairs,
        )
        value_grad = value_grad.reshape(-1, D)
        proj_grad_low = jnp.concatenate(
            [query_grad.reshape(-1, D), key_grad.reshape(-1, D), value_grad], axis=1
        ).astype(jnp.bfloat16)
        attention_share = links.scatter(
            *outer(
                own_at,
                other_at,
                [
                    (out_in_low, kept["context"], spans["out"]),
                    (kept["layer_input"], proj_grad_low, spans["proj"]),
                ],
                half_d,
            )
        )
        input_back = jnp.einsum(
            "tf,df->td", proj_grad_low, weights["proj"], preferred_element_type=f32
        )
        grad_rows = first_in_grad + input_back
        shares[layer_at] = (
            attention_share[:, half_d:],
            attention_share[:, :half_d],
            ff_share[:, half_ff:],
            ff_share[:, :half_ff],
        )
        small_grads[layer_at] = jnp.concatenate(
            [
                own_first(jnp.sum(value_grad, axis=0)),
                jnp.sum(first_in_grad, axis=0),
                own_first(jnp.sum(before_grad, axis=0)),
                jnp.sum(second_in_grad, axis=0),
                gain_one_grad,
                shift_one_grad,
                gain_two_grad,
                shift_two_grad,
            ]
        )

    masters = (proj_weight, out_weight, up_weight, down_weight)
    firsts = (proj_first, out_first, up_first, down_first)
    seconds = (proj_second, out_second, up_second, down_second)
    grads = [
        jnp.stack([shares[layer_at][kind_at] for layer_at in range(layers)]).reshape(
            masters[kind_at].shape
        )
        for kind_at in range(4)
    ]
    weight_square = jnp.stack(
        [jnp.sum(master * master, axis=tuple(range(1, master.ndim))) for master in masters]
    )
    small_size = small_params.size
    first_pack = jnp.concatenate(
        [
            jnp.stack(small_grads).reshape(-1),
            jnp.pad(weight_square.reshape(-1), (0, 128 - 4 * layers)),
        ]
    ).reshape(-1, 128)
    first_pack = links.total(first_pack).reshape(-1)
    small_grad = first_pack[:small_size].reshape(small_params.shape)
    weight_square = first_pack[small_size : small_size + 4 * layers].reshape(4, layers)

    square_part = sum(jnp.sum(grad * grad) for grad in grads)
    square_big = links.total(jnp.broadcast_to(square_part, (8, 128)))[0, 0]
    grad_norm = jnp.sqrt(square_big + jnp.sum(small_grad * small_grad))
    factor = clip_norm / jnp.maximum(grad_norm, clip_norm)
    moments = []
    updates = []
    for kind_at in range(4):
        first_new, second_new, direction = adam_parts(
            grads[kind_at], firsts[kind_at], seconds[kind_at], factor
        )
        moments.append((first_new, second_new))
        updates.append(direction + decay_rate * masters[kind_at])
    update_square = jnp.stack(
        [jnp.sum(update * update, axis=tuple(range(1, update.ndim))) for update in updates]
    )
    update_square = links.total(jnp.pad(update_square.reshape(1, -1), ((0, 7), (0, 128 - 4 * layers))))
    update_square = update_square[0, : 4 * layers].reshape(4, layers)
    ratio = jnp.sqrt(weight_square) / jnp.sqrt(update_square)

    def whole_rows(rows):
        other = links.sibling(rows)
        return jnp.where(
            core == 0, jnp.concatenate([rows, other]), jnp.concatenate([other, rows])
        )

    outputs = [whole_rows(hidden), whole_rows(grad_rows), grad_norm]
    for kind_at in range(4):
        master = masters[kind_at]
        scaled = ratio[kind_at].reshape((-1,) + (1,) * (master.ndim - 1))
        outputs += [
            moments[kind_at][0],
            moments[kind_at][1],
            master - matrix_rate * scaled * updates[kind_at],
        ]
    small_first_new, small_second_new, small_direction = adam_parts(
        small_grad, small_first, small_second, factor
    )
    outputs += [small_first_new, small_second_new, small_params - vector_rate * small_direction]
    return tuple(outputs)


def solution(mesh):
    proj = P(None, "dp", None, "tensor")
    matrix = P(None, "dp", "tensor")
    rows = P("dp", None)
    return jax.shard_map(
        local,
        mesh=mesh,
        in_specs=(rows, rows, P("dp"), proj, matrix, matrix, matrix, P())
        + (proj, proj)
        + (matrix,) * 6
        + (P(), P()),
        out_specs=(rows, rows, P()) + (proj,) * 3 + (matrix,) * 9 + (P(),) * 3,
        check_vma=False,
    )
```

time: 1750 us -> 789 us (0.45)
  waiting for transfers between devices: 1190 us -> 208 us
  Pallas kernels: 0 us -> 91.1 us
  blocking collectives: 81.9 us -> 0 us
  starting transfers between devices: 0.76 us -> 62.9 us
  matrix products: 238 us -> 203 us
    psum x10 -> x0, waiting for transfers between devices: 949 us -> none  [the longest x1 737 us: local(): lax.psum((big_totals[0], big_totals[1], big_totals[2], big_totals[3]), 'dp')]
    all_gather x4 -> x0, waiting for transfers between devices: 243 us -> none  [the longest x1 82.1 us: local(): lax.all_gather(up_weight.astype(jnp.bfloat16), 'dp', axis=1, tiled=True)]
    ppermute x0 -> x57, waiting for transfers between devices: none -> 208 us  [the longest x44 204 us: swap(): return lax.ppermute(value, ('dp', 'tensor'), pairs)]
    pallas_call x0 -> x8, Pallas kernels: none -> 91.1 us  [the longest x4 49.7 us: assemble(): pl.pallas_call(partial(assemble_kernel, widths=widths), out_shape=[jax.Sh...]
    psum x2 -> x0, blocking collectives: 81.9 us -> none  [the longest x1 42.6 us: local(): lax.psum((square_part, weight_square, small_partial), ('dp', 'tensor'))]
    ppermute x0 -> x57, starting transfers between devices: none -> 62.9 us  [the longest x44 59.2 us: swap(): return lax.ppermute(value, ('dp', 'tensor'), pairs)]
    dot_general x24 -> x16, matrix products: 144 us -> 93.7 us  [the longest x2 36.6 us: local(): jnp.einsum('td,df->tf', first_low, weights['up'], preferred_element_type=...]
    convert_element_type x8 -> x21, other arithmetic: 11.5 us -> 38.9 us  [the longest x16 34.3 us: scatter(): total = sum((piece[half:size].astype(f32) for piece in pieces)).astype(bf16)]
  transfers between devices with their start and end apart: 14 -> 57, of which waited for: 13 -> 26; matrix products, arithmetic and copies ran while one was open for 8% -> 27% of each run, Pallas kernels for 0% -> 7%
where the time goes in v1:
time: 789 us; the launch traced here: 780 us
  waiting for transfers between devices  208 us (26%)
  matrix products  203 us (26%)
  other arithmetic  131 us (17%)
  Pallas kernels  91.1 us (12%)
  local copies, waits for them, and re-layouts  76.4 us (10%)
  starting transfers between devices  62.9 us (8%)
  between operations  8.18 us (1%)
    ppermute x44, waiting for transfers between devices, swap(): return lax.ppermute(value, ('dp', 'tensor'), pairs)  204 us
    ppermute x44, starting transfers between devices, swap(): return lax.ppermute(value, ('dp', 'tensor'), pairs)  59.2 us
    pallas_call x4, Pallas kernels, assemble(): pl.pallas_call(partial(assemble_kernel, widths=widths), out_shape=[jax.Sh...  49.7 us
    pallas_call x4, Pallas kernels, outer(): pl.pallas_call(partial(outer_kernel, counts=counts, parts=parts, rows=row...  41.4 us
    dot_general x2, matrix products, local(): jnp.einsum('td,df->tf', first_low, weights['up'], preferred_element_type=...  36.6 us
    convert_element_type x16, other arithmetic, scatter(): total = sum((piece[half:size].astype(f32) for piece in pieces)).astype(bf16)  34.3 us
    dot_general x2, matrix products, attend_backward(): jnp.einsum('hqk,qhe->khe', total_low, pairs[0], preferred_element_type=jn...  33.5 us
    dot_general x2, matrix products, attend_backward(): jnp.einsum('hqk,khe->qhe', total_low, pairs[1], preferred_element_type=jn...  27.9 us
  transfers between devices with their start and end apart: 57, of which 26 were waited for; matrix products, arithmetic and copies ran while one was open for 27% of the time, Pallas kernels for 7%

profile of v1, /device:TPU:0, one launch (start us, length us, event | category | flops | bytes accessed | tf_op | source)
XLA Modules:
  0.0 780.4 jit_solution(493601068048500092)
XLA Ops:
  2.8 4.0 collective-permute-start
  11.4 3.0 collective-permute-start.5
  40.7 5.1 collective-permute-done.15
  57.8 11.7 %collective-permute-done.6 = bf16[2,48,3456]{2,1,0:T(8,128)(2,1)S(1)} collective-permute-done((bf16[2,48,3456]{2,1,0:T(8,128)(2,1)S(1)}, bf16[2,48,3456]{2,1,0:T(8,128)(2,1)S(1)}, u32[]{:S(2)}, u32[]{:S(2)}) %collective-permute-start.6) | collective-permute-done | bytes 663584 | tf_op jit(solution)/shard_map/ppermute | solution.py:68
  78.1 22.4 %collective-permute-done.7 = bf16[4,48,3456]{2,1,0:T(8,128)(2,1)S(1)} collective-permute-done((bf16[4,48,3456]{2,1,0:T(8,128)(2,1)S(1)}, bf16[4,48,3456]{2,1,0:T(8,128)(2,1)S(1)}, u32[]{:S(2)}, u32[]{:S(2)}) %collective-permute-start.7) | collective-permute-done | bytes 1327136 | tf_op jit(solution)/shard_map/ppermute | solution.py:68
  101.8 2.8 collective-permute-start.8
  110.6 26.3 %collective-permute-done.17 = bf16[4,48,3456]{2,1,0:T(8,128)(2,1)S(1)} collective-permute-done((bf16[4,48,3456]{2,1,0:T(8,128)(2,1)S(1)}, bf16[4,48,3456]{2,1,0:T(8,128)(2,1)S(1)}, u32[]{:S(2)}, u32[]{:S(2)}) %collective-permute-start.17) | collective-permute-done | bytes 1327136 | tf_op jit(solution)/shard_map/ppermute | solution.py:68
  139.8 9.3 %collective-permute-done.8 = bf16[8,48,3456]{2,1,0:T(8,128)(2,1)S(1)} collective-permute-done((bf16[8,48,3456]{2,1,0:T(8,128)(2,1)S(1)}, bf16[8,48,3456]{2,1,0:T(8,128)(2,1)S(1)}, u32[]{:S(2)}, u32[]{:S(2)}) %collective-permute-start.8) | collective-permute-done | bytes 2654240 | tf_op jit(solution)/shard_map/ppermute | solution.py:68
  153.2 11.0 %assemble.4 = bf16[16,48,2304]{2,1,0:T(8,128)(2,1)} custom-call(s32[16]{0:T(128)} %gather_fusion, s32[16]{0:T(128)} %gather_fusion.1, bf16[16,48,1152]{2,1,0:T(8,128)(2,1)} %copy-done.74, bf16[16,48,1152]{2,1,0:T(8,128)(2,1)} %collective-permute-done.4.other), custom_call_target="tpu_custom_call" | custom-call | tf_op jit(solution)/shard_map/assemble/pallas_call | solution.py:110
  164.3 6.2 fusion.126
  175.5 3.1 select_reduce_fusion.1
  181.3 3.3 fusion.69
  185.7 11.3 %assemble.6 = bf16[16,48,2304]{2,1,0:T(8,128)(2,1)} custom-call(s32[16]{0:T(128)} %gather_fusion, s32[16]{0:T(128)} %gather_fusion.1, bf16[16,48,1152]{2,1,0:T(8,128)(2,1)} %constant_dynamic-update-slice_fusion.10.own, bf16[16,48,1152]{2,1,0:T(8,128)(2,1)} %collective-permute-done.14.other), custom_call_target="tpu_custom_call" | custom-call | tf_op jit(solution)/shard_map/assemble/pallas_call | solution.py:110
  197.7 3.4 constant_dynamic-update-slice_fusion.15.own
  201.1 13.7 %assemble.5 = (bf16[16,48,768]{2,1,0:T(8,128)(2,1)}, bf16[16,48,3072]{2,1,0:T(8,128)(2,1)}, bf16[16,48,3072]{2,1,0:T(8,128)(2,1)}) custom-call(s32[16]{0:T(128)} %gather_fusion, s32[16]{0:T(128)} %gather_fusion.1, bf16[16,48,3456]{2,1,0:T(8,128)(2,1)} %constant_dynamic-update-slice_fusion.5.own, bf16[16,48,3456]{2,1,0:T(8,128)(2,1)} %collective-permute-done.9.other), custom_call_target="tpu_custom_call" | custom-call | tf_op jit(solution)/shard_map/assemble/pallas_call | solution.py:110
  218.0 18.4 %multiply_convert_fusion.1 = (bf16[512,3072]{1,0:T(8,128)(2,1)S(1)}, f32[512,3072]{1,0:T(8,128)}, f32[512,3072]{1,0:T(8,128)}) fusion(f32[3072]{0:T(1024)S(1)} %bitcast.221, bf16[512,768]{1,0:T(8,128)(2,1)S(1)} %fusion.70.refs_3_, bf16[768,3072]{1,0:T(8,128)(2,1)S(1)} %bitcast.233), kind=kOutput, calls=%fused_computation.49 | convolution fusion | flops 2519728128 | bytes 21245952 | tf_op jit(solution)/shard_map/td,df->tf/dot_general | solution.py:337
  236.5 2.8 fusion.128
  242.2 4.2 fusion.129
  252.1 6.7 select_reduce_fusion
  261.1 2.9 fusion.68
  265.2 13.6 %assemble.7 = (bf16[16,48,768]{2,1,0:T(8,128)(2,1)}, bf16[16,48,3072]{2,1,0:T(8,128)(2,1)}, bf16[16,48,3072]{2,1,0:T(8,128)(2,1)}) custom-call(s32[16]{0:T(128)} %gather_fusion, s32[16]{0:T(128)} %gather_fusion.1, bf16[16,48,3456]{2,1,0:T(8,128)(2,1)} %constant_dynamic-update-slice_fusion.15.own, bf16[16,48,3456]{2,1,0:T(8,128)(2,1)} %collective-permute-done.19.other), custom_call_target="tpu_custom_call" | custom-call | tf_op jit(solution)/shard_map/assemble/pallas_call | solution.py:110
  282.2 18.1 %multiply_convert_fusion = (bf16[512,3072]{1,0:T(8,128)(2,1)S(1)}, f32[512,3072]{1,0:T(8,128)S(1)}, f32[512,3072]{1,0:T(8,128)}) fusion(f32[3072]{0:T(1024)S(1)} %bitcast.223, bf16[512,768]{1,0:T(8,128)(2,1)S(1)} %fusion.72.refs_3_, bf16[768,3072]{1,0:T(8,128)(2,1)S(1)} %bitcast.243), kind=kOutput, calls=%fused_computation.36 | convolution fusion | flops 2519728128 | bytes 21245952 | tf_op jit(solution)/shard_map/td,df->tf/dot_general | solution.py:337
  300.3 2.8 fusion.131
  306.5 7.2 fusion.111
  313.7 3.1 multiply_reduce_fusion.3
  323.8 7.8 %bitcast_convert_fusion = (bf16[1,512,12,64]{1,3,2,0:T(8,128)(2,1)}, f32[12,64,512]{2,1,0:T(8,128)S(1)}) fusion(bf16[512,12,64]{0,2,1:T(8,128)(2,1)} %bitcast.188, f32[12,512,512]{1,2,0:T(8,128)} %copy-done.27, f32[12,512]{1,0:T(8,128)S(1)} %log_add_fusion.1, pred[512]{0:T(512)(128)(4,1)S(1)} %iota_compare_fusion.1), kind=kOutput, calls=%fused_computation.98 | convolution fusion | flops 412483584 | bytes 15753728 | tf_op jit(solution)/shard_map/vmap(hqk,qhe->khe)/dot_general | solution.py:230
  334.2 13.0 %outer.7 = (bf16[16,48,3072]{2,1,0:T(8,128)(2,1)}, bf16[16,48,3072]{2,1,0:T(8,128)(2,1)}) custom-call(s32[16]{0:T(128)S(1)} %copy-done.26, s32[16]{0:T(128)S(1)} %copy-done.25, bf16[512,768]{1,0:T(8,128)(2,1)S(1)} %copy-done.15, bf16[512,3072]{1,0:T(8,128)(2,1)S(1)} %get-tuple-element.117.refs_1_.refs_2_, ...), custom_call_target="tpu_custom_call" | custom-call | tf_op jit(solution)/shard_map/outer/pallas_call | solution.py:173
  347.2 9.4 %multiply_reduce_fusion.1 = (f32[12,512]{1,0:T(8,128)S(1)}, f32[12,512,512]{1,2,0:T(8,128)}) fusion(f32[12,512,512]{1,2,0:T(8,128)} %copy-done.27, f32[12,512]{1,0:T(8,128)S(1)} %log_add_fusion.1, pred[512]{0:T(512)(128)(4,1)S(1)} %iota_compare_fusion.1, bf16[512,12,64]{0,2,1:T(8,128)(2,1)S(1)} %bitcast.189, bf16[512,12,64]{0,2,1:T(8,128)(2,1)S(1)} %bitcast.197), kind=kOutput, calls=%fused_computation.8 | convolution fusion | flops 415229952 | bytes 26788352 | tf_op jit(solution)/shard_map/vmap(qhe,khe->hqk)/dot_general | solution.py:215
  356.6 12.2 %subtract_multiply_fusion = f32[12,512,512]{1,2,0:T(8,128)} fusion(f32[12,512,512]{1,2,0:T(8,128)} %get-tuple-element.200, f32[12,512,512]{1,2,0:T(8,128)S(1)} %bitcast.183, f32[12,512]{1,0:T(8,128)S(1)} %get-tuple-element.199, f32[12,512]{1,0:T(8,128)S(1)} %log_add_fusion.1, pred[512]{0:T(512)(128)(4,1)S(1)} %iota_compare_fusion.1), kind=kLoop, calls=%fused_computation.7 | loop fusion | flops 12582912 | bytes 37798400 | tf_op jit(solution)/shard_map/vmap()/mul | solution.py:218
  368.9 7.7 multiply_convert_fusion.4
  386.6 5.2 multiply_reduce_fusion.4
  394.5 9.8 %fusion.110 = (f32[3072]{0:T(1024)S(1)}, bf16[512,3072]{1,0:T(8,128)(2,1)S(1)}) fusion(f32[512,3072]{1,0:T(8,128)} %get-tuple-element.120, f32[512,3072]{1,0:T(8,128)} %get-tuple-element.184, f32[3072]{0:T(1024)S(1)} %bitcast.222, bf16[512,768]{1,0:T(8,128)(2,1)S(1)} %get-tuple-element.127.refs_0_, bf16[768,3072]{1,0:T(8,128)(2,1)} %bitcast.237), kind=kOutput, calls=%fused_computation.345 | convolution fusion | flops 2441081856 | bytes 21258240 | tf_op jit(solution)/shard_map/td,df->tf/dot_general | solution.py:374
  404.4 3.1 multiply_reduce_fusion.5
  412.5 8.2 %bitcast_convert_fusion.1 = (bf16[1,512,12,64]{1,3,2,0:T(8,128)(2,1)}, f32[12,64,512]{2,1,0:T(8,128)S(1)}) fusion(bf16[512,12,64]{0,2,1:T(8,128)(2,1)} %bitcast.205, f32[12,512,512]{1,2,0:T(8,128)} %copy-done.28, f32[12,512]{1,0:T(8,128)S(1)} %copy-done.103, pred[512]{0:T(512)(128)(4,1)S(1)} %iota_compare_fusion.1), kind=kOutput, calls=%fused_computation.100 | convolution fusion | flops 415629312 | bytes 15753728 | tf_op jit(solution)/shard_map/vmap(hqk,qhe->khe)/dot_general | solution.py:230
  423.2 12.7 %outer.6 = (bf16[16,48,3072]{2,1,0:T(8,128)(2,1)}, bf16[16,48,3072]{2,1,0:T(8,128)(2,1)}) custom-call(s32[16]{0:T(128)S(1)} %copy-done.26, s32[16]{0:T(128)S(1)} %copy-done.25, bf16[512,768]{1,0:T(8,128)(2,1)S(1)} %copy-done.17, bf16[512,3072]{1,0:T(8,128)(2,1)S(1)} %copy-done.3, bf16[512,3072]{1,0:T(8,128)(2,1)S(1)} %copy-done.3, ...), custom_call_target="tpu_custom_call" | custom-call | tf_op jit(solution)/shard_map/outer/pallas_call | solution.py:173
  435.9 6.4 fusion.132
  442.4 25.8 %multiply_convert_fusion.3 = bf16[12,64,512]{2,1,0:T(8,128)(2,1)} fusion(bf16[512,12,64]{0,2,1:T(8,128)(2,1)S(1)} %bitcast.200, f32[12,512,512]{1,2,0:T(8,128)} %subtract_multiply_fusion, f32[12,512,512]{1,2,0:T(8,128)} %fusion.132, f32[12,512,512]{1,2,0:T(8,128)} %copy-done.28, f32[12,512]{1,0:T(8,128)S(1)} %copy-done.103, ...), kind=kOutput, calls=%fused_computation.106 | convolution fusion | flops 438049280 | bytes 39346688 | tf_op jit(solution)/shard_map/vmap(hqk,khe->qhe)/dot_general | solution.py:223
  468.2 25.7 %multiply_convert_fusion.2 = bf16[12,64,512]{2,1,0:T(8,128)(2,1)} fusion(bf16[512,12,64]{0,2,1:T(8,128)(2,1)S(1)} %bitcast.202, f32[12,512,512]{1,2,0:T(8,128)} %subtract_multiply_fusion, f32[12,512,512]{1,2,0:T(8,128)} %fusion.132, f32[12,512,512]{1,2,0:T(8,128)} %copy-done.28, f32[12,512]{1,0:T(8,128)S(1)} %copy-done.103, ...), kind=kOutput, calls=%fused_computation.105 | convolution fusion | flops 438049280 | bytes 39346688 | tf_op jit(solution)/shard_map/vmap(hqk,qhe->khe)/dot_general | solution.py:227
  496.1 7.7 outer.5
  510.0 2.9 pad_maximum_fusion.3.refs_4_.refs_5_
  513.0 8.0 %outer.4 = (bf16[16,48,1536]{2,1,0:T(8,128)(2,1)S(1)}, bf16[16,48,1536]{2,1,0:T(8,128)(2,1)}) custom-call(s32[16]{0:T(128)S(1)} %copy-done.26, s32[16]{0:T(128)S(1)} %copy-done.25, bf16[512,768]{1,0:T(8,128)(2,1)S(1)} %copy-done.21, bf16[512,768]{1,0:T(8,128)(2,1)S(1)} %copy-done.6, bf16[512,768]{1,0:T(8,128)(2,1)S(1)} %copy-done.6, ...), custom_call_target="tpu_custom_call" | custom-call | tf_op jit(solution)/shard_map/outer/pallas_call | solution.py:173
  522.0 4.0 collective-permute-done.22
  534.2 8.4 %collective-permute-done.23 = bf16[8,48,1536]{2,1,0:T(8,128)(2,1)} collective-permute-done((bf16[8,48,1536]{2,1,0:T(8,128)(2,1)S(1)}, bf16[8,48,1536]{2,1,0:T(8,128)(2,1)}, u32[]{:S(2)}, u32[]{:S(2)}) %collective-permute-start.23) | collective-permute-done | bytes 1179680 | tf_op jit(solution)/shard_map/ppermute | solution.py:68
  546.1 15.6 %collective-permute-done.28 = bf16[8,48,1536]{2,1,0:T(8,128)(2,1)} collective-permute-done((bf16[8,48,1536]{2,1,0:T(8,128)(2,1)}, bf16[8,48,1536]{2,1,0:T(8,128)(2,1)}, u32[]{:S(2)}, u32[]{:S(2)}) %collective-permute-start.28) | collective-permute-done | bytes 1179680 | tf_op jit(solution)/shard_map/ppermute | solution.py:68
  574.5 3.8 collective-permute-done.25
  579.9 4.7 add_convert_fusion.1
  586.1 4.0 add_convert_fusion.2
  592.5 2.6 collective-permute-start.31
  596.5 4.4 collective-permute-done.31
  602.1 11.7 %collective-permute-done.38 = bf16[8,48,3072]{2,1,0:T(8,128)(2,1)} collective-permute-done((bf16[8,48,3072]{2,1,0:T(8,128)(2,1)}, bf16[8,48,3072]{2,1,0:T(8,128)(2,1)}, u32[]{:S(2)}, u32[]{:S(2)}) %collective-permute-start.38) | collective-permute-done | bytes 2359328 | tf_op jit(solution)/shard_map/ppermute | solution.py:68
  613.7 3.6 add_convert_fusion.3
  618.8 32.9 %collective-permute-done.33 = bf16[8,48,3072]{2,1,0:T(8,128)(2,1)} collective-permute-done((bf16[8,48,3072]{2,1,0:T(8,128)(2,1)}, bf16[8,48,3072]{2,1,0:T(8,128)(2,1)}, u32[]{:S(2)}, u32[]{:S(2)}) %collective-permute-start.33) | collective-permute-done | bytes 2359328 | tf_op jit(solution)/shard_map/ppermute | solution.py:68
  651.7 3.6 add_convert_fusion.4
  663.5 8.1 %collective-permute-done.34 = bf16[4,48,3072]{2,1,0:T(8,128)(2,1)S(1)} collective-permute-done((bf16[4,48,3072]{2,1,0:T(8,128)(2,1)}, bf16[4,48,3072]{2,1,0:T(8,128)(2,1)S(1)}, u32[]{:S(2)}, u32[]{:S(2)}) %collective-permute-start.34) | collective-permute-done | bytes 1179680 | tf_op jit(solution)/shard_map/ppermute | solution.py:68
  677.4 3.0 collective-permute-start.41
  680.3 12.7 %collective-permute-done.35 = bf16[2,48,3072]{2,1,0:T(8,128)(2,1)S(1)} collective-permute-done((bf16[2,48,3072]{2,1,0:T(8,128)(2,1)S(1)}, bf16[2,48,3072]{2,1,0:T(8,128)(2,1)S(1)}, u32[]{:S(2)}, u32[]{:S(2)}) %collective-permute-start.35) | collective-permute-done | bytes 589856 | tf_op jit(solution)/shard_map/ppermute | solution.py:68
  696.0 11.0 %collective-permute-done.36 = bf16[1,48,3072]{2,1,0:T(8,128)(2,1)S(1)} collective-permute-done((bf16[1,48,3072]{2,1,0:T(8,128)(2,1)S(1)}, bf16[1,48,3072]{2,1,0:T(8,128)(2,1)S(1)}, u32[]{:S(2)}, u32[]{:S(2)}) %collective-permute-start.36) | collective-permute-done | bytes 294944 | tf_op jit(solution)/shard_map/ppermute | solution.py:68
  711.8 2.8 collective-permute-start.43
  723.8 5.3 convolution_add_fusion
  735.4 3.0 multiply_reduce_fusion.20
  743.4 6.5 slice.742
  751.0 5.1 maximum_select_fusion
  758.1 5.0 maximum_select_fusion.1
  763.6 3.3 collective-permute-done.55
  (593 shorter events, 225.1 us)
Async XLA Ops:
  2.8 27.4 %collective-permute-start = (bf16[1,48,1152]{2,1,0:T(8,128)(2,1)}, bf16[1,48,1152]{2,1,0:T(8,128)(2,1)}, u32[]{:S(2)}, u32[]{:S(2)}) collective-permute-start(bf16[1,48,1152]{2,1,0:T(8,128)(2,1)} %bitcast.93), channel_id=1, source_target_pairs={{0,16},{2,18},{4,20},{6,22},{8,24},{10,26},{12,28},{14,30},{16,0},... | collective-permute-start | bytes 331784 | tf_op jit(solution)/shard_map/ppermute | solution.py:68
  6.9 26.3 %collective-permute-start.10 = (bf16[1,48,1152]{2,1,0:T(8,128)(2,1)S(1)}, bf16[1,48,1152]{2,1,0:T(8,128)(2,1)}, u32[]{:S(2)}, u32[]{:S(2)}) collective-permute-start(bf16[1,48,1152]{2,1,0:T(8,128)(2,1)S(1)} %bitcast.209), channel_id=1, source_target_pairs={{0,16},{2,18},{4,20},{6,22},{8,24},{10,26},{12,28},{14,30},{16,0},... | collective-permute-start | bytes 331784 | tf_op jit(solution)/shard_map/ppermute | solution.py:68
  11.4 28.2 %collective-permute-start.5 = (bf16[1,48,3456]{2,1,0:T(8,128)(2,1)S(1)}, bf16[1,48,3456]{2,1,0:T(8,128)(2,1)}, u32[]{:S(2)}, u32[]{:S(2)}) collective-permute-start(bf16[1,48,3456]{2,1,0:T(8,128)(2,1)S(1)} %maximum_bitcast_fusion), channel_id=1, source_target_pairs={{0,16},{2,18},{4,20},{6,22},{8,24},{10,26},{12,28},{14,30},{16,0},... | collective-permute-start | bytes 995336 | tf_op jit(solution)/shard_map/ppermute | solution.py:68
  14.4 31.3 %collective-permute-start.15 = (bf16[1,48,3456]{2,1,0:T(8,128)(2,1)S(1)}, bf16[1,48,3456]{2,1,0:T(8,128)(2,1)S(1)}, u32[]{:S(2)}, u32[]{:S(2)}) collective-permute-start(bf16[1,48,3456]{2,1,0:T(8,128)(2,1)S(1)} %maximum_bitcast_fusion.1), channel_id=1, source_target_pairs={{0,16},{2,18},{4,20},{6,22},{8,24},{10,26},{12,28},{14,30},{16,0},... | collective-permute-start | bytes 995336 | tf_op jit(solution)/shard_map/ppermute | solution.py:68
  26.7 188.1 %copy-start.4 = (bf16[512,768]{1,0:T(8,128)(2,1)}, bf16[512,768]{1,0:T(8,128)(2,1)S(1)}, u32[]{:S(2)}) copy-start(bf16[512,768]{1,0:T(8,128)(2,1)S(1)} %constant_dynamic-slice_fusion.2.refs_3_) | copy-start | bytes 2359300
  29.6 206.8 %copy-start.99 = (f32[768]{0:T(1024)}, f32[768]{0:T(1024)S(1)}, u32[]{:S(2)}) copy-start(f32[768]{0:T(1024)S(1)} %get-tuple-element.86) | copy-start | bytes 9220
  31.2 19.3 %collective-permute-start.1 = (bf16[2,48,1152]{2,1,0:T(8,128)(2,1)S(1)}, bf16[2,48,1152]{2,1,0:T(8,128)(2,1)S(1)}, u32[]{:S(2)}, u32[]{:S(2)}) collective-permute-start(bf16[2,48,1152]{2,1,0:T(8,128)(2,1)S(1)} %pad_maximum_fusion.14), channel_id=1, source_target_pairs={{0,8},{2,10},{4,12},{6,14},{8,0},{10,2},{12,4},{14,6},{16,24},{18,... | collective-permute-start | bytes 663560 | tf_op jit(solution)/shard_map/ppermute | solution.py:68
  34.1 21.1 %collective-permute-start.11 = (bf16[2,48,1152]{2,1,0:T(8,128)(2,1)S(1)}, bf16[2,48,1152]{2,1,0:T(8,128)(2,1)S(1)}, u32[]{:S(2)}, u32[]{:S(2)}) collective-permute-start(bf16[2,48,1152]{2,1,0:T(8,128)(2,1)S(1)} %pad_maximum_fusion.15), channel_id=1, source_target_pairs={{0,8},{2,10},{4,12},{6,14},{8,0},{10,2},{12,4},{14,6},{16,24},{18,... | collective-permute-start | bytes 663560 | tf_op jit(solution)/shard_map/ppermute | solution.py:68
  40.7 28.8 %collective-permute-start.6 = (bf16[2,48,3456]{2,1,0:T(8,128)(2,1)S(1)}, bf16[2,48,3456]{2,1,0:T(8,128)(2,1)S(1)}, u32[]{:S(2)}, u32[]{:S(2)}) collective-permute-start(bf16[2,48,3456]{2,1,0:T(8,128)(2,1)S(1)} %pad_maximum_fusion.8), channel_id=1, source_target_pairs={{0,8},{2,10},{4,12},{6,14},{8,0},{10,2},{12,4},{14,6},{16,24},{18,... | collective-permute-start | bytes 1990664 | tf_op jit(solution)/shard_map/ppermute | solution.py:68
  45.9 58.7 %collective-permute-start.16 = (bf16[2,48,3456]{2,1,0:T(8,128)(2,1)S(1)}, bf16[2,48,3456]{2,1,0:T(8,128)(2,1)S(1)}, u32[]{:S(2)}, u32[]{:S(2)}) collective-permute-start(bf16[2,48,3456]{2,1,0:T(8,128)(2,1)S(1)} %pad_maximum_fusion.9), channel_id=1, source_target_pairs={{0,8},{2,10},{4,12},{6,14},{8,0},{10,2},{12,4},{14,6},{16,24},{18,... | collective-permute-start | bytes 1990664 | tf_op jit(solution)/shard_map/ppermute | solution.py:68
  51.5 21.4 %collective-permute-start.2 = (bf16[4,48,1152]{2,1,0:T(8,128)(2,1)S(1)}, bf16[4,48,1152]{2,1,0:T(8,128)(2,1)S(1)}, u32[]{:S(2)}, u32[]{:S(2)}) collective-permute-start(bf16[4,48,1152]{2,1,0:T(8,128)(2,1)S(1)} %pad_maximum_fusion.12), channel_id=1, source_target_pairs={{0,2},{2,0},{4,6},{6,4},{8,10},{10,8},{12,14},{14,12},{16,18},{18,... | collective-permute-start | bytes 1327112 | tf_op jit(solution)/shard_map/ppermute | solution.py:68
  56.2 19.4 %collective-permute-start.12 = (bf16[4,48,1152]{2,1,0:T(8,128)(2,1)S(1)}, bf16[4,48,1152]{2,1,0:T(8,128)(2,1)S(1)}, u32[]{:S(2)}, u32[]{:S(2)}) collective-permute-start(bf16[4,48,1152]{2,1,0:T(8,128)(2,1)S(1)} %pad_maximum_fusion.13), channel_id=1, source_target_pairs={{0,2},{2,0},{4,6},{6,4},{8,10},{10,8},{12,14},{14,12},{16,18},{18,... | collective-permute-start | bytes 1327112 | tf_op jit(solution)/shard_map/ppermute | solution.py:68
  70.6 29.9 %collective-permute-start.7 = (bf16[4,48,3456]{2,1,0:T(8,128)(2,1)S(1)}, bf16[4,48,3456]{2,1,0:T(8,128)(2,1)S(1)}, u32[]{:S(2)}, u32[]{:S(2)}) collective-permute-start(bf16[4,48,3456]{2,1,0:T(8,128)(2,1)S(1)} %pad_maximum_fusion.4), channel_id=1, source_target_pairs={{0,2},{2,0},{4,6},{6,4},{8,10},{10,8},{12,14},{14,12},{16,18},{18,... | collective-permute-start | bytes 3981320 | tf_op jit(solution)/shard_map/ppermute | solution.py:68
  74.0 35.9 %collective-permute-start.3 = (bf16[8,48,1152]{2,1,0:T(8,128)(2,1)S(1)}, bf16[8,48,1152]{2,1,0:T(8,128)(2,1)S(1)}, u32[]{:S(2)}, u32[]{:S(2)}) collective-permute-start(bf16[8,48,1152]{2,1,0:T(8,128)(2,1)S(1)} %pad_maximum_fusion.6), channel_id=1, source_target_pairs={{0,4},{2,6},{4,0},{6,2},{8,12},{10,14},{12,8},{14,10},{16,20},{18,... | collective-permute-start | bytes 2654216 | tf_op jit(solution)/shard_map/ppermute | solution.py:68
  76.6 32.3 %collective-permute-start.13 = (bf16[8,48,1152]{2,1,0:T(8,128)(2,1)S(1)}, bf16[8,48,1152]{2,1,0:T(8,128)(2,1)S(1)}, u32[]{:S(2)}, u32[]{:S(2)}) collective-permute-start(bf16[8,48,1152]{2,1,0:T(8,128)(2,1)S(1)} %pad_maximum_fusion.7), channel_id=1, source_target_pairs={{0,4},{2,6},{4,0},{6,2},{8,12},{10,14},{12,8},{14,10},{16,20},{18,... | collective-permute-start | bytes 2654216 | tf_op jit(solution)/shard_map/ppermute | solution.py:68
  101.8 47.2 %collective-permute-start.8 = (bf16[8,48,3456]{2,1,0:T(8,128)(2,1)S(1)}, bf16[8,48,3456]{2,1,0:T(8,128)(2,1)S(1)}, u32[]{:S(2)}, u32[]{:S(2)}) collective-permute-start(bf16[8,48,3456]{2,1,0:T(8,128)(2,1)S(1)} %pad_maximum_fusion), channel_id=1, source_target_pairs={{0,4},{2,6},{4,0},{6,2},{8,12},{10,14},{12,8},{14,10},{16,20},{18,... | collective-permute-start | bytes 7962632 | tf_op jit(solution)/shard_map/ppermute | solution.py:68
  104.8 32.1 %collective-permute-start.17 = (bf16[4,48,3456]{2,1,0:T(8,128)(2,1)S(1)}, bf16[4,48,3456]{2,1,0:T(8,128)(2,1)S(1)}, u32[]{:S(2)}, u32[]{:S(2)}) collective-permute-start(bf16[4,48,3456]{2,1,0:T(8,128)(2,1)S(1)} %pad_maximum_fusion.5), channel_id=1, source_target_pairs={{0,2},{2,0},{4,6},{6,4},{8,10},{10,8},{12,14},{14,12},{16,18},{18,... | collective-permute-start | bytes 3981320 | tf_op jit(solution)/shard_map/ppermute | solution.py:68
  109.9 75.8 %collective-permute-start.14 = (bf16[16,48,1152]{2,1,0:T(8,128)(2,1)}, bf16[16,48,1152]{2,1,0:T(8,128)(2,1)}, u32[]{:S(2)}, u32[]{:S(2)}) collective-permute-start(bf16[16,48,1152]{2,1,0:T(8,128)(2,1)} %constant_dynamic-update-slice_fusion.10.own), channel_id=1, source_target_pairs={{0,1},{1,0},{2,3},{3,2},{4,5},{5,4},{6,7},{7,6},{8,9},{9,8},{10,11... | collective-permute-start | bytes 5308424 | tf_op jit(solution)/shard_map/ppermute | solution.py:71
  110.1 43.2 %collective-permute-start.4 = (bf16[16,48,1152]{2,1,0:T(8,128)(2,1)S(1)}, bf16[16,48,1152]{2,1,0:T(8,128)(2,1)}, u32[]{:S(2)}, u32[]{:S(2)}) collective-permute-start(bf16[16,48,1152]{2,1,0:T(8,128)(2,1)S(1)} %constant_dynamic-update-slice_fusion.own), channel_id=1, source_target_pairs={{0,1},{1,0},{2,3},{3,2},{4,5},{5,4},{6,7},{7,6},{8,9},{9,8},{10,11... | collective-permute-start | bytes 5308424 | tf_op jit(solution)/shard_map/ppermute | solution.py:71
  138.6 59.1 %collective-permute-start.18 = (bf16[8,48,3456]{2,1,0:T(8,128)(2,1)}, bf16[8,48,3456]{2,1,0:T(8,128)(2,1)}, u32[]{:S(2)}, u32[]{:S(2)}) collective-permute-start(bf16[8,48,3456]{2,1,0:T(8,128)(2,1)} %pad_maximum_fusion.1), channel_id=1, source_target_pairs={{0,4},{2,6},{4,0},{6,2},{8,12},{10,14},{12,8},{14,10},{16,20},{18,... | collective-permute-start | bytes 7962632 | tf_op jit(solution)/shard_map/ppermute | solution.py:68
  150.8 50.4 %collective-permute-start.9 = (bf16[16,48,3456]{2,1,0:T(8,128)(2,1)}, bf16[16,48,3456]{2,1,0:T(8,128)(2,1)}, u32[]{:S(2)}, u32[]{:S(2)}) collective-permute-start(bf16[16,48,3456]{2,1,0:T(8,128)(2,1)} %constant_dynamic-update-slice_fusion.5.own), channel_id=1, source_target_pairs={{0,1},{1,0},{2,3},{3,2},{4,5},{5,4},{6,7},{7,6},{8,9},{9,8},{10,11... | collective-permute-start | bytes 15925256 | tf_op jit(solution)/shard_map/ppermute | solution.py:71
  201.1 64.0 %collective-permute-start.19 = (bf16[16,48,3456]{2,1,0:T(8,128)(2,1)}, bf16[16,48,3456]{2,1,0:T(8,128)(2,1)}, u32[]{:S(2)}, u32[]{:S(2)}) collective-permute-start(bf16[16,48,3456]{2,1,0:T(8,128)(2,1)} %constant_dynamic-update-slice_fusion.15.own), channel_id=1, source_target_pairs={{0,1},{1,0},{2,3},{3,2},{4,5},{5,4},{6,7},{7,6},{8,9},{9,8},{10,11... | collective-permute-start | bytes 15925256 | tf_op jit(solution)/shard_map/ppermute | solution.py:71
  239.3 39.5 %copy-start.34 = (f32[512,768]{1,0:T(8,128)}, f32[512,768]{1,0:T(8,128)S(1)}, u32[]{:S(2)}) copy-start(f32[512,768]{1,0:T(8,128)S(1)} %get-tuple-element.186) | copy-start | bytes 4718596
  494.1 85.8 %collective-permute-start.37 = (bf16[16,48,3072]{2,1,0:T(8,128)(2,1)}, bf16[16,48,3072]{2,1,0:T(8,128)(2,1)}, u32[]{:S(2)}, u32[]{:S(2)}) collective-permute-start(bf16[16,48,3072]{2,1,0:T(8,128)(2,1)} %get-tuple-element.45), channel_id=1, source_target_pairs={{0,1},{1,0},{2,3},{3,2},{4,5},{5,4},{6,7},{7,6},{8,9},{9,8},{10,11... | collective-permute-start | bytes 14155784 | tf_op jit(solution)/shard_map/ppermute | solution.py:71
  505.2 22.7 %collective-permute-start.27 = (bf16[16,48,1536]{2,1,0:T(8,128)(2,1)}, bf16[16,48,1536]{2,1,0:T(8,128)(2,1)}, u32[]{:S(2)}, u32[]{:S(2)}) collective-permute-start(bf16[16,48,1536]{2,1,0:T(8,128)(2,1)} %get-tuple-element.41), channel_id=1, source_target_pairs={{0,1},{1,0},{2,3},{3,2},{4,5},{5,4},{6,7},{7,6},{8,9},{9,8},{10,11... | collective-permute-start | bytes 7077896 | tf_op jit(solution)/shard_map/ppermute | solution.py:71
  521.0 4.9 collective-permute-start.22
  521.9 64.2 %collective-permute-start.32 = (bf16[16,48,3072]{2,1,0:T(8,128)(2,1)}, bf16[16,48,3072]{2,1,0:T(8,128)(2,1)}, u32[]{:S(2)}, u32[]{:S(2)}) collective-permute-start(bf16[16,48,3072]{2,1,0:T(8,128)(2,1)} %get-tuple-element.43), channel_id=1, source_target_pairs={{0,1},{1,0},{2,3},{3,2},{4,5},{5,4},{6,7},{7,6},{8,9},{9,8},{10,11... | collective-permute-start | bytes 14155784 | tf_op jit(solution)/shard_map/ppermute | solution.py:71
  526.3 16.4 %collective-permute-start.23 = (bf16[8,48,1536]{2,1,0:T(8,128)(2,1)S(1)}, bf16[8,48,1536]{2,1,0:T(8,128)(2,1)}, u32[]{:S(2)}, u32[]{:S(2)}) collective-permute-start(bf16[8,48,1536]{2,1,0:T(8,128)(2,1)S(1)} %add_convert_fusion.6), channel_id=1, source_target_pairs={{0,4},{2,6},{4,0},{6,2},{8,12},{10,14},{12,8},{14,10},{16,20},{18,... | collective-permute-start | bytes 3538952 | tf_op jit(solution)/shard_map/ppermute | solution.py:68
  530.5 31.1 %collective-permute-start.28 = (bf16[8,48,1536]{2,1,0:T(8,128)(2,1)}, bf16[8,48,1536]{2,1,0:T(8,128)(2,1)}, u32[]{:S(2)}, u32[]{:S(2)}) collective-permute-start(bf16[8,48,1536]{2,1,0:T(8,128)(2,1)} %add_convert_fusion.5), channel_id=1, source_target_pairs={{0,4},{2,6},{4,0},{6,2},{8,12},{10,14},{12,8},{14,10},{16,20},{18,... | collective-permute-start | bytes 3538952 | tf_op jit(solution)/shard_map/ppermute | solution.py:68
  533.2 31.5 %copy-start.78 = (f32[16896]{0:T(1024)S(1)}, f32[16896]{0:T(1024)}, u32[]{:S(2)}) copy-start(f32[16896]{0:T(1024)} %reshape.623) | copy-start | bytes 202756
  534.2 30.5 %collective-permute-start.47 = (f32[133,128]{1,0:T(8,128)S(1)}, f32[133,128]{1,0:T(8,128)S(1)}, u32[]{:S(2)}, u32[]{:S(2)}) collective-permute-start(f32[133,128]{1,0:T(8,128)S(1)} %fusion.77), channel_id=1, source_target_pairs={{0,1},{1,0},{2,3},{3,2},{4,5},{5,4},{6,7},{7,6},{8,9},{9,8},{10,11... | collective-permute-start | bytes 204296 | tf_op jit(solution)/shard_map/ppermute | solution.py:71
  542.7 43.4 %slice-start.3 = ((s8[4718592]{0:T(1024)(128)(4,1)}), s8[4194304]{0:T(1024)(128)(4,1)S(1)}, s32[]{:S(2)}) async-start(s8[4718592]{0:T(1024)(128)(4,1)} %bitcast.194), calls=%async_computation.3 | async-start | bytes 8388608
  544.5 22.5 %collective-permute-start.24 = (bf16[4,48,1536]{2,1,0:T(8,128)(2,1)S(1)}, bf16[4,48,1536]{2,1,0:T(8,128)(2,1)S(1)}, u32[]{:S(2)}, u32[]{:S(2)}) collective-permute-start(bf16[4,48,1536]{2,1,0:T(8,128)(2,1)S(1)} %add_convert_fusion.14), channel_id=1, source_target_pairs={{0,2},{2,0},{4,6},{6,4},{8,10},{10,8},{12,14},{14,12},{16,18},{18,... | collective-permute-start | bytes 1769480 | tf_op jit(solution)/shard_map/ppermute | solution.py:68
  563.1 9.9 %collective-permute-start.29 = (bf16[4,48,1536]{2,1,0:T(8,128)(2,1)S(1)}, bf16[4,48,1536]{2,1,0:T(8,128)(2,1)S(1)}, u32[]{:S(2)}, u32[]{:S(2)}) collective-permute-start(bf16[4,48,1536]{2,1,0:T(8,128)(2,1)S(1)} %add_convert_fusion.13), channel_id=1, source_target_pairs={{0,2},{2,0},{4,6},{6,4},{8,10},{10,8},{12,14},{14,12},{16,18},{18,... | collective-permute-start | bytes 1769480 | tf_op jit(solution)/shard_map/ppermute | solution.py:68
  565.4 145.3 %collective-permute-start.48 = (f32[133,128]{1,0:T(8,128)}, f32[133,128]{1,0:T(8,128)}, u32[]{:S(2)}, u32[]{:S(2)}) collective-permute-start(f32[133,128]{1,0:T(8,128)} %fusion.180), channel_id=1, source_target_pairs={{0,16},{2,18},{4,20},{6,22},{8,24},{10,26},{12,28},{14,30},{16,0},... | collective-permute-start | bytes 204296 | tf_op jit(solution)/shard_map/ppermute | solution.py:68
  568.2 10.1 %collective-permute-start.25 = (bf16[2,48,1536]{2,1,0:T(8,128)(2,1)S(1)}, bf16[2,48,1536]{2,1,0:T(8,128)(2,1)S(1)}, u32[]{:S(2)}, u32[]{:S(2)}) collective-permute-start(bf16[2,48,1536]{2,1,0:T(8,128)(2,1)S(1)} %add_convert_fusion.18), channel_id=1, source_target_pairs={{0,8},{2,10},{4,12},{6,14},{8,0},{10,2},{12,4},{14,6},{16,24},{18,... | collective-permute-start | bytes 884744 | tf_op jit(solution)/shard_map/ppermute | solution.py:68
  574.5 16.2 %collective-permute-start.30 = (bf16[2,48,1536]{2,1,0:T(8,128)(2,1)S(1)}, bf16[2,48,1536]{2,1,0:T(8,128)(2,1)S(1)}, u32[]{:S(2)}, u32[]{:S(2)}) collective-permute-start(bf16[2,48,1536]{2,1,0:T(8,128)(2,1)S(1)} %add_convert_fusion.17), channel_id=1, source_target_pairs={{0,8},{2,10},{4,12},{6,14},{8,0},{10,2},{12,4},{14,6},{16,24},{18,... | collective-permute-start | bytes 884744 | tf_op jit(solution)/shard_map/ppermute | solution.py:68
  579.5 15.6 %collective-permute-start.26 = (bf16[1,48,1536]{2,1,0:T(8,128)(2,1)S(1)}, bf16[1,48,1536]{2,1,0:T(8,128)(2,1)S(1)}, u32[]{:S(2)}, u32[]{:S(2)}) collective-permute-start(bf16[1,48,1536]{2,1,0:T(8,128)(2,1)S(1)} %add_convert_fusion.20), channel_id=1, source_target_pairs={{0,16},{2,18},{4,20},{6,22},{8,24},{10,26},{12,28},{14,30},{16,0},... | collective-permute-start | bytes 442376 | tf_op jit(solution)/shard_map/ppermute | solution.py:68
  584.6 29.2 %collective-permute-start.38 = (bf16[8,48,3072]{2,1,0:T(8,128)(2,1)}, bf16[8,48,3072]{2,1,0:T(8,128)(2,1)}, u32[]{:S(2)}, u32[]{:S(2)}) collective-permute-start(bf16[8,48,3072]{2,1,0:T(8,128)(2,1)} %add_convert_fusion.1), channel_id=1, source_target_pairs={{0,4},{2,6},{4,0},{6,2},{8,12},{10,14},{12,8},{14,10},{16,20},{18,... | collective-permute-start | bytes 7077896 | tf_op jit(solution)/shard_map/ppermute | solution.py:68
  590.1 61.5 %collective-permute-start.33 = (bf16[8,48,3072]{2,1,0:T(8,128)(2,1)}, bf16[8,48,3072]{2,1,0:T(8,128)(2,1)}, u32[]{:S(2)}, u32[]{:S(2)}) collective-permute-start(bf16[8,48,3072]{2,1,0:T(8,128)(2,1)} %add_convert_fusion.2), channel_id=1, source_target_pairs={{0,4},{2,6},{4,0},{6,2},{8,12},{10,14},{12,8},{14,10},{16,20},{18,... | collective-permute-start | bytes 7077896 | tf_op jit(solution)/shard_map/ppermute | solution.py:68
  592.5 8.4 %collective-permute-start.31 = (bf16[1,48,1536]{2,1,0:T(8,128)(2,1)}, bf16[1,48,1536]{2,1,0:T(8,128)(2,1)S(1)}, u32[]{:S(2)}, u32[]{:S(2)}) collective-permute-start(bf16[1,48,1536]{2,1,0:T(8,128)(2,1)} %add_convert_fusion.19), channel_id=1, source_target_pairs={{0,16},{2,18},{4,20},{6,22},{8,24},{10,26},{12,28},{14,30},{16,0},... | collective-permute-start | bytes 442376 | tf_op jit(solution)/shard_map/ppermute | solution.py:68
  596.5 60.4 %copy-start.79 = (f32[1,48,384]{2,1,0:T(8,128)}, f32[1,48,384]{2,1,0:T(8,128)S(1)}, u32[]{:S(2)}) copy-start(f32[1,48,384]{2,1,0:T(8,128)S(1)} %slice_bitcast_fusion.11) | copy-start | bytes 221188
  617.3 42.2 %collective-permute-start.39 = (bf16[4,48,3072]{2,1,0:T(8,128)(2,1)}, bf16[4,48,3072]{2,1,0:T(8,128)(2,1)S(1)}, u32[]{:S(2)}, u32[]{:S(2)}) collective-permute-start(bf16[4,48,3072]{2,1,0:T(8,128)(2,1)} %add_convert_fusion.3), channel_id=1, source_target_pairs={{0,2},{2,0},{4,6},{6,4},{8,10},{10,8},{12,14},{14,12},{16,18},{18,... | collective-permute-start | bytes 3538952 | tf_op jit(solution)/shard_map/ppermute | solution.py:68
  655.2 16.4 %collective-permute-start.34 = (bf16[4,48,3072]{2,1,0:T(8,128)(2,1)}, bf16[4,48,3072]{2,1,0:T(8,128)(2,1)S(1)}, u32[]{:S(2)}, u32[]{:S(2)}) collective-permute-start(bf16[4,48,3072]{2,1,0:T(8,128)(2,1)} %add_convert_fusion.4), channel_id=1, source_target_pairs={{0,2},{2,0},{4,6},{6,4},{8,10},{10,8},{12,14},{14,12},{16,18},{18,... | collective-permute-start | bytes 3538952 | tf_op jit(solution)/shard_map/ppermute | solution.py:68
  661.3 14.7 %collective-permute-start.40 = (bf16[2,48,3072]{2,1,0:T(8,128)(2,1)S(1)}, bf16[2,48,3072]{2,1,0:T(8,128)(2,1)S(1)}, u32[]{:S(2)}, u32[]{:S(2)}) collective-permute-start(bf16[2,48,3072]{2,1,0:T(8,128)(2,1)S(1)} %add_convert_fusion.11), channel_id=1, source_target_pairs={{0,8},{2,10},{4,12},{6,14},{8,0},{10,2},{12,4},{14,6},{16,24},{18,... | collective-permute-start | bytes 1769480 | tf_op jit(solution)/shard_map/ppermute | solution.py:68
  673.9 19.2 %collective-permute-start.35 = (bf16[2,48,3072]{2,1,0:T(8,128)(2,1)S(1)}, bf16[2,48,3072]{2,1,0:T(8,128)(2,1)S(1)}, u32[]{:S(2)}, u32[]{:S(2)}) collective-permute-start(bf16[2,48,3072]{2,1,0:T(8,128)(2,1)S(1)} %add_convert_fusion.12), channel_id=1, source_target_pairs={{0,8},{2,10},{4,12},{6,14},{8,0},{10,2},{12,4},{14,6},{16,24},{18,... | collective-permute-start | bytes 1769480 | tf_op jit(solution)/shard_map/ppermute | solution.py:68
  677.4 17.1 %collective-permute-start.41 = (bf16[1,48,3072]{2,1,0:T(8,128)(2,1)S(1)}, bf16[1,48,3072]{2,1,0:T(8,128)(2,1)S(1)}, u32[]{:S(2)}, u32[]{:S(2)}) collective-permute-start(bf16[1,48,3072]{2,1,0:T(8,128)(2,1)S(1)} %add_convert_fusion.15), channel_id=1, source_target_pairs={{0,16},{2,18},{4,20},{6,22},{8,24},{10,26},{12,28},{14,30},{16,0},... | collective-permute-start | bytes 884744 | tf_op jit(solution)/shard_map/ppermute | solution.py:68
  694.4 12.5 %collective-permute-start.36 = (bf16[1,48,3072]{2,1,0:T(8,128)(2,1)S(1)}, bf16[1,48,3072]{2,1,0:T(8,128)(2,1)S(1)}, u32[]{:S(2)}, u32[]{:S(2)}) collective-permute-start(bf16[1,48,3072]{2,1,0:T(8,128)(2,1)S(1)} %add_convert_fusion.16), channel_id=1, source_target_pairs={{0,16},{2,18},{4,20},{6,22},{8,24},{10,26},{12,28},{14,30},{16,0},... | collective-permute-start | bytes 884744 | tf_op jit(solution)/shard_map/ppermute | solution.py:68
  710.6 1.2 collective-permute-start.42
  711.6 4.7 collective-permute-start.49
  711.8 6.4 collective-permute-start.43
  716.4 4.4 collective-permute-start.50
  718.2 3.9 collective-permute-start.44
  720.8 9.0 %collective-permute-start.51 = (f32[133,128]{1,0:T(8,128)S(1)}, f32[133,128]{1,0:T(8,128)S(1)}, u32[]{:S(2)}, u32[]{:S(2)}) collective-permute-start(f32[133,128]{1,0:T(8,128)S(1)} %add.694), channel_id=1, source_target_pairs={{0,4},{2,6},{4,0},{6,2},{8,12},{10,14},{12,8},{14,10},{16,20},{18,... | collective-permute-start | bytes 204296 | tf_op jit(solution)/shard_map/ppermute | solution.py:68
  722.0 7.7 collective-permute-start.45
  729.1 21.9 %collective-permute-start.20 = (f32[512,768]{1,0:T(8,128)}, f32[512,768]{1,0:T(8,128)}, u32[]{:S(2)}, u32[]{:S(2)}) collective-permute-start(f32[512,768]{1,0:T(8,128)} %get-tuple-element.125), channel_id=1, source_target_pairs={{0,1},{1,0},{2,3},{3,2},{4,5},{5,4},{6,7},{7,6},{8,9},{9,8},{10,11... | collective-permute-start | bytes 4718600 | tf_op jit(solution)/shard_map/ppermute | solution.py:71
  729.2 28.9 %collective-permute-start.21 = (f32[512,768]{1,0:T(8,128)}, f32[512,768]{1,0:T(8,128)}, u32[]{:S(2)}, u32[]{:S(2)}) collective-permute-start(f32[512,768]{1,0:T(8,128)} %convolution_add_fusion), channel_id=1, source_target_pairs={{0,1},{1,0},{2,3},{3,2},{4,5},{5,4},{6,7},{7,6},{8,9},{9,8},{10,11... | collective-permute-start | bytes 4718600 | tf_op jit(solution)/shard_map/ppermute | solution.py:71
  729.7 3.7 collective-permute-start.46
  740.3 31.0 %copy-start.86 = (f32[2,48,384]{2,1,0:T(8,128)}, f32[2,48,384]{2,1,0:T(8,128)S(1)}, u32[]{:S(2)}) copy-start(f32[2,48,384]{2,1,0:T(8,128)S(1)} %get-tuple-element.97) | copy-start | bytes 442372
  743.4 6.5 collective-permute-start.52
  749.9 6.3 collective-permute-start.53
  756.3 6.9 collective-permute-start.54
  763.2 3.7 collective-permute-start.55
  766.9 3.6 collective-permute-start.56
  (132 other events, 1287.6 us)

commit v2 on v1

v2 whole, which is shorter than its diff:
```python
from functools import partial
import math

import jax
import jax.numpy as jnp
import numpy as np
from jax import lax
from jax.experimental import pallas as pl
from jax.experimental.pallas import tpu as pltpu
from jax.sharding import PartitionSpec as P

D = 768
HEADS = 12
FF = 3072


beta_one = 0.9
beta_two = 0.999
adam_eps = 1e-06
decay_rate = 0.01
matrix_rate = 1.0
vector_rate = 0.3
clip_norm = 1.0
step_count = 10.0
norm_eps = 1e-06
masked_score = -1e30

f32 = jnp.float32
bf16 = jnp.bfloat16


def layer_norm(values, norm_gain, norm_shift):
    average = jnp.mean(values, axis=-1, keepdims=True)
    centered = values - average
    variance = jnp.mean(centered * centered, axis=-1, keepdims=True)
    return centered * lax.rsqrt(variance + norm_eps) * norm_gain + norm_shift


def split_vector(packed):
    bounds = [0, D, 2 * D, 2 * D + FF, 3 * D + FF, 4 * D + FF, 5 * D + FF, 6 * D + FF, 7 * D + FF]
    return [packed[bounds[place] : bounds[place + 1]] for place in range(8)]


class Links:
    def __init__(self, parts):
        self.parts = parts
        count = parts.bit_length() - 1
        high = list(range(count - 1, -1, -1))
        other = high[:-2] + high[-2:][::-1]
        self.orders = (other, high)
        self.masks = np.zeros((2, parts), np.int32)
        self.inverse = np.zeros((2, parts), np.int32)
        for core in range(2):
            for place in range(parts):
                mask = 0
                for stage in range(count):
                    if (place >> stage) & 1:
                        mask |= 1 << self.orders[core][stage]
                self.masks[core, place] = mask
                self.inverse[core, mask] = place
        self.stages = count
        self.last = ()

    def swap(self, value, stage):
        pairs = []
        for core in range(2):
            flip = 1 << self.orders[core][stage]
            pairs += [(2 * at + core, 2 * (at ^ flip) + core) for at in range(self.parts)]
        return lax.ppermute(value, ("dp", "tensor"), pairs)

    def sibling(self, value):
        return lax.ppermute(value, "tensor", [(0, 1), (1, 0)])

    def gather(self, share):
        return {"held": share[None], "stage": 0}

    def scatter(self, own, other):
        return {"pieces": [own], "other": other, "size": self.parts, "stage": self.stages}

    def advance(self, moves, rest=()):
        moves = [move for move in moves if self.running(move)]
        if not moves:
            return rest
        mine, rest, self.last = lax.optimization_barrier(
            ([move.get("held", move.get("pieces")) for move in moves], rest, self.last)
        )
        sending = []
        for move, value in zip(moves, mine):
            if "held" in move:
                come = move.pop("come", None)
                sending.append(value if come is None else jnp.concatenate([value, come], axis=0))
            elif "other" in move:
                sending.append(move["other"])
            else:
                half, size = move["size"] // 2, move["size"]
                move["pieces"] = value + move.pop("come")
                sending.append(sum(piece[half:size].astype(f32) for piece in move["pieces"]).astype(bf16))
        sending, rest, _ = lax.optimization_barrier((sending, rest, self.last))
        self.last = sending[0]
        for move, value in zip(moves, sending):
            if "held" in move:
                if move["stage"] < self.stages:
                    move["held"] = value
                    move["come"] = self.swap(value, move["stage"])
                else:
                    move["pair"] = (value, self.sibling(value), 0)
                    del move["held"]
                move["stage"] += 1
            elif "other" in move:
                move["come"] = [self.sibling(value)]
                del move["other"]
            else:
                move["size"] //= 2
                move["stage"] -= 1
                move["come"] = [self.swap(value, move["stage"])]
        return rest

    def running(self, move):
        return "held" in move or move.get("size", 1) > 1

    def finish(self, moves):
        for move in moves:
            while self.running(move):
                self.advance([move])
        return [sum(piece[0].astype(f32) for piece in move["pieces"] + move["come"]) for move in moves]

    def total(self, value):
        value = value + self.sibling(value)
        for stage in range(self.stages):
            value = value + self.swap(value, stage)
        return value


def dot_nt(left, right):
    return lax.dot_general(left, right, (((1,), (1,)), ((), ())), preferred_element_type=f32)


def dot_nn(left, right):
    return jnp.dot(left, right, preferred_element_type=f32)


def in_order(blocks, place_of):
    some = (0,) if len(blocks.shape) == 4 else ()
    return jnp.concatenate([blocks[(place_of[block], *some)] for block in range(blocks.shape[0])], axis=0)


def put_blocks(out, at, product, place_of):
    parts, _, rows, _ = out.shape
    for block in range(parts):
        out[place_of[block], at] = product[block * rows : (block + 1) * rows]


def norm_parts(values):
    centered = values - jnp.mean(values, axis=1, keepdims=True)
    variance = jnp.mean(centered * centered, axis=1, keepdims=True)
    scale = lax.rsqrt(variance + norm_eps)
    return centered * scale, scale


def norm_backward(values, gain, grad):
    unit, scale = norm_parts(values)
    scaled = grad * gain
    inner = scaled - jnp.mean(scaled, axis=1, keepdims=True)
    result = scale * (inner - unit * jnp.mean(scaled * unit, axis=1, keepdims=True))
    return result, jnp.sum(grad * unit, axis=0, keepdims=True), jnp.sum(grad, axis=0, keepdims=True)


def project_kernel(own_at, other_at, own_to, other_to, rows_in, own, other, bias, out):
    width = own.shape[-1]
    for half, (blocks, place_of) in enumerate(((own, own_at), (other, other_at))):
        weight = in_order(blocks, place_of)
        span = slice(half * width, (half + 1) * width)
        out[:, span] = (dot_nn(rows_in[...], weight) + bias[:, span]).astype(bf16)


def cost(microseconds):
    return pl.CostEstimate(flops=0, bytes_accessed=int(microseconds * 2.5e6), transcendentals=0)


def call(kernel, places, grid, ins, outs, scratch=(), name=None, time=1):
    spec = lambda block, index: pl.BlockSpec(block, lambda i, *at: index(i, at))
    return pl.pallas_call(
        kernel,
        out_shape=[jax.ShapeDtypeStruct(shape, kind) for shape, kind, _, _ in outs],
        grid_spec=pltpu.PrefetchScalarGridSpec(
            num_scalar_prefetch=4,
            grid=(grid,),
            in_specs=[spec(block, index) for _, block, index in ins],
            out_specs=[spec(block, index) for _, _, block, index in outs],
            scratch_shapes=list(scratch),
        ),
        compiler_params=pltpu.CompilerParams(
            dimension_semantics=("arbitrary",), vmem_limit_bytes=60 << 20
        ),
        cost_estimate=cost(time),
        name=name,
    )(*places, *[array for array, _, _ in ins])


def whole(array):
    return (array, array.shape, lambda i, at: (0,) * array.ndim)


def weight_tiles(pair, tile, count=1):
    own, other, first = pair
    tiles = []
    for half, array in enumerate((own, other)):
        parts, rows = array.shape[0], array.shape[-2]
        column = lambda i: first // tile + jnp.clip(i, 0, count - 1)
        if array.ndim == 3:
            tiles.append((array, (parts, rows, tile), lambda i, at: (0, 0, column(i))))
        else:
            index = lambda i, at, half=half, parts=parts: (0, at[half][parts], 0, column(i))
            tiles.append((array, (parts, 1, rows, tile), index))
    return tiles


def project(places, rows_in, pair, bias):
    rows = rows_in.shape[0]
    half = D // 2
    return call(
        project_kernel, places, 3,
        [whole(rows_in), *weight_tiles(pair, half, 3), (bias, (1, D), lambda i, at: (0, i))],
        [((rows, 3 * D), bf16, (rows, D), lambda i, at: (0, i))],
        name="project",
        time=7,
    )[0]


def feed_forward_kernel(
    own_at, other_at, own_to, other_to, hidden, context, out_own, out_other, up_own, up_other, down_own, down_other,
    bias_up, vectors, first_in, first_low, active, slope, second_in, hidden_new, hidden_low, first_out, total,
):
    step = pl.program_id(0)
    halves = ((own_at, up_own, down_own), (other_at, up_other, down_other))
    half_d = D // 2

    @pl.when(step == 0)
    def _():
        attended = dot_nt(context[:, :half_d], in_order(out_own, own_at))
        attended += dot_nt(context[:, half_d:], in_order(out_other, other_at))
        values = hidden[...].astype(f32) + attended + vectors[0:1]
        first_in[...] = values
        unit, _ = norm_parts(values)
        values = unit * vectors[1:2] + vectors[2:3]
        first_out[...] = values
        first_low[...] = values.astype(bf16)
        total[...] = values + vectors[3:4]

    for half, (place_of, up, down) in enumerate(halves):
        before = dot_nn(first_low[...], in_order(up, place_of)) + bias_up[half]
        shade = 0.5 * (1.0 + lax.erf(before * (1.0 / math.sqrt(2.0))))
        bell = jnp.exp(-0.5 * before * before) * (1.0 / math.sqrt(2.0 * math.pi))
        low = (before * shade).astype(bf16)
        active[half] = low
        slope[half] = shade + before * bell
        total[...] += dot_nt(low, in_order(down, place_of))

    @pl.when(step == pl.num_programs(0) - 1)
    def _():
        values = total[...]
        second_in[...] = values
        unit, _ = norm_parts(values)
        values = unit * vectors[4:5] + vectors[5:6]
        hidden_new[...] = values
        hidden_low[...] = values.astype(bf16)


def feed_forward(places, hidden, context, out_pair, up_pair, down_pair, bias_up, vectors, tile=384):
    rows = hidden.shape[0]
    half_ff = bias_up.shape[2]
    count = half_ff // tile
    flat = lambda kind: ((rows, D), kind, (rows, D), lambda i, at: (0, 0))
    tiled = lambda kind: ((2, rows, half_ff), kind, (2, rows, tile), lambda i, at: (0, 0, i))
    return call(
        feed_forward_kernel, places, count,
        [
            whole(hidden),
            whole(context),
            *weight_tiles(out_pair, D // 2),
            *weight_tiles(up_pair, tile, count),
            *weight_tiles(down_pair, tile, count),
            (bias_up, (2, 1, tile), lambda i, at: (0, 0, i)),
            whole(vectors),
        ],
        [flat(f32), flat(bf16), tiled(bf16), tiled(f32), flat(f32), flat(f32), flat(bf16)],
        [pltpu.VMEM((rows, D), f32), pltpu.VMEM((rows, D), f32)],
        name="feed_forward",
        time=18,
    )


def feed_backward_kernel(
    own_at, other_at, own_to, other_to, grad, second_in, first_low, active, slope,
    up_own, up_other, down_own, down_other, vectors, grads_own, grads_other, bias_grads, total,
    small, down_low, down_turned, first_turned,
):
    step = pl.program_id(0)
    halves = (
        (own_at, own_to, up_own, down_own, grads_own),
        (other_at, other_to, up_other, down_other, grads_other),
    )

    @pl.when(step == 0)
    def _():
        result, gain_grad, shift_grad = norm_backward(second_in[...], vectors[4:5], grad[...])
        small[...] = jnp.zeros_like(small)
        small[0:1] = jnp.sum(result, axis=0, keepdims=True)
        small[1:2] = gain_grad
        small[2:3] = shift_grad
        low = result.astype(bf16)
        down_low[...] = low
        down_turned[...] = low.T
        first_turned[...] = first_low[...].T
        total[...] = result

    for half, (place_of, place_to, up, down, grads) in enumerate(halves):
        act_grad = dot_nn(down_low[...], in_order(down, place_of))
        before_grad = act_grad * slope[half]
        bias_grads[half] = jnp.broadcast_to(jnp.sum(before_grad, axis=0, keepdims=True), bias_grads.shape[1:])
        low = before_grad.astype(bf16)
        put_blocks(grads, 0, dot_nn(down_turned[...], active[half]).astype(bf16), place_to)
        put_blocks(grads, 1, dot_nn(first_turned[...], low).astype(bf16), place_to)
        total[...] += dot_nt(low, in_order(up, place_of))


def context_backward_kernel(
    own_at, other_at, own_to, other_to, grad, first_in, out_own, out_other, vectors,
    first_in_grad, out_in_low, context_grad, small,
):
    half_d = D // 2
    result, gain_grad, shift_grad = norm_backward(first_in[...], vectors[1:2], grad[...])
    small[...] = jnp.zeros_like(small)
    small[0:1] = jnp.sum(result, axis=0, keepdims=True)
    small[1:2] = gain_grad
    small[2:3] = shift_grad
    first_in_grad[...] = result
    low = result.astype(bf16)
    out_in_low[...] = low
    context_grad[:, :half_d] = dot_nn(low, in_order(out_own, own_at)).astype(bf16)
    context_grad[:, half_d:] = dot_nn(low, in_order(out_other, other_at)).astype(bf16)


def context_backward(places, grad, first_in, out_pair, vectors):
    rows = grad.shape[0]
    flat = lambda kind: ((rows, D), kind, (rows, D), lambda i, at: (0, 0))
    return call(
        context_backward_kernel, places, 1,
        [
            whole(grad), whole(first_in),
            *weight_tiles(out_pair, D // 2),
            whole(vectors),
        ],
        [flat(f32), flat(bf16), flat(bf16), ((8, D), f32, (8, D), lambda i, at: (0, 0))],
        name="context_backward",
        time=6,
    )


def feed_backward(places, grad, kept, up_pair, down_pair, vectors, tile=384):
    second_in, first_low, active, slope = kept
    rows = grad.shape[0]
    half_ff = active.shape[2]
    count = half_ff // tile
    parts, block_rows = up_pair[0].shape[0], up_pair[0].shape[-2]
    tiled = lambda array: (array, (2, rows, tile), lambda i, at: (0, 0, i))
    grads = ((parts, 2, block_rows, half_ff), bf16, (parts, 2, block_rows, tile), lambda i, at: (0, 0, 0, i))
    return call(
        feed_backward_kernel, places, count,
        [
            whole(grad), whole(second_in), whole(first_low), tiled(active), tiled(slope),
            *weight_tiles(up_pair, tile, count),
            *weight_tiles(down_pair, tile, count),
            whole(vectors),
        ],
        [
            grads, grads,
            ((2, 8, half_ff), f32, (2, 8, tile), lambda i, at: (0, 0, i)),
            ((rows, D), f32, (rows, D), lambda i, at: (0, 0)),
            ((8, D), f32, (8, D), lambda i, at: (0, 0)),
        ],
        [pltpu.VMEM((rows, D), bf16), pltpu.VMEM((D, rows), bf16), pltpu.VMEM((D, rows), bf16)],
        name="feed_backward",
        time=22,
    )


def projection_grads_kernel(
    own_at, other_at, own_to, other_to, out_in_low, context, layer_input, head_grads,
    grads_own, grads_other, turned,
):
    step = pl.program_id(0)
    half_d = D // 2
    halves = ((own_to, grads_own), (other_to, grads_other))
    for when, left, right in (
        (step == 0, out_in_low, lambda span: context[:, span]),
        (step > 0, layer_input, lambda span: head_grads[0, :, span]),
    ):

        @pl.when(when)
        def _():
            @pl.when(step <= 1)
            def _():
                turned[...] = left[...].T

            for half, (place_to, grads) in enumerate(halves):
                span = slice(half * half_d, (half + 1) * half_d)
                put_blocks(grads, 0, dot_nn(turned[...], right(span)).astype(bf16), place_to)


def projection_grads(places, out_in_low, context, layer_input, head_grads, parts):
    rows = layer_input.shape[0]
    half = D // 2
    block_rows = D // parts
    grads = ((parts, 4, block_rows, half), bf16, (parts, 1, block_rows, half), lambda i, at: (0, i, 0, 0))
    return call(
        projection_grads_kernel, places, 4,
        [
            whole(out_in_low), whole(context), whole(layer_input),
            (head_grads, (1, rows, D), lambda i, at: (jnp.maximum(i - 1, 0), 0, 0)),
        ],
        [grads, grads],
        [pltpu.VMEM((D, rows), bf16)],
        name="projection_grads",
        time=9,
    )


def project_backward_kernel(
    own_at, other_at, own_to, other_to, head_grads, first_in_grad, own, other, input_grad
):
    half_d = D // 2

    @pl.when(pl.program_id(0) == 0)
    def _():
        input_grad[...] = first_in_grad[...]

    for half, (place_of, weight) in enumerate(((own_at, own), (other_at, other))):
        low = head_grads[0, :, half * half_d : (half + 1) * half_d]
        input_grad[...] += dot_nt(low, in_order(weight, place_of))


def project_backward(places, head_grads, first_in_grad, pair):
    rows = first_in_grad.shape[0]
    half = D // 2
    return call(
        project_backward_kernel, places, 3,
        [
            (head_grads, (1, rows, D), lambda i, at: (i, 0, 0)),
            whole(first_in_grad),
            *weight_tiles(pair, half, 3),
        ],
        [((rows, D), f32, (rows, D), lambda i, at: (0, 0))],
        name="project_backward",
        time=8,
    )[0]


def head_mask(width, scale):
    lane = lax.broadcasted_iota(jnp.int32, (1, 128), 1)
    return [jnp.where(lane // 64 == head, scale, 0.0).astype(bf16) for head in range(2)]

def attend_forward_kernel(lengths, *refs, depth):
    queries, keys, value_rows = refs[:depth], refs[depth:2*depth], refs[2*depth]
    context, log_norm = refs[2*depth+1:]
    length = lengths[pl.program_id(0)]
    key_all = [k[...] for k in keys]
    key_all = jnp.concatenate(key_all, axis=1) if depth>1 else key_all[0]
    turned = value_rows[...].T
    rows = key_all.shape[0]
    valid = lax.broadcasted_iota(jnp.int32, (rows, rows), 0) < length
    scaled = head_mask(64, 0.125)
    halves = []
    for head in range(2):
        query = [q[...] * scaled[head] for q in queries]
        query = jnp.concatenate(query, axis=1) if depth>1 else query[0]
        score = jnp.where(valid, dot_nt(key_all, query), masked_score)
        top = jnp.max(score, axis=0, keepdims=True)
        weight = jnp.exp(score - top)
        total = jnp.sum(weight, axis=0, keepdims=True)
        low = (weight * (1.0 / total)).astype(bf16)
        halves.append(jnp.dot(turned[64*head:64*head+64], low, preferred_element_type=f32))
        log_norm[0, head:head+1] = top + jnp.log(total)
    context[...] = jnp.concatenate(halves, axis=0).T.astype(bf16)

def attend_forward(lengths, projections, rows):
    depth=len(projections)
    seqs=lengths.shape[0]
    pairs=D//128
    col=lambda off: pl.BlockSpec((rows,128), lambda s,j,l,off=off:(s,off*pairs+j))
    return pl.pallas_call(
        partial(attend_forward_kernel, depth=depth),
        out_shape=[jax.ShapeDtypeStruct((seqs*rows,D),bf16), jax.ShapeDtypeStruct((seqs*pairs,8,rows),f32)],
        grid_spec=pltpu.PrefetchScalarGridSpec(num_scalar_prefetch=1, grid=(seqs,pairs),
            in_specs=[col(0)]*depth+[col(1)]*depth+[col(2)],
            out_specs=[pl.BlockSpec((rows,128),lambda s,j,l:(s,j)), pl.BlockSpec((1,8,rows),lambda s,j,l:(s*pairs+j,0,0))]),
        compiler_params=pltpu.CompilerParams(dimension_semantics=("arbitrary","arbitrary"),vmem_limit_bytes=48<<20),
        cost_estimate=cost(10),
        name="attend_forward",
    )(lengths, *projections, *projections, projections[0])

def attend_backward_kernel(lengths, *refs, depth, with_later, keep_total):
    queries, keys, value_rows = refs[:depth], refs[depth:2*depth], refs[2*depth]
    log_norm, context_grad = refs[2*depth+1:2*depth+3]
    at = 2*depth+3
    if with_later:
        later = refs[at]; at+=1
    grads, value_sum = refs[at:at+2]
    if keep_total: total_out = refs[at+2]
    length = lengths[pl.program_id(0)]
    key_all = [k[...] for k in keys]
    key_all = jnp.concatenate(key_all, axis=1) if depth>1 else key_all[0]
    rows = key_all.shape[0]
    valid = lax.broadcasted_iota(jnp.int32, (rows, rows), 0) < length
    scaled = head_mask(64, 0.125)
    plain = head_mask(64, 1.0)
    key_turned = (keys[0][...] * 0.125).astype(bf16).T
    query_halves = []
    key_grad = value_grad = None
    for head in range(2):
        query = [q[...] * scaled[head] for q in queries]
        query_own = query[0]
        query = jnp.concatenate(query, axis=1) if depth>1 else query[0]
        score = jnp.where(valid, dot_nt(key_all, query), masked_score)
        soft = jnp.exp(score - log_norm[0, head:head+1])
        grad_rows = context_grad[...] * plain[head]
        soft_grad = dot_nt(value_rows[...], grad_rows)
        product = soft * soft_grad
        total = product - soft * jnp.sum(product, axis=0, keepdims=True)
        if with_later: total = total + later[head]
        if keep_total: total_out[head] = total
        low = total.astype(bf16)
        query_halves.append(jnp.dot(key_turned[64*head:64*head+64], low, preferred_element_type=f32))
        kg = jnp.dot(low, query_own, preferred_element_type=f32)
        vg = jnp.dot(soft.astype(bf16), grad_rows, preferred_element_type=f32)
        key_grad = kg if key_grad is None else key_grad+kg
        value_grad = vg if value_grad is None else value_grad+vg
    grads[0] = jnp.concatenate(query_halves, axis=0).T.astype(bf16)
    grads[1] = key_grad.astype(bf16)
    grads[2] = value_grad.astype(bf16)
    sums = jnp.sum(value_grad, axis=0, keepdims=True)
    value_sum[0] = jnp.broadcast_to(sums, (8,128))

def attend_backward(lengths, projections, log_norm, context_grad, later, keep_total, rows):
    depth=len(projections)
    seqs=lengths.shape[0]
    pairs=D//128
    col=lambda off: pl.BlockSpec((rows,128), lambda s,j,l,off=off:(s,off*pairs+j))
    square=pl.BlockSpec((2,rows,rows),lambda s,j,l:(s*pairs+j,0,0))
    in_specs=[col(0)]*depth+[col(1)]*depth+[col(2)]+[pl.BlockSpec((1,8,rows),lambda s,j,l:(s*pairs+j,0,0)), col(0)]
    args=[*projections,*projections,projections[0],log_norm,context_grad]
    if later is not None:
        in_specs.append(square); args.append(later)
    out_shape=[jax.ShapeDtypeStruct((3,seqs*rows,D),bf16), jax.ShapeDtypeStruct((seqs,8,D),f32)]
    out_specs=[pl.BlockSpec((3,rows,128),lambda s,j,l:(0,s,j)), pl.BlockSpec((1,8,128),lambda s,j,l:(s,0,j))]
    if keep_total:
        out_shape.append(jax.ShapeDtypeStruct((seqs*pairs*2,rows,rows),f32)); out_specs.append(square)
    return pl.pallas_call(
        partial(attend_backward_kernel, depth=depth, with_later=later is not None, keep_total=keep_total),
        out_shape=out_shape,
        grid_spec=pltpu.PrefetchScalarGridSpec(num_scalar_prefetch=1, grid=(seqs,pairs), in_specs=in_specs, out_specs=out_specs),
        compiler_params=pltpu.CompilerParams(dimension_semantics=("arbitrary","arbitrary"),vmem_limit_bytes=48<<20),
        cost_estimate=cost(17),
        name="attend_backward",
    )(lengths,*args)


def adam_parts(gradient, first, second, factor):
    clipped = gradient * factor
    first_new = beta_one * first + (1.0 - beta_one) * clipped
    second_new = beta_two * second + (1.0 - beta_two) * clipped * clipped
    first_hat = first_new / (1.0 - beta_one**step_count)
    second_hat = second_new / (1.0 - beta_two**step_count)
    return (first_new, second_new, first_hat / (jnp.sqrt(second_hat) + adam_eps))


def local(
    tokens,
    cotangent,
    lengths,
    proj_weight,
    out_weight,
    up_weight,
    down_weight,
    small_params,
    proj_first,
    proj_second,
    out_first,
    out_second,
    up_first,
    up_second,
    down_first,
    down_second,
    small_first,
    small_second,
):
    layers = proj_weight.shape[0]
    seq_here = lengths.shape[0] // 2
    seq_len = tokens.shape[0] // lengths.shape[0]
    rows_here = seq_here * seq_len
    head_dim = D // HEADS
    half_d = proj_weight.shape[3]
    half_ff = up_weight.shape[2]
    row_count = proj_weight.shape[1]
    score_scale = 1.0 / math.sqrt(head_dim)
    core = lax.axis_index("tensor")
    parts = lax.axis_size("dp")
    links = Links(parts)
    at = lax.axis_index("dp")
    inverse = jnp.asarray(links.inverse)
    order = jnp.arange(parts, dtype=jnp.int32) ^ at
    own_at = inverse[core][order]
    other_at = inverse[1 - core][order]
    def with_half(places, half):
        return jnp.concatenate([places, half[None].astype(jnp.int32)])

    every = jnp.arange(parts, dtype=jnp.int32)
    exchanged = (own_at, other_at, own_at, other_at)
    in_turn = (with_half(every, core), with_half(every, 1 - core), own_at, other_at)
    turns = {(0, "proj"): exchanged, (0, "ff"): in_turn, (1, "proj"): in_turn, (1, "ff"): exchanged}

    table = {"proj": proj_weight, "out": out_weight, "up": up_weight, "down": down_weight}
    groups = [
        [(0, "proj")], [(0, "out"), (0, "up"), (0, "down")], [(1, "proj")], [(1, "out"), (1, "up"), (1, "down")],
    ]
    gathers = []
    for group in groups:
        share = [table[kind][layer_at].reshape(row_count, -1).astype(bf16) for layer_at, kind in group]
        gathers.append(links.gather(jnp.concatenate(share, axis=1) if len(share) > 1 else share[0]))
    one, two, three, four = gathers
    late = jnp.concatenate([two.pop("held")[0], three.pop("held")[0]], axis=1)
    late = lax.all_gather(late, ("dp", "tensor")).reshape(parts, 2, row_count, -1)
    two["pair"] = (late, late, 0)
    three["pair"] = (late, late, half_d + 2 * half_ff)

    def gathered(layer_at, kind):
        for group, move in zip(groups, gathers):
            widths = [math.prod(table[name].shape[2:]) for _, name in group]
            if (layer_at, kind) in group:
                while links.running(move):
                    links.advance([move])
                own, other, first = move["pair"]
                return own, other, first + sum(widths[: group.index((layer_at, kind))])

    def own_first(vector):
        half = vector.shape[-1] // 2
        return jnp.where(core == 0, vector, jnp.roll(vector, half, axis=-1))

    tokens = lax.dynamic_slice_in_dim(tokens, core * rows_here, rows_here)
    cotangent = lax.dynamic_slice_in_dim(cotangent, core * rows_here, rows_here)
    lengths = lax.dynamic_slice_in_dim(lengths, core * seq_here, seq_here)
    positions = jnp.arange(seq_len)
    key_valid = positions[None, :] < lengths[:, None]
    row_valid = key_valid.reshape(-1, 1)

    grad_rows = jnp.where(row_valid, cotangent.astype(f32), 0.0)
    vectors, value_bias, up_bias = [], [], []
    for layer_at in range(layers):
        bias_v, bias_o, bias_up, bias_down, gain_one, shift_one, gain_two, shift_two = split_vector(
            small_params[layer_at]
        )
        blank = jnp.zeros_like(bias_o)
        vectors.append(
            jnp.stack([bias_o, gain_one, shift_one, bias_down, gain_two, shift_two, blank, blank])
        )
        value_bias.append(jnp.concatenate([blank, blank, own_first(bias_v)])[None])
        up_bias.append(own_first(bias_up).reshape(2, 1, half_ff))
    masters = (proj_weight, out_weight, up_weight, down_weight)
    weight_square = jnp.stack(
        [jnp.sum(master * master, axis=tuple(range(1, master.ndim))) for master in masters], axis=1
    )

    links.advance([one])
    links.advance([one])
    links.advance([one])
    links.advance([one])
    prepared = (tokens, grad_rows, vectors, value_bias, up_bias, weight_square)
    (prepared,) = links.advance([four], (prepared,))
    tokens, grad_rows, vectors, value_bias, up_bias, weight_square = prepared
    (tokens,) = links.advance([one], (tokens,))

    saved = []
    hidden, hidden_low = tokens, tokens
    for layer_at in range(layers):
        places = turns[layer_at, "proj"]
        projected = project(places, hidden_low, gathered(layer_at, "proj"), value_bias[layer_at])
        if layer_at == 0:
            (projected,) = links.advance([four], (projected,))
        chain = [projected] + [earlier["projected"] for earlier in reversed(saved)]
        context, log_norm = attend_forward(lengths, chain, seq_len)
        if layer_at == 0:
            (context,) = links.advance([four], (context,))
            (context,) = links.advance([four], (context,))
        kept = {"layer_input": hidden_low, "projected": projected, "log_norm": log_norm, "context": context}
        (
            kept["first_in"], kept["first_low"], kept["active"], kept["slope"], kept["second_in"], hidden, hidden_low,
        ) = feed_forward(
            turns[layer_at, "ff"], hidden, context, gathered(layer_at, "out"),
            gathered(layer_at, "up"), gathered(layer_at, "down"), up_bias[layer_at], vectors[layer_at],
        )
        if layer_at == 0:
            (hidden_low,) = links.advance([four], (hidden_low,))
        saved.append(kept)

    sums = []
    smalls = [None] * layers
    later_total = None
    for layer_at in reversed(range(layers)):
        kept = saved[layer_at]
        places = turns[layer_at, "ff"]
        own, other, bias_sum, first_grad, second_small = feed_backward(
            places, grad_rows, [kept[name] for name in ("second_in", "first_low", "active", "slope")],
            gathered(layer_at, "up"), gathered(layer_at, "down"), vectors[layer_at],
        )
        ff_sum = links.scatter(own, other)
        (first_grad,) = links.advance(sums + [ff_sum], (first_grad,))
        first_in_grad, out_in_low, context_grad, first_small = context_backward(
            places, first_grad, kept["first_in"], gathered(layer_at, "out"), vectors[layer_at]
        )
        (context_grad,) = links.advance([ff_sum], (context_grad,))
        chain = [kept["projected"]] + [earlier["projected"] for earlier in reversed(saved[:layer_at])]
        results = attend_backward(
            lengths, chain, kept["log_norm"], context_grad, later_total, layer_at > 0, seq_len
        )
        head_grads, value_sum = results[:2]
        later_total = results[2] if layer_at > 0 else None
        (head_grads,) = links.advance(sums, (head_grads,))
        attention_sum = links.scatter(
            *projection_grads(exchanged, out_in_low, kept["context"], kept["layer_input"], head_grads, parts)
        )
        (head_grads,) = links.advance([ff_sum, attention_sum], (head_grads,))
        grad_rows = project_backward(turns[layer_at, "proj"], head_grads, first_in_grad, gathered(layer_at, "proj"))
        if layer_at > 0:
            (grad_rows,) = links.advance([attention_sum], (grad_rows,))
        sums += [ff_sum, attention_sum]
        smalls[layer_at] = jnp.concatenate(
            [
                own_first(jnp.sum(value_sum[:, 0], axis=0)),
                first_small[0],
                own_first(bias_sum[:, 0].reshape(-1)),
                second_small[0],
                first_small[1],
                first_small[2],
                second_small[1],
                second_small[2],
            ]
        )

    totals = links.finish(sums)[::-1]
    attention_sums, ff_sums = jnp.stack(totals[0::2]), jnp.stack(totals[1::2])
    grads = (
        attention_sums[:, 1:].transpose(0, 2, 1, 3), attention_sums[:, 0], ff_sums[:, 1], ff_sums[:, 0],
    )
    firsts = (proj_first, out_first, up_first, down_first)
    seconds = (proj_second, out_second, up_second, down_second)
    width = small_params.shape[1]
    pack = jnp.concatenate([jnp.stack(smalls), jnp.pad(weight_square, ((0, 0), (0, 124)))], axis=1)
    pack = links.total(pack)
    small_grad = pack[:, :width]
    weight_square = pack[:, width : width + 4].T

    square_part = sum(jnp.sum(grad * grad) for grad in grads)
    square_big = links.total(jnp.broadcast_to(square_part, (8, 128)))[0, 0]
    grad_norm = jnp.sqrt(square_big + jnp.sum(small_grad * small_grad))
    factor = clip_norm / jnp.maximum(grad_norm, clip_norm)
    moments = []
    updates = []
    for kind_at in range(4):
        first_new, second_new, direction = adam_parts(
            grads[kind_at], firsts[kind_at], seconds[kind_at], factor
        )
        moments.append((first_new, second_new))
        updates.append(direction + decay_rate * masters[kind_at])
    update_square = jnp.stack(
        [jnp.sum(update * update, axis=tuple(range(1, update.ndim))) for update in updates]
    )
    update_square = links.total(jnp.pad(update_square.reshape(1, -1), ((0, 7), (0, 128 - 4 * layers))))
    update_square = update_square[0, : 4 * layers].reshape(4, layers)
    ratio = jnp.sqrt(weight_square) / jnp.sqrt(update_square)

    gather_rows = partial(lax.all_gather, axis_name="tensor", axis=0, tiled=True)
    outputs = [gather_rows(hidden), gather_rows(grad_rows), grad_norm]
    for kind_at in range(4):
        master = masters[kind_at]
        scaled = ratio[kind_at].reshape((-1,) + (1,) * (master.ndim - 1))
        outputs += [
            moments[kind_at][0],
            moments[kind_at][1],
            master - matrix_rate * scaled * updates[kind_at],
        ]
    small_first_new, small_second_new, small_direction = adam_parts(
        small_grad, small_first, small_second, factor
    )
    outputs += [small_first_new, small_second_new, small_params - vector_rate * small_direction]
    return tuple(outputs)


def solution(mesh):
    proj = P(None, "dp", None, "tensor")
    matrix = P(None, "dp", "tensor")
    rows = P("dp", None)
    return jax.shard_map(
        local,
        mesh=mesh,
        in_specs=(rows, rows, P("dp"), proj, matrix, matrix, matrix, P())
        + (proj, proj)
        + (matrix,) * 6
        + (P(), P()),
        out_specs=(rows, rows, P()) + (proj,) * 3 + (matrix,) * 9 + (P(),) * 3,
        check_vma=False,
    )
```

time: 789 us -> 574 us (0.73)
  matrix products: 203 us -> 0 us
  Pallas kernels: 91.1 us -> 195 us
  other arithmetic: 131 us -> 72.9 us
  local copies, waits for them, and re-layouts: 76.4 us -> 29 us
  starting transfers between devices: 62.9 us -> 49.4 us
  between operations: 8.18 us -> 20.3 us
  waiting for transfers between devices: 208 us -> 197 us
    dot_general x28 -> x0, matrix products: 203 us -> none  [the longest x2 36.6 us: local(): jnp.einsum('td,df->tf', first_low, weights['up'], preferred_element_type=...]
    pallas_call x8 -> x16, Pallas kernels: 91.1 us -> 195 us  [the longest x12 141 us: call(): pl.pallas_call(kernel, out_shape=[jax.ShapeDtypeStruct(shape, kind) for s...]
    reshape x10 -> x0, local copies, waits for them, and re-layouts: 17.7 us -> none  [the longest x2 4.79 us: local(): query_grad.reshape(-1, D)]
    unnamed x304 -> x116, local copies, waits for them, and re-layouts: 27.4 us -> 14.1 us
    mul x2 -> x0, other arithmetic: 12.2 us -> none  [the longest x1 12.2 us: attend_backward(): soft * (soft_grad - jnp.sum(soft * soft_grad, axis=-1, keepdims=True))]
    ppermute x44 -> x36, waiting for transfers between devices: 204 us -> 192 us  [swap(): return lax.ppermute(value, ('dp', 'tensor'), pairs)]
    reduce_sum x17 -> x0, other arithmetic: 11.8 us -> none  [the longest x2 4.78 us: attend_forward(): row_sum = jnp.sum(exp_terms, axis=-1, keepdims=True)]
    ppermute x44 -> x36, starting transfers between devices: 59.2 us -> 48.5 us  [swap(): return lax.ppermute(value, ('dp', 'tensor'), pairs)]
  transfers between devices with their start and end apart: 57 -> 48, of which waited for: 26 -> 26; matrix products, arithmetic and copies ran while one was open for 27% -> 10% of each run, Pallas kernels for 7% -> 27%
where the time goes in v2:
time: 574 us; the launch traced here: 564 us
  waiting for transfers between devices  197 us (34%)
  Pallas kernels  195 us (34%)
  other arithmetic  72.9 us (13%)
  starting transfers between devices  49.4 us (9%)
  local copies, waits for them, and re-layouts  29 us (5%)
  between operations  20.3 us (4%)
    ppermute x36, waiting for transfers between devices, swap(): return lax.ppermute(value, ('dp', 'tensor'), pairs)  192 us
    pallas_call x12, Pallas kernels, call(): pl.pallas_call(kernel, out_shape=[jax.ShapeDtypeStruct(shape, kind) for s...  141 us
    ppermute x36, starting transfers between devices, swap(): return lax.ppermute(value, ('dp', 'tensor'), pairs)  48.5 us
    pallas_call x2, Pallas kernels, attend_backward(): pl.pallas_call(partial(attend_backward_kernel, depth=depth, with_later=la...  35.1 us
    convert_element_type x16, other arithmetic, advance(): sum((piece[half:size].astype(f32) for piece in move['pieces'])).astype(bf16)  32.5 us
    pallas_call x2, Pallas kernels, attend_forward(): pl.pallas_call(partial(attend_forward_kernel, depth=depth), out_shape=[ja...  19.6 us
    unnamed x116, local copies, waits for them, and re-layouts  14.1 us
  transfers between devices with their start and end apart: 48, of which 26 were waited for; matrix products, arithmetic and copies ran while one was open for 10% of the time, Pallas kernels for 27%

profile of v2, /device:TPU:0, one launch (start us, length us, event | category | flops | bytes accessed | tf_op | source)
XLA Modules:
  0.0 564.2 jit_solution(5676074500116179029)
XLA Ops:
  11.6 4.1 collective-permute-start
  23.6 7.5 %collective-permute-done.1 = bf16[2,48,1152]{2,1,0:T(8,128)(2,1)S(1)} collective-permute-done((bf16[2,48,1152]{2,1,0:T(8,128)(2,1)S(1)}, bf16[2,48,1152]{2,1,0:T(8,128)(2,1)S(1)}, u32[]{:S(2)}, u32[]{:S(2)}) %collective-permute-start.1) | collective-permute-done | bytes 221216 | tf_op jit(solution)/shard_map/ppermute | solution.py:69
  32.5 8.8 %collective-permute-done.2 = bf16[4,48,1152]{2,1,0:T(8,128)(2,1)S(1)} collective-permute-done((bf16[4,48,1152]{2,1,0:T(8,128)(2,1)S(1)}, bf16[4,48,1152]{2,1,0:T(8,128)(2,1)S(1)}, u32[]{:S(2)}, u32[]{:S(2)}) %collective-permute-start.2) | collective-permute-done | bytes 442400 | tf_op jit(solution)/shard_map/ppermute | solution.py:69
  43.9 16.9 %collective-permute-done.3 = bf16[8,48,1152]{2,1,0:T(8,128)(2,1)S(1)} collective-permute-done((bf16[8,48,1152]{2,1,0:T(8,128)(2,1)S(1)}, bf16[8,48,1152]{2,1,0:T(8,128)(2,1)S(1)}, u32[]{:S(2)}, u32[]{:S(2)}) %collective-permute-start.3) | collective-permute-done | bytes 884768 | tf_op jit(solution)/shard_map/ppermute | solution.py:69
  61.1 8.3 %collective-permute-start.5 = (bf16[1,48,3456]{2,1,0:T(8,128)(2,1)}, bf16[1,48,3456]{2,1,0:T(8,128)(2,1)}, u32[]{:S(2)}, u32[]{:S(2)}) collective-permute-start(bf16[1,48,3456]{2,1,0:T(8,128)(2,1)} %maximum_bitcast_fusion), channel_id=1, source_target_pairs={{0,16},{2,18},{4,20},{6,22},{8,24},{10,26},{12,28},{14,30},{16,0},... | collective-permute-start | bytes 995336 | tf_op jit(solution)/shard_map/ppermute | solution.py:69
  73.0 6.9 %project.2.refs_0_.refs_1_.refs_2_.refs_3_ = bf16[512,2304]{1,0:T(8,128)(2,1)} custom-call(s32[16]{0:T(128)} %gather_fusion, s32[16]{0:T(128)} %gather_fusion.1, s32[16]{0:T(128)} %gather_fusion, s32[16]{0:T(128)} %gather_fusion.1, bf16[512,768]{1,0:T(8,128)(2,1)} %constant_dynamic-slice_fusion.rows_in.hidden.layer_input, bf16[16,48,1152]{2,1,0:T(8,128)(2,1)} %copy-done.13, ...), custom_call_target="tpu_custom_call" | custom-call | bytes 17500000 | tf_op jit(solution)/shard_map/project/pallas_call | solution.py:182
  79.9 11.0 %collective-permute-done.5 = bf16[1,48,3456]{2,1,0:T(8,128)(2,1)} collective-permute-done((bf16[1,48,3456]{2,1,0:T(8,128)(2,1)}, bf16[1,48,3456]{2,1,0:T(8,128)(2,1)}, u32[]{:S(2)}, u32[]{:S(2)}) %collective-permute-start.5) | collective-permute-done | bytes 331808 | tf_op jit(solution)/shard_map/ppermute | solution.py:69
  93.8 9.5 %attend_forward.2 = (bf16[512,768]{1,0:T(8,128)(2,1)S(1)}, f32[6,8,512]{2,1,0:T(8,128)S(1)}) custom-call(s32[1]{0:T(128)} %dynamic_slice.18.lengths, bf16[512,2304]{1,0:T(8,128)(2,1)S(1)} %copy-done.2, bf16[512,2304]{1,0:T(8,128)(2,1)S(1)} %copy-done.2, bf16[512,2304]{1,0:T(8,128)(2,1)S(1)} %copy-done.2), custom_call_target="tpu_custom_call" | custom-call | bytes 25000000 | tf_op jit(solution)/shard_map/attend_forward/pallas_call | solution.py:491
  103.3 37.9 %collective-permute-done.6 = bf16[2,48,3456]{2,1,0:T(8,128)(2,1)S(1)} collective-permute-done((bf16[2,48,3456]{2,1,0:T(8,128)(2,1)S(1)}, bf16[2,48,3456]{2,1,0:T(8,128)(2,1)S(1)}, u32[]{:S(2)}, u32[]{:S(2)}) %collective-permute-start.6) | collective-permute-done | bytes 663584 | tf_op jit(solution)/shard_map/ppermute | solution.py:69
  142.7 16.5 %collective-permute-done.7 = bf16[4,48,3456]{2,1,0:T(8,128)(2,1)S(1)} collective-permute-done((bf16[4,48,3456]{2,1,0:T(8,128)(2,1)S(1)}, bf16[4,48,3456]{2,1,0:T(8,128)(2,1)S(1)}, u32[]{:S(2)}, u32[]{:S(2)}) %collective-permute-start.7) | collective-permute-done | bytes 1327136 | tf_op jit(solution)/shard_map/ppermute | solution.py:69
  159.5 1.8 collective-permute-start.8
  161.9 18.4 %feed_forward.2 = (f32[512,768]{1,0:T(8,128)}, bf16[512,768]{1,0:T(8,128)(2,1)}, bf16[2,512,1536]{2,1,0:T(8,128)(2,1)}, f32[2,512,1536]{2,1,0:T(8,128)}, f32[512...) custom-call(s32[17]{0:T(128)} %get-tuple-element.445.own_at, s32[17]{0:T(128)} %get-tuple-element.444.other_at, ...), custom_call_target="tpu_custom_call" | custom-call | bytes 45000000 | tf_op jit(solution)/shard_map/feed_forward/pallas_call | solution.py:182
  180.3 11.4 %collective-permute-done.8 = bf16[8,48,3456]{2,1,0:T(8,128)(2,1)} collective-permute-done((bf16[8,48,3456]{2,1,0:T(8,128)(2,1)S(1)}, bf16[8,48,3456]{2,1,0:T(8,128)(2,1)}, u32[]{:S(2)}, u32[]{:S(2)}) %collective-permute-start.8) | collective-permute-done | bytes 2654240 | tf_op jit(solution)/shard_map/ppermute | solution.py:69
  191.7 4.6 pad_maximum_fusion.out_own.up_own.down_own
  196.3 6.9 %project.3.refs_0_.refs_2_.refs_4_ = bf16[512,2304]{1,0:T(8,128)(2,1)} custom-call(s32[17]{0:T(128)} %get-tuple-element.445.own_at, s32[17]{0:T(128)} %get-tuple-element.444.other_at, s32[16]{0:T(128)} %gather_fusion, s32[16]{0:T(128)} %gather_fusion.1, bf16[512,768]{1,0:T(8,128)(2,1)} %get-tuple-element.223.rows_in.layer_input, ...), custom_call_target="tpu_custom_call" | custom-call | bytes 17500000 | tf_op jit(solution)/shard_map/project/pallas_call | solution.py:182
  204.9 10.1 %attend_forward.3 = (bf16[512,768]{1,0:T(8,128)(2,1)S(1)}, f32[6,8,512]{2,1,0:T(8,128)S(1)}) custom-call(s32[1]{0:T(128)} %dynamic_slice.18.lengths, bf16[512,2304]{1,0:T(8,128)(2,1)S(1)} %copy-done.5, bf16[512,2304]{1,0:T(8,128)(2,1)S(1)} %copy-done.3, bf16[512,2304]{1,0:T(8,128)(2,1)S(1)} %copy-done.5, bf16[512,2304]{1,0:T(8,128)(2,1)S(1)} %copy-done.3, ...), custom_call_target="tpu_custom_call" | custom-call | bytes 25000000 | tf_op jit(solution)/shard_map/attend_forward/pallas_call | solution.py:491
  215.9 19.3 %feed_forward.3 = (f32[512,768]{1,0:T(8,128)}, bf16[512,768]{1,0:T(8,128)(2,1)}, bf16[2,512,1536]{2,1,0:T(8,128)(2,1)}, f32[2,512,1536]{2,1,0:T(8,128)}, f32[512...) custom-call(s32[16]{0:T(128)} %gather_fusion, s32[16]{0:T(128)} %gather_fusion.1, s32[16]{0:T(128)} %gather_fusion, ...), custom_call_target="tpu_custom_call" | custom-call | bytes 45000000 | tf_op jit(solution)/shard_map/feed_forward/pallas_call | solution.py:182
  235.2 22.2 %feed_backward.2 = (bf16[16,2,48,1536]{3,2,1,0:T(8,128)(2,1)}, bf16[16,2,48,1536]{3,2,1,0:T(8,128)(2,1)}, f32[2,8,1536]{2,1,0:T(8,128)}, f32[512,768]{1,0:T(8,128)}, f32[8,768]{1,0:T(8,128)}) custom-call(s32[16]{0:T(128)} %gather_fusion, s32[16]{0:T(128)} %gather_fusion.1, s32[16]{0:T(128)} %gather_fusion, s32[16]{0:T(128)} %gather_fusion.1, ...), custom_call_target="tpu_custom_call" | custom-call | bytes 55000000 | tf_op jit(solution)/shard_map/feed_backward/pallas_call | solution.py:182
  257.8 5.9 %context_backward.2 = (f32[512,768]{1,0:T(8,128)}, bf16[512,768]{1,0:T(8,128)(2,1)}, bf16[512,768]{1,0:T(8,128)(2,1)}, f32[8,768]{1,0:T(8,128)}) custom-call(s32[16]{0:T(128)} %gather_fusion, s32[16]{0:T(128)} %gather_fusion.1, s32[16]{0:T(128)} %gather_fusion, s32[16]{0:T(128)} %gather_fusion.1, f32[512,768]{1,0:T(8,128)} %get-tuple-element.239.grad, ...), custom_call_target="tpu_custom_call" | custom-call | bytes 15000000 | tf_op jit(solution)/shard_map/context_backward/pallas_call | solution.py:182
  263.8 1.9 collective-permute-done.10
  265.7 3.1 add_convert_fusion.1
  268.8 1.8 collective-permute-start.11
  270.6 18.4 %attend_backward.2 = (bf16[3,512,768]{2,1,0:T(8,128)(2,1)S(1)}, f32[1,8,768]{2,1,0:T(8,128)S(1)}, f32[12,512,512]{2,1,0:T(8,128)}) custom-call(s32[1]{0:T(128)} %dynamic_slice.18.lengths, bf16[512,2304]{1,0:T(8,128)(2,1)S(1)} %copy-done.6, bf16[512,2304]{1,0:T(8,128)(2,1)} %project.2.refs_0_.refs_1_.refs_2_.refs_3_, bf16[512,2304]{1,0:T(8,128)(2,1)S(1)} %copy-done.6, ...), custom_call_target="tpu_custom_call" | custom-call | bytes 42500000 | tf_op jit(solution)/shard_map/attend_backward/pallas_call | solution.py:558
  290.4 8.7 %projection_grads.2 = (bf16[16,4,48,384]{3,2,1,0:T(8,128)(2,1)}, bf16[16,4,48,384]{3,2,1,0:T(8,128)(2,1)}) custom-call(s32[16]{0:T(128)} %gather_fusion, s32[16]{0:T(128)} %gather_fusion.1, s32[16]{0:T(128)} %gather_fusion, s32[16]{0:T(128)} %gather_fusion.1, bf16[512,768]{1,0:T(8,128)(2,1)} %get-tuple-element.241.out_in_low, bf16[512,768]{1,0:T(8,128)(2,1)} %copy-done.10, ...), custom_call_target="tpu_custom_call" | custom-call | bytes 22500000 | tf_op jit(solution)/shard_map/projection_grads/pallas_call | solution.py:182
  299.1 3.5 add_convert_fusion.5
  303.8 7.7 %project_backward.2.grad = f32[512,768]{1,0:T(8,128)} custom-call(s32[17]{0:T(128)} %get-tuple-element.445.own_at, s32[17]{0:T(128)} %get-tuple-element.444.other_at, s32[16]{0:T(128)} %gather_fusion, s32[16]{0:T(128)} %gather_fusion.1, bf16[3,512,768]{2,1,0:T(8,128)(2,1)} %copy-done.7, f32[512,768]{1,0:T(8,128)} %get-tuple-element.256.first_in_grad, ...), custom_call_target="tpu_custom_call" | custom-call | bytes 20000000 | tf_op jit(solution)/shard_map/project_backward/pallas_call | solution.py:182
  314.0 21.8 %feed_backward.3 = (bf16[16,2,48,1536]{3,2,1,0:T(8,128)(2,1)}, bf16[16,2,48,1536]{3,2,1,0:T(8,128)(2,1)}, f32[2,8,1536]{2,1,0:T(8,128)}, f32[512,768]{1,0:T(8,128)}, f32[8,768]{1,0:T(8,128)}) custom-call(s32[17]{0:T(128)} %get-tuple-element.445.own_at, s32[17]{0:T(128)} %get-tuple-element.444.other_at, s32[16]{0:T(128)} %gather_fusion, s32[16]{0:T(128)} %gather_fusion.1, ...), custom_call_target="tpu_custom_call" | custom-call | bytes 55000000 | tf_op jit(solution)/shard_map/feed_backward/pallas_call | solution.py:182
  335.8 2.7 add_convert_fusion.9
  338.5 2.3 add_convert_fusion.8
  340.8 5.9 %context_backward.3 = (f32[512,768]{1,0:T(8,128)}, bf16[512,768]{1,0:T(8,128)(2,1)}, bf16[512,768]{1,0:T(8,128)(2,1)}, f32[8,768]{1,0:T(8,128)}) custom-call(s32[17]{0:T(128)} %get-tuple-element.445.own_at, s32[17]{0:T(128)} %get-tuple-element.444.other_at, s32[16]{0:T(128)} %gather_fusion, s32[16]{0:T(128)} %gather_fusion.1, ...), custom_call_target="tpu_custom_call" | custom-call | bytes 15000000 | tf_op jit(solution)/shard_map/context_backward/pallas_call | solution.py:182
  346.8 2.3 collective-permute-done.15
  349.1 4.6 add_convert_fusion
  359.6 16.7 %attend_backward.3 = (bf16[3,512,768]{2,1,0:T(8,128)(2,1)S(1)}, f32[1,8,768]{2,1,0:T(8,128)S(1)}) custom-call(s32[1]{0:T(128)} %dynamic_slice.18.lengths, bf16[512,2304]{1,0:T(8,128)(2,1)S(1)} %copy-done.4, bf16[512,2304]{1,0:T(8,128)(2,1)S(1)} %copy-done.4, bf16[512,2304]{1,0:T(8,128)(2,1)S(1)} %copy-done.4, f32[6,8,512]{2,1,0:T(8,128)S(1)} %get-tuple-element.283.refs_3_, ...), custom_call_target="tpu_custom_call" | custom-call | bytes 42500000 | tf_op jit(solution)/shard_map/attend_backward/pallas_call | solution.py:558
  380.1 2.1 add_convert_fusion.13
  382.3 8.8 %projection_grads.3 = (bf16[16,4,48,384]{3,2,1,0:T(8,128)(2,1)}, bf16[16,4,48,384]{3,2,1,0:T(8,128)(2,1)}) custom-call(s32[16]{0:T(128)} %gather_fusion, s32[16]{0:T(128)} %gather_fusion.1, s32[16]{0:T(128)} %gather_fusion, s32[16]{0:T(128)} %gather_fusion.1, bf16[512,768]{1,0:T(8,128)(2,1)} %get-tuple-element.282.out_in_low, bf16[512,768]{1,0:T(8,128)(2,1)} %copy-done.9, ...), custom_call_target="tpu_custom_call" | custom-call | bytes 22500000 | tf_op jit(solution)/shard_map/projection_grads/pallas_call | solution.py:182
  391.0 2.6 add_convert_fusion.3
  398.5 2.1 collective-permute-start.19
  400.6 7.6 %collective-permute-done.19 = bf16[2,4,48,384]{3,2,1,0:T(8,128)(2,1)S(1)} collective-permute-done((bf16[2,4,48,384]{3,2,1,0:T(8,128)(2,1)S(1)}, bf16[2,4,48,384]{3,2,1,0:T(8,128)(2,1)S(1)}, u32[]{:S(2)}, u32[]{:S(2)}) %collective-permute-start.19) | collective-permute-done | bytes 294944 | tf_op jit(solution)/shard_map/ppermute | solution.py:69
  408.2 1.9 add_convert_fusion.15
  410.1 1.9 add_convert_fusion.7
  412.0 1.8 collective-permute-start.21
  413.9 13.3 %collective-permute-done.21 = bf16[2,2,48,1536]{3,2,1,0:T(8,128)(2,1)S(1)} collective-permute-done((bf16[2,2,48,1536]{3,2,1,0:T(8,128)(2,1)S(1)}, bf16[2,2,48,1536]{3,2,1,0:T(8,128)(2,1)S(1)}, u32[]{:S(2)}, u32[]{:S(2)}) %collective-permute-start.21) | collective-permute-done | bytes 589856 | tf_op jit(solution)/shard_map/ppermute | solution.py:69
  427.2 2.0 add_convert_fusion.11
  430.8 15.0 %collective-permute-done.23 = bf16[8,4,48,384]{3,2,1,0:T(8,128)(2,1)S(1)} collective-permute-done((bf16[8,4,48,384]{3,2,1,0:T(8,128)(2,1)S(1)}, bf16[8,4,48,384]{3,2,1,0:T(8,128)(2,1)S(1)}, u32[]{:S(2)}, u32[]{:S(2)}) %collective-permute-start.23) | collective-permute-done | bytes 1179680 | tf_op jit(solution)/shard_map/ppermute | solution.py:69
  447.4 2.6 collective-permute-start.29
  450.0 8.7 %collective-permute-done.36 = f32[2,8576]{1,0:T(2,128)S(1)} collective-permute-done((f32[2,8576]{1,0:T(2,128)S(1)}, f32[2,8576]{1,0:T(2,128)S(1)}, u32[]{:S(2)}, u32[]{:S(2)}) %collective-permute-start.36) | collective-permute-done | bytes 68640 | tf_op jit(solution)/shard_map/ppermute | solution.py:69
  459.4 4.2 collective-permute-start.27
  464.6 3.8 collective-permute-done.29
  469.8 8.1 %project_backward.3 = f32[512,768]{1,0:T(8,128)} custom-call(s32[16]{0:T(128)} %gather_fusion, s32[16]{0:T(128)} %gather_fusion.1, s32[16]{0:T(128)} %gather_fusion, s32[16]{0:T(128)} %gather_fusion.1, bf16[3,512,768]{2,1,0:T(8,128)(2,1)} %copy-done.8, f32[512,768]{1,0:T(8,128)} %get-tuple-element.306.first_in_grad, bf16[16,48,1152]{2,1,0:T(8,128)(2,1)} %copy-done.13, ...), custom_call_target="tpu_custom_call" | custom-call | bytes 20000000 | tf_op jit(solution)/shard_map/project_backward/pallas_call | solution.py:182
  480.7 3.0 collective-permute-start.26
  483.6 9.4 %collective-permute-done.28 = bf16[1,2,48,1536]{3,2,1,0:T(8,128)(2,1)S(1)} collective-permute-done((bf16[1,2,48,1536]{3,2,1,0:T(8,128)(2,1)S(1)}, bf16[1,2,48,1536]{3,2,1,0:T(8,128)(2,1)S(1)}, u32[]{:S(2)}, u32[]{:S(2)}) %collective-permute-start.28) | collective-permute-done | bytes 294944 | tf_op jit(solution)/shard_map/ppermute | solution.py:69
  504.4 3.1 collective-permute-done.38
  509.0 3.6 collective-permute-done.32
  513.4 2.8 collective-permute-done.33
  517.5 2.3 collective-permute-done.34
  521.8 2.0 multiply_reduce_fusion.9
  523.8 2.4 multiply_reduce_fusion.6
  526.2 1.9 multiply_reduce_fusion.1
  530.3 3.7 collective-permute-done.41
  534.0 3.6 collective-permute-done.42
  538.3 2.9 collective-permute-done.43
  541.8 1.9 multiply_subtract_fusion.4
  546.0 2.5 multiply_subtract_fusion
  551.4 1.7 copy.83
  (292 shorter events, 81.1 us)
Async XLA Ops:
  7.2 11.7 %copy-start = (bf16[1024,768]{1,0:T(8,128)(2,1)S(1)}, bf16[1024,768]{1,0:T(8,128)(2,1)}, u32[]{:S(2)}) copy-start(bf16[1024,768]{1,0:T(8,128)(2,1)} %param.19) | copy-start | bytes 4718596
  7.2 154.6 %all-gather.9.cloned.1.call-start = ((), (), s32[]{:S(2)}) async-start(), calls=%async_computation.2 | async-start | bytes 14598144 | tf_op jit(solution)/shard_map/all_gather | solution.py:632
  11.5 526.8 %all-gather.5.cloned.1.call-start = ((), (), s32[]{:S(2)}) async-start(), calls=%async_computation | async-start | bytes 4718592 | tf_op jit(solution)/shard_map/all_gather | solution.py:782
  11.6 9.5 %collective-permute-start = (bf16[1,48,1152]{2,1,0:T(8,128)(2,1)S(1)}, bf16[1,48,1152]{2,1,0:T(8,128)(2,1)S(1)}, u32[]{:S(2)}, u32[]{:S(2)}) collective-permute-start(bf16[1,48,1152]{2,1,0:T(8,128)(2,1)S(1)} %bitcast.118), channel_id=1, source_target_pairs={{0,16},{2,18},{4,20},{6,22},{8,24},{10,26},{12,28},{14,30},{16,0},... | collective-permute-start | bytes 331784 | tf_op jit(solution)/shard_map/ppermute | solution.py:69
  21.1 10.0 %collective-permute-start.1 = (bf16[2,48,1152]{2,1,0:T(8,128)(2,1)S(1)}, bf16[2,48,1152]{2,1,0:T(8,128)(2,1)S(1)}, u32[]{:S(2)}, u32[]{:S(2)}) collective-permute-start(bf16[2,48,1152]{2,1,0:T(8,128)(2,1)S(1)} %pad_maximum_fusion.9), channel_id=1, source_target_pairs={{0,8},{2,10},{4,12},{6,14},{8,0},{10,2},{12,4},{14,6},{16,24},{18,... | collective-permute-start | bytes 663560 | tf_op jit(solution)/shard_map/ppermute | solution.py:69
  31.2 10.1 %collective-permute-start.2 = (bf16[4,48,1152]{2,1,0:T(8,128)(2,1)S(1)}, bf16[4,48,1152]{2,1,0:T(8,128)(2,1)S(1)}, u32[]{:S(2)}, u32[]{:S(2)}) collective-permute-start(bf16[4,48,1152]{2,1,0:T(8,128)(2,1)S(1)} %pad_maximum_fusion.7), channel_id=1, source_target_pairs={{0,2},{2,0},{4,6},{6,4},{8,10},{10,8},{12,14},{14,12},{16,18},{18,... | collective-permute-start | bytes 1327112 | tf_op jit(solution)/shard_map/ppermute | solution.py:69
  41.4 28.0 %copy-start.48 = (s32[2,16]{1,0:T(2,128)S(1)}, s32[2,16]{1,0:T(2,128)}, u32[]{:S(2)}) copy-start(s32[2,16]{1,0:T(2,128)} %constant.41.clone) | copy-start | bytes 388
  41.4 19.4 %collective-permute-start.3 = (bf16[8,48,1152]{2,1,0:T(8,128)(2,1)S(1)}, bf16[8,48,1152]{2,1,0:T(8,128)(2,1)S(1)}, u32[]{:S(2)}, u32[]{:S(2)}) collective-permute-start(bf16[8,48,1152]{2,1,0:T(8,128)(2,1)S(1)} %pad_maximum_fusion.4), channel_id=1, source_target_pairs={{0,4},{2,6},{4,0},{6,2},{8,12},{10,14},{12,8},{14,10},{16,20},{18,... | collective-permute-start | bytes 2654216 | tf_op jit(solution)/shard_map/ppermute | solution.py:69
  61.0 10.8 %collective-permute-start.4 = (bf16[16,48,1152]{2,1,0:T(8,128)(2,1)S(1)}, bf16[16,48,1152]{2,1,0:T(8,128)(2,1)S(1)}, u32[]{:S(2)}, u32[]{:S(2)}) collective-permute-start(bf16[16,48,1152]{2,1,0:T(8,128)(2,1)S(1)} %pad_maximum_fusion.2.own), channel_id=1, source_target_pairs={{0,1},{1,0},{2,3},{3,2},{4,5},{5,4},{6,7},{7,6},{8,9},{9,8},{10,11... | collective-permute-start | bytes 5308424 | tf_op jit(solution)/shard_map/ppermute | solution.py:72
  61.1 29.8 %collective-permute-start.5 = (bf16[1,48,3456]{2,1,0:T(8,128)(2,1)}, bf16[1,48,3456]{2,1,0:T(8,128)(2,1)}, u32[]{:S(2)}, u32[]{:S(2)}) collective-permute-start(bf16[1,48,3456]{2,1,0:T(8,128)(2,1)} %maximum_bitcast_fusion), channel_id=1, source_target_pairs={{0,16},{2,18},{4,20},{6,22},{8,24},{10,26},{12,28},{14,30},{16,0},... | collective-permute-start | bytes 995336 | tf_op jit(solution)/shard_map/ppermute | solution.py:69
  71.8 19.1 %copy-start.28 = (bf16[1,48,3456]{2,1,0:T(8,128)(2,1)S(1)}, bf16[1,48,3456]{2,1,0:T(8,128)(2,1)}, u32[]{:S(2)}) copy-start(bf16[1,48,3456]{2,1,0:T(8,128)(2,1)} %maximum_bitcast_fusion) | copy-start | bytes 995332
  92.0 49.2 %collective-permute-start.6 = (bf16[2,48,3456]{2,1,0:T(8,128)(2,1)S(1)}, bf16[2,48,3456]{2,1,0:T(8,128)(2,1)S(1)}, u32[]{:S(2)}, u32[]{:S(2)}) collective-permute-start(bf16[2,48,3456]{2,1,0:T(8,128)(2,1)S(1)} %pad_maximum_fusion.5), channel_id=1, source_target_pairs={{0,8},{2,10},{4,12},{6,14},{8,0},{10,2},{12,4},{14,6},{16,24},{18,... | collective-permute-start | bytes 1990664 | tf_op jit(solution)/shard_map/ppermute | solution.py:69
  103.3 56.2 %copy-start.9 = (bf16[512,768]{1,0:T(8,128)(2,1)}, bf16[512,768]{1,0:T(8,128)(2,1)S(1)}, u32[]{:S(2)}) copy-start(bf16[512,768]{1,0:T(8,128)(2,1)S(1)} %get-tuple-element.215.context) | copy-start | bytes 2359300
  141.4 17.8 %collective-permute-start.7 = (bf16[4,48,3456]{2,1,0:T(8,128)(2,1)S(1)}, bf16[4,48,3456]{2,1,0:T(8,128)(2,1)S(1)}, u32[]{:S(2)}, u32[]{:S(2)}) collective-permute-start(bf16[4,48,3456]{2,1,0:T(8,128)(2,1)S(1)} %pad_maximum_fusion.3), channel_id=1, source_target_pairs={{0,2},{2,0},{4,6},{6,4},{8,10},{10,8},{12,14},{14,12},{16,18},{18,... | collective-permute-start | bytes 3981320 | tf_op jit(solution)/shard_map/ppermute | solution.py:69
  159.5 32.2 %collective-permute-start.8 = (bf16[8,48,3456]{2,1,0:T(8,128)(2,1)S(1)}, bf16[8,48,3456]{2,1,0:T(8,128)(2,1)}, u32[]{:S(2)}, u32[]{:S(2)}) collective-permute-start(bf16[8,48,3456]{2,1,0:T(8,128)(2,1)S(1)} %pad_maximum_fusion.1), channel_id=1, source_target_pairs={{0,4},{2,6},{4,0},{6,2},{8,12},{10,14},{12,8},{14,10},{16,20},{18,... | collective-permute-start | bytes 7962632 | tf_op jit(solution)/shard_map/ppermute | solution.py:69
  196.3 19.6 %collective-permute-start.9 = (bf16[16,48,3456]{2,1,0:T(8,128)(2,1)}, bf16[16,48,3456]{2,1,0:T(8,128)(2,1)}, u32[]{:S(2)}, u32[]{:S(2)}) collective-permute-start(bf16[16,48,3456]{2,1,0:T(8,128)(2,1)} %pad_maximum_fusion.out_own.up_own.down_own), channel_id=1, source_target_pairs={{0,1},{1,0},{2,3},{3,2},{4,5},{5,4},{6,7},{7,6},{8,9},{9,8},{10,11... | collective-permute-start | bytes 15925256 | tf_op jit(solution)/shard_map/ppermute | solution.py:72
  257.4 8.3 %collective-permute-start.10 = (bf16[16,2,48,1536]{3,2,1,0:T(8,128)(2,1)}, bf16[16,2,48,1536]{3,2,1,0:T(8,128)(2,1)}, u32[]{:S(2)}, u32[]{:S(2)}) collective-permute-start(bf16[16,2,48,1536]{3,2,1,0:T(8,128)(2,1)} %get-tuple-element.244), channel_id=1, source_target_pairs={{0,1},{1,0},{2,3},{3,2},{4,5},{5,4},{6,7},{7,6},{8,9},{9,8},{10,11... | collective-permute-start | bytes 14155784 | tf_op jit(solution)/shard_map/ppermute | solution.py:72
  268.8 30.3 %collective-permute-start.11 = (bf16[8,2,48,1536]{3,2,1,0:T(8,128)(2,1)S(1)}, bf16[8,2,48,1536]{3,2,1,0:T(8,128)(2,1)}, u32[]{:S(2)}, u32[]{:S(2)}) collective-permute-start(bf16[8,2,48,1536]{3,2,1,0:T(8,128)(2,1)S(1)} %add_convert_fusion.1), channel_id=1, source_target_pairs={{0,4},{2,6},{4,0},{6,2},{8,12},{10,14},{12,8},{14,10},{16,20},{18,... | collective-permute-start | bytes 7077896 | tf_op jit(solution)/shard_map/ppermute | solution.py:69
  302.6 8.8 %collective-permute-start.12 = (bf16[16,4,48,384]{3,2,1,0:T(8,128)(2,1)}, bf16[16,4,48,384]{3,2,1,0:T(8,128)(2,1)}, u32[]{:S(2)}, u32[]{:S(2)}) collective-permute-start(bf16[16,4,48,384]{3,2,1,0:T(8,128)(2,1)} %get-tuple-element.259), channel_id=1, source_target_pairs={{0,1},{1,0},{2,3},{3,2},{4,5},{5,4},{6,7},{7,6},{8,9},{9,8},{10,11... | collective-permute-start | bytes 7077896 | tf_op jit(solution)/shard_map/ppermute | solution.py:72
  302.6 33.2 %collective-permute-start.13 = (bf16[4,2,48,1536]{3,2,1,0:T(8,128)(2,1)}, bf16[4,2,48,1536]{3,2,1,0:T(8,128)(2,1)}, u32[]{:S(2)}, u32[]{:S(2)}) collective-permute-start(bf16[4,2,48,1536]{3,2,1,0:T(8,128)(2,1)} %add_convert_fusion.5), channel_id=1, source_target_pairs={{0,2},{2,0},{4,6},{6,4},{8,10},{10,8},{12,14},{14,12},{16,18},{18,... | collective-permute-start | bytes 3538952 | tf_op jit(solution)/shard_map/ppermute | solution.py:69
  313.0 25.5 %collective-permute-start.14 = (bf16[8,4,48,384]{3,2,1,0:T(8,128)(2,1)S(1)}, bf16[8,4,48,384]{3,2,1,0:T(8,128)(2,1)}, u32[]{:S(2)}, u32[]{:S(2)}) collective-permute-start(bf16[8,4,48,384]{3,2,1,0:T(8,128)(2,1)S(1)} %add_convert_fusion.4), channel_id=1, source_target_pairs={{0,4},{2,6},{4,0},{6,2},{8,12},{10,14},{12,8},{14,10},{16,20},{18,... | collective-permute-start | bytes 3538952 | tf_op jit(solution)/shard_map/ppermute | solution.py:69
  340.8 8.3 %collective-permute-start.15 = (bf16[16,2,48,1536]{3,2,1,0:T(8,128)(2,1)}, bf16[16,2,48,1536]{3,2,1,0:T(8,128)(2,1)}, u32[]{:S(2)}, u32[]{:S(2)}) collective-permute-start(bf16[16,2,48,1536]{3,2,1,0:T(8,128)(2,1)} %get-tuple-element.281), channel_id=1, source_target_pairs={{0,1},{1,0},{2,3},{3,2},{4,5},{5,4},{6,7},{7,6},{8,9},{9,8},{10,11... | collective-permute-start | bytes 14155784 | tf_op jit(solution)/shard_map/ppermute | solution.py:72
  346.8 12.8 %copy-start.11 = (bf16[512,768]{1,0:T(8,128)(2,1)S(1)}, bf16[512,768]{1,0:T(8,128)(2,1)}, u32[]{:S(2)}) copy-start(bf16[512,768]{1,0:T(8,128)(2,1)} %get-tuple-element.285.refs_4_) | copy-start | bytes 2359300
  353.7 37.3 %collective-permute-start.18 = (bf16[8,2,48,1536]{3,2,1,0:T(8,128)(2,1)}, bf16[8,2,48,1536]{3,2,1,0:T(8,128)(2,1)}, u32[]{:S(2)}, u32[]{:S(2)}) collective-permute-start(bf16[8,2,48,1536]{3,2,1,0:T(8,128)(2,1)} %add_convert_fusion), channel_id=1, source_target_pairs={{0,4},{2,6},{4,0},{6,2},{8,12},{10,14},{12,8},{14,10},{16,20},{18,... | collective-permute-start | bytes 7077896 | tf_op jit(solution)/shard_map/ppermute | solution.py:69
  355.8 182.6 %all-gather.7.cloned.1.call-start = ((), (), s32[]{:S(2)}) async-start(), calls=%async_computation.1 | async-start | bytes 4718592 | tf_op jit(solution)/shard_map/all_gather | solution.py:782
  358.5 19.3 %collective-permute-start.17 = (bf16[4,4,48,384]{3,2,1,0:T(8,128)(2,1)}, bf16[4,4,48,384]{3,2,1,0:T(8,128)(2,1)S(1)}, u32[]{:S(2)}, u32[]{:S(2)}) collective-permute-start(bf16[4,4,48,384]{3,2,1,0:T(8,128)(2,1)} %add_convert_fusion.8), channel_id=1, source_target_pairs={{0,2},{2,0},{4,6},{6,4},{8,10},{10,8},{12,14},{14,12},{16,18},{18,... | collective-permute-start | bytes 1769480 | tf_op jit(solution)/shard_map/ppermute | solution.py:69
  359.5 19.8 %collective-permute-start.16 = (bf16[2,2,48,1536]{3,2,1,0:T(8,128)(2,1)}, bf16[2,2,48,1536]{3,2,1,0:T(8,128)(2,1)S(1)}, u32[]{:S(2)}, u32[]{:S(2)}) collective-permute-start(bf16[2,2,48,1536]{3,2,1,0:T(8,128)(2,1)} %add_convert_fusion.9), channel_id=1, source_target_pairs={{0,8},{2,10},{4,12},{6,14},{8,0},{10,2},{12,4},{14,6},{16,24},{18,... | collective-permute-start | bytes 1769480 | tf_op jit(solution)/shard_map/ppermute | solution.py:69
  393.6 16.5 %collective-permute-start.20 = (bf16[4,2,48,1536]{3,2,1,0:T(8,128)(2,1)S(1)}, bf16[4,2,48,1536]{3,2,1,0:T(8,128)(2,1)S(1)}, u32[]{:S(2)}, u32[]{:S(2)}) collective-permute-start(bf16[4,2,48,1536]{3,2,1,0:T(8,128)(2,1)S(1)} %add_convert_fusion.3), channel_id=1, source_target_pairs={{0,2},{2,0},{4,6},{6,4},{8,10},{10,8},{12,14},{14,12},{16,18},{18,... | collective-permute-start | bytes 3538952 | tf_op jit(solution)/shard_map/ppermute | solution.py:69
  398.4 30.9 %collective-permute-start.22 = (bf16[16,4,48,384]{3,2,1,0:T(8,128)(2,1)S(1)}, bf16[16,4,48,384]{3,2,1,0:T(8,128)(2,1)S(1)}, u32[]{:S(2)}, u32[]{:S(2)}) collective-permute-start(bf16[16,4,48,384]{3,2,1,0:T(8,128)(2,1)S(1)} %copy-done.49), channel_id=1, source_target_pairs={{0,1},{1,0},{2,3},{3,2},{4,5},{5,4},{6,7},{7,6},{8,9},{9,8},{10,11... | collective-permute-start | bytes 7077896 | tf_op jit(solution)/shard_map/ppermute | solution.py:72
  398.5 9.8 %collective-permute-start.19 = (bf16[2,4,48,384]{3,2,1,0:T(8,128)(2,1)S(1)}, bf16[2,4,48,384]{3,2,1,0:T(8,128)(2,1)S(1)}, u32[]{:S(2)}, u32[]{:S(2)}) collective-permute-start(bf16[2,4,48,384]{3,2,1,0:T(8,128)(2,1)S(1)} %add_convert_fusion.12), channel_id=1, source_target_pairs={{0,8},{2,10},{4,12},{6,14},{8,0},{10,2},{12,4},{14,6},{16,24},{18,... | collective-permute-start | bytes 884744 | tf_op jit(solution)/shard_map/ppermute | solution.py:69
  410.1 19.1 %copy-start.22 = (bf16[16,4,48,384]{3,2,1,0:T(8,128)(2,1)S(1)}, bf16[16,4,48,384]{3,2,1,0:T(8,128)(2,1)}, u32[]{:S(2)}) copy-start(bf16[16,4,48,384]{3,2,1,0:T(8,128)(2,1)} %get-tuple-element.327) | copy-start | bytes 7077892
  412.0 15.2 %collective-permute-start.21 = (bf16[2,2,48,1536]{3,2,1,0:T(8,128)(2,1)S(1)}, bf16[2,2,48,1536]{3,2,1,0:T(8,128)(2,1)S(1)}, u32[]{:S(2)}, u32[]{:S(2)}) collective-permute-start(bf16[2,2,48,1536]{3,2,1,0:T(8,128)(2,1)S(1)} %add_convert_fusion.7), channel_id=1, source_target_pairs={{0,8},{2,10},{4,12},{6,14},{8,0},{10,2},{12,4},{14,6},{16,24},{18,... | collective-permute-start | bytes 1769480 | tf_op jit(solution)/shard_map/ppermute | solution.py:69
  429.2 18.2 %copy-start.45 = (bf16[1,2,48,1536]{3,2,1,0:T(8,128)(2,1)S(1)}, bf16[1,2,48,1536]{3,2,1,0:T(8,128)(2,1)}, u32[]{:S(2)}) copy-start(bf16[1,2,48,1536]{3,2,1,0:T(8,128)(2,1)} %add_convert_fusion.13) | copy-start | bytes 884740
  429.3 34.4 %copy-start.23 = (bf16[16,4,48,384]{3,2,1,0:T(8,128)(2,1)}, bf16[16,4,48,384]{3,2,1,0:T(8,128)(2,1)S(1)}, u32[]{:S(2)}) copy-start(bf16[16,4,48,384]{3,2,1,0:T(8,128)(2,1)S(1)} %collective-permute-done.22) | copy-start | bytes 7077892
  429.6 38.7 %copy-start.34 = (bf16[2,2,48,1536]{3,2,1,0:T(8,128)(2,1)S(1)}, bf16[2,2,48,1536]{3,2,1,0:T(8,128)(2,1)}, u32[]{:S(2)}) copy-start(bf16[2,2,48,1536]{3,2,1,0:T(8,128)(2,1)} %copy-done.33) | copy-start | bytes 1769476
  429.6 16.3 %collective-permute-start.23 = (bf16[8,4,48,384]{3,2,1,0:T(8,128)(2,1)S(1)}, bf16[8,4,48,384]{3,2,1,0:T(8,128)(2,1)S(1)}, u32[]{:S(2)}, u32[]{:S(2)}) collective-permute-start(bf16[8,4,48,384]{3,2,1,0:T(8,128)(2,1)S(1)} %add_convert_fusion.2), channel_id=1, source_target_pairs={{0,4},{2,6},{4,0},{6,2},{8,12},{10,14},{12,8},{14,10},{16,20},{18,... | collective-permute-start | bytes 3538952 | tf_op jit(solution)/shard_map/ppermute | solution.py:69
  430.8 16.2 %collective-permute-start.35 = (f32[2,8576]{1,0:T(2,128)S(1)}, f32[2,8576]{1,0:T(2,128)S(1)}, u32[]{:S(2)}, u32[]{:S(2)}) collective-permute-start(f32[2,8576]{1,0:T(2,128)S(1)} %fusion.11), channel_id=1, source_target_pairs={{0,1},{1,0},{2,3},{3,2},{4,5},{5,4},{6,7},{7,6},{8,9},{9,8},{10,11... | collective-permute-start | bytes 205832 | tf_op jit(solution)/shard_map/ppermute | solution.py:72
  445.9 23.9 %copy-start.31 = (bf16[8,4,48,384]{3,2,1,0:T(8,128)(2,1)}, bf16[8,4,48,384]{3,2,1,0:T(8,128)(2,1)S(1)}, u32[]{:S(2)}) copy-start(bf16[8,4,48,384]{3,2,1,0:T(8,128)(2,1)S(1)} %collective-permute-done.23) | copy-start | bytes 3538948
  446.1 17.6 %collective-permute-start.24 = (bf16[4,4,48,384]{3,2,1,0:T(8,128)(2,1)S(1)}, bf16[4,4,48,384]{3,2,1,0:T(8,128)(2,1)S(1)}, u32[]{:S(2)}, u32[]{:S(2)}) collective-permute-start(bf16[4,4,48,384]{3,2,1,0:T(8,128)(2,1)S(1)} %add_convert_fusion.6), channel_id=1, source_target_pairs={{0,2},{2,0},{4,6},{6,4},{8,10},{10,8},{12,14},{14,12},{16,18},{18,... | collective-permute-start | bytes 1769480 | tf_op jit(solution)/shard_map/ppermute | solution.py:69
  447.1 11.7 %collective-permute-start.36 = (f32[2,8576]{1,0:T(2,128)S(1)}, f32[2,8576]{1,0:T(2,128)S(1)}, u32[]{:S(2)}, u32[]{:S(2)}) collective-permute-start(f32[2,8576]{1,0:T(2,128)S(1)} %fusion.34), channel_id=1, source_target_pairs={{0,16},{2,18},{4,20},{6,22},{8,24},{10,26},{12,28},{14,30},{16,0},... | collective-permute-start | bytes 205832 | tf_op jit(solution)/shard_map/ppermute | solution.py:69
  447.4 20.9 %collective-permute-start.29 = (bf16[1,2,48,1536]{3,2,1,0:T(8,128)(2,1)S(1)}, bf16[1,2,48,1536]{3,2,1,0:T(8,128)(2,1)S(1)}, u32[]{:S(2)}, u32[]{:S(2)}) collective-permute-start(bf16[1,2,48,1536]{3,2,1,0:T(8,128)(2,1)S(1)} %copy-done.45), channel_id=1, source_target_pairs={{0,16},{2,18},{4,20},{6,22},{8,24},{10,26},{12,28},{14,30},{16,0},... | collective-permute-start | bytes 884744 | tf_op jit(solution)/shard_map/ppermute | solution.py:69
  459.4 42.7 %collective-permute-start.37 = (f32[2,8576]{1,0:T(2,128)}, f32[2,8576]{1,0:T(2,128)}, u32[]{:S(2)}, u32[]{:S(2)}) collective-permute-start(f32[2,8576]{1,0:T(2,128)} %add.427), channel_id=1, source_target_pairs={{0,8},{2,10},{4,12},{6,14},{8,0},{10,2},{12,4},{14,6},{16,24},{18,... | collective-permute-start | bytes 205832 | tf_op jit(solution)/shard_map/ppermute | solution.py:69
  459.4 18.6 %collective-permute-start.27 = (bf16[1,4,48,384]{3,2,1,0:T(8,128)(2,1)}, bf16[1,4,48,384]{3,2,1,0:T(8,128)(2,1)}, u32[]{:S(2)}, u32[]{:S(2)}) collective-permute-start(bf16[1,4,48,384]{3,2,1,0:T(8,128)(2,1)} %add_convert_fusion.15), channel_id=1, source_target_pairs={{0,16},{2,18},{4,20},{6,22},{8,24},{10,26},{12,28},{14,30},{16,0},... | collective-permute-start | bytes 442376 | tf_op jit(solution)/shard_map/ppermute | solution.py:69
  464.6 14.8 %collective-permute-start.25 = (bf16[2,4,48,384]{3,2,1,0:T(8,128)(2,1)}, bf16[2,4,48,384]{3,2,1,0:T(8,128)(2,1)}, u32[]{:S(2)}, u32[]{:S(2)}) collective-permute-start(bf16[2,4,48,384]{3,2,1,0:T(8,128)(2,1)} %add_convert_fusion.10), channel_id=1, source_target_pairs={{0,8},{2,10},{4,12},{6,14},{8,0},{10,2},{12,4},{14,6},{16,24},{18,... | collective-permute-start | bytes 884744 | tf_op jit(solution)/shard_map/ppermute | solution.py:69
  477.9 15.0 %collective-permute-start.28 = (bf16[1,2,48,1536]{3,2,1,0:T(8,128)(2,1)S(1)}, bf16[1,2,48,1536]{3,2,1,0:T(8,128)(2,1)S(1)}, u32[]{:S(2)}, u32[]{:S(2)}) collective-permute-start(bf16[1,2,48,1536]{3,2,1,0:T(8,128)(2,1)S(1)} %copy-done.46), channel_id=1, source_target_pairs={{0,16},{2,18},{4,20},{6,22},{8,24},{10,26},{12,28},{14,30},{16,0},... | collective-permute-start | bytes 884744 | tf_op jit(solution)/shard_map/ppermute | solution.py:69
  480.7 15.4 %collective-permute-start.26 = (bf16[1,4,48,384]{3,2,1,0:T(8,128)(2,1)S(1)}, bf16[1,4,48,384]{3,2,1,0:T(8,128)(2,1)S(1)}, u32[]{:S(2)}, u32[]{:S(2)}) collective-permute-start(bf16[1,4,48,384]{3,2,1,0:T(8,128)(2,1)S(1)} %add_convert_fusion.14), channel_id=1, source_target_pairs={{0,16},{2,18},{4,20},{6,22},{8,24},{10,26},{12,28},{14,30},{16,0},... | collective-permute-start | bytes 442376 | tf_op jit(solution)/shard_map/ppermute | solution.py:69
  495.1 26.7 %copy-start.30 = (f32[2,48,384]{2,1,0:T(8,128)S(1)}, f32[2,48,384]{2,1,0:T(8,128)}, u32[]{:S(2)}) copy-start(f32[2,48,384]{2,1,0:T(8,128)} %param.23) | copy-start | bytes 442372
  495.8 28.0 %copy-start.18 = (f32[2,48,3,384]{3,1,2,0:T(8,128)S(1)}, f32[2,48,3,384]{3,1,2,0:T(8,128)}, u32[]{:S(2)}) copy-start(f32[2,48,3,384]{3,1,2,0:T(8,128)} %param.22) | copy-start | bytes 1327108
  499.3 26.8 %copy-start.16 = (f32[2,48,1536]{2,1,0:T(8,128)S(1)}, f32[2,48,1536]{2,1,0:T(8,128)}, u32[]{:S(2)}) copy-start(f32[2,48,1536]{2,1,0:T(8,128)} %param.25) | copy-start | bytes 1769476
  499.3 26.8 %copy-start.17 = (f32[2,48,1536]{2,1,0:T(8,128)S(1)}, f32[2,48,1536]{2,1,0:T(8,128)}, u32[]{:S(2)}) copy-start(f32[2,48,1536]{2,1,0:T(8,128)} %param.24) | copy-start | bytes 1769476
  502.0 2.3 collective-permute-start.30
  503.1 4.4 collective-permute-start.38
  504.4 4.6 collective-permute-start.31
  507.5 5.8 %collective-permute-start.39 = (f32[2,8576]{1,0:T(2,128)S(1)}, f32[2,8576]{1,0:T(2,128)S(1)}, u32[]{:S(2)}, u32[]{:S(2)}) collective-permute-start(f32[2,8576]{1,0:T(2,128)S(1)} %add.429), channel_id=1, source_target_pairs={{0,4},{2,6},{4,0},{6,2},{8,12},{10,14},{12,8},{14,10},{16,20},{18,... | collective-permute-start | bytes 205832 | tf_op jit(solution)/shard_map/ppermute | solution.py:69
  509.0 3.6 collective-permute-start.32
  512.6 3.6 collective-permute-start.33
  516.2 3.6 collective-permute-start.34
  528.2 21.4 %copy-start.24 = (f32[2,48,1536]{2,1,0:T(8,128)}, f32[2,48,1536]{2,1,0:T(8,128)S(1)}, u32[]{:S(2)}) copy-start(f32[2,48,1536]{2,1,0:T(8,128)S(1)} %get-tuple-element.479) | copy-start | bytes 1769476
  528.2 20.3 %copy-start.25 = (f32[2,48,1536]{2,1,0:T(8,128)S(1)}, f32[2,48,1536]{2,1,0:T(8,128)}, u32[]{:S(2)}) copy-start(f32[2,48,1536]{2,1,0:T(8,128)} %get-tuple-element.480) | copy-start | bytes 1769476
  528.3 1.2 collective-permute-start.40
  529.5 4.5 collective-permute-start.41
  534.0 3.6 collective-permute-start.42
  537.6 3.6 collective-permute-start.43
  541.2 3.6 collective-permute-start.44
  (35 other events, 164.2 us)
Sparse Core Ops, SparseCore 0:
  11.6 135.4 all-gather.8
  355.9 9.3 all-gather.4
  478.0 9.0 all-gather.6

commit v3 on v2

v3 whole, which is shorter than its diff:
```python
from functools import partial
import math

import jax
import jax.numpy as jnp
import numpy as np
from jax import lax
from jax.experimental import pallas as pl
from jax.experimental.pallas import tpu as pltpu
from jax.sharding import PartitionSpec as P

D = 768
HEADS = 12
FF = 3072


beta_one = 0.9
beta_two = 0.999
adam_eps = 1e-06
decay_rate = 0.01
matrix_rate = 1.0
vector_rate = 0.3
clip_norm = 1.0
step_count = 10.0
norm_eps = 1e-06
masked_score = -1e30

f32 = jnp.float32
bf16 = jnp.bfloat16


class Links:
    def __init__(self, parts):
        self.parts = parts
        count = parts.bit_length() - 1
        high = list(range(count - 1, -1, -1))
        other = high[:-2] + high[-2:][::-1]
        self.orders = (other, high)
        self.inverse = np.zeros((2, parts), np.int32)
        for core in range(2):
            for place in range(parts):
                mask = 0
                for stage in range(count):
                    if (place >> stage) & 1:
                        mask |= 1 << self.orders[core][stage]
                self.inverse[core, mask] = place
        self.stages = count
        self.last = ()
        every = np.arange(parts)
        self.table = np.zeros((2, parts, 6, parts + 1), np.int32)
        for core in range(2):
            for at in range(parts):
                for half, side in enumerate((core, 1 - core)):
                    differs = [((every ^ at) >> bit) & 1 for bit in self.orders[side][-2:]]
                    zoned = (2 * differs[1] + differs[0]) * (parts // 4) + every // 4
                    rows = (self.inverse[side, every ^ at], zoned, every)
                    for kind, row in enumerate(rows):
                        self.table[core, at, 2 * kind + half, :parts] = row
                        self.table[core, at, 2 * kind + half, parts] = side

    def swap(self, value, *stages):
        pairs = []
        for core in range(2):
            flip = sum(1 << self.orders[core][stage] for stage in stages)
            pairs += [(2 * at + core, 2 * (at ^ flip) + core) for at in range(self.parts)]
        return lax.ppermute(value, ("dp", "tensor"), pairs)

    def sibling(self, value):
        return lax.ppermute(value, "tensor", [(0, 1), (1, 0)])

    def gather(self, share):
        return {"held": share[None], "stage": 0}

    def gather_last(self, held):
        return {"held": held, "stage": self.stages - 2}

    def total(self, value):
        return {"value": value, "step": 0}

    def scatter(self, own, other):
        return {"pieces": [own], "other": other, "size": self.parts, "stage": self.stages}

    def advance(self, moves, rest=()):
        moves = [move for move in moves if self.running(move)]
        if not moves:
            return rest
        mine, rest, self.last = lax.optimization_barrier(
            ([move.get("held", move.get("value", move.get("pieces"))) for move in moves], rest, self.last)
        )
        sending = []
        for move, value in zip(moves, mine):
            if "held" in move:
                come = move.pop("come", None)
                sending.append(value if come is None else jnp.concatenate([value, come], axis=0))
            elif "value" in move:
                sending.append(self.summed(value, move.pop("come", [])))
            elif "other" in move:
                sending.append(move["other"])
            else:
                half, size = move["size"] // 2, move["size"]
                move["pieces"] = value + move.pop("come")
                sending.append(sum(piece[half:size].astype(f32) for piece in move["pieces"]).astype(bf16))
        sending, rest, _ = lax.optimization_barrier((sending, rest, self.last))
        self.last = sending[0]
        for move, value in zip(moves, sending):
            if "held" in move:
                move["held"] = value
                move["come"] = self.swap(value, move["stage"])
                move["stage"] += 1
            elif "value" in move:
                move["value"] = value
                low, high = 2 * move["step"] - 2, 2 * move["step"] - 1
                if move["step"] == 0:
                    move["come"] = [self.sibling(value)]
                elif high < self.stages:
                    move["come"] = [self.swap(value, low), self.swap(value, high), self.swap(value, low, high)]
                else:
                    move["come"] = [self.swap(value, low)]
                move["step"] += 1
            elif "other" in move:
                move["come"] = [self.sibling(value)]
                del move["other"]
            else:
                move["size"] //= 2
                move["stage"] -= 1
                move["come"] = [self.swap(value, move["stage"])]
        return rest

    def pair(self, move, rest=()):
        held, rest = lax.optimization_barrier((move.pop("held"), rest))
        held = jnp.concatenate([held, move.pop("come")], axis=0)
        move["pair"] = (held, self.sibling(held), 0)
        return rest

    def summed(self, value, come):
        if len(come) == 3:
            return (value + come[0]) + (come[1] + come[2])
        return value + come[0] if come else value

    def running(self, move):
        return move.get("stage", 0) < self.stages if "held" in move else move.get("size", 1) > 1 or 2 * move.get("step", self.stages) < self.stages + 2

    def settle(self, moves, rest):
        pieces, rest = lax.optimization_barrier(([move["pieces"] for move in moves], rest))
        for move, value in zip(moves, pieces):
            move["pieces"] = value
        return lax.optimization_barrier((self.finish(moves), rest))

    def finish(self, moves):
        for move in moves:
            while self.running(move):
                self.advance([move])
        if "value" in moves[0]:
            return [self.summed(move["value"], move["come"]) for move in moves]
        return [sum(piece[0].astype(f32) for piece in move["pieces"] + move["come"]) for move in moves]


def dot_nt(left, right):
    return lax.dot_general(left, right, (((1,), (1,)), ((), ())), preferred_element_type=f32)


def dot_nn(left, right):
    return jnp.dot(left, right, preferred_element_type=f32)


def in_order(blocks, place_of):
    some = (0,) if len(blocks.shape) == 4 else ()
    return jnp.concatenate([blocks[(place_of[block], *some)] for block in range(blocks.shape[0])], axis=0)


def put_blocks(out, at, product, place_of):
    parts, _, rows, _ = out.shape
    for block in range(parts):
        out[place_of[block], at] = product[block * rows : (block + 1) * rows]


def norm_parts(values):
    centered = values - jnp.mean(values, axis=1, keepdims=True)
    variance = jnp.mean(centered * centered, axis=1, keepdims=True)
    scale = lax.rsqrt(variance + norm_eps)
    return centered * scale, scale


def norm_backward(values, gain, grad):
    unit, scale = norm_parts(values)
    scaled = grad * gain
    inner = scaled - jnp.mean(scaled, axis=1, keepdims=True)
    result = scale * (inner - unit * jnp.mean(scaled * unit, axis=1, keepdims=True))
    return result, jnp.sum(grad * unit, axis=0, keepdims=True), jnp.sum(grad, axis=0, keepdims=True)


def project_kernel(own_at, other_at, own_to, other_to, rows_in, own, other, bias, out):
    width = own.shape[-1]
    for half, (blocks, place_of) in enumerate(((own, own_at), (other, other_at))):
        weight = in_order(blocks, place_of)
        span = slice(half * width, (half + 1) * width)
        out[:, span] = (dot_nn(rows_in[...], weight) + bias[:, span]).astype(bf16)


def cost(microseconds):
    return pl.CostEstimate(flops=0, bytes_accessed=int(microseconds * 2.5e6), transcendentals=0)


class Row:
    def __init__(self, table, row):
        self.table, self.row = table, row

    def __getitem__(self, place):
        return self.table[self.row, place]


def call(kernel, places, grid, ins, outs, scratch=(), name=None, time=1):
    table, pair = places
    weight_rows = lambda at: (Row(at, 2 * pair), Row(at, 2 * pair + 1))
    spec = lambda block, index: pl.BlockSpec(block, lambda i, at: index(i, weight_rows(at)))
    return pl.pallas_call(
        lambda at, *refs: kernel(*weight_rows(at), Row(at, 0), Row(at, 1), *refs),
        out_shape=[jax.ShapeDtypeStruct(shape, kind) for shape, kind, _, _ in outs],
        grid_spec=pltpu.PrefetchScalarGridSpec(
            num_scalar_prefetch=1,
            grid=(grid,),
            in_specs=[spec(block, index) for _, block, index in ins],
            out_specs=[spec(block, index) for _, _, block, index in outs],
            scratch_shapes=list(scratch),
        ),
        compiler_params=pltpu.CompilerParams(
            dimension_semantics=("arbitrary",), vmem_limit_bytes=60 << 20
        ),
        cost_estimate=cost(time),
        name=name,
    )(table, *[array for array, _, _ in ins])


def whole(array):
    return (array, array.shape, lambda i, at: (0,) * array.ndim)


def weight_tiles(pair, tile, count=1):
    own, other, first = pair
    tiles = []
    for half, array in enumerate((own, other)):
        parts, rows = array.shape[0], array.shape[-2]
        column = lambda i: first // tile + jnp.clip(i, 0, count - 1)
        if array.ndim == 3:
            tiles.append((array, (parts, rows, tile), lambda i, at: (0, 0, column(i))))
        else:
            index = lambda i, at, half=half, parts=parts: (0, at[half][parts], 0, column(i))
            tiles.append((array, (parts, 1, rows, tile), index))
    return tiles


def project(places, rows_in, pair, bias):
    rows = rows_in.shape[0]
    half = D // 2
    return call(
        project_kernel, places, 3,
        [whole(rows_in), *weight_tiles(pair, half, 3), (bias, (1, D), lambda i, at: (0, i))],
        [((rows, 3 * D), bf16, (rows, D), lambda i, at: (0, i))],
        name="project",
        time=7,
    )[0]


def feed_forward_kernel(
    own_at, other_at, own_to, other_to, hidden, context, out_own, out_other, up_own, up_other, down_own, down_other,
    bias_up, vectors, *refs, with_grad,
):
    if with_grad:
        grad, first_in, first_low, first_turned, active, slope, hidden_new, *turned, second_in = refs
        total = second_in
    else:
        first_in, first_low, first_turned, active, slope, hidden_new, second_in, hidden_low, hidden_turned = refs
        total = second_in
    step = pl.program_id(0)
    halves = ((own_at, up_own, down_own), (other_at, up_other, down_other))
    half_d = D // 2

    @pl.when(step == 0)
    def _():
        attended = dot_nt(context[:, :half_d], in_order(out_own, own_at))
        attended += dot_nt(context[:, half_d:], in_order(out_other, other_at))
        values = hidden[...].astype(f32) + attended + vectors[0:1]
        first_in[...] = values
        unit, _ = norm_parts(values)
        values = unit * vectors[1:2] + vectors[2:3]
        low = values.astype(bf16)
        first_low[...] = low
        first_turned[...] = low.T
        total[...] = values + vectors[3:4]

    for half, (place_of, up, down) in enumerate(halves):
        before = dot_nn(first_low[...], in_order(up, place_of)) + bias_up[half]
        shade = 0.5 * (1.0 + lax.erf(before * (1.0 / math.sqrt(2.0))))
        bell = jnp.exp(-0.5 * before * before) * (1.0 / math.sqrt(2.0 * math.pi))
        low = (before * shade).astype(bf16)
        active[half] = low
        slope[half] = shade + before * bell
        total[...] += dot_nt(low, in_order(down, place_of))

    @pl.when(step == pl.num_programs(0) - 1)
    def _():
        unit, _ = norm_parts(second_in[...])
        values = unit * vectors[4:5] + vectors[5:6]
        hidden_new[...] = values
        if with_grad:
            norm_turn(second_in[...], vectors[4:5], grad[...], *turned)
        else:
            low = values.astype(bf16)
            hidden_low[...] = low
            hidden_turned[...] = low.T


def feed_forward(places, hidden, context, out_pair, up_pair, down_pair, bias_up, vectors, grad=None, tile=384):
    rows = hidden.shape[0]
    half_ff = bias_up.shape[2]
    count = half_ff // tile
    flat = lambda kind: ((rows, D), kind, (rows, D), lambda i, at: (0, 0))
    tiled = lambda kind: ((2, rows, half_ff), kind, (2, rows, tile), lambda i, at: (0, 0, i))
    turned = ((D, rows), bf16, (D, rows), lambda i, at: (0, 0))
    return call(
        partial(feed_forward_kernel, with_grad=grad is not None), places, count,
        [
            whole(hidden),
            whole(context),
            *weight_tiles(out_pair, D // 2),
            *weight_tiles(up_pair, tile, count),
            *weight_tiles(down_pair, tile, count),
            (bias_up, (2, 1, tile), lambda i, at: (0, 0, i)),
            whole(vectors),
            *([] if grad is None else [whole(grad)]),
        ],
        [
            flat(f32), flat(bf16), turned, tiled(bf16), tiled(f32), flat(f32),
            *([flat(f32), flat(bf16), turned] if grad is None else norm_turn_outs(rows)),
        ],
        [] if grad is None else [pltpu.VMEM((rows, D), f32)],
        name="feed_forward",
        time=18,
    )


def norm_turn(values, gain, grad, total, down_low, down_turned, small):
    result, gain_grad, shift_grad = norm_backward(values, gain, grad)
    small[...] = jnp.zeros_like(small)
    small[0:1] = jnp.sum(result, axis=0, keepdims=True)
    small[1:2] = gain_grad
    small[2:3] = shift_grad
    total[...] = result
    low = result.astype(bf16)
    down_low[...] = low
    down_turned[...] = low.T


def norm_turn_outs(rows):
    flat = lambda kind: ((rows, D), kind, (rows, D), lambda i, at: (0, 0))
    turned = ((D, rows), bf16, (D, rows), lambda i, at: (0, 0))
    return [flat(f32), flat(bf16), turned, ((8, D), f32, (8, D), lambda i, at: (0, 0))]


def feed_backward_kernel(
    own_at, other_at, own_to, other_to, total_in, down_low, down_turned, first_turned, active, slope,
    up_own, up_other, down_own, down_other, grads_own, grads_other, bias_grads, total,
):
    halves = (
        (own_at, own_to, up_own, down_own, grads_own),
        (other_at, other_to, up_other, down_other, grads_other),
    )

    @pl.when(pl.program_id(0) == 0)
    def _():
        total[...] = total_in[...]

    for half, (place_of, place_to, up, down, grads) in enumerate(halves):
        act_grad = dot_nn(down_low[...], in_order(down, place_of))
        before_grad = act_grad * slope[half]
        bias_grads[half] = jnp.broadcast_to(jnp.sum(before_grad, axis=0, keepdims=True), bias_grads.shape[1:])
        low = before_grad.astype(bf16)
        put_blocks(grads, 0, dot_nn(down_turned[...], active[half]).astype(bf16), place_to)
        put_blocks(grads, 1, dot_nn(first_turned[...], low).astype(bf16), place_to)
        total[...] += dot_nt(low, in_order(up, place_of))


def context_backward_kernel(
    own_at, other_at, own_to, other_to, grad, first_in, out_own, out_other, vectors,
    first_in_grad, out_in_turned, context_grad, small,
):
    half_d = D // 2
    result, gain_grad, shift_grad = norm_backward(first_in[...], vectors[1:2], grad[...])
    small[...] = jnp.zeros_like(small)
    small[0:1] = jnp.sum(result, axis=0, keepdims=True)
    small[1:2] = gain_grad
    small[2:3] = shift_grad
    first_in_grad[...] = result
    low = result.astype(bf16)
    out_in_turned[...] = low.T
    context_grad[:, :half_d] = dot_nn(low, in_order(out_own, own_at)).astype(bf16)
    context_grad[:, half_d:] = dot_nn(low, in_order(out_other, other_at)).astype(bf16)


def context_backward(places, grad, first_in, out_pair, vectors):
    rows = grad.shape[0]
    flat = lambda kind: ((rows, D), kind, (rows, D), lambda i, at: (0, 0))
    return call(
        context_backward_kernel, places, 1,
        [
            whole(grad), whole(first_in),
            *weight_tiles(out_pair, D // 2),
            whole(vectors),
        ],
        [
            flat(f32), ((D, rows), bf16, (D, rows), lambda i, at: (0, 0)), flat(bf16),
            ((8, D), f32, (8, D), lambda i, at: (0, 0)),
        ],
        name="context_backward",
        time=6,
    )


def feed_backward(places, total, down_low, down_turned, kept, up_pair, down_pair, parts, tile=384):
    first_turned, active, slope = kept
    rows = total.shape[0]
    half_ff = active.shape[2]
    count = half_ff // tile
    block_rows = D // parts
    tiled = lambda array: (array, (2, rows, tile), lambda i, at: (0, 0, i))
    grads = ((parts, 2, block_rows, count * tile), bf16, (parts, 2, block_rows, tile), lambda i, at: (0, 0, 0, i))
    return call(
        feed_backward_kernel, places, count,
        [
            whole(total), whole(down_low), whole(down_turned), whole(first_turned), tiled(active), tiled(slope),
            *weight_tiles(up_pair, tile, count),
            *weight_tiles(down_pair, tile, count),
        ],
        [
            grads, grads,
            ((2, 8, count * tile), f32, (2, 8, tile), lambda i, at: (0, 0, i)),
            ((rows, D), f32, (rows, D), lambda i, at: (0, 0)),
        ],
        name="feed_backward",
        time=20,
    )


def projection_grads_kernel(
    own_at, other_at, own_to, other_to, out_in_turned, context, input_turned, head_grads,
    grads_own, grads_other,
):
    step = pl.program_id(0)
    half_d = D // 2
    halves = ((own_to, grads_own), (other_to, grads_other))
    for when, left, right in (
        (step == 0, out_in_turned, lambda span: context[:, span]),
        (step > 0, input_turned, lambda span: head_grads[0, :, span]),
    ):

        @pl.when(when)
        def _():
            for half, (place_to, grads) in enumerate(halves):
                span = slice(half * half_d, (half + 1) * half_d)
                put_blocks(grads, 0, dot_nn(left[...], right(span)).astype(bf16), place_to)


def projection_grads(places, out_in_turned, context, input_turned, head_grads, parts):
    rows = context.shape[0]
    half = D // 2
    block_rows = D // parts
    grads = ((parts, 4, block_rows, half), bf16, (parts, 1, block_rows, half), lambda i, at: (0, i, 0, 0))
    return call(
        projection_grads_kernel, places, 4,
        [
            whole(out_in_turned), whole(context), whole(input_turned),
            (head_grads, (1, rows, D), lambda i, at: (jnp.maximum(i - 1, 0), 0, 0)),
        ],
        [grads, grads],
        name="projection_grads",
        time=9,
    )


def project_backward_kernel(
    own_at, other_at, own_to, other_to, head_grads, first_in_grad, own, other, *refs, with_norm
):
    half_d = D // 2
    step = pl.program_id(0)
    if with_norm:
        second_in, vectors, *turned, input_grad = refs
    else:
        (input_grad,) = refs

    @pl.when(step == 0)
    def _():
        input_grad[...] = first_in_grad[...]

    for half, (place_of, weight) in enumerate(((own_at, own), (other_at, other))):
        low = head_grads[0, :, half * half_d : (half + 1) * half_d]
        input_grad[...] += dot_nt(low, in_order(weight, place_of))

    if with_norm:

        @pl.when(step == pl.num_programs(0) - 1)
        def _():
            norm_turn(second_in[...], vectors[4:5], input_grad[...], *turned)


def project_backward(places, head_grads, first_in_grad, pair, earlier=()):
    rows = first_in_grad.shape[0]
    half = D // 2
    return call(
        partial(project_backward_kernel, with_norm=bool(earlier)), places, 3,
        [
            (head_grads, (1, rows, D), lambda i, at: (i, 0, 0)),
            whole(first_in_grad),
            *weight_tiles(pair, half, 3),
            *map(whole, earlier),
        ],
        norm_turn_outs(rows) if earlier else [((rows, D), f32, (rows, D), lambda i, at: (0, 0))],
        [pltpu.VMEM((rows, D), f32)] if earlier else [],
        name="project_backward",
        time=8,
    )


def join_kernel(core, *refs):
    step = pl.program_id(0)
    count = len(refs) // 3
    for one in range(count):
        own, other, out = refs[2 * one], refs[2 * one + 1], refs[2 * count + one]

        @pl.when(step == core[0])
        def _():
            out[...] = own[...]

        @pl.when(step != core[0])
        def _():
            out[...] = other[...]


def join(core, pairs):
    rows, cols = pairs[0][0].shape
    spec = pl.BlockSpec((rows, cols), lambda i, at: (0, 0))
    return pl.pallas_call(
        join_kernel,
        out_shape=[jax.ShapeDtypeStruct((2 * rows, cols), f32) for _ in pairs],
        grid_spec=pltpu.PrefetchScalarGridSpec(
            num_scalar_prefetch=1,
            grid=(2,),
            in_specs=[spec] * (2 * len(pairs)),
            out_specs=[pl.BlockSpec((rows, cols), lambda i, at: (i, 0)) for _ in pairs],
        ),
        compiler_params=pltpu.CompilerParams(
            dimension_semantics=("arbitrary",), vmem_limit_bytes=60 << 20
        ),
        cost_estimate=cost(4),
        name="join",
    )(core, *[rows_of for pair in pairs for rows_of in pair])


bounds = [0, D, 2 * D, 2 * D + FF, 3 * D + FF, 4 * D + FF, 5 * D + FF, 6 * D + FF, 7 * D + FF]


def swapped(core, vector):
    half = vector.shape[1] // 2
    first, second = vector[:, :half], vector[:, half:]
    return jnp.where(core == 0, first, second), jnp.where(core == 0, second, first)


def prepare_kernel(core, lengths, tokens, cotangent, small, tokens_own, tokens_turned, grad, *outs):
    step = pl.program_id(0)
    length = lengths[core[0] * pl.num_programs(0) + step]
    tokens_own[...] = tokens[...]
    tokens_turned[...] = tokens[...].T
    valid = lax.broadcasted_iota(jnp.int32, grad.shape, 0) < length
    grad[...] = jnp.where(valid, cotangent[...].astype(f32), 0.0)

    @pl.when(step == 0)
    def _():
        for layer_at in range(small.shape[0]):
            vectors, value_bias, up_bias = outs[3 * layer_at : 3 * layer_at + 3]
            part = lambda place: small[layer_at : layer_at + 1, bounds[place] : bounds[place + 1]]
            vectors[...] = jnp.zeros_like(vectors)
            for row, place in enumerate((1, 4, 5, 3, 6, 7)):
                vectors[row : row + 1] = part(place)
            value_bias[...] = jnp.zeros_like(value_bias)
            first, second = swapped(core[0], part(0))
            value_bias[:, 2 * D : 2 * D + D // 2] = first
            value_bias[:, 2 * D + D // 2 :] = second
            up_bias[0], up_bias[1] = swapped(core[0], part(2))


def prepare(core, lengths, tokens, cotangent, small):
    layers = small.shape[0]
    seqs = lengths.shape[0] // 2
    rows = tokens.shape[0] // lengths.shape[0]
    mine = pl.BlockSpec((rows, D), lambda s, c, l: (c[0] * seqs + s, 0))
    fixed = lambda shape: pl.BlockSpec(shape, lambda s, c, l: (0,) * len(shape))
    shapes = [(8, D), (1, 3 * D), (2, 1, FF // 2)] * layers
    return pl.pallas_call(
        prepare_kernel,
        out_shape=[
            jax.ShapeDtypeStruct((seqs * rows, D), bf16),
            jax.ShapeDtypeStruct((D, seqs * rows), bf16),
            jax.ShapeDtypeStruct((seqs * rows, D), f32),
            *[jax.ShapeDtypeStruct(shape, f32) for shape in shapes],
        ],
        grid_spec=pltpu.PrefetchScalarGridSpec(
            num_scalar_prefetch=2,
            grid=(seqs,),
            in_specs=[mine, mine, fixed(small.shape)],
            out_specs=[
                pl.BlockSpec((rows, D), lambda s, c, l: (s, 0)),
                pl.BlockSpec((D, rows), lambda s, c, l: (0, s)),
                pl.BlockSpec((rows, D), lambda s, c, l: (s, 0)),
                *[fixed(shape) for shape in shapes],
            ],
        ),
        compiler_params=pltpu.CompilerParams(
            dimension_semantics=("arbitrary",), vmem_limit_bytes=48 << 20
        ),
        cost_estimate=cost(3),
        name="prepare",
    )(core, lengths, tokens, cotangent, small)


def pack_kernel(core, *refs, counts):
    out = refs[-1]
    squares = refs[-2]
    at = 0
    for layer_at, count in enumerate(counts):
        value_sum, first_small, second_small, *bias_sums = refs[at : at + 3 + count]
        at += 3 + count
        row = slice(layer_at, layer_at + 1)

        def put(place, values, start=0):
            first = bounds[place] + start
            out[row, first : first + values.shape[1]] = values

        total = value_sum[0, 0:1]
        for seq in range(1, value_sum.shape[0]):
            total = total + value_sum[seq, 0:1]
        for half, values in enumerate(swapped(core[0], total)):
            put(0, values, half * (D // 2))
        put(1, first_small[0:1])
        width = bias_sums[0].shape[2]
        for place, bias_sum in enumerate(bias_sums):
            own, other = bias_sum[0, 0:1], bias_sum[1, 0:1]
            put(2, jnp.where(core[0] == 0, own, other), place * width)
            put(2, jnp.where(core[0] == 0, other, own), FF // 2 + place * width)
        put(3, second_small[0:1])
        for place, values in ((4, first_small[1:2]), (5, first_small[2:3])):
            put(place, values)
        for place, values in ((6, second_small[1:2]), (7, second_small[2:3])):
            put(place, values)
        out[row, bounds[-1] :] = squares[row]


def pack(core, layers, squares):
    arrays = [array for value, first, second, sums in layers for array in (value, first, second, *sums)]
    arrays.append(squares)
    return pl.pallas_call(
        partial(pack_kernel, counts=[len(sums) for _, _, _, sums in layers]),
        out_shape=jax.ShapeDtypeStruct((len(layers), bounds[-1] + 128), f32),
        grid_spec=pltpu.PrefetchScalarGridSpec(
            num_scalar_prefetch=1,
            grid=(1,),
            in_specs=[pl.BlockSpec(array.shape, lambda i, c, n=array.ndim: (0,) * n) for array in arrays],
            out_specs=pl.BlockSpec((len(layers), bounds[-1] + 128), lambda i, c: (0, 0)),
        ),
        compiler_params=pltpu.CompilerParams(dimension_semantics=("arbitrary",)),
        cost_estimate=cost(2),
        name="pack",
    )(core, *arrays)


def head_mask(width, scale):
    lane = lax.broadcasted_iota(jnp.int32, (1, 128), 1)
    return [jnp.where(lane // 64 == head, scale, 0.0).astype(bf16) for head in range(2)]

def attend_forward_kernel(core, lengths, *refs, depth):
    queries, keys, value_rows = refs[:depth], refs[depth:2*depth], refs[2*depth]
    context, log_norm = refs[2*depth+1:]
    length = lengths[core[0] * pl.num_programs(0) + pl.program_id(0)]
    key_all = [k[...] for k in keys]
    key_all = jnp.concatenate(key_all, axis=1) if depth>1 else key_all[0]
    turned = value_rows[...].T
    rows = key_all.shape[0]
    valid = lax.broadcasted_iota(jnp.int32, (rows, rows), 0) < length
    scaled = head_mask(64, 0.125)
    halves = []
    for head in range(2):
        query = [q[...] * scaled[head] for q in queries]
        query = jnp.concatenate(query, axis=1) if depth>1 else query[0]
        score = jnp.where(valid, dot_nt(key_all, query), masked_score)
        top = jnp.max(score, axis=0, keepdims=True)
        weight = jnp.exp(score - top)
        total = jnp.sum(weight, axis=0, keepdims=True)
        low = (weight * (1.0 / total)).astype(bf16)
        halves.append(jnp.dot(turned[64*head:64*head+64], low, preferred_element_type=f32))
        log_norm[0, head:head+1] = top + jnp.log(total)
    context[...] = jnp.concatenate(halves, axis=0).T.astype(bf16)

def attend_forward(core, lengths, projections, rows):
    depth=len(projections)
    seqs = lengths.shape[0] // 2
    pairs=D//128
    col=lambda off: pl.BlockSpec((rows,128), lambda s,j,c,l,off=off:(s,off*pairs+j))
    return pl.pallas_call(
        partial(attend_forward_kernel, depth=depth),
        out_shape=[jax.ShapeDtypeStruct((seqs*rows,D),bf16), jax.ShapeDtypeStruct((seqs*pairs,8,rows),f32)],
        grid_spec=pltpu.PrefetchScalarGridSpec(num_scalar_prefetch=2, grid=(seqs,pairs),
            in_specs=[col(0)]*depth+[col(1)]*depth+[col(2)],
            out_specs=[pl.BlockSpec((rows,128),lambda s,j,c,l:(s,j)), pl.BlockSpec((1,8,rows),lambda s,j,c,l:(s*pairs+j,0,0))]),
        compiler_params=pltpu.CompilerParams(dimension_semantics=("arbitrary","arbitrary"),vmem_limit_bytes=48<<20),
        cost_estimate=cost(10),
        name="attend_forward",
    )(core, lengths, *projections, *projections, projections[0])

def attend_backward_kernel(core, lengths, *refs, depth, with_later, keep_total):
    queries, keys, value_rows = refs[:depth], refs[depth:2*depth], refs[2*depth]
    log_norm, context_grad = refs[2*depth+1:2*depth+3]
    at = 2*depth+3
    if with_later:
        later = refs[at]; at+=1
    grads, value_sum = refs[at:at+2]
    if keep_total: total_out = refs[at+2]
    length = lengths[core[0] * pl.num_programs(0) + pl.program_id(0)]
    key_all = [k[...] for k in keys]
    key_all = jnp.concatenate(key_all, axis=1) if depth>1 else key_all[0]
    rows = key_all.shape[0]
    valid = lax.broadcasted_iota(jnp.int32, (rows, rows), 0) < length
    scaled = head_mask(64, 0.125)
    plain = head_mask(64, 1.0)
    key_turned = (keys[0][...] * 0.125).astype(bf16).T
    query_halves = []
    key_grad = value_grad = None
    for head in range(2):
        query = [q[...] * scaled[head] for q in queries]
        query_own = query[0]
        query = jnp.concatenate(query, axis=1) if depth>1 else query[0]
        score = jnp.where(valid, dot_nt(key_all, query), masked_score)
        soft = jnp.exp(score - log_norm[0, head:head+1])
        grad_rows = context_grad[...] * plain[head]
        soft_grad = dot_nt(value_rows[...], grad_rows)
        product = soft * soft_grad
        total = product - soft * jnp.sum(product, axis=0, keepdims=True)
        if with_later: total = total + later[head]
        if keep_total: total_out[head] = total
        low = total.astype(bf16)
        query_halves.append(jnp.dot(key_turned[64*head:64*head+64], low, preferred_element_type=f32))
        kg = jnp.dot(low, query_own, preferred_element_type=f32)
        vg = jnp.dot(soft.astype(bf16), grad_rows, preferred_element_type=f32)
        key_grad = kg if key_grad is None else key_grad+kg
        value_grad = vg if value_grad is None else value_grad+vg
    grads[0] = jnp.concatenate(query_halves, axis=0).T.astype(bf16)
    grads[1] = key_grad.astype(bf16)
    grads[2] = value_grad.astype(bf16)
    sums = jnp.sum(value_grad, axis=0, keepdims=True)
    value_sum[0] = jnp.broadcast_to(sums, (8,128))

def attend_backward(core, lengths, projections, log_norm, context_grad, later, keep_total, rows):
    depth=len(projections)
    seqs = lengths.shape[0] // 2
    pairs=D//128
    col=lambda off: pl.BlockSpec((rows,128), lambda s,j,c,l,off=off:(s,off*pairs+j))
    square=pl.BlockSpec((2,rows,rows),lambda s,j,c,l:(s*pairs+j,0,0))
    in_specs=[col(0)]*depth+[col(1)]*depth+[col(2)]+[pl.BlockSpec((1,8,rows),lambda s,j,c,l:(s*pairs+j,0,0)), col(0)]
    args=[*projections,*projections,projections[0],log_norm,context_grad]
    if later is not None:
        in_specs.append(square); args.append(later)
    out_shape=[jax.ShapeDtypeStruct((3,seqs*rows,D),bf16), jax.ShapeDtypeStruct((seqs,8,D),f32)]
    out_specs=[pl.BlockSpec((3,rows,128),lambda s,j,c,l:(0,s,j)), pl.BlockSpec((1,8,128),lambda s,j,c,l:(s,0,j))]
    if keep_total:
        out_shape.append(jax.ShapeDtypeStruct((seqs*pairs*2,rows,rows),f32)); out_specs.append(square)
    return pl.pallas_call(
        partial(attend_backward_kernel, depth=depth, with_later=later is not None, keep_total=keep_total),
        out_shape=out_shape,
        grid_spec=pltpu.PrefetchScalarGridSpec(num_scalar_prefetch=2, grid=(seqs,pairs), in_specs=in_specs, out_specs=out_specs),
        compiler_params=pltpu.CompilerParams(dimension_semantics=("arbitrary","arbitrary"),vmem_limit_bytes=48<<20),
        cost_estimate=cost(17),
        name="attend_backward",
    )(core, lengths, *args)


def adam_parts(gradient, first, second, factor):
    clipped = gradient * factor
    first_new = beta_one * first + (1.0 - beta_one) * clipped
    second_new = beta_two * second + (1.0 - beta_two) * clipped * clipped
    first_hat = first_new / (1.0 - beta_one**step_count)
    second_hat = second_new / (1.0 - beta_two**step_count)
    return (first_new, second_new, first_hat / (jnp.sqrt(second_hat) + adam_eps))


def local(
    tokens,
    cotangent,
    lengths,
    proj_weight,
    out_weight,
    up_weight,
    down_weight,
    small_params,
    proj_first,
    proj_second,
    out_first,
    out_second,
    up_first,
    up_second,
    down_first,
    down_second,
    small_first,
    small_second,
):
    layers = proj_weight.shape[0]
    seq_len = tokens.shape[0] // lengths.shape[0]
    half_d = proj_weight.shape[3]
    half_ff = up_weight.shape[2]
    row_count = proj_weight.shape[1]
    parts = lax.axis_size("dp")
    links = Links(parts)
    places = lax.axis_index("tensor") * parts + lax.axis_index("dp")
    places = lax.dynamic_index_in_dim(
        jnp.asarray(links.table.reshape(2 * parts, 6, parts + 1)), places, 0, keepdims=False
    )
    exchanged, by_zone = (places, 0), (places, 1)
    in_turn = (places, 2)
    turns = {(0, "proj"): by_zone, (0, "ff"): by_zone, (1, "proj"): in_turn, (1, "ff"): in_turn}
    core = lax.axis_index("tensor")[None].astype(jnp.int32)

    table = {"proj": proj_weight, "out": out_weight, "up": up_weight, "down": down_weight}
    groups = [
        [(0, "proj")], [(0, "out"), (0, "up"), (0, "down")], [(1, "proj")], [(1, "out"), (1, "up"), (1, "down")],
    ]
    gathers = []
    for group in groups:
        share = [table[kind][layer_at].reshape(row_count, -1).astype(bf16) for layer_at, kind in group]
        gathers.append(links.gather(jnp.concatenate(share, axis=1) if len(share) > 1 else share[0]))
    one, two, three, four = gathers
    zone = [[first + 4 * step for step in range(parts // 4)] for first in range(4)]
    near = jnp.concatenate([move["held"][0] for move in (one, two)], axis=1)
    near = lax.all_gather(near, "dp", axis_index_groups=zone)
    prepared = prepare(core, lengths, tokens, cotangent, small_params)
    last = jnp.concatenate([move.pop("held")[0] for move in (three, four)], axis=1)
    near, last, prepared = lax.optimization_barrier((near, last, prepared))
    hidden, hidden_turned, grad_rows, *prepared = prepared
    vectors, value_bias, up_bias = prepared[0::3], prepared[1::3], prepared[2::3]
    last = lax.all_gather(last, ("dp", "tensor")).reshape(parts, 2, row_count, -1)
    three["pair"], four["pair"] = (last, last, 0), (last, last, 3 * half_d)
    one.update(links.gather_last(near[:, :, : 3 * half_d]))
    two.update(links.gather_last(near[:, :, 3 * half_d :]))
    links.advance([one])
    links.advance([one])
    (hidden,) = links.advance([two], (hidden,))

    def gathered(layer_at, kind):
        for group, move in zip(groups, gathers):
            widths = [math.prod(table[name].shape[2:]) for _, name in group]
            if (layer_at, kind) in group:
                while links.running(move):
                    links.advance([move])
                if "held" in move:
                    links.pair(move)
                own, other, first = move["pair"]
                return own, other, first + sum(widths[: group.index((layer_at, kind))])

    saved = []
    hidden_low = hidden
    masters = (proj_weight, out_weight, up_weight, down_weight)
    for layer_at in range(layers):
        projected = project(
            turns[layer_at, "proj"], hidden_low, gathered(layer_at, "proj"), value_bias[layer_at]
        )
        if layer_at == 0:
            (projected,) = links.advance([two], (projected,))
        chain = [projected] + [earlier["projected"] for earlier in reversed(saved)]
        context, log_norm = attend_forward(core, lengths, chain, seq_len)
        if layer_at == 0:
            late_masters, context = lax.optimization_barrier((masters, context))
            squares = [jnp.sum(one * one, axis=tuple(range(1, one.ndim))) for one in late_masters]
            squares = jnp.pad(jnp.stack(squares, axis=1), ((0, 0), (0, 124)))
            squares, context = links.pair(two, (squares, context))
        kept = {
            "input_turned": hidden_turned, "projected": projected, "log_norm": log_norm, "context": context,
        }
        (
            kept["first_in"], kept["first_low"], kept["first_turned"], kept["active"], kept["slope"], hidden, *rest,
        ) = feed_forward(
            turns[layer_at, "ff"], hidden, context, gathered(layer_at, "out"), gathered(layer_at, "up"),
            gathered(layer_at, "down"), up_bias[layer_at], vectors[layer_at],
            grad_rows if layer_at == layers - 1 else None,
        )
        if layer_at == layers - 1:
            turned_grad = rest
        else:
            kept["second_in"], hidden_low, hidden_turned = rest
        saved.append(kept)

    smalls = [None] * layers
    later_total = None
    before = []
    for layer_at in reversed(range(layers)):
        kept = saved[layer_at]
        places_ff = turns[layer_at, "ff"]
        first_grad, down_low, down_turned, second_small = turned_grad
        own, other, bias_sum, first_grad = feed_backward(
            places_ff, first_grad, down_low, down_turned,
            [kept[name] for name in ("first_turned", "active", "slope")],
            gathered(layer_at, "up"), gathered(layer_at, "down"), parts,
        )
        ff_sum = links.scatter(own, other)
        (first_grad,) = links.advance(before + [ff_sum], (first_grad,))
        first_in_grad, out_in_turned, context_grad, first_small = context_backward(
            places_ff, first_grad, kept["first_in"], gathered(layer_at, "out"), vectors[layer_at]
        )
        (context_grad,) = links.advance([ff_sum] + before[1:], (context_grad,))
        chain = [kept["projected"]] + [earlier["projected"] for earlier in reversed(saved[:layer_at])]
        results = attend_backward(
            core, lengths, chain, kept["log_norm"], context_grad, later_total, layer_at > 0, seq_len
        )
        head_grads, value_sum = results[:2]
        later_total = results[2] if layer_at > 0 else None
        smalls[layer_at] = (value_sum, first_small, second_small, [bias_sum])
        if layer_at == 0:
            (head_grads,) = links.advance(before, (head_grads,))
            packed = pack(core, smalls, squares)
            packed, head_grads = links.advance([ff_sum], (packed, head_grads))
            packed = links.total(packed)
        attention_sum = links.scatter(
            *projection_grads(
                exchanged, out_in_turned, kept["context"], kept["input_turned"], head_grads, parts
            )
        )
        if layer_at > 0:
            (head_grads,) = links.advance([ff_sum, attention_sum], (head_grads,))
            turned_grad = project_backward(
                turns[layer_at, "proj"], head_grads, first_in_grad, gathered(layer_at, "proj"),
                (saved[layer_at - 1]["second_in"], vectors[layer_at - 1]),
            )
            turned_grad = links.advance([attention_sum], turned_grad)
        else:
            links.advance([attention_sum, packed])
            (head_grads,) = links.advance([attention_sum, before[1]], (head_grads,))
            (grad_rows,) = project_backward(
                turns[layer_at, "proj"], head_grads, first_in_grad, gathered(layer_at, "proj")
            )
        before += [ff_sum, attention_sum]

    width = small_params.shape[1]
    (grad_rows,) = links.advance([ff_sum, attention_sum], (grad_rows,))
    later_sums, grad_rows = links.settle(before[:2], grad_rows)
    sent = (links.sibling(grad_rows), links.sibling(hidden))
    links.advance([packed])
    links.advance([attention_sum])
    links.advance([ff_sum])
    hidden, grad_rows = join(core, ((hidden, sent[1]), (grad_rows, sent[0])))
    hidden, grad_rows = links.advance([packed], (hidden, grad_rows))
    links.advance([attention_sum])
    packed = links.finish([packed])[0]
    small_grad = packed[:, :width]
    weight_square = packed[:, width : width + 4].T

    ff_sums, attention_sums = (
        jnp.stack([earlier, later]) for earlier, later in zip(links.finish([ff_sum, attention_sum]), later_sums)
    )
    grads = (
        attention_sums[:, 1:].transpose(0, 2, 1, 3), attention_sums[:, 0], ff_sums[:, 1], ff_sums[:, 0],
    )
    firsts = (proj_first, out_first, up_first, down_first)
    seconds = (proj_second, out_second, up_second, down_second)
    square_part = sum(jnp.sum(grad * grad) for grad in grads)
    square_big = links.finish([links.total(jnp.broadcast_to(square_part, (8, 128)))])[0][0, 0]
    grad_norm = jnp.sqrt(square_big + jnp.sum(small_grad * small_grad))
    factor = clip_norm / jnp.maximum(grad_norm, clip_norm)
    moments = []
    updates = []
    for kind_at in range(4):
        first_new, second_new, direction = adam_parts(
            grads[kind_at], firsts[kind_at], seconds[kind_at], factor
        )
        moments.append((first_new, second_new))
        updates.append(direction + decay_rate * masters[kind_at])
    update_square = jnp.stack(
        [jnp.sum(update * update, axis=tuple(range(1, update.ndim))) for update in updates]
    )
    update_square = jnp.pad(update_square.reshape(1, -1), ((0, 7), (0, 128 - 4 * layers)))
    update_square = links.finish([links.total(update_square)])[0]
    update_square = update_square[0, : 4 * layers].reshape(4, layers)
    ratio = jnp.sqrt(weight_square) / jnp.sqrt(update_square)

    outputs = [hidden, grad_rows, grad_norm]
    for kind_at in range(4):
        master = masters[kind_at]
        scaled = ratio[kind_at].reshape((-1,) + (1,) * (master.ndim - 1))
        outputs += [
            moments[kind_at][0],
            moments[kind_at][1],
            master - matrix_rate * scaled * updates[kind_at],
        ]
    small_first_new, small_second_new, small_direction = adam_parts(
        small_grad, small_first, small_second, factor
    )
    outputs += [small_first_new, small_second_new, small_params - vector_rate * small_direction]
    return tuple(outputs)


def solution(mesh):
    proj = P(None, "dp", None, "tensor")
    matrix = P(None, "dp", "tensor")
    rows = P("dp", None)
    return jax.shard_map(
        local,
        mesh=mesh,
        in_specs=(rows, rows, P("dp"), proj, matrix, matrix, matrix, P())
        + (proj, proj)
        + (matrix,) * 6
        + (P(), P()),
        out_specs=(rows, rows, P()) + (proj,) * 3 + (matrix,) * 9 + (P(),) * 3,
        check_vma=False,
    )
```

time: 574 us -> 563 us (0.981)
  waiting for transfers between devices: 197 us -> 179 us
  Pallas kernels: 195 us -> 207 us
    ppermute x36 -> x38, waiting for transfers between devices: 192 us -> 126 us  [swap(): return lax.ppermute(value, ('dp', 'tensor'), pairs)]
    all_gather x3 -> x2, waiting for transfers between devices: 0.01 us -> 33.5 us  [the longest x1 33.5 us: local(): near = lax.all_gather(near, 'dp', axis_index_groups=zone)]
    ppermute x9 -> x11, waiting for transfers between devices: 5.41 us -> 19.4 us  [sibling(): return lax.ppermute(value, 'tensor', [(0, 1), (1, 0)])]
    pallas_call x12 -> x15, Pallas kernels: 141 us -> 152 us  [the longest x12 142 us: call(): pl.pallas_call(lambda at, *refs: kernel(*weight_rows(at), Row(at, 0), Row...]
    convert_element_type x16, other arithmetic: 32.5 us -> 39.4 us  [advance(): sum((piece[half:size].astype(f32) for piece in move['pieces'])).astype(bf16)]
    ppermute x36 -> x38, starting transfers between devices: 48.5 us -> 43.9 us  [swap(): return lax.ppermute(value, ('dp', 'tensor'), pairs)]
    unnamed x116 -> x111, local copies, waits for them, and re-layouts: 14.1 us -> 18.5 us
  transfers between devices with their start and end apart: 48 -> 51, of which waited for: 26 -> 26; matrix products, arithmetic and copies ran while one was open for 10% -> 10% of each run, Pallas kernels for 27% -> 25%
where the time goes in v3:
time: 563 us; the launch traced here: 553 us
  Pallas kernels  207 us (37%)
  waiting for transfers between devices  179 us (32%)
  other arithmetic  76.3 us (14%)
  starting transfers between devices  45.1 us (8%)
  local copies, waits for them, and re-layouts  25.9 us (5%)
  between operations  20.3 us (4%)
    pallas_call x12, Pallas kernels, call(): pl.pallas_call(lambda at, *refs: kernel(*weight_rows(at), Row(at, 0), Row...  142 us
    ppermute x38, waiting for transfers between devices, swap(): return lax.ppermute(value, ('dp', 'tensor'), pairs)  126 us
    ppermute x38, starting transfers between devices, swap(): return lax.ppermute(value, ('dp', 'tensor'), pairs)  43.9 us
    convert_element_type x16, other arithmetic, advance(): sum((piece[half:size].astype(f32) for piece in move['pieces'])).astype(bf16)  39.4 us
    pallas_call x2, Pallas kernels, attend_backward(): pl.pallas_call(partial(attend_backward_kernel, depth=depth, with_later=la...  34.8 us
    all_gather x1, waiting for transfers between devices, local(): near = lax.all_gather(near, 'dp', axis_index_groups=zone)  33.5 us
    pallas_call x2, Pallas kernels, attend_forward(): pl.pallas_call(partial(attend_forward_kernel, depth=depth), out_shape=[ja...  19.7 us
    ppermute x11, waiting for transfers between devices, sibling(): return lax.ppermute(value, 'tensor', [(0, 1), (1, 0)])  19.4 us
  transfers between devices with their start and end apart: 51, of which 26 were waited for; matrix products, arithmetic and copies ran while one was open for 10% of the time, Pallas kernels for 25%

profile of v3, /device:TPU:0, one launch (start us, length us, event | category | flops | bytes accessed | tf_op | source)
XLA Modules:
  0.0 553.2 jit_solution(12282621459775819237)
XLA Ops:
  11.9 2.1 prepare.1
  21.4 33.5 %all-gather.5.cloned.1.call-done = bf16[192,4608]{1,0:T(8,128)(2,1)} async-done(((bf16[48,4608]{1,0:T(8,128)(2,1)}), bf16[192,4608]{1,0:T(8,128)(2,1)}) %all-gather.5.cloned.1.call-update) | async-done | bytes 1769488 | tf_op jit(solution)/shard_map/all_gather | solution.py:839
  57.5 6.8 %collective-permute-done = bf16[4,48,1152]{2,1,0:T(8,128)(2,1)S(1)} collective-permute-done((bf16[4,48,1152]{2,1,0:T(8,128)(2,1)S(1)}, bf16[4,48,1152]{2,1,0:T(8,128)(2,1)S(1)}, u32[]{:S(2)}, u32[]{:S(2)}) %collective-permute-start) | collective-permute-done | bytes 442400 | tf_op jit(solution)/shard_map/ppermute | solution.py:66
  66.0 14.7 %collective-permute-done.1 = bf16[8,48,1152]{2,1,0:T(8,128)(2,1)S(1)} collective-permute-done((bf16[8,48,1152]{2,1,0:T(8,128)(2,1)S(1)}, bf16[8,48,1152]{2,1,0:T(8,128)(2,1)S(1)}, u32[]{:S(2)}, u32[]{:S(2)}) %collective-permute-start.1) | collective-permute-done | bytes 884768 | tf_op jit(solution)/shard_map/ppermute | solution.py:66
  85.1 7.3 %project.2.refs_0_.refs_1_.refs_2_.refs_3_ = bf16[512,2304]{1,0:T(8,128)(2,1)} custom-call(s32[6,17]{1,0:T(8,128)} %dynamic-slice_bitcast_fusion.at, bf16[512,768]{1,0:T(8,128)(2,1)} %copy-done.7, bf16[16,48,1152]{2,1,0:T(8,128)(2,1)} %copy-done.25, bf16[16,48,1152]{2,1,0:T(8,128)(2,1)} %collective-permute-done.2.refs_2_.refs_3_, f32[1,2304]{1,0:T(1,128)} %copy-done.23), custom_call_target="tpu_custom_call" | custom-call | bytes 17500000 | tf_op jit(solution)/shard_map/project/pallas_call | solution.py:216
  92.4 21.1 %collective-permute-done.3 = bf16[4,48,3456]{2,1,0:T(8,128)(2,1)} collective-permute-done((bf16[4,48,3456]{2,1,0:T(8,128)(2,1)}, bf16[4,48,3456]{2,1,0:T(8,128)(2,1)}, u32[]{:S(2)}, u32[]{:S(2)}) %collective-permute-start.3) | collective-permute-done | bytes 1327136 | tf_op jit(solution)/shard_map/ppermute | solution.py:66
  113.5 3.5 pad_maximum_fusion
  117.9 9.6 %attend_forward.2 = (bf16[512,768]{1,0:T(8,128)(2,1)S(1)}, f32[6,8,512]{2,1,0:T(8,128)S(1)}) custom-call(s32[1]{0:T(128)} %bitcast.8.core, s32[2]{0:T(128)S(1)} %copy-done.19, bf16[512,2304]{1,0:T(8,128)(2,1)S(1)} %copy-done, bf16[512,2304]{1,0:T(8,128)(2,1)S(1)} %copy-done, bf16[512,2304]{1,0:T(8,128)(2,1)S(1)} %copy-done), custom_call_target="tpu_custom_call" | custom-call | bytes 25000000 | tf_op jit(solution)/shard_map/attend_forward/pallas_call | solution.py:706
  131.1 1.9 constant_dynamic-update-slice_fusion.1
  133.1 41.5 %collective-permute-done.4 = bf16[8,48,3456]{2,1,0:T(8,128)(2,1)} collective-permute-done((bf16[8,48,3456]{2,1,0:T(8,128)(2,1)}, bf16[8,48,3456]{2,1,0:T(8,128)(2,1)}, u32[]{:S(2)}, u32[]{:S(2)}) %collective-permute-start.4) | collective-permute-done | bytes 2654240 | tf_op jit(solution)/shard_map/ppermute | solution.py:66
  174.6 2.1 constant_dynamic-update-slice_fusion.refs_2_.refs_4_.refs_6_.refs_8_
  176.7 2.3 copy-done.24
  179.1 9.3 %collective-permute-done.5.refs_3_.refs_5_.refs_7_.refs_9_ = bf16[16,48,3456]{2,1,0:T(8,128)(2,1)} collective-permute-done((bf16[16,48,3456]{2,1,0:T(8,128)(2,1)S(1)}, bf16[16,48,3456]{2,1,0:T(8,128)(2,1)}, u32[]{:S(2)}, u32[]{:S(2)}) %collective-permute-start.5) | collective-permute-done | bytes 5308448 | tf_op jit(solution)/shard_map/ppermute | solution.py:69
  188.3 19.3 %feed_forward.2 = (f32[512,768]{1,0:T(8,128)}, bf16[512,768]{1,0:T(8,128)(2,1)}, bf16[768,512]{1,0:T(8,128)(2,1)}, bf16[2,512,1536]{2,1,0:T(8,128)(2,1)}, f32[2,...) custom-call(s32[6,17]{1,0:T(8,128)} %dynamic-slice_bitcast_fusion.at, ...), custom_call_target="tpu_custom_call" | custom-call | bytes 45000000 | tf_op jit(solution)/shard_map/feed_forward/pallas_call | solution.py:216
  207.7 6.8 %project.3.refs_0_.refs_2_.refs_4_ = bf16[512,2304]{1,0:T(8,128)(2,1)} custom-call(s32[6,17]{1,0:T(8,128)} %dynamic-slice_bitcast_fusion.at, bf16[512,768]{1,0:T(8,128)(2,1)} %get-tuple-element.257.refs_0_, bf16[16,2,48,4608]{3,2,1,0:T(8,128)(2,1)} %bitcast.88, bf16[16,2,48,4608]{3,2,1,0:T(8,128)(2,1)} %bitcast.89, f32[1,2304]{1,0:T(1,128)} %copy-done.22), custom_call_target="tpu_custom_call" | custom-call | bytes 17500000 | tf_op jit(solution)/shard_map/project/pallas_call | solution.py:216
  216.1 10.1 %attend_forward.3 = (bf16[512,768]{1,0:T(8,128)(2,1)S(1)}, f32[6,8,512]{2,1,0:T(8,128)S(1)}) custom-call(s32[1]{0:T(128)} %bitcast.8.core, s32[2]{0:T(128)S(1)} %copy-done.19, bf16[512,2304]{1,0:T(8,128)(2,1)S(1)} %copy-done.2, bf16[512,2304]{1,0:T(8,128)(2,1)S(1)} %copy-done, bf16[512,2304]{1,0:T(8,128)(2,1)S(1)} %copy-done.2, ...), custom_call_target="tpu_custom_call" | custom-call | bytes 25000000 | tf_op jit(solution)/shard_map/attend_forward/pallas_call | solution.py:706
  227.1 21.4 %feed_forward.3 = (f32[512,768]{1,0:T(8,128)}, bf16[512,768]{1,0:T(8,128)(2,1)}, bf16[768,512]{1,0:T(8,128)(2,1)}, bf16[2,512,1536]{2,1,0:T(8,128)(2,1)}, f32[2,...) custom-call(s32[6,17]{1,0:T(8,128)} %dynamic-slice_bitcast_fusion.at, ...), custom_call_target="tpu_custom_call" | custom-call | bytes 45000000 | tf_op jit(solution)/shard_map/feed_forward/pallas_call | solution.py:216
  248.6 20.3 %feed_backward.2 = (bf16[16,2,48,1536]{3,2,1,0:T(8,128)(2,1)}, bf16[16,2,48,1536]{3,2,1,0:T(8,128)(2,1)}, f32[2,8,1536]{2,1,0:T(8,128)}, f32[512,768]{1,0:T(8,128)}) custom-call(s32[6,17]{1,0:T(8,128)} %dynamic-slice_bitcast_fusion.at, f32[512,768]{1,0:T(8,128)} %get-tuple-element.264.refs_0_, bf16[512,768]{1,0:T(8,128)(2,1)} %get-tuple-element.265.refs_1_, ...), custom_call_target="tpu_custom_call" | custom-call | bytes 50000000 | tf_op jit(solution)/shard_map/feed_backward/pallas_call | solution.py:216
  269.3 6.0 %context_backward.2 = (f32[512,768]{1,0:T(8,128)}, bf16[768,512]{1,0:T(8,128)(2,1)}, bf16[512,768]{1,0:T(8,128)(2,1)}, f32[8,768]{1,0:T(8,128)}) custom-call(s32[6,17]{1,0:T(8,128)} %dynamic-slice_bitcast_fusion.at, f32[512,768]{1,0:T(8,128)} %get-tuple-element.274.refs_0_, f32[512,768]{1,0:T(8,128)} %get-tuple-element.275.refs_1_, ...), custom_call_target="tpu_custom_call" | custom-call | bytes 15000000 | tf_op jit(solution)/shard_map/context_backward/pallas_call | solution.py:216
  275.3 1.8 collective-permute-done.6
  277.2 3.1 add_convert_fusion.1
  281.4 18.4 %attend_backward.2 = (bf16[3,512,768]{2,1,0:T(8,128)(2,1)S(1)}, f32[1,8,768]{2,1,0:T(8,128)S(1)}, f32[12,512,512]{2,1,0:T(8,128)}) custom-call(s32[1]{0:T(128)} %bitcast.8.core, s32[2]{0:T(128)S(1)} %copy-done.19, bf16[512,2304]{1,0:T(8,128)(2,1)S(1)} %copy-done.3, bf16[512,2304]{1,0:T(8,128)(2,1)} %project.2.refs_0_.refs_1_.refs_2_.refs_3_, ...), custom_call_target="tpu_custom_call" | custom-call | bytes 42500000 | tf_op jit(solution)/shard_map/attend_backward/pallas_call | solution.py:773
  301.8 8.2 %projection_grads.2 = (bf16[16,4,48,384]{3,2,1,0:T(8,128)(2,1)}, bf16[16,4,48,384]{3,2,1,0:T(8,128)(2,1)}) custom-call(s32[6,17]{1,0:T(8,128)} %dynamic-slice_bitcast_fusion.at, bf16[768,512]{1,0:T(8,128)(2,1)} %get-tuple-element.279.refs_0_, bf16[512,768]{1,0:T(8,128)(2,1)} %copy-done.6, bf16[768,512]{1,0:T(8,128)(2,1)} %get-tuple-element.280.refs_2_, ...), custom_call_target="tpu_custom_call" | custom-call | bytes 22500000 | tf_op jit(solution)/shard_map/projection_grads/pallas_call | solution.py:216
  310.1 3.5 add_convert_fusion.5
  314.7 10.0 %project_backward.2 = (f32[512,768]{1,0:T(8,128)}, bf16[512,768]{1,0:T(8,128)(2,1)}, bf16[768,512]{1,0:T(8,128)(2,1)}, f32[8,768]{1,0:T(8,128)}) custom-call(s32[6,17]{1,0:T(8,128)} %dynamic-slice_bitcast_fusion.at, bf16[3,512,768]{2,1,0:T(8,128)(2,1)} %copy-done.4, f32[512,768]{1,0:T(8,128)} %get-tuple-element.292.refs_1_, ...), custom_call_target="tpu_custom_call" | custom-call | bytes 20000000 | tf_op jit(solution)/shard_map/project_backward/pallas_call | solution.py:216
  324.7 2.6 add_convert_fusion.4
  328.5 21.1 %feed_backward.3 = (bf16[16,2,48,1536]{3,2,1,0:T(8,128)(2,1)}, bf16[16,2,48,1536]{3,2,1,0:T(8,128)(2,1)}, f32[2,8,1536]{2,1,0:T(8,128)}, f32[512,768]{1,0:T(8,128)}) custom-call(s32[6,17]{1,0:T(8,128)} %dynamic-slice_bitcast_fusion.at, f32[512,768]{1,0:T(8,128)} %get-tuple-element.305.refs_0_, bf16[512,768]{1,0:T(8,128)(2,1)} %get-tuple-element.306.refs_1_, ...), custom_call_target="tpu_custom_call" | custom-call | bytes 50000000 | tf_op jit(solution)/shard_map/feed_backward/pallas_call | solution.py:216
  349.6 2.7 add_convert_fusion.9
  352.3 2.3 add_convert_fusion.8
  355.3 6.0 %context_backward.3 = (f32[512,768]{1,0:T(8,128)}, bf16[768,512]{1,0:T(8,128)(2,1)}, bf16[512,768]{1,0:T(8,128)(2,1)}, f32[8,768]{1,0:T(8,128)}) custom-call(s32[6,17]{1,0:T(8,128)} %dynamic-slice_bitcast_fusion.at, f32[512,768]{1,0:T(8,128)} %get-tuple-element.321.refs_0_, f32[512,768]{1,0:T(8,128)} %get-tuple-element.322.refs_1_, ...), custom_call_target="tpu_custom_call" | custom-call | bytes 15000000 | tf_op jit(solution)/shard_map/context_backward/pallas_call | solution.py:216
  361.3 3.5 collective-permute-done.12
  364.8 2.0 add_convert_fusion.13
  366.8 3.2 add_convert_fusion
  371.8 16.5 %attend_backward.3 = (bf16[3,512,768]{2,1,0:T(8,128)(2,1)S(1)}, f32[1,8,768]{2,1,0:T(8,128)S(1)}) custom-call(s32[1]{0:T(128)} %bitcast.8.core, s32[2]{0:T(128)S(1)} %copy-done.19, bf16[512,2304]{1,0:T(8,128)(2,1)S(1)} %copy-done.1, bf16[512,2304]{1,0:T(8,128)(2,1)S(1)} %copy-done.1, bf16[512,2304]{1,0:T(8,128)(2,1)S(1)} %copy-done.1, ...), custom_call_target="tpu_custom_call" | custom-call | bytes 42500000 | tf_op jit(solution)/shard_map/attend_backward/pallas_call | solution.py:773
  393.1 2.2 add_convert_fusion.12
  395.3 3.1 collective-permute-done.14
  398.4 1.9 add_convert_fusion.15
  400.3 3.5 add_convert_fusion.3
  403.7 8.2 %projection_grads.3 = (bf16[16,4,48,384]{3,2,1,0:T(8,128)(2,1)}, bf16[16,4,48,384]{3,2,1,0:T(8,128)(2,1)}) custom-call(s32[6,17]{1,0:T(8,128)} %dynamic-slice_bitcast_fusion.at, bf16[768,512]{1,0:T(8,128)(2,1)} %get-tuple-element.323.refs_0_, bf16[512,768]{1,0:T(8,128)(2,1)} %copy-done.8, bf16[768,512]{1,0:T(8,128)(2,1)} %copy-done.13, ...), custom_call_target="tpu_custom_call" | custom-call | bytes 22500000 | tf_op jit(solution)/shard_map/projection_grads/pallas_call | solution.py:216
  412.9 3.8 collective-permute-done.16
  416.7 3.4 add_convert_fusion.2
  424.0 7.8 %project_backward.3.refs_2_ = f32[512,768]{1,0:T(8,128)} custom-call(s32[6,17]{1,0:T(8,128)} %dynamic-slice_bitcast_fusion.at, bf16[3,512,768]{2,1,0:T(8,128)(2,1)} %copy-done.5, f32[512,768]{1,0:T(8,128)} %get-tuple-element.375.refs_1_, bf16[16,48,1152]{2,1,0:T(8,128)(2,1)} %copy-done.25, bf16[16,48,1152]{2,1,0:T(8,128)(2,1)} %collective-permute-done.2.refs_2_.refs_3_), custom_call_target="tpu_custom_call" | custom-call | bytes 20000000 | tf_op jit(solution)/shard_map/project_backward/pallas_call | solution.py:216
  431.8 1.9 collective-permute-done.17
  433.7 1.9 add_convert_fusion.7
  435.6 5.1 collective-permute-done.18
  442.2 2.1 collective-permute-done.22
  448.5 2.2 collective-permute-done.19
  450.7 1.8 collective-permute-start.26
  452.5 4.6 collective-permute-done.24
  457.1 2.2 add_convert_fusion.11
  459.3 6.6 %collective-permute-done.25 = bf16[2,2,48,1536]{3,2,1,0:T(8,128)(2,1)S(1)} collective-permute-done((bf16[2,2,48,1536]{3,2,1,0:T(8,128)(2,1)S(1)}, bf16[2,2,48,1536]{3,2,1,0:T(8,128)(2,1)S(1)}, u32[]{:S(2)}, u32[]{:S(2)}) %collective-permute-start.25) | collective-permute-done | bytes 589856 | tf_op jit(solution)/shard_map/ppermute | solution.py:66
  465.9 2.1 collective-permute-start.28
  468.0 2.2 add_convert_fusion.10
  470.2 2.3 collective-permute-start.31
  472.5 6.0 %join.1 = (f32[1024,768]{1,0:T(8,128)}, f32[1024,768]{1,0:T(8,128)}) custom-call(s32[1]{0:T(128)} %bitcast.8.core, f32[512,768]{1,0:T(8,128)} %get-tuple-element.385.refs_0_, f32[512,768]{1,0:T(8,128)} %collective-permute-done.20.refs_1_, f32[512,768]{1,0:T(8,128)} %project_backward.3.refs_2_, f32[512,768]{1,0:T(8,128)} %copy-done.41), custom_call_target="tpu_custom_call" | custom-call | bytes 10000000 | tf_op jit(solution)/shard_map/join/pallas_call | solution.py:541
  480.2 3.8 collective-permute-done.29
  506.2 2.6 collective-permute-done.35
  513.8 2.2 collective-permute-done.38
  517.9 2.6 multiply_reduce_fusion.6
  521.7 2.3 multiply_reduce_fusion.1
  525.3 2.8 collective-permute-start.44
  529.8 3.7 collective-permute-done.45
  534.4 2.5 collective-permute-start.48
  539.4 2.5 multiply_subtract_fusion
  (249 shorter events, 88.6 us)
Async XLA Ops:
  7.2 47.7 %all-gather.5.cloned.1.call-start = ((), (), s32[]{:S(2)}) async-start(), calls=%async_computation | async-start | bytes 2211840 | tf_op jit(solution)/shard_map/all_gather | solution.py:839
  11.7 196.0 %all-gather.7.cloned.1.call-start = ((), (), s32[]{:S(2)}) async-start(), calls=%async_computation.1 | async-start | bytes 14598144 | tf_op jit(solution)/shard_map/all_gather | solution.py:845
  56.0 25.0 %copy-start.38 = (bf16[192,4608]{1,0:T(8,128)(2,1)S(1)}, bf16[192,4608]{1,0:T(8,128)(2,1)}, u32[]{:S(2)}) copy-start(bf16[192,4608]{1,0:T(8,128)(2,1)} %all-gather.5.cloned.1.call-done) | copy-start | bytes 5308420
  56.0 8.4 %collective-permute-start = (bf16[4,48,1152]{2,1,0:T(8,128)(2,1)S(1)}, bf16[4,48,1152]{2,1,0:T(8,128)(2,1)S(1)}, u32[]{:S(2)}, u32[]{:S(2)}) collective-permute-start(bf16[4,48,1152]{2,1,0:T(8,128)(2,1)S(1)} %slice.311), channel_id=1, source_target_pairs={{0,2},{2,0},{4,6},{6,4},{8,10},{10,8},{12,14},{14,12},{16,18},{18,... | collective-permute-start | bytes 1327112 | tf_op jit(solution)/shard_map/ppermute | solution.py:66
  64.4 16.3 %collective-permute-start.1 = (bf16[8,48,1152]{2,1,0:T(8,128)(2,1)S(1)}, bf16[8,48,1152]{2,1,0:T(8,128)(2,1)S(1)}, u32[]{:S(2)}, u32[]{:S(2)}) collective-permute-start(bf16[8,48,1152]{2,1,0:T(8,128)(2,1)S(1)} %pad_maximum_fusion.2), channel_id=1, source_target_pairs={{0,4},{2,6},{4,0},{6,2},{8,12},{10,14},{12,8},{14,10},{16,20},{18,... | collective-permute-start | bytes 2654216 | tf_op jit(solution)/shard_map/ppermute | solution.py:66
  80.9 4.2 collective-permute-start.2
  82.3 31.1 %collective-permute-start.3 = (bf16[4,48,3456]{2,1,0:T(8,128)(2,1)}, bf16[4,48,3456]{2,1,0:T(8,128)(2,1)}, u32[]{:S(2)}, u32[]{:S(2)}) collective-permute-start(bf16[4,48,3456]{2,1,0:T(8,128)(2,1)} %slice.310), channel_id=1, source_target_pairs={{0,2},{2,0},{4,6},{6,4},{8,10},{10,8},{12,14},{14,12},{16,18},{18,... | collective-permute-start | bytes 3981320 | tf_op jit(solution)/shard_map/ppermute | solution.py:66
  92.4 25.6 %copy-start = (bf16[512,2304]{1,0:T(8,128)(2,1)S(1)}, bf16[512,2304]{1,0:T(8,128)(2,1)}, u32[]{:S(2)}) copy-start(bf16[512,2304]{1,0:T(8,128)(2,1)} %project.2.refs_0_.refs_1_.refs_2_.refs_3_) | copy-start | bytes 7077892
  117.0 11.4 %copy-start.28 = (f32[2,48,3,384]{3,1,2,0:T(8,128)S(1)}, f32[2,48,3,384]{3,1,2,0:T(8,128)}, u32[]{:S(2)}) copy-start(f32[2,48,3,384]{3,1,2,0:T(8,128)} %param.22) | copy-start | bytes 1327108
  117.0 13.2 %copy-start.26 = (f32[2,48,1536]{2,1,0:T(8,128)S(1)}, f32[2,48,1536]{2,1,0:T(8,128)}, u32[]{:S(2)}) copy-start(f32[2,48,1536]{2,1,0:T(8,128)} %param.25) | copy-start | bytes 1769476
  117.0 57.6 %collective-permute-start.4 = (bf16[8,48,3456]{2,1,0:T(8,128)(2,1)}, bf16[8,48,3456]{2,1,0:T(8,128)(2,1)}, u32[]{:S(2)}, u32[]{:S(2)}) collective-permute-start(bf16[8,48,3456]{2,1,0:T(8,128)(2,1)} %pad_maximum_fusion), channel_id=1, source_target_pairs={{0,4},{2,6},{4,0},{6,2},{8,12},{10,14},{12,8},{14,10},{16,20},{18,... | collective-permute-start | bytes 7962632 | tf_op jit(solution)/shard_map/ppermute | solution.py:66
  179.1 9.3 %collective-permute-start.5 = (bf16[16,48,3456]{2,1,0:T(8,128)(2,1)S(1)}, bf16[16,48,3456]{2,1,0:T(8,128)(2,1)}, u32[]{:S(2)}, u32[]{:S(2)}) collective-permute-start(bf16[16,48,3456]{2,1,0:T(8,128)(2,1)S(1)} %constant_dynamic-update-slice_fusion.refs_2_.refs_4_.refs_6_.refs_8_), channel_id=1, source_target_pairs={{0,1},{1,0},{2,3},{3,2},{4,5},{5,4},{6,7},{7,6},{8,9},{9,8},{10,11... | collective-permute-start | bytes 15925256 | tf_op jit(solution)/shard_map/ppermute | solution.py:69
  268.8 8.3 %collective-permute-start.6 = (bf16[16,2,48,1536]{3,2,1,0:T(8,128)(2,1)}, bf16[16,2,48,1536]{3,2,1,0:T(8,128)(2,1)}, u32[]{:S(2)}, u32[]{:S(2)}) collective-permute-start(bf16[16,2,48,1536]{3,2,1,0:T(8,128)(2,1)} %get-tuple-element.277), channel_id=1, source_target_pairs={{0,1},{1,0},{2,3},{3,2},{4,5},{5,4},{6,7},{7,6},{8,9},{9,8},{10,11... | collective-permute-start | bytes 14155784 | tf_op jit(solution)/shard_map/ppermute | solution.py:69
  280.2 29.8 %collective-permute-start.7 = (bf16[8,2,48,1536]{3,2,1,0:T(8,128)(2,1)S(1)}, bf16[8,2,48,1536]{3,2,1,0:T(8,128)(2,1)}, u32[]{:S(2)}, u32[]{:S(2)}) collective-permute-start(bf16[8,2,48,1536]{3,2,1,0:T(8,128)(2,1)S(1)} %add_convert_fusion.1), channel_id=1, source_target_pairs={{0,4},{2,6},{4,0},{6,2},{8,12},{10,14},{12,8},{14,10},{16,20},{18,... | collective-permute-start | bytes 7077896 | tf_op jit(solution)/shard_map/ppermute | solution.py:66
  313.6 11.1 %collective-permute-start.8 = (bf16[16,4,48,384]{3,2,1,0:T(8,128)(2,1)}, bf16[16,4,48,384]{3,2,1,0:T(8,128)(2,1)}, u32[]{:S(2)}, u32[]{:S(2)}) collective-permute-start(bf16[16,4,48,384]{3,2,1,0:T(8,128)(2,1)} %get-tuple-element.300), channel_id=1, source_target_pairs={{0,1},{1,0},{2,3},{3,2},{4,5},{5,4},{6,7},{7,6},{8,9},{9,8},{10,11... | collective-permute-start | bytes 7077896 | tf_op jit(solution)/shard_map/ppermute | solution.py:69
  314.0 35.6 %collective-permute-start.9 = (bf16[4,2,48,1536]{3,2,1,0:T(8,128)(2,1)}, bf16[4,2,48,1536]{3,2,1,0:T(8,128)(2,1)}, u32[]{:S(2)}, u32[]{:S(2)}) collective-permute-start(bf16[4,2,48,1536]{3,2,1,0:T(8,128)(2,1)} %add_convert_fusion.5), channel_id=1, source_target_pairs={{0,2},{2,0},{4,6},{6,4},{8,10},{10,8},{12,14},{14,12},{16,18},{18,... | collective-permute-start | bytes 3538952 | tf_op jit(solution)/shard_map/ppermute | solution.py:66
  314.7 10.0 %copy-start.31 = (bf16[16,4,48,384]{3,2,1,0:T(8,128)(2,1)S(1)}, bf16[16,4,48,384]{3,2,1,0:T(8,128)(2,1)}, u32[]{:S(2)}) copy-start(bf16[16,4,48,384]{3,2,1,0:T(8,128)(2,1)} %get-tuple-element.392) | copy-start | bytes 7077892
  327.3 25.0 %collective-permute-start.10 = (bf16[8,4,48,384]{3,2,1,0:T(8,128)(2,1)}, bf16[8,4,48,384]{3,2,1,0:T(8,128)(2,1)}, u32[]{:S(2)}, u32[]{:S(2)}) collective-permute-start(bf16[8,4,48,384]{3,2,1,0:T(8,128)(2,1)} %add_convert_fusion.4), channel_id=1, source_target_pairs={{0,4},{2,6},{4,0},{6,2},{8,12},{10,14},{12,8},{14,10},{16,20},{18,... | collective-permute-start | bytes 3538952 | tf_op jit(solution)/shard_map/ppermute | solution.py:66
  354.6 12.2 %collective-permute-start.11 = (bf16[16,2,48,1536]{3,2,1,0:T(8,128)(2,1)}, bf16[16,2,48,1536]{3,2,1,0:T(8,128)(2,1)}, u32[]{:S(2)}, u32[]{:S(2)}) collective-permute-start(bf16[16,2,48,1536]{3,2,1,0:T(8,128)(2,1)} %get-tuple-element.328), channel_id=1, source_target_pairs={{0,1},{1,0},{2,3},{3,2},{4,5},{5,4},{6,7},{7,6},{8,9},{9,8},{10,11... | collective-permute-start | bytes 14155784 | tf_op jit(solution)/shard_map/ppermute | solution.py:69
  354.6 10.2 %collective-permute-start.12 = (bf16[4,4,48,384]{3,2,1,0:T(8,128)(2,1)}, bf16[4,4,48,384]{3,2,1,0:T(8,128)(2,1)}, u32[]{:S(2)}, u32[]{:S(2)}) collective-permute-start(bf16[4,4,48,384]{3,2,1,0:T(8,128)(2,1)} %add_convert_fusion.8), channel_id=1, source_target_pairs={{0,2},{2,0},{4,6},{6,4},{8,10},{10,8},{12,14},{14,12},{16,18},{18,... | collective-permute-start | bytes 1769480 | tf_op jit(solution)/shard_map/ppermute | solution.py:66
  370.0 30.2 %collective-permute-start.15 = (bf16[8,2,48,1536]{3,2,1,0:T(8,128)(2,1)S(1)}, bf16[8,2,48,1536]{3,2,1,0:T(8,128)(2,1)}, u32[]{:S(2)}, u32[]{:S(2)}) collective-permute-start(bf16[8,2,48,1536]{3,2,1,0:T(8,128)(2,1)S(1)} %add_convert_fusion), channel_id=1, source_target_pairs={{0,4},{2,6},{4,0},{6,2},{8,12},{10,14},{12,8},{14,10},{16,20},{18,... | collective-permute-start | bytes 7077896 | tf_op jit(solution)/shard_map/ppermute | solution.py:66
  370.9 22.1 %collective-permute-start.13 = (bf16[2,2,48,1536]{3,2,1,0:T(8,128)(2,1)}, bf16[2,2,48,1536]{3,2,1,0:T(8,128)(2,1)}, u32[]{:S(2)}, u32[]{:S(2)}) collective-permute-start(bf16[2,2,48,1536]{3,2,1,0:T(8,128)(2,1)} %add_convert_fusion.9), channel_id=1, source_target_pairs={{0,8},{2,10},{4,12},{6,14},{8,0},{10,2},{12,4},{14,6},{16,24},{18,... | collective-permute-start | bytes 1769480 | tf_op jit(solution)/shard_map/ppermute | solution.py:66
  390.3 8.1 %collective-permute-start.14 = (bf16[2,4,48,384]{3,2,1,0:T(8,128)(2,1)}, bf16[2,4,48,384]{3,2,1,0:T(8,128)(2,1)S(1)}, u32[]{:S(2)}, u32[]{:S(2)}) collective-permute-start(bf16[2,4,48,384]{3,2,1,0:T(8,128)(2,1)} %add_convert_fusion.13), channel_id=1, source_target_pairs={{0,8},{2,10},{4,12},{6,14},{8,0},{10,2},{12,4},{14,6},{16,24},{18,... | collective-permute-start | bytes 884744 | tf_op jit(solution)/shard_map/ppermute | solution.py:66
  412.0 4.7 collective-permute-start.16
  412.0 21.7 %collective-permute-start.17 = (bf16[4,2,48,1536]{3,2,1,0:T(8,128)(2,1)}, bf16[4,2,48,1536]{3,2,1,0:T(8,128)(2,1)}, u32[]{:S(2)}, u32[]{:S(2)}) collective-permute-start(bf16[4,2,48,1536]{3,2,1,0:T(8,128)(2,1)} %add_convert_fusion.3), channel_id=1, source_target_pairs={{0,2},{2,0},{4,6},{6,4},{8,10},{10,8},{12,14},{14,12},{16,18},{18,... | collective-permute-start | bytes 3538952 | tf_op jit(solution)/shard_map/ppermute | solution.py:66
  416.7 24.0 %copy-start.32 = (bf16[16,4,48,384]{3,2,1,0:T(8,128)(2,1)}, bf16[16,4,48,384]{3,2,1,0:T(8,128)(2,1)S(1)}, u32[]{:S(2)}) copy-start(bf16[16,4,48,384]{3,2,1,0:T(8,128)(2,1)S(1)} %collective-permute-done.16) | copy-start | bytes 7077892
  420.1 20.5 %collective-permute-start.18 = (bf16[8,4,48,384]{3,2,1,0:T(8,128)(2,1)}, bf16[8,4,48,384]{3,2,1,0:T(8,128)(2,1)}, u32[]{:S(2)}, u32[]{:S(2)}) collective-permute-start(bf16[8,4,48,384]{3,2,1,0:T(8,128)(2,1)} %add_convert_fusion.2), channel_id=1, source_target_pairs={{0,4},{2,6},{4,0},{6,2},{8,12},{10,14},{12,8},{14,10},{16,20},{18,... | collective-permute-start | bytes 3538952 | tf_op jit(solution)/shard_map/ppermute | solution.py:66
  421.1 49.1 %collective-permute-start.20 = (f32[512,768]{1,0:T(8,128)}, f32[512,768]{1,0:T(8,128)}, u32[]{:S(2)}, u32[]{:S(2)}) collective-permute-start(f32[512,768]{1,0:T(8,128)} %get-tuple-element.385.refs_0_), channel_id=1, source_target_pairs={{0,1},{1,0},{2,3},{3,2},{4,5},{5,4},{6,7},{7,6},{8,9},{9,8},{10,11... | collective-permute-start | bytes 4718600 | tf_op jit(solution)/shard_map/ppermute | solution.py:69
  421.1 24.4 %collective-permute-start.21 = (bf16[1,2,48,1536]{3,2,1,0:T(8,128)(2,1)}, bf16[1,2,48,1536]{3,2,1,0:T(8,128)(2,1)S(1)}, u32[]{:S(2)}, u32[]{:S(2)}) collective-permute-start(bf16[1,2,48,1536]{3,2,1,0:T(8,128)(2,1)} %add_convert_fusion.12), channel_id=1, source_target_pairs={{0,16},{2,18},{4,20},{6,22},{8,24},{10,26},{12,28},{14,30},{16,0},... | collective-permute-start | bytes 884744 | tf_op jit(solution)/shard_map/ppermute | solution.py:66
  422.7 21.6 %collective-permute-start.22 = (bf16[1,4,48,384]{3,2,1,0:T(8,128)(2,1)}, bf16[1,4,48,384]{3,2,1,0:T(8,128)(2,1)S(1)}, u32[]{:S(2)}, u32[]{:S(2)}) collective-permute-start(bf16[1,4,48,384]{3,2,1,0:T(8,128)(2,1)} %add_convert_fusion.15), channel_id=1, source_target_pairs={{0,16},{2,18},{4,20},{6,22},{8,24},{10,26},{12,28},{14,30},{16,0},... | collective-permute-start | bytes 442376 | tf_op jit(solution)/shard_map/ppermute | solution.py:66
  447.1 23.1 %collective-permute-start.23 = (f32[512,768]{1,0:T(8,128)S(1)}, f32[512,768]{1,0:T(8,128)S(1)}, u32[]{:S(2)}, u32[]{:S(2)}) collective-permute-start(f32[512,768]{1,0:T(8,128)S(1)} %copy-done.30), channel_id=1, source_target_pairs={{0,1},{1,0},{2,3},{3,2},{4,5},{5,4},{6,7},{7,6},{8,9},{9,8},{10,11... | collective-permute-start | bytes 4718600 | tf_op jit(solution)/shard_map/ppermute | solution.py:69
  447.2 9.9 %collective-permute-start.24 = (bf16[4,4,48,384]{3,2,1,0:T(8,128)(2,1)S(1)}, bf16[4,4,48,384]{3,2,1,0:T(8,128)(2,1)S(1)}, u32[]{:S(2)}, u32[]{:S(2)}) collective-permute-start(bf16[4,4,48,384]{3,2,1,0:T(8,128)(2,1)S(1)} %add_convert_fusion.6), channel_id=1, source_target_pairs={{0,2},{2,0},{4,6},{6,4},{8,10},{10,8},{12,14},{14,12},{16,18},{18,... | collective-permute-start | bytes 1769480 | tf_op jit(solution)/shard_map/ppermute | solution.py:66
  448.5 17.4 %collective-permute-start.25 = (bf16[2,2,48,1536]{3,2,1,0:T(8,128)(2,1)S(1)}, bf16[2,2,48,1536]{3,2,1,0:T(8,128)(2,1)S(1)}, u32[]{:S(2)}, u32[]{:S(2)}) collective-permute-start(bf16[2,2,48,1536]{3,2,1,0:T(8,128)(2,1)S(1)} %add_convert_fusion.7), channel_id=1, source_target_pairs={{0,8},{2,10},{4,12},{6,14},{8,0},{10,2},{12,4},{14,6},{16,24},{18,... | collective-permute-start | bytes 1769480 | tf_op jit(solution)/shard_map/ppermute | solution.py:66
  448.5 2.2 collective-permute-start.19
  450.7 27.8 %collective-permute-start.26 = (f32[2,8576]{1,0:T(2,128)S(1)}, f32[2,8576]{1,0:T(2,128)}, u32[]{:S(2)}, u32[]{:S(2)}) collective-permute-start(f32[2,8576]{1,0:T(2,128)S(1)} %add.383), channel_id=1, source_target_pairs={{0,16},{2,18},{4,20},{6,22},{8,24},{10,26},{12,28},{14,30},{16,0},... | collective-permute-start | bytes 205832 | tf_op jit(solution)/shard_map/ppermute | solution.py:66
  457.1 26.9 %copy-start.43 = (bf16[4,4,48,384]{3,2,1,0:T(8,128)(2,1)}, bf16[4,4,48,384]{3,2,1,0:T(8,128)(2,1)S(1)}, u32[]{:S(2)}) copy-start(bf16[4,4,48,384]{3,2,1,0:T(8,128)(2,1)S(1)} %collective-permute-done.24) | copy-start | bytes 1769476
  457.1 21.4 %collective-permute-start.27 = (f32[2,8576]{1,0:T(2,128)S(1)}, f32[2,8576]{1,0:T(2,128)}, u32[]{:S(2)}, u32[]{:S(2)}) collective-permute-start(f32[2,8576]{1,0:T(2,128)S(1)} %add.383), channel_id=1, source_target_pairs={{0,8},{2,10},{4,12},{6,14},{8,0},{10,2},{12,4},{14,6},{16,24},{18,... | collective-permute-start | bytes 205832 | tf_op jit(solution)/shard_map/ppermute | solution.py:66
  465.9 12.6 %collective-permute-start.28 = (f32[2,8576]{1,0:T(2,128)S(1)}, f32[2,8576]{1,0:T(2,128)}, u32[]{:S(2)}, u32[]{:S(2)}) collective-permute-start(f32[2,8576]{1,0:T(2,128)S(1)} %add.383), channel_id=1, source_target_pairs={{0,24},{2,26},{4,28},{6,30},{8,16},{10,18},{12,20},{14,22},{16,8},... | collective-permute-start | bytes 205832 | tf_op jit(solution)/shard_map/ppermute | solution.py:66
  470.2 13.9 %collective-permute-start.29 = (bf16[2,4,48,384]{3,2,1,0:T(8,128)(2,1)}, bf16[2,4,48,384]{3,2,1,0:T(8,128)(2,1)}, u32[]{:S(2)}, u32[]{:S(2)}) collective-permute-start(bf16[2,4,48,384]{3,2,1,0:T(8,128)(2,1)} %add_convert_fusion.11), channel_id=1, source_target_pairs={{0,8},{2,10},{4,12},{6,14},{8,0},{10,2},{12,4},{14,6},{16,24},{18,... | collective-permute-start | bytes 884744 | tf_op jit(solution)/shard_map/ppermute | solution.py:66
  470.2 15.1 %collective-permute-start.31 = (bf16[1,2,48,1536]{3,2,1,0:T(8,128)(2,1)}, bf16[1,2,48,1536]{3,2,1,0:T(8,128)(2,1)S(1)}, u32[]{:S(2)}, u32[]{:S(2)}) collective-permute-start(bf16[1,2,48,1536]{3,2,1,0:T(8,128)(2,1)} %add_convert_fusion.10), channel_id=1, source_target_pairs={{0,16},{2,18},{4,20},{6,22},{8,24},{10,26},{12,28},{14,30},{16,0},... | collective-permute-start | bytes 884744 | tf_op jit(solution)/shard_map/ppermute | solution.py:66
  485.3 8.3 %collective-permute-start.30 = (bf16[1,4,48,384]{3,2,1,0:T(8,128)(2,1)S(1)}, bf16[1,4,48,384]{3,2,1,0:T(8,128)(2,1)S(1)}, u32[]{:S(2)}, u32[]{:S(2)}) collective-permute-start(bf16[1,4,48,384]{3,2,1,0:T(8,128)(2,1)S(1)} %add_convert_fusion.14), channel_id=1, source_target_pairs={{0,16},{2,18},{4,20},{6,22},{8,24},{10,26},{12,28},{14,30},{16,0},... | collective-permute-start | bytes 442376 | tf_op jit(solution)/shard_map/ppermute | solution.py:66
  487.7 30.2 %copy-start.29 = (f32[2,48,3,384]{3,1,2,0:T(8,128)S(1)}, f32[2,48,3,384]{3,1,2,0:T(8,128)}, u32[]{:S(2)}) copy-start(f32[2,48,3,384]{3,1,2,0:T(8,128)} %param.22) | copy-start | bytes 1327108
  488.4 15.0 %collective-permute-start.39 = (f32[2,8576]{1,0:T(2,128)}, f32[2,8576]{1,0:T(2,128)S(1)}, u32[]{:S(2)}, u32[]{:S(2)}) collective-permute-start(f32[2,8576]{1,0:T(2,128)} %add_add_fusion.1), channel_id=1, source_target_pairs={{0,2},{2,0},{4,6},{6,4},{8,10},{10,8},{12,14},{14,12},{16,18},{18,... | collective-permute-start | bytes 205832 | tf_op jit(solution)/shard_map/ppermute | solution.py:66
  489.9 15.2 %collective-permute-start.40 = (f32[2,8576]{1,0:T(2,128)}, f32[2,8576]{1,0:T(2,128)}, u32[]{:S(2)}, u32[]{:S(2)}) collective-permute-start(f32[2,8576]{1,0:T(2,128)} %add_add_fusion.1), channel_id=1, source_target_pairs={{0,4},{2,6},{4,0},{6,2},{8,12},{10,14},{12,8},{14,10},{16,20},{18,... | collective-permute-start | bytes 205832 | tf_op jit(solution)/shard_map/ppermute | solution.py:66
  491.1 14.1 %collective-permute-start.41 = (f32[2,8576]{1,0:T(2,128)}, f32[2,8576]{1,0:T(2,128)}, u32[]{:S(2)}, u32[]{:S(2)}) collective-permute-start(f32[2,8576]{1,0:T(2,128)} %add_add_fusion.1), channel_id=1, source_target_pairs={{0,6},{2,4},{4,2},{6,0},{8,14},{10,12},{12,10},{14,8},{16,22},{18,... | collective-permute-start | bytes 205832 | tf_op jit(solution)/shard_map/ppermute | solution.py:66
  496.2 25.5 %copy-start.27 = (f32[2,48,1536]{2,1,0:T(8,128)S(1)}, f32[2,48,1536]{2,1,0:T(8,128)}, u32[]{:S(2)}) copy-start(f32[2,48,1536]{2,1,0:T(8,128)} %param.24) | copy-start | bytes 1769476
  499.5 1.2 collective-permute-start.32
  500.7 5.5 collective-permute-start.33
  501.9 4.2 collective-permute-start.34
  503.4 5.4 collective-permute-start.35
  508.8 4.2 collective-permute-start.36
  510.1 3.6 collective-permute-start.37
  511.4 4.5 collective-permute-start.38
  521.7 21.4 %copy-start.49 = (f32[2,48,384]{2,1,0:T(8,128)}, f32[2,48,384]{2,1,0:T(8,128)S(1)}, u32[]{:S(2)}) copy-start(f32[2,48,384]{2,1,0:T(8,128)S(1)} %get-tuple-element.439) | copy-start | bytes 442372
  521.7 21.4 %copy-start.50 = (f32[2,48,384]{2,1,0:T(8,128)}, f32[2,48,384]{2,1,0:T(8,128)S(1)}, u32[]{:S(2)}) copy-start(f32[2,48,384]{2,1,0:T(8,128)S(1)} %get-tuple-element.440) | copy-start | bytes 442372
  524.0 17.9 %copy-start.33 = (f32[2,48,1536]{2,1,0:T(8,128)S(1)}, f32[2,48,1536]{2,1,0:T(8,128)}, u32[]{:S(2)}) copy-start(f32[2,48,1536]{2,1,0:T(8,128)} %get-tuple-element.442) | copy-start | bytes 1769476
  524.0 17.9 %copy-start.34 = (f32[2,48,1536]{2,1,0:T(8,128)S(1)}, f32[2,48,1536]{2,1,0:T(8,128)}, u32[]{:S(2)}) copy-start(f32[2,48,1536]{2,1,0:T(8,128)} %get-tuple-element.443) | copy-start | bytes 1769476
  524.1 1.2 collective-permute-start.42
  525.3 4.5 collective-permute-start.43
  525.3 4.5 collective-permute-start.44
  528.1 5.4 collective-permute-start.45
  533.5 5.3 collective-permute-start.46
  533.6 5.2 collective-permute-start.47
  534.4 4.5 collective-permute-start.48
  (41 other events, 108.6 us)
Sparse Core Ops, SparseCore 0:
  11.8 43.0 all-gather.4
  58.4 123.3 all-gather.6

commit v4 on v3

--- a/solution.py
+++ b/solution.py
@@ -47,13 +47,11 @@
         self.stages = count
         self.last = ()
         every = np.arange(parts)
-        self.table = np.zeros((2, parts, 6, parts + 1), np.int32)
+        self.table = np.zeros((2, parts, 4, parts + 1), np.int32)
         for core in range(2):
             for at in range(parts):
                 for half, side in enumerate((core, 1 - core)):
-                    differs = [((every ^ at) >> bit) & 1 for bit in self.orders[side][-2:]]
-                    zoned = (2 * differs[1] + differs[0]) * (parts // 4) + every // 4
-                    rows = (self.inverse[side, every ^ at], zoned, every)
+                    rows = (self.inverse[side, every ^ at], every)
                     for kind, row in enumerate(rows):
                         self.table[core, at, 2 * kind + half, :parts] = row
                         self.table[core, at, 2 * kind + half, parts] = side
@@ -70,9 +68,6 @@
 
     def gather(self, share):
         return {"held": share[None], "stage": 0}
-
-    def gather_last(self, held):
-        return {"held": held, "stage": self.stages - 2}
 
     def total(self, value):
         return {"value": value, "step": 0}
@@ -127,6 +122,8 @@
         return rest
 
     def pair(self, move, rest=()):
+        while self.running(move):
+            self.advance([move])
         held, rest = lax.optimization_barrier((move.pop("held"), rest))
         held = jnp.concatenate([held, move.pop("come")], axis=0)
         move["pair"] = (held, self.sibling(held), 0)
@@ -224,7 +221,7 @@
             scratch_shapes=list(scratch),
         ),
         compiler_params=pltpu.CompilerParams(
-            dimension_semantics=("arbitrary",), vmem_limit_bytes=60 << 20
+            dimension_semantics=("arbitrary",), vmem_limit_bytes=44 << 20
         ),
         cost_estimate=cost(time),
         name=name,
@@ -266,10 +263,10 @@
     bias_up, vectors, *refs, with_grad,
 ):
     if with_grad:
-        grad, first_in, first_low, first_turned, active, slope, hidden_new, *turned, second_in = refs
+        grad, first_in, first_turned, active, slope, hidden_new, *turned, first_low, second_in = refs
         total = second_in
     else:
-        first_in, first_low, first_turned, active, slope, hidden_new, second_in, hidden_low, hidden_turned = refs
+        first_in, first_turned, active, slope, hidden_new, second_in, hidden_low, hidden_turned, first_low = refs
         total = second_in
     step = pl.program_id(0)
     halves = ((own_at, up_own, down_own), (other_at, up_other, down_other))
@@ -310,7 +307,7 @@
             hidden_turned[...] = low.T
 
 
-def feed_forward(places, hidden, context, out_pair, up_pair, down_pair, bias_up, vectors, grad=None, tile=384):
+def feed_forward(places, hidden, context, out_pair, up_pair, down_pair, bias_up, vectors, grad=None, tile=512):
     rows = hidden.shape[0]
     half_ff = bias_up.shape[2]
     count = half_ff // tile
@@ -330,10 +327,10 @@
             *([] if grad is None else [whole(grad)]),
         ],
         [
-            flat(f32), flat(bf16), turned, tiled(bf16), tiled(f32), flat(f32),
+            flat(f32), turned, tiled(bf16), tiled(f32), flat(f32),
             *([flat(f32), flat(bf16), turned] if grad is None else norm_turn_outs(rows)),
         ],
-        [] if grad is None else [pltpu.VMEM((rows, D), f32)],
+        [pltpu.VMEM((rows, D), bf16)] + ([] if grad is None else [pltpu.VMEM((rows, D), f32)]),
         name="feed_forward",
         time=18,
     )
@@ -416,7 +413,7 @@
     )
 
 
-def feed_backward(places, total, down_low, down_turned, kept, up_pair, down_pair, parts, tile=384):
+def feed_backward(places, total, down_low, down_turned, kept, up_pair, down_pair, parts, tile=512):
     first_turned, active, slope = kept
     rows = total.shape[0]
     half_ff = active.shape[2]
@@ -548,7 +545,7 @@
             out_specs=[pl.BlockSpec((rows, cols), lambda i, at: (i, 0)) for _ in pairs],
         ),
         compiler_params=pltpu.CompilerParams(
-            dimension_semantics=("arbitrary",), vmem_limit_bytes=60 << 20
+            dimension_semantics=("arbitrary",), vmem_limit_bytes=44 << 20
         ),
         cost_estimate=cost(4),
         name="join",
@@ -614,7 +611,7 @@
             ],
         ),
         compiler_params=pltpu.CompilerParams(
-            dimension_semantics=("arbitrary",), vmem_limit_bytes=48 << 20
+            dimension_semantics=("arbitrary",), vmem_limit_bytes=24 << 20
         ),
         cost_estimate=cost(3),
         name="prepare",
@@ -709,7 +706,7 @@
         grid_spec=pltpu.PrefetchScalarGridSpec(num_scalar_prefetch=2, grid=(seqs,pairs),
             in_specs=[col(0)]*depth+[col(1)]*depth+[col(2)],
             out_specs=[pl.BlockSpec((rows,128),lambda s,j,c,l:(s,j)), pl.BlockSpec((1,8,rows),lambda s,j,c,l:(s*pairs+j,0,0))]),
-        compiler_params=pltpu.CompilerParams(dimension_semantics=("arbitrary","arbitrary"),vmem_limit_bytes=48<<20),
+        compiler_params=pltpu.CompilerParams(dimension_semantics=("arbitrary","arbitrary"),vmem_limit_bytes=24 << 20),
         cost_estimate=cost(10),
         name="attend_forward",
     )(core, lengths, *projections, *projections, projections[0])
@@ -774,7 +771,7 @@
         partial(attend_backward_kernel, depth=depth, with_later=later is not None, keep_total=keep_total),
         out_shape=out_shape,
         grid_spec=pltpu.PrefetchScalarGridSpec(num_scalar_prefetch=2, grid=(seqs,pairs), in_specs=in_specs, out_specs=out_specs),
-        compiler_params=pltpu.CompilerParams(dimension_semantics=("arbitrary","arbitrary"),vmem_limit_bytes=48<<20),
+        compiler_params=pltpu.CompilerParams(dimension_semantics=("arbitrary","arbitrary"),vmem_limit_bytes=24 << 20),
         cost_estimate=cost(17),
         name="attend_backward",
     )(core, lengths, *args)
@@ -818,37 +815,31 @@
     links = Links(parts)
     places = lax.axis_index("tensor") * parts + lax.axis_index("dp")
     places = lax.dynamic_index_in_dim(
-        jnp.asarray(links.table.reshape(2 * parts, 6, parts + 1)), places, 0, keepdims=False
-    )
-    exchanged, by_zone = (places, 0), (places, 1)
-    in_turn = (places, 2)
-    turns = {(0, "proj"): by_zone, (0, "ff"): by_zone, (1, "proj"): in_turn, (1, "ff"): in_turn}
+        jnp.asarray(links.table.reshape(2 * parts, 4, parts + 1)), places, 0, keepdims=False
+    )
+    exchanged, in_turn = (places, 0), (places, 1)
+    turns = {(0, "proj"): exchanged, (0, "ff"): in_turn, (1, "proj"): in_turn, (1, "ff"): exchanged}
     core = lax.axis_index("tensor")[None].astype(jnp.int32)
 
     table = {"proj": proj_weight, "out": out_weight, "up": up_weight, "down": down_weight}
     groups = [
-        [(0, "proj")], [(0, "out"), (0, "up"), (0, "down")], [(1, "proj")], [(1, "out"), (1, "up"), (1, "down")],
+        [(0, "proj")], [(0, "up"), (0, "down"), (0, "out")], [(1, "proj")], [(1, "up"), (1, "down"), (1, "out")],
     ]
     gathers = []
     for group in groups:
         share = [table[kind][layer_at].reshape(row_count, -1).astype(bf16) for layer_at, kind in group]
         gathers.append(links.gather(jnp.concatenate(share, axis=1) if len(share) > 1 else share[0]))
     one, two, three, four = gathers
-    zone = [[first + 4 * step for step in range(parts // 4)] for first in range(4)]
-    near = jnp.concatenate([move["held"][0] for move in (one, two)], axis=1)
-    near = lax.all_gather(near, "dp", axis_index_groups=zone)
-    prepared = prepare(core, lengths, tokens, cotangent, small_params)
-    last = jnp.concatenate([move.pop("held")[0] for move in (three, four)], axis=1)
-    near, last, prepared = lax.optimization_barrier((near, last, prepared))
+    last = jnp.concatenate([move.pop("held")[0] for move in (two, three)], axis=1)
+    last = lax.all_gather(last, ("dp", "tensor")).reshape(parts, 2, row_count, -1)
+    two["pair"], three["pair"] = (last, last, 0), (last, last, half_d + 2 * half_ff)
+    links.advance([one])
+    prepared = links.advance([one], prepare(core, lengths, tokens, cotangent, small_params))
     hidden, hidden_turned, grad_rows, *prepared = prepared
     vectors, value_bias, up_bias = prepared[0::3], prepared[1::3], prepared[2::3]
-    last = lax.all_gather(last, ("dp", "tensor")).reshape(parts, 2, row_count, -1)
-    three["pair"], four["pair"] = (last, last, 0), (last, last, 3 * half_d)
-    one.update(links.gather_last(near[:, :, : 3 * half_d]))
-    two.update(links.gather_last(near[:, :, 3 * half_d :]))
     links.advance([one])
     links.advance([one])
-    (hidden,) = links.advance([two], (hidden,))
+    (hidden,) = links.advance([four], (hidden,))
 
     def gathered(layer_at, kind):
         for group, move in zip(groups, gathers):
@@ -869,19 +860,22 @@
             turns[layer_at, "proj"], hidden_low, gathered(layer_at, "proj"), value_bias[layer_at]
         )
         if layer_at == 0:
-            (projected,) = links.advance([two], (projected,))
+            (projected,) = links.advance([four], (projected,))
         chain = [projected] + [earlier["projected"] for earlier in reversed(saved)]
         context, log_norm = attend_forward(core, lengths, chain, seq_len)
+        if layer_at > 0:
+            (context,) = links.pair(four, (context,))
         if layer_at == 0:
             late_masters, context = lax.optimization_barrier((masters, context))
             squares = [jnp.sum(one * one, axis=tuple(range(1, one.ndim))) for one in late_masters]
             squares = jnp.pad(jnp.stack(squares, axis=1), ((0, 0), (0, 124)))
-            squares, context = links.pair(two, (squares, context))
+            squares, context = links.advance([four], (squares, context))
+            (context,) = links.advance([four], (context,))
         kept = {
             "input_turned": hidden_turned, "projected": projected, "log_norm": log_norm, "context": context,
         }
         (
-            kept["first_in"], kept["first_low"], kept["first_turned"], kept["active"], kept["slope"], hidden, *rest,
+            kept["first_in"], kept["first_turned"], kept["active"], kept["slope"], hidden, *rest,
         ) = feed_forward(
             turns[layer_at, "ff"], hidden, context, gathered(layer_at, "out"), gathered(layer_at, "up"),
             gathered(layer_at, "down"), up_bias[layer_at], vectors[layer_at],

time: 563 us -> 535 us (0.950)
  Pallas kernels: 207 us -> 158 us
  local copies, waits for them, and re-layouts: 25.9 us -> 46.1 us
  starting transfers between devices: 45.1 us -> 59.3 us
  other arithmetic: 76.3 us -> 67.8 us
  waiting for transfers between devices: 179 us -> 173 us
    pallas_call x12, Pallas kernels: 142 us -> 101 us  [call(): pl.pallas_call(lambda at, *refs: kernel(*weight_rows(at), Row(at, 0), Row...]
    all_gather x1 -> x0, waiting for transfers between devices: 33.5 us -> none  [local(): near = lax.all_gather(near, 'dp', axis_index_groups=zone)]
    ppermute x38 -> x42, waiting for transfers between devices: 126 us -> 156 us  [swap(): return lax.ppermute(value, ('dp', 'tensor'), pairs)]
    unnamed x111 -> x192, local copies, waits for them, and re-layouts: 18.5 us -> 40.4 us
    ppermute x38 -> x42, starting transfers between devices: 43.9 us -> 58.3 us  [swap(): return lax.ppermute(value, ('dp', 'tensor'), pairs)]
    convert_element_type x16, other arithmetic: 39.4 us -> 30.5 us  [advance(): sum((piece[half:size].astype(f32) for piece in move['pieces'])).astype(bf16)]
  transfers between devices with their start and end apart: 51 -> 54, of which waited for: 26 -> 29; matrix products, arithmetic and copies ran while one was open for 10% -> 8% of each run, Pallas kernels for 25% -> 23%
where the time goes in v4:
time: 535 us; the launch traced here: 525 us
  waiting for transfers between devices  173 us (32%)
  Pallas kernels  158 us (30%)
  other arithmetic  67.8 us (13%)
  starting transfers between devices  59.3 us (11%)
  local copies, waits for them, and re-layouts  46.1 us (9%)
  between operations  20.7 us (4%)
    ppermute x42, waiting for transfers between devices, swap(): return lax.ppermute(value, ('dp', 'tensor'), pairs)  156 us
    pallas_call x12, Pallas kernels, call(): pl.pallas_call(lambda at, *refs: kernel(*weight_rows(at), Row(at, 0), Row...  101 us
    ppermute x42, starting transfers between devices, swap(): return lax.ppermute(value, ('dp', 'tensor'), pairs)  58.3 us
    unnamed x192, local copies, waits for them, and re-layouts  40.4 us
    pallas_call x2, Pallas kernels, attend_backward(): pl.pallas_call(partial(attend_backward_kernel, depth=depth, with_later=la...  31.3 us
    convert_element_type x16, other arithmetic, advance(): sum((piece[half:size].astype(f32) for piece in move['pieces'])).astype(bf16)  30.5 us
    pallas_call x2, Pallas kernels, attend_forward(): pl.pallas_call(partial(attend_forward_kernel, depth=depth), out_shape=[ja...  19.6 us
    ppermute x11, waiting for transfers between devices, sibling(): return lax.ppermute(value, 'tensor', [(0, 1), (1, 0)])  17.2 us
  transfers between devices with their start and end apart: 54, of which 29 were waited for; matrix products, arithmetic and copies ran while one was open for 8% of the time, Pallas kernels for 23%

profile of v4, /device:TPU:0, one launch (start us, length us, event | category | flops | bytes accessed | tf_op | source)
XLA Modules:
  0.0 524.8 jit_solution(17049092029797648410)
XLA Ops:
  11.9 4.1 collective-permute-start
  17.1 4.3 collective-permute-done
  22.3 9.3 %collective-permute-done.1 = bf16[2,48,1152]{2,1,0:T(8,128)(2,1)S(1)} collective-permute-done((bf16[2,48,1152]{2,1,0:T(8,128)(2,1)S(1)}, bf16[2,48,1152]{2,1,0:T(8,128)(2,1)S(1)}, u32[]{:S(2)}, u32[]{:S(2)}) %collective-permute-start.1) | collective-permute-done | bytes 221216 | tf_op jit(solution)/shard_map/ppermute | solution.py:64
  32.7 8.4 %collective-permute-done.2 = bf16[4,48,1152]{2,1,0:T(8,128)(2,1)S(1)} collective-permute-done((bf16[4,48,1152]{2,1,0:T(8,128)(2,1)S(1)}, bf16[4,48,1152]{2,1,0:T(8,128)(2,1)S(1)}, u32[]{:S(2)}, u32[]{:S(2)}) %collective-permute-start.2) | collective-permute-done | bytes 442400 | tf_op jit(solution)/shard_map/ppermute | solution.py:64
  42.3 18.4 %collective-permute-done.3 = bf16[8,48,1152]{2,1,0:T(8,128)(2,1)S(1)} collective-permute-done((bf16[8,48,1152]{2,1,0:T(8,128)(2,1)S(1)}, bf16[8,48,1152]{2,1,0:T(8,128)(2,1)S(1)}, u32[]{:S(2)}, u32[]{:S(2)}) %collective-permute-start.3) | collective-permute-done | bytes 884768 | tf_op jit(solution)/shard_map/ppermute | solution.py:64
  63.0 8.8 %collective-permute-start.5 = (bf16[1,48,3456]{2,1,0:T(8,128)(2,1)}, bf16[1,48,3456]{2,1,0:T(8,128)(2,1)}, u32[]{:S(2)}, u32[]{:S(2)}) collective-permute-start(bf16[1,48,3456]{2,1,0:T(8,128)(2,1)} %maximum_bitcast_fusion), channel_id=1, source_target_pairs={{0,16},{2,18},{4,20},{6,22},{8,24},{10,26},{12,28},{14,30},{16,0},... | collective-permute-start | bytes 995336 | tf_op jit(solution)/shard_map/ppermute | solution.py:64
  78.5 4.1 project.2.refs_0_.refs_1_.refs_2_.refs_3_
  82.6 16.5 %collective-permute-done.5 = bf16[1,48,3456]{2,1,0:T(8,128)(2,1)} collective-permute-done((bf16[1,48,3456]{2,1,0:T(8,128)(2,1)}, bf16[1,48,3456]{2,1,0:T(8,128)(2,1)}, u32[]{:S(2)}, u32[]{:S(2)}) %collective-permute-start.5) | collective-permute-done | bytes 331808 | tf_op jit(solution)/shard_map/ppermute | solution.py:64
  99.1 2.0 pad_maximum_fusion.4
  101.1 9.5 %attend_forward.2 = (bf16[512,768]{1,0:T(8,128)(2,1)S(1)}, f32[6,8,512]{2,1,0:T(8,128)S(1)}) custom-call(s32[1]{0:T(128)} %bitcast.5.core, s32[2]{0:T(128)S(1)} %copy-done.53, bf16[512,2304]{1,0:T(8,128)(2,1)S(1)} %project.2.refs_0_.refs_1_.refs_2_.refs_3_, bf16[512,2304]{1,0:T(8,128)(2,1)S(1)} %project.2.refs_0_.refs_1_.refs_2_.refs_3_, ...), custom_call_target="tpu_custom_call" | custom-call | bytes 25000000 | tf_op jit(solution)/shard_map/attend_forward/pallas_call | solution.py:703
  114.4 29.0 %collective-permute-done.6 = bf16[2,48,3456]{2,1,0:T(8,128)(2,1)} collective-permute-done((bf16[2,48,3456]{2,1,0:T(8,128)(2,1)}, bf16[2,48,3456]{2,1,0:T(8,128)(2,1)}, u32[]{:S(2)}, u32[]{:S(2)}) %collective-permute-start.6) | collective-permute-done | bytes 663584 | tf_op jit(solution)/shard_map/ppermute | solution.py:64
  145.9 16.7 %collective-permute-done.7 = bf16[4,48,3456]{2,1,0:T(8,128)(2,1)S(1)} collective-permute-done((bf16[4,48,3456]{2,1,0:T(8,128)(2,1)S(1)}, bf16[4,48,3456]{2,1,0:T(8,128)(2,1)S(1)}, u32[]{:S(2)}, u32[]{:S(2)}) %collective-permute-start.7) | collective-permute-done | bytes 1327136 | tf_op jit(solution)/shard_map/ppermute | solution.py:64
  167.1 14.8 %feed_forward.2 = (f32[512,768]{1,0:T(8,128)S(1)}, bf16[768,512]{1,0:T(8,128)(2,1)S(1)}, bf16[2,512,1536]{2,1,0:T(8,128)(2,1)}, f32[2,512,1536]{2,1,0:T(8,128)},...) custom-call(s32[4,17]{1,0:T(4,128)S(1)} %dynamic-slice_bitcast_fusio, ...), custom_call_target="tpu_custom_call" | custom-call | bytes 45000000 | tf_op jit(solution)/shard_map/feed_forward/pallas_call | solution.py:213
  181.9 5.2 project.3.refs_0_.refs_2_.refs_4_
  187.2 10.1 %attend_forward.3 = (bf16[512,768]{1,0:T(8,128)(2,1)S(1)}, f32[6,8,512]{2,1,0:T(8,128)S(1)}) custom-call(s32[1]{0:T(128)} %bitcast.5.core, s32[2]{0:T(128)S(1)} %copy-done.53, bf16[512,2304]{1,0:T(8,128)(2,1)S(1)} %project.3.refs_0_.refs_2_.refs_4_, bf16[512,2304]{1,0:T(8,128)(2,1)S(1)} %project.2.refs_0_.refs_1_.refs_2_.refs_3_, ...), custom_call_target="tpu_custom_call" | custom-call | bytes 25000000 | tf_op jit(solution)/shard_map/attend_forward/pallas_call | solution.py:703
  197.3 1.9 constant_dynamic-update-slice_fusion.1
  199.3 2.1 constant_dynamic-update-slice_fusion.refs_2_.refs_4_.refs_6_.refs_8_
  201.5 8.7 %collective-permute-done.9.refs_3_.refs_5_.refs_7_.refs_9_ = bf16[16,48,3456]{2,1,0:T(8,128)(2,1)S(1)} collective-permute-done((bf16[16,48,3456]{2,1,0:T(8,128)(2,1)S(1)}, bf16[16,48,3456]{2,1,0:T(8,128)(2,1)S(1)}, u32[]{:S(2)}, u32[]{:S(2)}) %collective-permute-start.9) | collective-permute-done | bytes 5308448 | tf_op jit(solution)/shard_map/ppermute | solution.py:67
  210.2 2.4 copy-done.63
  212.6 16.7 %feed_forward.3 = (f32[512,768]{1,0:T(8,128)S(1)}, bf16[768,512]{1,0:T(8,128)(2,1)S(1)}, bf16[2,512,1536]{2,1,0:T(8,128)(2,1)}, f32[2,512,1536]{2,1,0:T(8,128)},...) custom-call(s32[4,17]{1,0:T(4,128)S(1)} %dynamic-slice_bitcast_fusio, ...), custom_call_target="tpu_custom_call" | custom-call | bytes 45000000 | tf_op jit(solution)/shard_map/feed_forward/pallas_call | solution.py:213
  233.4 1.9 copy-done.14
  236.7 15.4 %feed_backward.2 = (bf16[16,2,48,1536]{3,2,1,0:T(8,128)(2,1)}, bf16[16,2,48,1536]{3,2,1,0:T(8,128)(2,1)}, f32[2,8,1536]{2,1,0:T(8,128)S(1)}, f32[512,768]{1,0:T(8,128)S(1)}) custom-call(s32[4,17]{1,0:T(4,128)S(1)} %dynamic-slice_bitcast_fusion.at, f32[512,768]{1,0:T(8,128)S(1)} %copy-done.18, bf16[512,768]{1,0:T(8,128)(2,1)S(1)} %get-tuple-element.303.refs_1_, ...), custom_call_target="tpu_custom_call" | custom-call | bytes 50000000 | tf_op jit(solution)/shard_map/feed_backward/pallas_call | solution.py:213
  256.1 3.7 context_backward.2
  261.4 4.5 add_convert_fusion.1
  266.4 16.4 %attend_backward.2 = (bf16[3,512,768]{2,1,0:T(8,128)(2,1)S(1)}, f32[1,8,768]{2,1,0:T(8,128)S(1)}, f32[12,512,512]{2,1,0:T(8,128)S(1)}) custom-call(s32[1]{0:T(128)} %bitcast.5.core, s32[2]{0:T(128)S(1)} %copy-done.53, bf16[512,2304]{1,0:T(8,128)(2,1)S(1)} %project.3.refs_0_.refs_2_.refs_4_, bf16[512,2304]{1,0:T(8,128)(2,1)S(1)} %project.2.refs_0_.refs_1_.refs_2_.refs_3_, ...), custom_call_target="tpu_custom_call" | custom-call | bytes 42500000 | tf_op jit(solution)/shard_map/attend_backward/pallas_call | solution.py:770
  282.8 4.5 copy-done.3
  287.3 5.6 %projection_grads.2 = (bf16[16,4,48,384]{3,2,1,0:T(8,128)(2,1)S(1)}, bf16[16,4,48,384]{3,2,1,0:T(8,128)(2,1)}) custom-call(s32[4,17]{1,0:T(4,128)S(1)} %dynamic-slice_bitcast_fusion.at, bf16[768,512]{1,0:T(8,128)(2,1)S(1)} %get-tuple-element.317.refs_0_, bf16[512,768]{1,0:T(8,128)(2,1)S(1)} %get-tuple-element.297.refs_1_, bf16[768,512]{1,0:T(8,128)(2,1)S(1)} %copy-done.36, ...), custom_call_target="tpu_custom_call" | custom-call | bytes 22500000 | tf_op jit(solution)/shard_map/projection_grads/pallas_call | solution.py:213
  293.0 2.1 collective-permute-done.11
  295.1 3.5 add_convert_fusion.5
  299.6 6.5 %project_backward.2 = (f32[512,768]{1,0:T(8,128)S(1)}, bf16[512,768]{1,0:T(8,128)(2,1)S(1)}, bf16[768,512]{1,0:T(8,128)(2,1)S(1)}, f32[8,768]{1,0:T(8,128)S(1)}) custom-call(s32[4,17]{1,0:T(4,128)S(1)} %dynamic-slice_bitcast_fusion.at, bf16[3,512,768]{2,1,0:T(8,128)(2,1)S(1)} %get-tuple-element.329.refs_3_.refs_0_, ...), custom_call_target="tpu_custom_call" | custom-call | bytes 20000000 | tf_op jit(solution)/shard_map/project_backward/pallas_call | solution.py:213
  307.3 2.2 copy-done.13
  312.0 15.6 %feed_backward.3 = (bf16[16,2,48,1536]{3,2,1,0:T(8,128)(2,1)}, bf16[16,2,48,1536]{3,2,1,0:T(8,128)(2,1)}, f32[2,8,1536]{2,1,0:T(8,128)S(1)}, f32[512,768]{1,0:T(8,128)S(1)}) custom-call(s32[4,17]{1,0:T(4,128)S(1)} %dynamic-slice_bitcast_fusion.at, f32[512,768]{1,0:T(8,128)S(1)} %copy-done.30, bf16[512,768]{1,0:T(8,128)(2,1)S(1)} %get-tuple-element.344.refs_1_, ...), custom_call_target="tpu_custom_call" | custom-call | bytes 50000000 | tf_op jit(solution)/shard_map/feed_backward/pallas_call | solution.py:213
  327.6 2.7 add_convert_fusion.9
  332.8 4.0 context_backward.3
  336.9 4.8 collective-permute-done.16
  341.7 2.0 add_convert_fusion.13
  343.8 3.8 add_convert_fusion
  348.8 4.6 copy-done.4
  353.4 14.9 %attend_backward.3 = (bf16[3,512,768]{2,1,0:T(8,128)(2,1)S(1)}, f32[1,8,768]{2,1,0:T(8,128)S(1)}) custom-call(s32[1]{0:T(128)} %bitcast.5.core, s32[2]{0:T(128)S(1)} %copy-done.53, bf16[512,2304]{1,0:T(8,128)(2,1)S(1)} %project.2.refs_0_.refs_1_.refs_2_.refs_3_, bf16[512,2304]{1,0:T(8,128)(2,1)S(1)} %project.2.refs_0_.refs_1_.refs_2_.refs_3_, ...), custom_call_target="tpu_custom_call" | custom-call | bytes 42500000 | tf_op jit(solution)/shard_map/attend_backward/pallas_call | solution.py:770
  370.3 2.0 collective-permute-start.18
  375.4 3.1 collective-permute-done.18
  379.8 3.6 add_convert_fusion.3
  383.5 5.0 projection_grads.3
  389.7 3.4 collective-permute-done.20
  395.0 2.4 collective-permute-start.26
  397.4 4.1 project_backward.3.refs_2_
  401.5 12.5 %collective-permute-done.21 = bf16[4,2,48,1536]{3,2,1,0:T(8,128)(2,1)} collective-permute-done((bf16[4,2,48,1536]{3,2,1,0:T(8,128)(2,1)}, bf16[4,2,48,1536]{3,2,1,0:T(8,128)(2,1)}, u32[]{:S(2)}, u32[]{:S(2)}) %collective-permute-start.21) | collective-permute-done | bytes 1179680 | tf_op jit(solution)/shard_map/ppermute | solution.py:64
  414.0 1.9 add_convert_fusion.7
  424.9 5.7 %collective-permute-done.28 = bf16[4,4,48,384]{3,2,1,0:T(8,128)(2,1)S(1)} collective-permute-done((bf16[4,4,48,384]{3,2,1,0:T(8,128)(2,1)S(1)}, bf16[4,4,48,384]{3,2,1,0:T(8,128)(2,1)S(1)}, u32[]{:S(2)}, u32[]{:S(2)}) %collective-permute-start.28) | collective-permute-done | bytes 589856 | tf_op jit(solution)/shard_map/ppermute | solution.py:64
  433.4 5.6 %collective-permute-done.29 = bf16[2,2,48,1536]{3,2,1,0:T(8,128)(2,1)S(1)} collective-permute-done((bf16[2,2,48,1536]{3,2,1,0:T(8,128)(2,1)S(1)}, bf16[2,2,48,1536]{3,2,1,0:T(8,128)(2,1)S(1)}, u32[]{:S(2)}, u32[]{:S(2)}) %collective-permute-start.29) | collective-permute-done | bytes 589856 | tf_op jit(solution)/shard_map/ppermute | solution.py:64
  441.6 3.3 collective-permute-start.35
  444.9 3.2 join.1
  448.8 6.8 %collective-permute-done.33 = bf16[2,4,48,384]{3,2,1,0:T(8,128)(2,1)S(1)} collective-permute-done((bf16[2,4,48,384]{3,2,1,0:T(8,128)(2,1)S(1)}, bf16[2,4,48,384]{3,2,1,0:T(8,128)(2,1)S(1)}, u32[]{:S(2)}, u32[]{:S(2)}) %collective-permute-start.33) | collective-permute-done | bytes 294944 | tf_op jit(solution)/shard_map/ppermute | solution.py:64
  461.9 1.8 collective-permute-start.45
  474.2 2.2 collective-permute-start.39
  477.5 2.1 collective-permute-done.39
  487.9 2.5 multiply_reduce_fusion.6
  492.2 1.9 multiply_reduce_fusion.1
  495.5 2.2 collective-permute-start.48
  497.7 2.1 collective-permute-start.49
  500.0 3.1 collective-permute-done.49
  504.1 1.9 collective-permute-start.51
  508.4 2.0 collective-permute-done.52
  511.0 2.5 multiply_subtract_fusion
  (338 shorter events, 105.1 us)
Async XLA Ops:
  7.2 158.8 %all-gather.3.cloned.1.call-start = ((), (), s32[]{:S(2)}) async-start(), calls=%async_computation | async-start | bytes 14598144 | tf_op jit(solution)/shard_map/all_gather | solution.py:834
  11.9 9.5 %collective-permute-start = (bf16[1,48,1152]{2,1,0:T(8,128)(2,1)S(1)}, bf16[1,48,1152]{2,1,0:T(8,128)(2,1)S(1)}, u32[]{:S(2)}, u32[]{:S(2)}) collective-permute-start(bf16[1,48,1152]{2,1,0:T(8,128)(2,1)S(1)} %bitcast.114), channel_id=1, source_target_pairs={{0,16},{2,18},{4,20},{6,22},{8,24},{10,26},{12,28},{14,30},{16,0},... | collective-permute-start | bytes 331784 | tf_op jit(solution)/shard_map/ppermute | solution.py:64
  17.0 43.8 %copy-start.10 = (bf16[512,768]{1,0:T(8,128)(2,1)}, bf16[512,768]{1,0:T(8,128)(2,1)S(1)}, u32[]{:S(2)}) copy-start(bf16[512,768]{1,0:T(8,128)(2,1)S(1)} %get-tuple-element.269.refs_0_) | copy-start | bytes 2359300
  17.0 43.8 %copy-start.16 = (f32[512,768]{1,0:T(8,128)}, f32[512,768]{1,0:T(8,128)S(1)}, u32[]{:S(2)}) copy-start(f32[512,768]{1,0:T(8,128)S(1)} %get-tuple-element.301.refs_10_) | copy-start | bytes 4718596
  17.0 43.8 %copy-start.33 = (bf16[768,512]{1,0:T(8,128)(2,1)}, bf16[768,512]{1,0:T(8,128)(2,1)S(1)}, u32[]{:S(2)}) copy-start(bf16[768,512]{1,0:T(8,128)(2,1)S(1)} %get-tuple-element.362.refs_2_) | copy-start | bytes 2359300
  17.1 43.8 %copy-start.41 = (f32[8,768]{1,0:T(8,128)}, f32[8,768]{1,0:T(8,128)S(1)}, u32[]{:S(2)}) copy-start(f32[8,768]{1,0:T(8,128)S(1)} %get-tuple-element.291.refs_9_.refs_5_.refs_4_) | copy-start | bytes 73732
  17.1 43.8 %copy-start.43 = (f32[8,768]{1,0:T(8,128)}, f32[8,768]{1,0:T(8,128)S(1)}, u32[]{:S(2)}) copy-start(f32[8,768]{1,0:T(8,128)S(1)} %get-tuple-element.300.refs_9_.refs_4_) | copy-start | bytes 73732
  17.1 43.8 %copy-start.54 = (f32[2,1,1536]{2,1,0:T(1,128)}, f32[2,1,1536]{2,1,0:T(1,128)S(1)}, u32[]{:S(2)}) copy-start(f32[2,1,1536]{2,1,0:T(1,128)S(1)} %get-tuple-element.299.refs_8_) | copy-start | bytes 36868
  17.1 43.8 %copy-start.56 = (f32[2,1,1536]{2,1,0:T(1,128)}, f32[2,1,1536]{2,1,0:T(1,128)S(1)}, u32[]{:S(2)}) copy-start(f32[2,1,1536]{2,1,0:T(1,128)S(1)} %get-tuple-element.290.refs_8_) | copy-start | bytes 36868
  17.1 43.8 %copy-start.58 = (f32[1,2304]{1,0:T(1,128)}, f32[1,2304]{1,0:T(1,128)S(1)}, u32[]{:S(2)}) copy-start(f32[1,2304]{1,0:T(1,128)S(1)} %get-tuple-element.295.refs_3_) | copy-start | bytes 27652
  17.1 43.8 %copy-start.60 = (f32[1,2304]{1,0:T(1,128)}, f32[1,2304]{1,0:T(1,128)S(1)}, u32[]{:S(2)}) copy-start(f32[1,2304]{1,0:T(1,128)S(1)} %get-tuple-element.271.refs_3_) | copy-start | bytes 27652
  21.5 10.0 %collective-permute-start.1 = (bf16[2,48,1152]{2,1,0:T(8,128)(2,1)S(1)}, bf16[2,48,1152]{2,1,0:T(8,128)(2,1)S(1)}, u32[]{:S(2)}, u32[]{:S(2)}) collective-permute-start(bf16[2,48,1152]{2,1,0:T(8,128)(2,1)S(1)} %pad_maximum_fusion.8), channel_id=1, source_target_pairs={{0,8},{2,10},{4,12},{6,14},{8,0},{10,2},{12,4},{14,6},{16,24},{18,... | collective-permute-start | bytes 663560 | tf_op jit(solution)/shard_map/ppermute | solution.py:64
  31.6 9.5 %collective-permute-start.2 = (bf16[4,48,1152]{2,1,0:T(8,128)(2,1)S(1)}, bf16[4,48,1152]{2,1,0:T(8,128)(2,1)S(1)}, u32[]{:S(2)}, u32[]{:S(2)}) collective-permute-start(bf16[4,48,1152]{2,1,0:T(8,128)(2,1)S(1)} %pad_maximum_fusion.6), channel_id=1, source_target_pairs={{0,2},{2,0},{4,6},{6,4},{8,10},{10,8},{12,14},{14,12},{16,18},{18,... | collective-permute-start | bytes 1327112 | tf_op jit(solution)/shard_map/ppermute | solution.py:64
  41.3 19.4 %collective-permute-start.3 = (bf16[8,48,1152]{2,1,0:T(8,128)(2,1)S(1)}, bf16[8,48,1152]{2,1,0:T(8,128)(2,1)S(1)}, u32[]{:S(2)}, u32[]{:S(2)}) collective-permute-start(bf16[8,48,1152]{2,1,0:T(8,128)(2,1)S(1)} %pad_maximum_fusion.3), channel_id=1, source_target_pairs={{0,4},{2,6},{4,0},{6,2},{8,12},{10,14},{12,8},{14,10},{16,20},{18,... | collective-permute-start | bytes 2654216 | tf_op jit(solution)/shard_map/ppermute | solution.py:64
  61.0 11.5 %collective-permute-start.4 = (bf16[16,48,1152]{2,1,0:T(8,128)(2,1)S(1)}, bf16[16,48,1152]{2,1,0:T(8,128)(2,1)S(1)}, u32[]{:S(2)}, u32[]{:S(2)}) collective-permute-start(bf16[16,48,1152]{2,1,0:T(8,128)(2,1)S(1)} %pad_maximum_fusion.1.refs_1_.refs_2_), channel_id=1, source_target_pairs={{0,1},{1,0},{2,3},{3,2},{4,5},{5,4},{6,7},{7,6},{8,9},{9,8},{10,11... | collective-permute-start | bytes 5308424 | tf_op jit(solution)/shard_map/ppermute | solution.py:67
  63.0 36.1 %collective-permute-start.5 = (bf16[1,48,3456]{2,1,0:T(8,128)(2,1)}, bf16[1,48,3456]{2,1,0:T(8,128)(2,1)}, u32[]{:S(2)}, u32[]{:S(2)}) collective-permute-start(bf16[1,48,3456]{2,1,0:T(8,128)(2,1)} %maximum_bitcast_fusion), channel_id=1, source_target_pairs={{0,16},{2,18},{4,20},{6,22},{8,24},{10,26},{12,28},{14,30},{16,0},... | collective-permute-start | bytes 995336 | tf_op jit(solution)/shard_map/ppermute | solution.py:64
  101.1 42.3 %collective-permute-start.6 = (bf16[2,48,3456]{2,1,0:T(8,128)(2,1)}, bf16[2,48,3456]{2,1,0:T(8,128)(2,1)}, u32[]{:S(2)}, u32[]{:S(2)}) collective-permute-start(bf16[2,48,3456]{2,1,0:T(8,128)(2,1)} %pad_maximum_fusion.4), channel_id=1, source_target_pairs={{0,8},{2,10},{4,12},{6,14},{8,0},{10,2},{12,4},{14,6},{16,24},{18,... | collective-permute-start | bytes 1990664 | tf_op jit(solution)/shard_map/ppermute | solution.py:64
  144.8 17.8 %collective-permute-start.7 = (bf16[4,48,3456]{2,1,0:T(8,128)(2,1)S(1)}, bf16[4,48,3456]{2,1,0:T(8,128)(2,1)S(1)}, u32[]{:S(2)}, u32[]{:S(2)}) collective-permute-start(bf16[4,48,3456]{2,1,0:T(8,128)(2,1)S(1)} %pad_maximum_fusion.2), channel_id=1, source_target_pairs={{0,2},{2,0},{4,6},{6,4},{8,10},{10,8},{12,14},{14,12},{16,18},{18,... | collective-permute-start | bytes 3981320 | tf_op jit(solution)/shard_map/ppermute | solution.py:64
  164.4 34.8 %collective-permute-start.8 = (bf16[8,48,3456]{2,1,0:T(8,128)(2,1)}, bf16[8,48,3456]{2,1,0:T(8,128)(2,1)}, u32[]{:S(2)}, u32[]{:S(2)}) collective-permute-start(bf16[8,48,3456]{2,1,0:T(8,128)(2,1)} %pad_maximum_fusion), channel_id=1, source_target_pairs={{0,4},{2,6},{4,0},{6,2},{8,12},{10,14},{12,8},{14,10},{16,20},{18,... | collective-permute-start | bytes 7962632 | tf_op jit(solution)/shard_map/ppermute | solution.py:64
  201.4 8.8 %collective-permute-start.9 = (bf16[16,48,3456]{2,1,0:T(8,128)(2,1)S(1)}, bf16[16,48,3456]{2,1,0:T(8,128)(2,1)S(1)}, u32[]{:S(2)}, u32[]{:S(2)}) collective-permute-start(bf16[16,48,3456]{2,1,0:T(8,128)(2,1)S(1)} %constant_dynamic-update-slice_fusion.refs_2_.refs_4_.refs_6_.refs_8_), channel_id=1, source_target_pairs={{0,1},{1,0},{2,3},{3,2},{4,5},{5,4},{6,7},{7,6},{8,9},{9,8},{10,11... | collective-permute-start | bytes 15925256 | tf_op jit(solution)/shard_map/ppermute | solution.py:67
  253.2 8.3 %collective-permute-start.10 = (bf16[16,2,48,1536]{3,2,1,0:T(8,128)(2,1)}, bf16[16,2,48,1536]{3,2,1,0:T(8,128)(2,1)}, u32[]{:S(2)}, u32[]{:S(2)}) collective-permute-start(bf16[16,2,48,1536]{3,2,1,0:T(8,128)(2,1)} %get-tuple-element.315), channel_id=1, source_target_pairs={{0,1},{1,0},{2,3},{3,2},{4,5},{5,4},{6,7},{7,6},{8,9},{9,8},{10,11... | collective-permute-start | bytes 14155784 | tf_op jit(solution)/shard_map/ppermute | solution.py:67
  265.9 29.2 %collective-permute-start.11 = (bf16[8,2,48,1536]{3,2,1,0:T(8,128)(2,1)}, bf16[8,2,48,1536]{3,2,1,0:T(8,128)(2,1)}, u32[]{:S(2)}, u32[]{:S(2)}) collective-permute-start(bf16[8,2,48,1536]{3,2,1,0:T(8,128)(2,1)} %add_convert_fusion.1), channel_id=1, source_target_pairs={{0,4},{2,6},{4,0},{6,2},{8,12},{10,14},{12,8},{14,10},{16,20},{18,... | collective-permute-start | bytes 7077896 | tf_op jit(solution)/shard_map/ppermute | solution.py:64
  293.0 48.7 %copy-start.15 = (bf16[16,4,48,384]{3,2,1,0:T(8,128)(2,1)}, bf16[16,4,48,384]{3,2,1,0:T(8,128)(2,1)S(1)}, u32[]{:S(2)}) copy-start(bf16[16,4,48,384]{3,2,1,0:T(8,128)(2,1)S(1)} %get-tuple-element.430) | copy-start | bytes 7077892
  298.6 7.6 %collective-permute-start.12 = (bf16[16,4,48,384]{3,2,1,0:T(8,128)(2,1)}, bf16[16,4,48,384]{3,2,1,0:T(8,128)(2,1)S(1)}, u32[]{:S(2)}, u32[]{:S(2)}) collective-permute-start(bf16[16,4,48,384]{3,2,1,0:T(8,128)(2,1)} %get-tuple-element.338), channel_id=1, source_target_pairs={{0,1},{1,0},{2,3},{3,2},{4,5},{5,4},{6,7},{7,6},{8,9},{9,8},{10,11... | collective-permute-start | bytes 7077896 | tf_op jit(solution)/shard_map/ppermute | solution.py:67
  298.6 29.0 %collective-permute-start.13 = (bf16[4,2,48,1536]{3,2,1,0:T(8,128)(2,1)}, bf16[4,2,48,1536]{3,2,1,0:T(8,128)(2,1)}, u32[]{:S(2)}, u32[]{:S(2)}) collective-permute-start(bf16[4,2,48,1536]{3,2,1,0:T(8,128)(2,1)} %add_convert_fusion.5), channel_id=1, source_target_pairs={{0,2},{2,0},{4,6},{6,4},{8,10},{10,8},{12,14},{14,12},{16,18},{18,... | collective-permute-start | bytes 3538952 | tf_op jit(solution)/shard_map/ppermute | solution.py:64
  306.5 23.9 %collective-permute-start.14 = (bf16[8,4,48,384]{3,2,1,0:T(8,128)(2,1)S(1)}, bf16[8,4,48,384]{3,2,1,0:T(8,128)(2,1)}, u32[]{:S(2)}, u32[]{:S(2)}) collective-permute-start(bf16[8,4,48,384]{3,2,1,0:T(8,128)(2,1)S(1)} %add_convert_fusion.4), channel_id=1, source_target_pairs={{0,4},{2,6},{4,0},{6,2},{8,12},{10,14},{12,8},{14,10},{16,20},{18,... | collective-permute-start | bytes 3538952 | tf_op jit(solution)/shard_map/ppermute | solution.py:64
  331.7 12.1 %collective-permute-start.15 = (bf16[16,2,48,1536]{3,2,1,0:T(8,128)(2,1)}, bf16[16,2,48,1536]{3,2,1,0:T(8,128)(2,1)}, u32[]{:S(2)}, u32[]{:S(2)}) collective-permute-start(bf16[16,2,48,1536]{3,2,1,0:T(8,128)(2,1)} %get-tuple-element.366), channel_id=1, source_target_pairs={{0,1},{1,0},{2,3},{3,2},{4,5},{5,4},{6,7},{7,6},{8,9},{9,8},{10,11... | collective-permute-start | bytes 14155784 | tf_op jit(solution)/shard_map/ppermute | solution.py:67
  331.8 9.9 %collective-permute-start.16 = (bf16[4,4,48,384]{3,2,1,0:T(8,128)(2,1)S(1)}, bf16[4,4,48,384]{3,2,1,0:T(8,128)(2,1)S(1)}, u32[]{:S(2)}, u32[]{:S(2)}) collective-permute-start(bf16[4,4,48,384]{3,2,1,0:T(8,128)(2,1)S(1)} %add_convert_fusion.8), channel_id=1, source_target_pairs={{0,2},{2,0},{4,6},{6,4},{8,10},{10,8},{12,14},{14,12},{16,18},{18,... | collective-permute-start | bytes 1769480 | tf_op jit(solution)/shard_map/ppermute | solution.py:64
  347.6 32.2 %collective-permute-start.19 = (bf16[8,2,48,1536]{3,2,1,0:T(8,128)(2,1)}, bf16[8,2,48,1536]{3,2,1,0:T(8,128)(2,1)}, u32[]{:S(2)}, u32[]{:S(2)}) collective-permute-start(bf16[8,2,48,1536]{3,2,1,0:T(8,128)(2,1)} %add_convert_fusion), channel_id=1, source_target_pairs={{0,4},{2,6},{4,0},{6,2},{8,12},{10,14},{12,8},{14,10},{16,20},{18,... | collective-permute-start | bytes 7077896 | tf_op jit(solution)/shard_map/ppermute | solution.py:64
  348.8 25.1 %collective-permute-start.17 = (bf16[2,2,48,1536]{3,2,1,0:T(8,128)(2,1)}, bf16[2,2,48,1536]{3,2,1,0:T(8,128)(2,1)}, u32[]{:S(2)}, u32[]{:S(2)}) collective-permute-start(bf16[2,2,48,1536]{3,2,1,0:T(8,128)(2,1)} %add_convert_fusion.9), channel_id=1, source_target_pairs={{0,8},{2,10},{4,12},{6,14},{8,0},{10,2},{12,4},{14,6},{16,24},{18,... | collective-permute-start | bytes 1769480 | tf_op jit(solution)/shard_map/ppermute | solution.py:64
  370.3 8.3 %collective-permute-start.18 = (bf16[2,4,48,384]{3,2,1,0:T(8,128)(2,1)}, bf16[2,4,48,384]{3,2,1,0:T(8,128)(2,1)S(1)}, u32[]{:S(2)}, u32[]{:S(2)}) collective-permute-start(bf16[2,4,48,384]{3,2,1,0:T(8,128)(2,1)} %add_convert_fusion.13), channel_id=1, source_target_pairs={{0,8},{2,10},{4,12},{6,14},{8,0},{10,2},{12,4},{14,6},{16,24},{18,... | collective-permute-start | bytes 884744 | tf_op jit(solution)/shard_map/ppermute | solution.py:64
  388.5 4.6 collective-permute-start.20
  388.6 25.4 %collective-permute-start.21 = (bf16[4,2,48,1536]{3,2,1,0:T(8,128)(2,1)}, bf16[4,2,48,1536]{3,2,1,0:T(8,128)(2,1)}, u32[]{:S(2)}, u32[]{:S(2)}) collective-permute-start(bf16[4,2,48,1536]{3,2,1,0:T(8,128)(2,1)} %add_convert_fusion.3), channel_id=1, source_target_pairs={{0,2},{2,0},{4,6},{6,4},{8,10},{10,8},{12,14},{14,12},{16,18},{18,... | collective-permute-start | bytes 3538952 | tf_op jit(solution)/shard_map/ppermute | solution.py:64
  393.5 23.7 %collective-permute-start.22 = (bf16[8,4,48,384]{3,2,1,0:T(8,128)(2,1)S(1)}, bf16[8,4,48,384]{3,2,1,0:T(8,128)(2,1)S(1)}, u32[]{:S(2)}, u32[]{:S(2)}) collective-permute-start(bf16[8,4,48,384]{3,2,1,0:T(8,128)(2,1)S(1)} %add_convert_fusion.2), channel_id=1, source_target_pairs={{0,4},{2,6},{4,0},{6,2},{8,12},{10,14},{12,8},{14,10},{16,20},{18,... | collective-permute-start | bytes 3538952 | tf_op jit(solution)/shard_map/ppermute | solution.py:64
  394.4 47.1 %collective-permute-start.24 = (f32[512,768]{1,0:T(8,128)S(1)}, f32[512,768]{1,0:T(8,128)S(1)}, u32[]{:S(2)}, u32[]{:S(2)}) collective-permute-start(f32[512,768]{1,0:T(8,128)S(1)} %copy-done.28), channel_id=1, source_target_pairs={{0,1},{1,0},{2,3},{3,2},{4,5},{5,4},{6,7},{7,6},{8,9},{9,8},{10,11... | collective-permute-start | bytes 4718600 | tf_op jit(solution)/shard_map/ppermute | solution.py:67
  394.4 24.3 %collective-permute-start.25 = (bf16[1,2,48,1536]{3,2,1,0:T(8,128)(2,1)S(1)}, bf16[1,2,48,1536]{3,2,1,0:T(8,128)(2,1)S(1)}, u32[]{:S(2)}, u32[]{:S(2)}) collective-permute-start(bf16[1,2,48,1536]{3,2,1,0:T(8,128)(2,1)S(1)} %add_convert_fusion.12), channel_id=1, source_target_pairs={{0,16},{2,18},{4,20},{6,22},{8,24},{10,26},{12,28},{14,30},{16,0},... | collective-permute-start | bytes 884744 | tf_op jit(solution)/shard_map/ppermute | solution.py:64
  395.0 22.5 %collective-permute-start.26 = (bf16[1,4,48,384]{3,2,1,0:T(8,128)(2,1)S(1)}, bf16[1,4,48,384]{3,2,1,0:T(8,128)(2,1)S(1)}, u32[]{:S(2)}, u32[]{:S(2)}) collective-permute-start(bf16[1,4,48,384]{3,2,1,0:T(8,128)(2,1)S(1)} %add_convert_fusion.15), channel_id=1, source_target_pairs={{0,16},{2,18},{4,20},{6,22},{8,24},{10,26},{12,28},{14,30},{16,0},... | collective-permute-start | bytes 442376 | tf_op jit(solution)/shard_map/ppermute | solution.py:64
  420.3 21.3 %collective-permute-start.27 = (f32[512,768]{1,0:T(8,128)S(1)}, f32[512,768]{1,0:T(8,128)S(1)}, u32[]{:S(2)}, u32[]{:S(2)}) collective-permute-start(f32[512,768]{1,0:T(8,128)S(1)} %project_backward.3.refs_2_), channel_id=1, source_target_pairs={{0,1},{1,0},{2,3},{3,2},{4,5},{5,4},{6,7},{7,6},{8,9},{9,8},{10,11... | collective-permute-start | bytes 4718600 | tf_op jit(solution)/shard_map/ppermute | solution.py:67
  420.7 9.9 %collective-permute-start.28 = (bf16[4,4,48,384]{3,2,1,0:T(8,128)(2,1)S(1)}, bf16[4,4,48,384]{3,2,1,0:T(8,128)(2,1)S(1)}, u32[]{:S(2)}, u32[]{:S(2)}) collective-permute-start(bf16[4,4,48,384]{3,2,1,0:T(8,128)(2,1)S(1)} %add_convert_fusion.6), channel_id=1, source_target_pairs={{0,2},{2,0},{4,6},{6,4},{8,10},{10,8},{12,14},{14,12},{16,18},{18,... | collective-permute-start | bytes 1769480 | tf_op jit(solution)/shard_map/ppermute | solution.py:64
  421.7 17.3 %collective-permute-start.29 = (bf16[2,2,48,1536]{3,2,1,0:T(8,128)(2,1)S(1)}, bf16[2,2,48,1536]{3,2,1,0:T(8,128)(2,1)S(1)}, u32[]{:S(2)}, u32[]{:S(2)}) collective-permute-start(bf16[2,2,48,1536]{3,2,1,0:T(8,128)(2,1)S(1)} %add_convert_fusion.7), channel_id=1, source_target_pairs={{0,8},{2,10},{4,12},{6,14},{8,0},{10,2},{12,4},{14,6},{16,24},{18,... | collective-permute-start | bytes 1769480 | tf_op jit(solution)/shard_map/ppermute | solution.py:64
  423.5 1.3 collective-permute-start.23
  424.8 23.3 %collective-permute-start.30 = (f32[2,8576]{1,0:T(2,128)S(1)}, f32[2,8576]{1,0:T(2,128)S(1)}, u32[]{:S(2)}, u32[]{:S(2)}) collective-permute-start(f32[2,8576]{1,0:T(2,128)S(1)} %add.383), channel_id=1, source_target_pairs={{0,16},{2,18},{4,20},{6,22},{8,24},{10,26},{12,28},{14,30},{16,0},... | collective-permute-start | bytes 205832 | tf_op jit(solution)/shard_map/ppermute | solution.py:64
  430.6 17.5 %collective-permute-start.31 = (f32[2,8576]{1,0:T(2,128)S(1)}, f32[2,8576]{1,0:T(2,128)S(1)}, u32[]{:S(2)}, u32[]{:S(2)}) collective-permute-start(f32[2,8576]{1,0:T(2,128)S(1)} %add.383), channel_id=1, source_target_pairs={{0,8},{2,10},{4,12},{6,14},{8,0},{10,2},{12,4},{14,6},{16,24},{18,... | collective-permute-start | bytes 205832 | tf_op jit(solution)/shard_map/ppermute | solution.py:64
  439.0 9.1 %collective-permute-start.32 = (f32[2,8576]{1,0:T(2,128)S(1)}, f32[2,8576]{1,0:T(2,128)S(1)}, u32[]{:S(2)}, u32[]{:S(2)}) collective-permute-start(f32[2,8576]{1,0:T(2,128)S(1)} %add.383), channel_id=1, source_target_pairs={{0,24},{2,26},{4,28},{6,30},{8,16},{10,18},{12,20},{14,22},{16,8},... | collective-permute-start | bytes 205832 | tf_op jit(solution)/shard_map/ppermute | solution.py:64
  441.5 14.1 %collective-permute-start.33 = (bf16[2,4,48,384]{3,2,1,0:T(8,128)(2,1)S(1)}, bf16[2,4,48,384]{3,2,1,0:T(8,128)(2,1)S(1)}, u32[]{:S(2)}, u32[]{:S(2)}) collective-permute-start(bf16[2,4,48,384]{3,2,1,0:T(8,128)(2,1)S(1)} %add_convert_fusion.11), channel_id=1, source_target_pairs={{0,8},{2,10},{4,12},{6,14},{8,0},{10,2},{12,4},{14,6},{16,24},{18,... | collective-permute-start | bytes 884744 | tf_op jit(solution)/shard_map/ppermute | solution.py:64
  441.6 15.7 %collective-permute-start.35 = (bf16[1,2,48,1536]{3,2,1,0:T(8,128)(2,1)S(1)}, bf16[1,2,48,1536]{3,2,1,0:T(8,128)(2,1)S(1)}, u32[]{:S(2)}, u32[]{:S(2)}) collective-permute-start(bf16[1,2,48,1536]{3,2,1,0:T(8,128)(2,1)S(1)} %add_convert_fusion.10), channel_id=1, source_target_pairs={{0,16},{2,18},{4,20},{6,22},{8,24},{10,26},{12,28},{14,30},{16,0},... | collective-permute-start | bytes 884744 | tf_op jit(solution)/shard_map/ppermute | solution.py:64
  456.6 8.6 %collective-permute-start.34 = (bf16[1,4,48,384]{3,2,1,0:T(8,128)(2,1)S(1)}, bf16[1,4,48,384]{3,2,1,0:T(8,128)(2,1)S(1)}, u32[]{:S(2)}, u32[]{:S(2)}) collective-permute-start(bf16[1,4,48,384]{3,2,1,0:T(8,128)(2,1)S(1)} %add_convert_fusion.14), channel_id=1, source_target_pairs={{0,16},{2,18},{4,20},{6,22},{8,24},{10,26},{12,28},{14,30},{16,0},... | collective-permute-start | bytes 442376 | tf_op jit(solution)/shard_map/ppermute | solution.py:64
  460.2 14.0 %collective-permute-start.43 = (f32[2,8576]{1,0:T(2,128)}, f32[2,8576]{1,0:T(2,128)}, u32[]{:S(2)}, u32[]{:S(2)}) collective-permute-start(f32[2,8576]{1,0:T(2,128)} %add_add_fusion.1), channel_id=1, source_target_pairs={{0,2},{2,0},{4,6},{6,4},{8,10},{10,8},{12,14},{14,12},{16,18},{18,... | collective-permute-start | bytes 205832 | tf_op jit(solution)/shard_map/ppermute | solution.py:64
  461.5 14.9 %collective-permute-start.44 = (f32[2,8576]{1,0:T(2,128)}, f32[2,8576]{1,0:T(2,128)}, u32[]{:S(2)}, u32[]{:S(2)}) collective-permute-start(f32[2,8576]{1,0:T(2,128)} %add_add_fusion.1), channel_id=1, source_target_pairs={{0,4},{2,6},{4,0},{6,2},{8,12},{10,14},{12,8},{14,10},{16,20},{18,... | collective-permute-start | bytes 205832 | tf_op jit(solution)/shard_map/ppermute | solution.py:64
  461.9 14.6 %collective-permute-start.45 = (f32[2,8576]{1,0:T(2,128)}, f32[2,8576]{1,0:T(2,128)}, u32[]{:S(2)}, u32[]{:S(2)}) collective-permute-start(f32[2,8576]{1,0:T(2,128)} %add_add_fusion.1), channel_id=1, source_target_pairs={{0,6},{2,4},{4,2},{6,0},{8,14},{10,12},{12,10},{14,8},{16,22},{18,... | collective-permute-start | bytes 205832 | tf_op jit(solution)/shard_map/ppermute | solution.py:64
  470.8 1.2 collective-permute-start.36
  472.0 5.5 %collective-permute-start.37 = (f32[8,128]{1,0:T(8,128)S(1)}, f32[8,128]{1,0:T(8,128)S(1)}, u32[]{:S(2)}, u32[]{:S(2)}) collective-permute-start(f32[8,128]{1,0:T(8,128)S(1)} %add.423), channel_id=1, source_target_pairs={{0,16},{2,18},{4,20},{6,22},{8,24},{10,26},{12,28},{14,30},{16,0},... | collective-permute-start | bytes 12296 | tf_op jit(solution)/shard_map/ppermute | solution.py:64
  472.9 4.6 collective-permute-start.38
  474.2 5.4 %collective-permute-start.39 = (f32[8,128]{1,0:T(8,128)S(1)}, f32[8,128]{1,0:T(8,128)S(1)}, u32[]{:S(2)}, u32[]{:S(2)}) collective-permute-start(f32[8,128]{1,0:T(8,128)S(1)} %add.423), channel_id=1, source_target_pairs={{0,24},{2,26},{4,28},{6,30},{8,16},{10,18},{12,20},{14,22},{16,8},... | collective-permute-start | bytes 12296 | tf_op jit(solution)/shard_map/ppermute | solution.py:64
  479.6 4.2 collective-permute-start.40
  480.8 3.6 collective-permute-start.41
  481.4 4.5 collective-permute-start.42
  494.3 1.2 collective-permute-start.46
  495.5 4.5 collective-permute-start.47
  495.5 4.5 collective-permute-start.48
  497.7 5.4 %collective-permute-start.49 = (f32[8,128]{1,0:T(8,128)S(1)}, f32[8,128]{1,0:T(8,128)S(1)}, u32[]{:S(2)}, u32[]{:S(2)}) collective-permute-start(f32[8,128]{1,0:T(8,128)S(1)} %add.452), channel_id=1, source_target_pairs={{0,24},{2,26},{4,28},{6,30},{8,16},{10,18},{12,20},{14,22},{16,8},... | collective-permute-start | bytes 12296 | tf_op jit(solution)/shard_map/ppermute | solution.py:64
  503.1 5.3 %collective-permute-start.50 = (f32[8,128]{1,0:T(8,128)S(1)}, f32[8,128]{1,0:T(8,128)S(1)}, u32[]{:S(2)}, u32[]{:S(2)}) collective-permute-start(f32[8,128]{1,0:T(8,128)S(1)} %add_add_fusion.3), channel_id=1, source_target_pairs={{0,2},{2,0},{4,6},{6,4},{8,10},{10,8},{12,14},{14,12},{16,18},{18,... | collective-permute-start | bytes 12296 | tf_op jit(solution)/shard_map/ppermute | solution.py:64
  504.1 4.3 collective-permute-start.51
  506.0 4.5 collective-permute-start.52
  (85 other events, 703.6 us)
Sparse Core Ops, SparseCore 0:
  12.0 130.5 all-gather.2

commit v5 on v4

--- a/solution.py
+++ b/solution.py
@@ -124,9 +124,18 @@
     def pair(self, move, rest=()):
         while self.running(move):
             self.advance([move])
-        held, rest = lax.optimization_barrier((move.pop("held"), rest))
-        held = jnp.concatenate([held, move.pop("come")], axis=0)
-        move["pair"] = (held, self.sibling(held), 0)
+        held, come = move.pop("held"), move.pop("come")
+        if "swapped" not in move:
+            move["swapped"] = self.sibling(held)
+        held, come, rest = lax.optimization_barrier((held, come, rest))
+        swapped = [move.pop("swapped"), self.sibling(come)]
+        held = jnp.concatenate([held, come], axis=0)
+        move["pair"] = (held, jnp.concatenate(swapped, axis=0), 0)
+        return rest
+
+    def swap_early(self, move, rest):
+        value, rest, self.last = lax.optimization_barrier((move["held"], rest, self.last))
+        move["swapped"] = self.sibling(value)
         return rest
 
     def summed(self, value, come):
@@ -221,7 +230,7 @@
             scratch_shapes=list(scratch),
         ),
         compiler_params=pltpu.CompilerParams(
-            dimension_semantics=("arbitrary",), vmem_limit_bytes=44 << 20
+            dimension_semantics=("arbitrary",), vmem_limit_bytes=38 << 20
         ),
         cost_estimate=cost(time),
         name=name,
@@ -545,7 +554,7 @@
             out_specs=[pl.BlockSpec((rows, cols), lambda i, at: (i, 0)) for _ in pairs],
         ),
         compiler_params=pltpu.CompilerParams(
-            dimension_semantics=("arbitrary",), vmem_limit_bytes=44 << 20
+            dimension_semantics=("arbitrary",), vmem_limit_bytes=38 << 20
         ),
         cost_estimate=cost(4),
         name="join",
@@ -611,7 +620,7 @@
             ],
         ),
         compiler_params=pltpu.CompilerParams(
-            dimension_semantics=("arbitrary",), vmem_limit_bytes=24 << 20
+            dimension_semantics=("arbitrary",), vmem_limit_bytes=44 << 20
         ),
         cost_estimate=cost(3),
         name="prepare",
@@ -706,7 +715,7 @@
         grid_spec=pltpu.PrefetchScalarGridSpec(num_scalar_prefetch=2, grid=(seqs,pairs),
             in_specs=[col(0)]*depth+[col(1)]*depth+[col(2)],
             out_specs=[pl.BlockSpec((rows,128),lambda s,j,c,l:(s,j)), pl.BlockSpec((1,8,rows),lambda s,j,c,l:(s*pairs+j,0,0))]),
-        compiler_params=pltpu.CompilerParams(dimension_semantics=("arbitrary","arbitrary"),vmem_limit_bytes=24 << 20),
+        compiler_params=pltpu.CompilerParams(dimension_semantics=("arbitrary","arbitrary"),vmem_limit_bytes=44 << 20),
         cost_estimate=cost(10),
         name="attend_forward",
     )(core, lengths, *projections, *projections, projections[0])
@@ -771,7 +780,7 @@
         partial(attend_backward_kernel, depth=depth, with_later=later is not None, keep_total=keep_total),
         out_shape=out_shape,
         grid_spec=pltpu.PrefetchScalarGridSpec(num_scalar_prefetch=2, grid=(seqs,pairs), in_specs=in_specs, out_specs=out_specs),
-        compiler_params=pltpu.CompilerParams(dimension_semantics=("arbitrary","arbitrary"),vmem_limit_bytes=24 << 20),
+        compiler_params=pltpu.CompilerParams(dimension_semantics=("arbitrary","arbitrary"),vmem_limit_bytes=44 << 20),
         cost_estimate=cost(17),
         name="attend_backward",
     )(core, lengths, *args)
@@ -839,6 +848,8 @@
     vectors, value_bias, up_bias = prepared[0::3], prepared[1::3], prepared[2::3]
     links.advance([one])
     links.advance([one])
+    if not links.running(one):
+        (hidden,) = links.swap_early(one, (hidden,))
     (hidden,) = links.advance([four], (hidden,))
 
     def gathered(layer_at, kind):
@@ -871,6 +882,8 @@
             squares = jnp.pad(jnp.stack(squares, axis=1), ((0, 0), (0, 124)))
             squares, context = links.advance([four], (squares, context))
             (context,) = links.advance([four], (context,))
+            if not links.running(four):
+                (context,) = links.swap_early(four, (context,))
         kept = {
             "input_turned": hidden_turned, "projected": projected, "log_norm": log_norm, "context": context,
         }

time: 535 us -> 518 us (0.968); the launches traced: 525 us -> 515 us
  other arithmetic: 67.8 us -> 61.4 us
    ppermute x11 -> x13, waiting for transfers between devices: 17.2 us -> 8.37 us  [sibling(): return lax.ppermute(value, 'tensor', [(0, 1), (1, 0)])]
    ppermute x42, waiting for transfers between devices: 156 us -> 164 us  [swap(): return lax.ppermute(value, ('dp', 'tensor'), pairs)]
    unnamed x192 -> x175, local copies, waits for them, and re-layouts: 40.4 us -> 36.7 us
  transfers between devices with their start and end apart: 54 -> 56, of which waited for: 29 -> 28; matrix products, arithmetic and copies ran while one was open for 8% -> 8% of each run, Pallas kernels for 23% -> 24%
where the time goes in v5:
time: 518 us; the launch traced here: 515 us
  waiting for transfers between devices  172 us (33%)
  Pallas kernels  158 us (31%)
  other arithmetic  61.4 us (12%)
  starting transfers between devices  58.7 us (11%)
  local copies, waits for them, and re-layouts  43.7 us (8%)
  between operations  20.5 us (4%)
    ppermute x42, waiting for transfers between devices, swap(): return lax.ppermute(value, ('dp', 'tensor'), pairs)  164 us
    pallas_call x12, Pallas kernels, call(): pl.pallas_call(lambda at, *refs: kernel(*weight_rows(at), Row(at, 0), Row...  98.9 us
    ppermute x42, starting transfers between devices, swap(): return lax.ppermute(value, ('dp', 'tensor'), pairs)  57.7 us
    unnamed x175, local copies, waits for them, and re-layouts  36.7 us
    pallas_call x2, Pallas kernels, attend_backward(): pl.pallas_call(partial(attend_backward_kernel, depth=depth, with_later=la...  34.2 us
    convert_element_type x16, other arithmetic, advance(): sum((piece[half:size].astype(f32) for piece in move['pieces'])).astype(bf16)  26.7 us
    pallas_call x2, Pallas kernels, attend_forward(): pl.pallas_call(partial(attend_forward_kernel, depth=depth), out_shape=[ja...  19.6 us
  transfers between devices with their start and end apart: 56, of which 28 were waited for; matrix products, arithmetic and copies ran while one was open for 8% of the time, Pallas kernels for 24%

profile of v5, /device:TPU:0, one launch (start us, length us, event | category | flops | bytes accessed | tf_op | source)
XLA Modules:
  0.0 515.0 jit_solution(10285747159168082875)
XLA Ops:
  12.6 4.0 collective-permute-start
  24.2 11.2 %collective-permute-done.1 = bf16[2,48,1152]{2,1,0:T(8,128)(2,1)S(1)} collective-permute-done((bf16[2,48,1152]{2,1,0:T(8,128)(2,1)S(1)}, bf16[2,48,1152]{2,1,0:T(8,128)(2,1)S(1)}, u32[]{:S(2)}, u32[]{:S(2)}) %collective-permute-start.1) | collective-permute-done | bytes 221216 | tf_op jit(solution)/shard_map/ppermute | solution.py:64
  36.6 7.2 %collective-permute-done.2 = bf16[4,48,1152]{2,1,0:T(8,128)(2,1)S(1)} collective-permute-done((bf16[4,48,1152]{2,1,0:T(8,128)(2,1)S(1)}, bf16[4,48,1152]{2,1,0:T(8,128)(2,1)S(1)}, u32[]{:S(2)}, u32[]{:S(2)}) %collective-permute-start.2) | collective-permute-done | bytes 442400 | tf_op jit(solution)/shard_map/ppermute | solution.py:64
  45.0 18.4 %collective-permute-done.3 = bf16[8,48,1152]{2,1,0:T(8,128)(2,1)S(1)} collective-permute-done((bf16[8,48,1152]{2,1,0:T(8,128)(2,1)S(1)}, bf16[8,48,1152]{2,1,0:T(8,128)(2,1)S(1)}, u32[]{:S(2)}, u32[]{:S(2)}) %collective-permute-start.3) | collective-permute-done | bytes 884768 | tf_op jit(solution)/shard_map/ppermute | solution.py:64
  64.0 7.6 %collective-permute-start.6 = (bf16[1,48,3456]{2,1,0:T(8,128)(2,1)S(1)}, bf16[1,48,3456]{2,1,0:T(8,128)(2,1)S(1)}, u32[]{:S(2)}, u32[]{:S(2)}) collective-permute-start(bf16[1,48,3456]{2,1,0:T(8,128)(2,1)S(1)} %maximum_bitcast_fusion), channel_id=1, source_target_pairs={{0,16},{2,18},{4,20},{6,22},{8,24},{10,26},{12,28},{14,30},{16,0},... | collective-permute-start | bytes 995336 | tf_op jit(solution)/shard_map/ppermute | solution.py:64
  72.1 4.4 project.2.refs_0_.refs_1_.refs_2_.refs_3_
  76.5 16.1 %collective-permute-done.6 = bf16[1,48,3456]{2,1,0:T(8,128)(2,1)S(1)} collective-permute-done((bf16[1,48,3456]{2,1,0:T(8,128)(2,1)S(1)}, bf16[1,48,3456]{2,1,0:T(8,128)(2,1)S(1)}, u32[]{:S(2)}, u32[]{:S(2)}) %collective-permute-start.6) | collective-permute-done | bytes 331808 | tf_op jit(solution)/shard_map/ppermute | solution.py:64
  93.5 9.5 %attend_forward.2 = (bf16[512,768]{1,0:T(8,128)(2,1)S(1)}, f32[6,8,512]{2,1,0:T(8,128)S(1)}) custom-call(s32[1]{0:T(128)} %bitcast.5.core, s32[2]{0:T(128)S(1)} %copy-done.53, bf16[512,2304]{1,0:T(8,128)(2,1)S(1)} %project.2.refs_0_.refs_1_.refs_2_.refs_3_, bf16[512,2304]{1,0:T(8,128)(2,1)S(1)} %project.2.refs_0_.refs_1_.refs_2_.refs_3_, ...), custom_call_target="tpu_custom_call" | custom-call | bytes 25000000 | tf_op jit(solution)/shard_map/attend_forward/pallas_call | solution.py:712
  106.8 36.1 %collective-permute-done.7 = bf16[2,48,3456]{2,1,0:T(8,128)(2,1)} collective-permute-done((bf16[2,48,3456]{2,1,0:T(8,128)(2,1)}, bf16[2,48,3456]{2,1,0:T(8,128)(2,1)}, u32[]{:S(2)}, u32[]{:S(2)}) %collective-permute-start.7) | collective-permute-done | bytes 663584 | tf_op jit(solution)/shard_map/ppermute | solution.py:64
  145.4 16.7 %collective-permute-done.8 = bf16[4,48,3456]{2,1,0:T(8,128)(2,1)S(1)} collective-permute-done((bf16[4,48,3456]{2,1,0:T(8,128)(2,1)S(1)}, bf16[4,48,3456]{2,1,0:T(8,128)(2,1)S(1)}, u32[]{:S(2)}, u32[]{:S(2)}) %collective-permute-start.8) | collective-permute-done | bytes 1327136 | tf_op jit(solution)/shard_map/ppermute | solution.py:64
  162.1 1.8 pad_maximum_fusion
  166.6 14.2 %feed_forward.2 = (f32[512,768]{1,0:T(8,128)S(1)}, bf16[768,512]{1,0:T(8,128)(2,1)S(1)}, bf16[2,512,1536]{2,1,0:T(8,128)(2,1)S(1)}, f32[2,512,1536]{2,1,0:T(8,12...) custom-call(s32[4,17]{1,0:T(4,128)S(1)} %dynamic-slice_bitcast_fusio, ...), custom_call_target="tpu_custom_call" | custom-call | bytes 45000000 | tf_op jit(solution)/shard_map/feed_forward/pallas_call | solution.py:222
  186.0 5.2 %project.3.refs_0_.refs_2_.refs_4_ = bf16[512,2304]{1,0:T(8,128)(2,1)S(1)} custom-call(s32[4,17]{1,0:T(4,128)S(1)} %dynamic-slice_bitcast_fusion.at, bf16[512,768]{1,0:T(8,128)(2,1)S(1)} %get-tuple-element.302.refs_0_, bf16[16,2,48,4608]{3,2,1,0:T(8,128)(2,1)} %bitcast.97, bf16[16,2,48,4608]{3,2,1,0:T(8,128)(2,1)} %bitcast.98, ...), custom_call_target="tpu_custom_call" | custom-call | bytes 17500000 | tf_op jit(solution)/shard_map/project/pallas_call | solution.py:222
  191.2 10.1 %attend_forward.3 = (bf16[512,768]{1,0:T(8,128)(2,1)S(1)}, f32[6,8,512]{2,1,0:T(8,128)S(1)}) custom-call(s32[1]{0:T(128)} %bitcast.5.core, s32[2]{0:T(128)S(1)} %copy-done.53, bf16[512,2304]{1,0:T(8,128)(2,1)S(1)} %project.3.refs_0_.refs_2_.refs_4_, bf16[512,2304]{1,0:T(8,128)(2,1)S(1)} %project.2.refs_0_.refs_1_.refs_2_.refs_3_, ...), custom_call_target="tpu_custom_call" | custom-call | bytes 25000000 | tf_op jit(solution)/shard_map/attend_forward/pallas_call | solution.py:712
  201.9 1.9 constant_dynamic-update-slice_fusion.7
  203.9 1.9 constant_dynamic-update-slice_fusion.5
  205.8 2.1 constant_dynamic-update-slice_fusion.4.refs_2_.refs_4_.refs_6_.refs_8_
  208.3 2.3 copy-done
  210.6 2.4 copy-done.54
  213.0 15.6 %feed_forward.3 = (f32[512,768]{1,0:T(8,128)S(1)}, bf16[768,512]{1,0:T(8,128)(2,1)S(1)}, bf16[2,512,1536]{2,1,0:T(8,128)(2,1)S(1)}, f32[2,512,1536]{2,1,0:T(8,12...) custom-call(s32[4,17]{1,0:T(4,128)S(1)} %dynamic-slice_bitcast_fusio, ...), custom_call_target="tpu_custom_call" | custom-call | bytes 45000000 | tf_op jit(solution)/shard_map/feed_forward/pallas_call | solution.py:222
  233.2 2.0 copy-done.15
  235.3 15.5 %feed_backward.2 = (bf16[16,2,48,1536]{3,2,1,0:T(8,128)(2,1)S(1)}, bf16[16,2,48,1536]{3,2,1,0:T(8,128)(2,1)}, f32[2,8,1536]{2,1,0:T(8,128)S(1)}, f32[512,768]{1,0:T(8,128)S(1)}) custom-call(s32[4,17]{1,0:T(4,128)S(1)} %dynamic-slice_bitcast_fusion.at, f32[512,768]{1,0:T(8,128)S(1)} %get-tuple-element.312.refs_0_, ...), custom_call_target="tpu_custom_call" | custom-call | bytes 50000000 | tf_op jit(solution)/shard_map/feed_backward/pallas_call | solution.py:222
  250.7 2.1 copy-done.8
  257.5 3.9 context_backward.2
  262.9 2.4 add_convert_fusion.1
  265.9 17.7 %attend_backward.2 = (bf16[3,512,768]{2,1,0:T(8,128)(2,1)S(1)}, f32[1,8,768]{2,1,0:T(8,128)S(1)}, f32[12,512,512]{2,1,0:T(8,128)}) custom-call(s32[1]{0:T(128)} %bitcast.5.core, s32[2]{0:T(128)S(1)} %copy-done.53, bf16[512,2304]{1,0:T(8,128)(2,1)S(1)} %project.3.refs_0_.refs_2_.refs_4_, bf16[512,2304]{1,0:T(8,128)(2,1)S(1)} %project.2.refs_0_.refs_1_.refs_2_.refs_3_, ...), custom_call_target="tpu_custom_call" | custom-call | bytes 42500000 | tf_op jit(solution)/shard_map/attend_backward/pallas_call | solution.py:779
  285.3 5.0 projection_grads.2
  290.4 3.9 collective-permute-done.13
  294.3 3.1 add_convert_fusion.5
  298.4 6.5 %project_backward.2 = (f32[512,768]{1,0:T(8,128)S(1)}, bf16[512,768]{1,0:T(8,128)(2,1)S(1)}, bf16[768,512]{1,0:T(8,128)(2,1)S(1)}, f32[8,768]{1,0:T(8,128)S(1)}) custom-call(s32[4,17]{1,0:T(4,128)S(1)} %dynamic-slice_bitcast_fusion.at, bf16[3,512,768]{2,1,0:T(8,128)(2,1)S(1)} %get-tuple-element.339.refs_3_.refs_0_, ...), custom_call_target="tpu_custom_call" | custom-call | bytes 20000000 | tf_op jit(solution)/shard_map/project_backward/pallas_call | solution.py:222
  305.0 1.7 add_convert_fusion.4
  307.3 15.6 %feed_backward.3 = (bf16[16,2,48,1536]{3,2,1,0:T(8,128)(2,1)S(1)}, bf16[16,2,48,1536]{3,2,1,0:T(8,128)(2,1)}, f32[2,8,1536]{2,1,0:T(8,128)S(1)}, f32[512,768]{1,0:T(8,128)S(1)}) custom-call(s32[4,17]{1,0:T(4,128)S(1)} %dynamic-slice_bitcast_fusion.at, f32[512,768]{1,0:T(8,128)S(1)} %get-tuple-element.353.refs_0_, ...), custom_call_target="tpu_custom_call" | custom-call | bytes 50000000 | tf_op jit(solution)/shard_map/feed_backward/pallas_call | solution.py:222
  322.9 4.0 add_convert_fusion.9
  329.7 3.8 context_backward.3
  333.5 5.1 collective-permute-done.18
  338.7 2.1 add_convert_fusion.13
  340.8 2.5 add_convert_fusion
  345.1 16.4 %attend_backward.3 = (bf16[3,512,768]{2,1,0:T(8,128)(2,1)S(1)}, f32[1,8,768]{2,1,0:T(8,128)S(1)}) custom-call(s32[1]{0:T(128)} %bitcast.5.core, s32[2]{0:T(128)S(1)} %copy-done.53, bf16[512,2304]{1,0:T(8,128)(2,1)S(1)} %project.2.refs_0_.refs_1_.refs_2_.refs_3_, bf16[512,2304]{1,0:T(8,128)(2,1)S(1)} %project.2.refs_0_.refs_1_.refs_2_.refs_3_, ...), custom_call_target="tpu_custom_call" | custom-call | bytes 42500000 | tf_op jit(solution)/shard_map/attend_backward/pallas_call | solution.py:779
  363.6 2.0 collective-permute-start.20
  368.7 2.8 collective-permute-done.20
  372.8 2.6 add_convert_fusion.3
  375.9 5.0 projection_grads.3
  382.2 3.4 collective-permute-done.22
  388.1 2.3 collective-permute-start.28
  390.4 4.1 project_backward.3.refs_2_
  394.5 11.3 %collective-permute-done.23 = bf16[4,2,48,1536]{3,2,1,0:T(8,128)(2,1)S(1)} collective-permute-done((bf16[4,2,48,1536]{3,2,1,0:T(8,128)(2,1)S(1)}, bf16[4,2,48,1536]{3,2,1,0:T(8,128)(2,1)S(1)}, u32[]{:S(2)}, u32[]{:S(2)}) %collective-permute-start.23) | collective-permute-done | bytes 1179680 | tf_op jit(solution)/shard_map/ppermute | solution.py:64
  407.6 1.8 collective-permute-done.24
  417.7 5.5 %collective-permute-done.30 = bf16[4,4,48,384]{3,2,1,0:T(8,128)(2,1)S(1)} collective-permute-done((bf16[4,4,48,384]{3,2,1,0:T(8,128)(2,1)S(1)}, bf16[4,4,48,384]{3,2,1,0:T(8,128)(2,1)S(1)}, u32[]{:S(2)}, u32[]{:S(2)}) %collective-permute-start.30) | collective-permute-done | bytes 589856 | tf_op jit(solution)/shard_map/ppermute | solution.py:64
  424.7 7.1 %collective-permute-done.31 = bf16[2,2,48,1536]{3,2,1,0:T(8,128)(2,1)S(1)} collective-permute-done((bf16[2,2,48,1536]{3,2,1,0:T(8,128)(2,1)S(1)}, bf16[2,2,48,1536]{3,2,1,0:T(8,128)(2,1)S(1)}, u32[]{:S(2)}, u32[]{:S(2)}) %collective-permute-start.31) | collective-permute-done | bytes 589856 | tf_op jit(solution)/shard_map/ppermute | solution.py:64
  434.3 3.2 collective-permute-start.37
  437.6 3.2 join.1
  440.8 7.6 %collective-permute-done.35 = bf16[2,4,48,384]{3,2,1,0:T(8,128)(2,1)S(1)} collective-permute-done((bf16[2,4,48,384]{3,2,1,0:T(8,128)(2,1)S(1)}, bf16[2,4,48,384]{3,2,1,0:T(8,128)(2,1)S(1)}, u32[]{:S(2)}, u32[]{:S(2)}) %collective-permute-start.35) | collective-permute-done | bytes 294944 | tf_op jit(solution)/shard_map/ppermute | solution.py:64
  453.5 2.1 collective-permute-start.46
  467.7 2.7 collective-permute-done.41
  471.3 1.9 collective-permute-start.43
  474.9 2.8 collective-permute-done.44
  479.7 2.6 multiply_reduce_fusion.6
  482.3 1.8 multiply_reduce_fusion.9
  484.1 1.9 multiply_reduce_fusion.1
  487.4 2.7 collective-permute-start.50
  491.9 3.6 collective-permute-done.51
  496.2 2.7 collective-permute-start.54
  499.0 1.8 multiply_subtract_fusion.4
  501.3 2.5 multiply_subtract_fusion
  (327 shorter events, 101.2 us)
Async XLA Ops:
  7.2 158.2 %all-gather.3.cloned.1.call-start = ((), (), s32[]{:S(2)}) async-start(), calls=%async_computation | async-start | bytes 14598144 | tf_op jit(solution)/shard_map/all_gather | solution.py:843
  12.6 9.8 %collective-permute-start = (bf16[1,48,1152]{2,1,0:T(8,128)(2,1)}, bf16[1,48,1152]{2,1,0:T(8,128)(2,1)}, u32[]{:S(2)}, u32[]{:S(2)}) collective-permute-start(bf16[1,48,1152]{2,1,0:T(8,128)(2,1)} %bitcast.31), channel_id=1, source_target_pairs={{0,16},{2,18},{4,20},{6,22},{8,24},{10,26},{12,28},{14,30},{16,0},... | collective-permute-start | bytes 331784 | tf_op jit(solution)/shard_map/ppermute | solution.py:64
  21.1 50.9 %copy-start.10 = (bf16[512,768]{1,0:T(8,128)(2,1)}, bf16[512,768]{1,0:T(8,128)(2,1)S(1)}, u32[]{:S(2)}) copy-start(bf16[512,768]{1,0:T(8,128)(2,1)S(1)} %get-tuple-element.273.refs_0_) | copy-start | bytes 2359300
  21.1 23.8 %copy-start.68 = (bf16[48,1536]{1,0:T(8,128)(2,1)S(1)}, bf16[48,1536]{1,0:T(8,128)(2,1)}, u32[]{:S(2)}) copy-start(bf16[48,1536]{1,0:T(8,128)(2,1)} %get-tuple-element.503) | copy-start | bytes 442372
  21.1 23.8 %copy-start.69 = (bf16[48,1536]{1,0:T(8,128)(2,1)S(1)}, bf16[48,1536]{1,0:T(8,128)(2,1)}, u32[]{:S(2)}) copy-start(bf16[48,1536]{1,0:T(8,128)(2,1)} %get-tuple-element.508) | copy-start | bytes 442372
  23.4 12.0 %collective-permute-start.1 = (bf16[2,48,1152]{2,1,0:T(8,128)(2,1)S(1)}, bf16[2,48,1152]{2,1,0:T(8,128)(2,1)S(1)}, u32[]{:S(2)}, u32[]{:S(2)}) collective-permute-start(bf16[2,48,1152]{2,1,0:T(8,128)(2,1)S(1)} %pad_maximum_fusion.7), channel_id=1, source_target_pairs={{0,8},{2,10},{4,12},{6,14},{8,0},{10,2},{12,4},{14,6},{16,24},{18,... | collective-permute-start | bytes 663560 | tf_op jit(solution)/shard_map/ppermute | solution.py:64
  35.4 8.4 %collective-permute-start.2 = (bf16[4,48,1152]{2,1,0:T(8,128)(2,1)S(1)}, bf16[4,48,1152]{2,1,0:T(8,128)(2,1)S(1)}, u32[]{:S(2)}, u32[]{:S(2)}) collective-permute-start(bf16[4,48,1152]{2,1,0:T(8,128)(2,1)S(1)} %pad_maximum_fusion.5), channel_id=1, source_target_pairs={{0,2},{2,0},{4,6},{6,4},{8,10},{10,8},{12,14},{14,12},{16,18},{18,... | collective-permute-start | bytes 1327112 | tf_op jit(solution)/shard_map/ppermute | solution.py:64
  43.9 19.4 %collective-permute-start.3 = (bf16[8,48,1152]{2,1,0:T(8,128)(2,1)S(1)}, bf16[8,48,1152]{2,1,0:T(8,128)(2,1)S(1)}, u32[]{:S(2)}, u32[]{:S(2)}) collective-permute-start(bf16[8,48,1152]{2,1,0:T(8,128)(2,1)S(1)} %pad_maximum_fusion.2), channel_id=1, source_target_pairs={{0,4},{2,6},{4,0},{6,2},{8,12},{10,14},{12,8},{14,10},{16,20},{18,... | collective-permute-start | bytes 2654216 | tf_op jit(solution)/shard_map/ppermute | solution.py:64
  44.9 26.9 %collective-permute-start.4 = (bf16[8,48,1152]{2,1,0:T(8,128)(2,1)S(1)}, bf16[8,48,1152]{2,1,0:T(8,128)(2,1)S(1)}, u32[]{:S(2)}, u32[]{:S(2)}) collective-permute-start(bf16[8,48,1152]{2,1,0:T(8,128)(2,1)S(1)} %pad_maximum_fusion.2), channel_id=1, source_target_pairs={{0,1},{1,0},{2,3},{3,2},{4,5},{5,4},{6,7},{7,6},{8,9},{9,8},{10,11... | collective-permute-start | bytes 2654216 | tf_op jit(solution)/shard_map/ppermute | solution.py:67
  63.3 8.6 %collective-permute-start.5 = (bf16[8,48,1152]{2,1,0:T(8,128)(2,1)S(1)}, bf16[8,48,1152]{2,1,0:T(8,128)(2,1)S(1)}, u32[]{:S(2)}, u32[]{:S(2)}) collective-permute-start(bf16[8,48,1152]{2,1,0:T(8,128)(2,1)S(1)} %collective-permute-done.3), channel_id=1, source_target_pairs={{0,1},{1,0},{2,3},{3,2},{4,5},{5,4},{6,7},{7,6},{8,9},{9,8},{10,11... | collective-permute-start | bytes 2654216 | tf_op jit(solution)/shard_map/ppermute | solution.py:67
  64.0 28.5 %collective-permute-start.6 = (bf16[1,48,3456]{2,1,0:T(8,128)(2,1)S(1)}, bf16[1,48,3456]{2,1,0:T(8,128)(2,1)S(1)}, u32[]{:S(2)}, u32[]{:S(2)}) collective-permute-start(bf16[1,48,3456]{2,1,0:T(8,128)(2,1)S(1)} %maximum_bitcast_fusion), channel_id=1, source_target_pairs={{0,16},{2,18},{4,20},{6,22},{8,24},{10,26},{12,28},{14,30},{16,0},... | collective-permute-start | bytes 995336 | tf_op jit(solution)/shard_map/ppermute | solution.py:64
  93.5 49.4 %collective-permute-start.7 = (bf16[2,48,3456]{2,1,0:T(8,128)(2,1)}, bf16[2,48,3456]{2,1,0:T(8,128)(2,1)}, u32[]{:S(2)}, u32[]{:S(2)}) collective-permute-start(bf16[2,48,3456]{2,1,0:T(8,128)(2,1)} %pad_maximum_fusion.3), channel_id=1, source_target_pairs={{0,8},{2,10},{4,12},{6,14},{8,0},{10,2},{12,4},{14,6},{16,24},{18,... | collective-permute-start | bytes 1990664 | tf_op jit(solution)/shard_map/ppermute | solution.py:64
  144.3 17.8 %collective-permute-start.8 = (bf16[4,48,3456]{2,1,0:T(8,128)(2,1)S(1)}, bf16[4,48,3456]{2,1,0:T(8,128)(2,1)S(1)}, u32[]{:S(2)}, u32[]{:S(2)}) collective-permute-start(bf16[4,48,3456]{2,1,0:T(8,128)(2,1)S(1)} %pad_maximum_fusion.1), channel_id=1, source_target_pairs={{0,2},{2,0},{4,6},{6,4},{8,10},{10,8},{12,14},{14,12},{16,18},{18,... | collective-permute-start | bytes 3981320 | tf_op jit(solution)/shard_map/ppermute | solution.py:64
  163.9 37.4 %collective-permute-start.9 = (bf16[8,48,3456]{2,1,0:T(8,128)(2,1)}, bf16[8,48,3456]{2,1,0:T(8,128)(2,1)}, u32[]{:S(2)}, u32[]{:S(2)}) collective-permute-start(bf16[8,48,3456]{2,1,0:T(8,128)(2,1)} %pad_maximum_fusion), channel_id=1, source_target_pairs={{0,4},{2,6},{4,0},{6,2},{8,12},{10,14},{12,8},{14,10},{16,20},{18,... | collective-permute-start | bytes 7962632 | tf_op jit(solution)/shard_map/ppermute | solution.py:64
  165.4 36.5 %collective-permute-start.10 = (bf16[8,48,3456]{2,1,0:T(8,128)(2,1)}, bf16[8,48,3456]{2,1,0:T(8,128)(2,1)}, u32[]{:S(2)}, u32[]{:S(2)}) collective-permute-start(bf16[8,48,3456]{2,1,0:T(8,128)(2,1)} %pad_maximum_fusion), channel_id=1, source_target_pairs={{0,1},{1,0},{2,3},{3,2},{4,5},{5,4},{6,7},{7,6},{8,9},{9,8},{10,11... | collective-permute-start | bytes 7962632 | tf_op jit(solution)/shard_map/ppermute | solution.py:67
  201.4 6.6 %collective-permute-start.11 = (bf16[8,48,3456]{2,1,0:T(8,128)(2,1)}, bf16[8,48,3456]{2,1,0:T(8,128)(2,1)S(1)}, u32[]{:S(2)}, u32[]{:S(2)}) collective-permute-start(bf16[8,48,3456]{2,1,0:T(8,128)(2,1)} %collective-permute-done.9), channel_id=1, source_target_pairs={{0,1},{1,0},{2,3},{3,2},{4,5},{5,4},{6,7},{7,6},{8,9},{9,8},{10,11... | collective-permute-start | bytes 7962632 | tf_op jit(solution)/shard_map/ppermute | solution.py:67
  233.2 21.4 %slice-start = ((s8[5308416]{0:T(1024)(128)(4,1)}), s8[4194304]{0:T(1024)(128)(4,1)S(1)}, s32[]{:S(2)}) async-start(s8[5308416]{0:T(1024)(128)(4,1)} %bitcast.89), calls=%async_computation.1 | async-start | bytes 8388608
  254.7 8.3 %collective-permute-start.12 = (bf16[16,2,48,1536]{3,2,1,0:T(8,128)(2,1)}, bf16[16,2,48,1536]{3,2,1,0:T(8,128)(2,1)}, u32[]{:S(2)}, u32[]{:S(2)}) collective-permute-start(bf16[16,2,48,1536]{3,2,1,0:T(8,128)(2,1)} %get-tuple-element.325), channel_id=1, source_target_pairs={{0,1},{1,0},{2,3},{3,2},{4,5},{5,4},{6,7},{7,6},{8,9},{9,8},{10,11... | collective-permute-start | bytes 14155784 | tf_op jit(solution)/shard_map/ppermute | solution.py:67
  265.3 29.0 %collective-permute-start.13 = (bf16[8,2,48,1536]{3,2,1,0:T(8,128)(2,1)S(1)}, bf16[8,2,48,1536]{3,2,1,0:T(8,128)(2,1)}, u32[]{:S(2)}, u32[]{:S(2)}) collective-permute-start(bf16[8,2,48,1536]{3,2,1,0:T(8,128)(2,1)S(1)} %add_convert_fusion.1), channel_id=1, source_target_pairs={{0,4},{2,6},{4,0},{6,2},{8,12},{10,14},{12,8},{14,10},{16,20},{18,... | collective-permute-start | bytes 7077896 | tf_op jit(solution)/shard_map/ppermute | solution.py:64
  290.4 48.3 %copy-start.16 = (bf16[16,4,48,384]{3,2,1,0:T(8,128)(2,1)}, bf16[16,4,48,384]{3,2,1,0:T(8,128)(2,1)S(1)}, u32[]{:S(2)}) copy-start(bf16[16,4,48,384]{3,2,1,0:T(8,128)(2,1)S(1)} %get-tuple-element.440) | copy-start | bytes 7077892
  297.4 7.5 %collective-permute-start.14 = (bf16[16,4,48,384]{3,2,1,0:T(8,128)(2,1)S(1)}, bf16[16,4,48,384]{3,2,1,0:T(8,128)(2,1)}, u32[]{:S(2)}, u32[]{:S(2)}) collective-permute-start(bf16[16,4,48,384]{3,2,1,0:T(8,128)(2,1)S(1)} %get-tuple-element.348), channel_id=1, source_target_pairs={{0,1},{1,0},{2,3},{3,2},{4,5},{5,4},{6,7},{7,6},{8,9},{9,8},{10,11... | collective-permute-start | bytes 7077896 | tf_op jit(solution)/shard_map/ppermute | solution.py:67
  297.4 25.5 %collective-permute-start.15 = (bf16[4,2,48,1536]{3,2,1,0:T(8,128)(2,1)}, bf16[4,2,48,1536]{3,2,1,0:T(8,128)(2,1)}, u32[]{:S(2)}, u32[]{:S(2)}) collective-permute-start(bf16[4,2,48,1536]{3,2,1,0:T(8,128)(2,1)} %add_convert_fusion.5), channel_id=1, source_target_pairs={{0,2},{2,0},{4,6},{6,4},{8,10},{10,8},{12,14},{14,12},{16,18},{18,... | collective-permute-start | bytes 3538952 | tf_op jit(solution)/shard_map/ppermute | solution.py:64
  306.7 20.2 %collective-permute-start.16 = (bf16[8,4,48,384]{3,2,1,0:T(8,128)(2,1)S(1)}, bf16[8,4,48,384]{3,2,1,0:T(8,128)(2,1)S(1)}, u32[]{:S(2)}, u32[]{:S(2)}) collective-permute-start(bf16[8,4,48,384]{3,2,1,0:T(8,128)(2,1)S(1)} %add_convert_fusion.4), channel_id=1, source_target_pairs={{0,4},{2,6},{4,0},{6,2},{8,12},{10,14},{12,8},{14,10},{16,20},{18,... | collective-permute-start | bytes 3538952 | tf_op jit(solution)/shard_map/ppermute | solution.py:64
  328.6 12.2 %collective-permute-start.17 = (bf16[16,2,48,1536]{3,2,1,0:T(8,128)(2,1)}, bf16[16,2,48,1536]{3,2,1,0:T(8,128)(2,1)S(1)}, u32[]{:S(2)}, u32[]{:S(2)}) collective-permute-start(bf16[16,2,48,1536]{3,2,1,0:T(8,128)(2,1)} %get-tuple-element.376), channel_id=1, source_target_pairs={{0,1},{1,0},{2,3},{3,2},{4,5},{5,4},{6,7},{7,6},{8,9},{9,8},{10,11... | collective-permute-start | bytes 14155784 | tf_op jit(solution)/shard_map/ppermute | solution.py:67
  328.7 9.9 %collective-permute-start.18 = (bf16[4,4,48,384]{3,2,1,0:T(8,128)(2,1)S(1)}, bf16[4,4,48,384]{3,2,1,0:T(8,128)(2,1)S(1)}, u32[]{:S(2)}, u32[]{:S(2)}) collective-permute-start(bf16[4,4,48,384]{3,2,1,0:T(8,128)(2,1)S(1)} %add_convert_fusion.8), channel_id=1, source_target_pairs={{0,2},{2,0},{4,6},{6,4},{8,10},{10,8},{12,14},{14,12},{16,18},{18,... | collective-permute-start | bytes 1769480 | tf_op jit(solution)/shard_map/ppermute | solution.py:64
  343.6 29.2 %collective-permute-start.21 = (bf16[8,2,48,1536]{3,2,1,0:T(8,128)(2,1)}, bf16[8,2,48,1536]{3,2,1,0:T(8,128)(2,1)}, u32[]{:S(2)}, u32[]{:S(2)}) collective-permute-start(bf16[8,2,48,1536]{3,2,1,0:T(8,128)(2,1)} %add_convert_fusion), channel_id=1, source_target_pairs={{0,4},{2,6},{4,0},{6,2},{8,12},{10,14},{12,8},{14,10},{16,20},{18,... | collective-permute-start | bytes 7077896 | tf_op jit(solution)/shard_map/ppermute | solution.py:64
  345.1 22.1 %collective-permute-start.19 = (bf16[2,2,48,1536]{3,2,1,0:T(8,128)(2,1)}, bf16[2,2,48,1536]{3,2,1,0:T(8,128)(2,1)}, u32[]{:S(2)}, u32[]{:S(2)}) collective-permute-start(bf16[2,2,48,1536]{3,2,1,0:T(8,128)(2,1)} %add_convert_fusion.9), channel_id=1, source_target_pairs={{0,8},{2,10},{4,12},{6,14},{8,0},{10,2},{12,4},{14,6},{16,24},{18,... | collective-permute-start | bytes 1769480 | tf_op jit(solution)/shard_map/ppermute | solution.py:64
  363.6 7.9 %collective-permute-start.20 = (bf16[2,4,48,384]{3,2,1,0:T(8,128)(2,1)}, bf16[2,4,48,384]{3,2,1,0:T(8,128)(2,1)S(1)}, u32[]{:S(2)}, u32[]{:S(2)}) collective-permute-start(bf16[2,4,48,384]{3,2,1,0:T(8,128)(2,1)} %add_convert_fusion.13), channel_id=1, source_target_pairs={{0,8},{2,10},{4,12},{6,14},{8,0},{10,2},{12,4},{14,6},{16,24},{18,... | collective-permute-start | bytes 884744 | tf_op jit(solution)/shard_map/ppermute | solution.py:64
  380.9 4.6 collective-permute-start.22
  381.0 24.9 %collective-permute-start.23 = (bf16[4,2,48,1536]{3,2,1,0:T(8,128)(2,1)S(1)}, bf16[4,2,48,1536]{3,2,1,0:T(8,128)(2,1)S(1)}, u32[]{:S(2)}, u32[]{:S(2)}) collective-permute-start(bf16[4,2,48,1536]{3,2,1,0:T(8,128)(2,1)S(1)} %add_convert_fusion.3), channel_id=1, source_target_pairs={{0,2},{2,0},{4,6},{6,4},{8,10},{10,8},{12,14},{14,12},{16,18},{18,... | collective-permute-start | bytes 3538952 | tf_op jit(solution)/shard_map/ppermute | solution.py:64
  385.8 23.6 %collective-permute-start.24 = (bf16[8,4,48,384]{3,2,1,0:T(8,128)(2,1)S(1)}, bf16[8,4,48,384]{3,2,1,0:T(8,128)(2,1)S(1)}, u32[]{:S(2)}, u32[]{:S(2)}) collective-permute-start(bf16[8,4,48,384]{3,2,1,0:T(8,128)(2,1)S(1)} %add_convert_fusion.2), channel_id=1, source_target_pairs={{0,4},{2,6},{4,0},{6,2},{8,12},{10,14},{12,8},{14,10},{16,20},{18,... | collective-permute-start | bytes 3538952 | tf_op jit(solution)/shard_map/ppermute | solution.py:64
  387.5 46.8 %collective-permute-start.26 = (f32[512,768]{1,0:T(8,128)S(1)}, f32[512,768]{1,0:T(8,128)S(1)}, u32[]{:S(2)}, u32[]{:S(2)}) collective-permute-start(f32[512,768]{1,0:T(8,128)S(1)} %copy-done.34), channel_id=1, source_target_pairs={{0,1},{1,0},{2,3},{3,2},{4,5},{5,4},{6,7},{7,6},{8,9},{9,8},{10,11... | collective-permute-start | bytes 4718600 | tf_op jit(solution)/shard_map/ppermute | solution.py:67
  387.5 24.2 %collective-permute-start.27 = (bf16[1,2,48,1536]{3,2,1,0:T(8,128)(2,1)S(1)}, bf16[1,2,48,1536]{3,2,1,0:T(8,128)(2,1)S(1)}, u32[]{:S(2)}, u32[]{:S(2)}) collective-permute-start(bf16[1,2,48,1536]{3,2,1,0:T(8,128)(2,1)S(1)} %add_convert_fusion.12), channel_id=1, source_target_pairs={{0,16},{2,18},{4,20},{6,22},{8,24},{10,26},{12,28},{14,30},{16,0},... | collective-permute-start | bytes 884744 | tf_op jit(solution)/shard_map/ppermute | solution.py:64
  388.1 22.3 %collective-permute-start.28 = (bf16[1,4,48,384]{3,2,1,0:T(8,128)(2,1)S(1)}, bf16[1,4,48,384]{3,2,1,0:T(8,128)(2,1)S(1)}, u32[]{:S(2)}, u32[]{:S(2)}) collective-permute-start(bf16[1,4,48,384]{3,2,1,0:T(8,128)(2,1)S(1)} %add_convert_fusion.15), channel_id=1, source_target_pairs={{0,16},{2,18},{4,20},{6,22},{8,24},{10,26},{12,28},{14,30},{16,0},... | collective-permute-start | bytes 442376 | tf_op jit(solution)/shard_map/ppermute | solution.py:64
  413.2 21.1 %collective-permute-start.29 = (f32[512,768]{1,0:T(8,128)S(1)}, f32[512,768]{1,0:T(8,128)S(1)}, u32[]{:S(2)}, u32[]{:S(2)}) collective-permute-start(f32[512,768]{1,0:T(8,128)S(1)} %project_backward.3.refs_2_), channel_id=1, source_target_pairs={{0,1},{1,0},{2,3},{3,2},{4,5},{5,4},{6,7},{7,6},{8,9},{9,8},{10,11... | collective-permute-start | bytes 4718600 | tf_op jit(solution)/shard_map/ppermute | solution.py:67
  413.3 9.9 %collective-permute-start.30 = (bf16[4,4,48,384]{3,2,1,0:T(8,128)(2,1)S(1)}, bf16[4,4,48,384]{3,2,1,0:T(8,128)(2,1)S(1)}, u32[]{:S(2)}, u32[]{:S(2)}) collective-permute-start(bf16[4,4,48,384]{3,2,1,0:T(8,128)(2,1)S(1)} %add_convert_fusion.6), channel_id=1, source_target_pairs={{0,2},{2,0},{4,6},{6,4},{8,10},{10,8},{12,14},{14,12},{16,18},{18,... | collective-permute-start | bytes 1769480 | tf_op jit(solution)/shard_map/ppermute | solution.py:64
  414.3 17.4 %collective-permute-start.31 = (bf16[2,2,48,1536]{3,2,1,0:T(8,128)(2,1)S(1)}, bf16[2,2,48,1536]{3,2,1,0:T(8,128)(2,1)S(1)}, u32[]{:S(2)}, u32[]{:S(2)}) collective-permute-start(bf16[2,2,48,1536]{3,2,1,0:T(8,128)(2,1)S(1)} %add_convert_fusion.7), channel_id=1, source_target_pairs={{0,8},{2,10},{4,12},{6,14},{8,0},{10,2},{12,4},{14,6},{16,24},{18,... | collective-permute-start | bytes 1769480 | tf_op jit(solution)/shard_map/ppermute | solution.py:64
  415.7 1.3 collective-permute-start.25
  417.0 23.7 %collective-permute-start.32 = (f32[2,8576]{1,0:T(2,128)S(1)}, f32[2,8576]{1,0:T(2,128)S(1)}, u32[]{:S(2)}, u32[]{:S(2)}) collective-permute-start(f32[2,8576]{1,0:T(2,128)S(1)} %add.383), channel_id=1, source_target_pairs={{0,16},{2,18},{4,20},{6,22},{8,24},{10,26},{12,28},{14,30},{16,0},... | collective-permute-start | bytes 205832 | tf_op jit(solution)/shard_map/ppermute | solution.py:64
  423.2 17.5 %collective-permute-start.33 = (f32[2,8576]{1,0:T(2,128)S(1)}, f32[2,8576]{1,0:T(2,128)S(1)}, u32[]{:S(2)}, u32[]{:S(2)}) collective-permute-start(f32[2,8576]{1,0:T(2,128)S(1)} %add.383), channel_id=1, source_target_pairs={{0,8},{2,10},{4,12},{6,14},{8,0},{10,2},{12,4},{14,6},{16,24},{18,... | collective-permute-start | bytes 205832 | tf_op jit(solution)/shard_map/ppermute | solution.py:64
  431.7 9.0 %collective-permute-start.34 = (f32[2,8576]{1,0:T(2,128)S(1)}, f32[2,8576]{1,0:T(2,128)S(1)}, u32[]{:S(2)}, u32[]{:S(2)}) collective-permute-start(f32[2,8576]{1,0:T(2,128)S(1)} %add.383), channel_id=1, source_target_pairs={{0,24},{2,26},{4,28},{6,30},{8,16},{10,18},{12,20},{14,22},{16,8},... | collective-permute-start | bytes 205832 | tf_op jit(solution)/shard_map/ppermute | solution.py:64
  434.2 14.2 %collective-permute-start.35 = (bf16[2,4,48,384]{3,2,1,0:T(8,128)(2,1)S(1)}, bf16[2,4,48,384]{3,2,1,0:T(8,128)(2,1)S(1)}, u32[]{:S(2)}, u32[]{:S(2)}) collective-permute-start(bf16[2,4,48,384]{3,2,1,0:T(8,128)(2,1)S(1)} %add_convert_fusion.11), channel_id=1, source_target_pairs={{0,8},{2,10},{4,12},{6,14},{8,0},{10,2},{12,4},{14,6},{16,24},{18,... | collective-permute-start | bytes 884744 | tf_op jit(solution)/shard_map/ppermute | solution.py:64
  434.3 15.3 %collective-permute-start.37 = (bf16[1,2,48,1536]{3,2,1,0:T(8,128)(2,1)S(1)}, bf16[1,2,48,1536]{3,2,1,0:T(8,128)(2,1)S(1)}, u32[]{:S(2)}, u32[]{:S(2)}) collective-permute-start(bf16[1,2,48,1536]{3,2,1,0:T(8,128)(2,1)S(1)} %add_convert_fusion.10), channel_id=1, source_target_pairs={{0,16},{2,18},{4,20},{6,22},{8,24},{10,26},{12,28},{14,30},{16,0},... | collective-permute-start | bytes 884744 | tf_op jit(solution)/shard_map/ppermute | solution.py:64
  448.5 7.8 %collective-permute-start.36 = (bf16[1,4,48,384]{3,2,1,0:T(8,128)(2,1)S(1)}, bf16[1,4,48,384]{3,2,1,0:T(8,128)(2,1)S(1)}, u32[]{:S(2)}, u32[]{:S(2)}) collective-permute-start(bf16[1,4,48,384]{3,2,1,0:T(8,128)(2,1)S(1)} %add_convert_fusion.14), channel_id=1, source_target_pairs={{0,16},{2,18},{4,20},{6,22},{8,24},{10,26},{12,28},{14,30},{16,0},... | collective-permute-start | bytes 442376 | tf_op jit(solution)/shard_map/ppermute | solution.py:64
  451.8 27.9 %copy-start.59 = (f32[2,48,3,384]{3,1,2,0:T(8,128)S(1)}, f32[2,48,3,384]{3,1,2,0:T(8,128)}, u32[]{:S(2)}) copy-start(f32[2,48,3,384]{3,1,2,0:T(8,128)} %param.22) | copy-start | bytes 1327108
  452.5 12.5 %collective-permute-start.45 = (f32[2,8576]{1,0:T(2,128)S(1)}, f32[2,8576]{1,0:T(2,128)}, u32[]{:S(2)}, u32[]{:S(2)}) collective-permute-start(f32[2,8576]{1,0:T(2,128)S(1)} %add_add_fusion.1), channel_id=1, source_target_pairs={{0,2},{2,0},{4,6},{6,4},{8,10},{10,8},{12,14},{14,12},{16,18},{18,... | collective-permute-start | bytes 205832 | tf_op jit(solution)/shard_map/ppermute | solution.py:64
  453.5 13.2 %collective-permute-start.46 = (f32[2,8576]{1,0:T(2,128)S(1)}, f32[2,8576]{1,0:T(2,128)}, u32[]{:S(2)}, u32[]{:S(2)}) collective-permute-start(f32[2,8576]{1,0:T(2,128)S(1)} %add_add_fusion.1), channel_id=1, source_target_pairs={{0,4},{2,6},{4,0},{6,2},{8,12},{10,14},{12,8},{14,10},{16,20},{18,... | collective-permute-start | bytes 205832 | tf_op jit(solution)/shard_map/ppermute | solution.py:64
  455.5 11.1 %collective-permute-start.47 = (f32[2,8576]{1,0:T(2,128)S(1)}, f32[2,8576]{1,0:T(2,128)}, u32[]{:S(2)}, u32[]{:S(2)}) collective-permute-start(f32[2,8576]{1,0:T(2,128)S(1)} %add_add_fusion.1), channel_id=1, source_target_pairs={{0,6},{2,4},{4,2},{6,0},{8,14},{10,12},{12,10},{14,8},{16,22},{18,... | collective-permute-start | bytes 205832 | tf_op jit(solution)/shard_map/ppermute | solution.py:64
  457.7 26.4 %copy-start.56 = (f32[2,48,1536]{2,1,0:T(8,128)S(1)}, f32[2,48,1536]{2,1,0:T(8,128)}, u32[]{:S(2)}) copy-start(f32[2,48,1536]{2,1,0:T(8,128)} %param.25) | copy-start | bytes 1769476
  457.7 26.4 %copy-start.57 = (f32[2,48,1536]{2,1,0:T(8,128)S(1)}, f32[2,48,1536]{2,1,0:T(8,128)}, u32[]{:S(2)}) copy-start(f32[2,48,1536]{2,1,0:T(8,128)} %param.24) | copy-start | bytes 1769476
  461.0 1.2 collective-permute-start.38
  462.3 5.4 %collective-permute-start.39 = (f32[8,128]{1,0:T(8,128)S(1)}, f32[8,128]{1,0:T(8,128)S(1)}, u32[]{:S(2)}, u32[]{:S(2)}) collective-permute-start(f32[8,128]{1,0:T(8,128)S(1)} %add.423), channel_id=1, source_target_pairs={{0,16},{2,18},{4,20},{6,22},{8,24},{10,26},{12,28},{14,30},{16,0},... | collective-permute-start | bytes 12296 | tf_op jit(solution)/shard_map/ppermute | solution.py:64
  463.8 3.9 collective-permute-start.40
  465.0 5.4 %collective-permute-start.41 = (f32[8,128]{1,0:T(8,128)S(1)}, f32[8,128]{1,0:T(8,128)S(1)}, u32[]{:S(2)}, u32[]{:S(2)}) collective-permute-start(f32[8,128]{1,0:T(8,128)S(1)} %add.423), channel_id=1, source_target_pairs={{0,24},{2,26},{4,28},{6,30},{8,16},{10,18},{12,20},{14,22},{16,8},... | collective-permute-start | bytes 12296 | tf_op jit(solution)/shard_map/ppermute | solution.py:64
  470.4 4.2 collective-permute-start.42
  471.3 3.6 collective-permute-start.43
  473.2 4.5 collective-permute-start.44
  486.2 1.2 collective-permute-start.48
  487.4 4.5 collective-permute-start.49
  487.4 4.5 collective-permute-start.50
  490.1 5.4 %collective-permute-start.51 = (f32[8,128]{1,0:T(8,128)S(1)}, f32[8,128]{1,0:T(8,128)S(1)}, u32[]{:S(2)}, u32[]{:S(2)}) collective-permute-start(f32[8,128]{1,0:T(8,128)S(1)} %add.452), channel_id=1, source_target_pairs={{0,24},{2,26},{4,28},{6,30},{8,16},{10,18},{12,20},{14,22},{16,8},... | collective-permute-start | bytes 12296 | tf_op jit(solution)/shard_map/ppermute | solution.py:64
  495.5 5.3 %collective-permute-start.52 = (f32[8,128]{1,0:T(8,128)S(1)}, f32[8,128]{1,0:T(8,128)S(1)}, u32[]{:S(2)}, u32[]{:S(2)}) collective-permute-start(f32[8,128]{1,0:T(8,128)S(1)} %add_add_fusion.3), channel_id=1, source_target_pairs={{0,2},{2,0},{4,6},{6,4},{8,10},{10,8},{12,14},{14,12},{16,18},{18,... | collective-permute-start | bytes 12296 | tf_op jit(solution)/shard_map/ppermute | solution.py:64
  496.2 4.6 collective-permute-start.53
  496.2 4.5 collective-permute-start.54
  (77 other events, 405.6 us)
Sparse Core Ops, SparseCore 0:
  12.1 136.4 all-gather.2

commit v6 on v5

--- a/solution.py
+++ b/solution.py
@@ -620,7 +620,7 @@
             ],
         ),
         compiler_params=pltpu.CompilerParams(
-            dimension_semantics=("arbitrary",), vmem_limit_bytes=44 << 20
+            dimension_semantics=("arbitrary",), vmem_limit_bytes=50 << 20
         ),
         cost_estimate=cost(3),
         name="prepare",
@@ -715,7 +715,7 @@
         grid_spec=pltpu.PrefetchScalarGridSpec(num_scalar_prefetch=2, grid=(seqs,pairs),
             in_specs=[col(0)]*depth+[col(1)]*depth+[col(2)],
             out_specs=[pl.BlockSpec((rows,128),lambda s,j,c,l:(s,j)), pl.BlockSpec((1,8,rows),lambda s,j,c,l:(s*pairs+j,0,0))]),
-        compiler_params=pltpu.CompilerParams(dimension_semantics=("arbitrary","arbitrary"),vmem_limit_bytes=44 << 20),
+        compiler_params=pltpu.CompilerParams(dimension_semantics=("arbitrary","arbitrary"),vmem_limit_bytes=50 << 20),
         cost_estimate=cost(10),
         name="attend_forward",
     )(core, lengths, *projections, *projections, projections[0])
@@ -780,7 +780,7 @@
         partial(attend_backward_kernel, depth=depth, with_later=later is not None, keep_total=keep_total),
         out_shape=out_shape,
         grid_spec=pltpu.PrefetchScalarGridSpec(num_scalar_prefetch=2, grid=(seqs,pairs), in_specs=in_specs, out_specs=out_specs),
-        compiler_params=pltpu.CompilerParams(dimension_semantics=("arbitrary","arbitrary"),vmem_limit_bytes=44 << 20),
+        compiler_params=pltpu.CompilerParams(dimension_semantics=("arbitrary","arbitrary"),vmem_limit_bytes=50 << 20),
         cost_estimate=cost(17),
         name="attend_backward",
     )(core, lengths, *args)

time: 518 us -> 513 us (level)
  local copies, waits for them, and re-layouts: 43.7 us -> 34.9 us
    unnamed x175 -> x155, local copies, waits for them, and re-layouts: 36.7 us -> 27.4 us
  transfers between devices with their start and end apart: 56 -> 56, of which waited for: 28 -> 29; matrix products, arithmetic and copies ran while one was open for 8% -> 9% of each run, Pallas kernels for 24% -> 25%
where the time goes in v6:
time: 513 us; the launch traced here: 510 us
  waiting for transfers between devices  173 us (34%)
  Pallas kernels  162 us (32%)
  other arithmetic  60.8 us (12%)
  starting transfers between devices  58.4 us (11%)
  local copies, waits for them, and re-layouts  34.9 us (7%)
  between operations  20.4 us (4%)
    ppermute x42, waiting for transfers between devices, swap(): return lax.ppermute(value, ('dp', 'tensor'), pairs)  162 us
    pallas_call x12, Pallas kernels, call(): pl.pallas_call(lambda at, *refs: kernel(*weight_rows(at), Row(at, 0), Row...  99.8 us
    ppermute x42, starting transfers between devices, swap(): return lax.ppermute(value, ('dp', 'tensor'), pairs)  56.4 us
    pallas_call x2, Pallas kernels, attend_backward(): pl.pallas_call(partial(attend_backward_kernel, depth=depth, with_later=la...  34.6 us
    unnamed x155, local copies, waits for them, and re-layouts  27.4 us
    convert_element_type x16, other arithmetic, advance(): sum((piece[half:size].astype(f32) for piece in move['pieces'])).astype(bf16)  23.9 us
    pallas_call x2, Pallas kernels, attend_forward(): pl.pallas_call(partial(attend_forward_kernel, depth=depth), out_shape=[ja...  20.4 us
    ppermute x13, waiting for transfers between devices, sibling(): return lax.ppermute(value, 'tensor', [(0, 1), (1, 0)])  11.1 us
  transfers between devices with their start and end apart: 56, of which 29 were waited for; matrix products, arithmetic and copies ran while one was open for 9% of the time, Pallas kernels for 25%

profile of v6, /device:TPU:0, one launch (start us, length us, event | category | flops | bytes accessed | tf_op | source)
XLA Modules:
  0.0 509.5 jit_solution(5298181608079914150)
XLA Ops:
  11.9 4.0 collective-permute-start
  16.0 2.3 prepare.1
  19.2 2.5 collective-permute-done
  23.5 11.2 %collective-permute-done.1 = bf16[2,48,1152]{2,1,0:T(8,128)(2,1)S(1)} collective-permute-done((bf16[2,48,1152]{2,1,0:T(8,128)(2,1)S(1)}, bf16[2,48,1152]{2,1,0:T(8,128)(2,1)S(1)}, u32[]{:S(2)}, u32[]{:S(2)}) %collective-permute-start.1) | collective-permute-done | bytes 221216 | tf_op jit(solution)/shard_map/ppermute | solution.py:64
  35.7 7.4 %collective-permute-done.2 = bf16[4,48,1152]{2,1,0:T(8,128)(2,1)S(1)} collective-permute-done((bf16[4,48,1152]{2,1,0:T(8,128)(2,1)S(1)}, bf16[4,48,1152]{2,1,0:T(8,128)(2,1)S(1)}, u32[]{:S(2)}, u32[]{:S(2)}) %collective-permute-start.2) | collective-permute-done | bytes 442400 | tf_op jit(solution)/shard_map/ppermute | solution.py:64
  46.0 17.8 %collective-permute-done.3 = bf16[8,48,1152]{2,1,0:T(8,128)(2,1)} collective-permute-done((bf16[8,48,1152]{2,1,0:T(8,128)(2,1)}, bf16[8,48,1152]{2,1,0:T(8,128)(2,1)}, u32[]{:S(2)}, u32[]{:S(2)}) %collective-permute-start.3) | collective-permute-done | bytes 884768 | tf_op jit(solution)/shard_map/ppermute | solution.py:64
  65.0 7.7 %collective-permute-start.6 = (bf16[1,48,3456]{2,1,0:T(8,128)(2,1)S(1)}, bf16[1,48,3456]{2,1,0:T(8,128)(2,1)S(1)}, u32[]{:S(2)}, u32[]{:S(2)}) collective-permute-start(bf16[1,48,3456]{2,1,0:T(8,128)(2,1)S(1)} %maximum_bitcast_fusion), channel_id=1, source_target_pairs={{0,16},{2,18},{4,20},{6,22},{8,24},{10,26},{12,28},{14,30},{16,0},... | collective-permute-start | bytes 995336 | tf_op jit(solution)/shard_map/ppermute | solution.py:64
  75.5 4.4 project.2.refs_0_.refs_1_.refs_2_.refs_3_
  80.0 11.9 %collective-permute-done.6 = bf16[1,48,3456]{2,1,0:T(8,128)(2,1)S(1)} collective-permute-done((bf16[1,48,3456]{2,1,0:T(8,128)(2,1)S(1)}, bf16[1,48,3456]{2,1,0:T(8,128)(2,1)S(1)}, u32[]{:S(2)}, u32[]{:S(2)}) %collective-permute-start.6) | collective-permute-done | bytes 331808 | tf_op jit(solution)/shard_map/ppermute | solution.py:64
  92.8 9.5 %attend_forward.2 = (bf16[512,768]{1,0:T(8,128)(2,1)S(1)}, f32[6,8,512]{2,1,0:T(8,128)S(1)}) custom-call(s32[1]{0:T(128)} %bitcast.5.core, s32[2]{0:T(128)S(1)} %copy-done.44, bf16[512,2304]{1,0:T(8,128)(2,1)S(1)} %project.2.refs_0_.refs_1_.refs_2_.refs_3_, bf16[512,2304]{1,0:T(8,128)(2,1)S(1)} %project.2.refs_0_.refs_1_.refs_2_.refs_3_, ...), custom_call_target="tpu_custom_call" | custom-call | bytes 25000000 | tf_op jit(solution)/shard_map/attend_forward/pallas_call | solution.py:712
  106.1 35.9 %collective-permute-done.7 = bf16[2,48,3456]{2,1,0:T(8,128)(2,1)} collective-permute-done((bf16[2,48,3456]{2,1,0:T(8,128)(2,1)}, bf16[2,48,3456]{2,1,0:T(8,128)(2,1)}, u32[]{:S(2)}, u32[]{:S(2)}) %collective-permute-start.7) | collective-permute-done | bytes 663584 | tf_op jit(solution)/shard_map/ppermute | solution.py:64
  144.4 17.2 %collective-permute-done.8 = bf16[4,48,3456]{2,1,0:T(8,128)(2,1)S(1)} collective-permute-done((bf16[4,48,3456]{2,1,0:T(8,128)(2,1)S(1)}, bf16[4,48,3456]{2,1,0:T(8,128)(2,1)S(1)}, u32[]{:S(2)}, u32[]{:S(2)}) %collective-permute-start.8) | collective-permute-done | bytes 1327136 | tf_op jit(solution)/shard_map/ppermute | solution.py:64
  164.8 14.2 %feed_forward.2 = (f32[512,768]{1,0:T(8,128)S(1)}, bf16[768,512]{1,0:T(8,128)(2,1)S(1)}, bf16[2,512,1536]{2,1,0:T(8,128)(2,1)S(1)}, f32[2,512,1536]{2,1,0:T(8,12...) custom-call(s32[4,17]{1,0:T(4,128)S(1)} %dynamic-slice_bitcast_fusio, ...), custom_call_target="tpu_custom_call" | custom-call | bytes 45000000 | tf_op jit(solution)/shard_map/feed_forward/pallas_call | solution.py:222
  186.0 5.2 %project.3.refs_0_.refs_2_.refs_4_ = bf16[512,2304]{1,0:T(8,128)(2,1)S(1)} custom-call(s32[4,17]{1,0:T(4,128)S(1)} %dynamic-slice_bitcast_fusion.at, bf16[512,768]{1,0:T(8,128)(2,1)S(1)} %get-tuple-element.302.refs_0_, bf16[16,2,48,4608]{3,2,1,0:T(8,128)(2,1)} %bitcast.97, bf16[16,2,48,4608]{3,2,1,0:T(8,128)(2,1)} %bitcast.98, ...), custom_call_target="tpu_custom_call" | custom-call | bytes 17500000 | tf_op jit(solution)/shard_map/project/pallas_call | solution.py:222
  191.3 10.9 %attend_forward.3 = (bf16[512,768]{1,0:T(8,128)(2,1)S(1)}, f32[6,8,512]{2,1,0:T(8,128)S(1)}) custom-call(s32[1]{0:T(128)} %bitcast.5.core, s32[2]{0:T(128)S(1)} %copy-done.44, bf16[512,2304]{1,0:T(8,128)(2,1)S(1)} %project.3.refs_0_.refs_2_.refs_4_, bf16[512,2304]{1,0:T(8,128)(2,1)} %copy-done, bf16[512,2304]{1,0:T(8,128)(2,1)S(1)} %project.3.refs_0_.refs_2_.refs_4_, ...), custom_call_target="tpu_custom_call" | custom-call | bytes 25000000 | tf_op jit(solution)/shard_map/attend_forward/pallas_call | solution.py:712
  202.8 1.9 constant_dynamic-update-slice_fusion.7
  204.7 1.9 constant_dynamic-update-slice_fusion.5
  206.7 2.1 constant_dynamic-update-slice_fusion.4.refs_2_.refs_4_.refs_6_.refs_8_
  209.2 2.0 copy-done.1
  211.2 2.4 copy-done.45
  213.5 15.8 %feed_forward.3 = (f32[512,768]{1,0:T(8,128)S(1)}, bf16[768,512]{1,0:T(8,128)(2,1)S(1)}, bf16[2,512,1536]{2,1,0:T(8,128)(2,1)S(1)}, f32[2,512,1536]{2,1,0:T(8,12...) custom-call(s32[4,17]{1,0:T(4,128)S(1)} %dynamic-slice_bitcast_fusio, ...), custom_call_target="tpu_custom_call" | custom-call | bytes 45000000 | tf_op jit(solution)/shard_map/feed_forward/pallas_call | solution.py:222
  232.1 2.0 copy-done.12
  234.2 15.4 %feed_backward.2 = (bf16[16,2,48,1536]{3,2,1,0:T(8,128)(2,1)S(1)}, bf16[16,2,48,1536]{3,2,1,0:T(8,128)(2,1)}, f32[2,8,1536]{2,1,0:T(8,128)S(1)}, f32[512,768]{1,0:T(8,128)S(1)}) custom-call(s32[4,17]{1,0:T(4,128)S(1)} %dynamic-slice_bitcast_fusion.at, f32[512,768]{1,0:T(8,128)S(1)} %get-tuple-element.312.refs_0_, ...), custom_call_target="tpu_custom_call" | custom-call | bytes 50000000 | tf_op jit(solution)/shard_map/feed_backward/pallas_call | solution.py:222
  250.2 4.1 context_backward.2
  254.3 4.0 collective-permute-done.12
  258.3 2.6 add_convert_fusion.1
  261.8 18.3 %attend_backward.2 = (bf16[3,512,768]{2,1,0:T(8,128)(2,1)S(1)}, f32[1,8,768]{2,1,0:T(8,128)S(1)}, f32[12,512,512]{2,1,0:T(8,128)}) custom-call(s32[1]{0:T(128)} %bitcast.5.core, s32[2]{0:T(128)S(1)} %copy-done.44, bf16[512,2304]{1,0:T(8,128)(2,1)} %copy-done.2, bf16[512,2304]{1,0:T(8,128)(2,1)} %copy-done, bf16[512,2304]{1,0:T(8,128)(2,1)} %copy-done.2, ...), custom_call_target="tpu_custom_call" | custom-call | bytes 42500000 | tf_op jit(solution)/shard_map/attend_backward/pallas_call | solution.py:779
  281.2 5.6 %projection_grads.2 = (bf16[16,4,48,384]{3,2,1,0:T(8,128)(2,1)S(1)}, bf16[16,4,48,384]{3,2,1,0:T(8,128)(2,1)}) custom-call(s32[4,17]{1,0:T(4,128)S(1)} %dynamic-slice_bitcast_fusion.at, bf16[768,512]{1,0:T(8,128)(2,1)S(1)} %copy-done.33, bf16[512,768]{1,0:T(8,128)(2,1)S(1)} %get-tuple-element.305.refs_1_, bf16[768,512]{1,0:T(8,128)(2,1)S(1)} %copy-done.29, ...), custom_call_target="tpu_custom_call" | custom-call | bytes 22500000 | tf_op jit(solution)/shard_map/projection_grads/pallas_call | solution.py:222
  286.9 3.6 collective-permute-done.13
  290.5 3.1 add_convert_fusion.5
  294.2 6.5 %project_backward.2 = (f32[512,768]{1,0:T(8,128)S(1)}, bf16[512,768]{1,0:T(8,128)(2,1)S(1)}, bf16[768,512]{1,0:T(8,128)(2,1)S(1)}, f32[8,768]{1,0:T(8,128)S(1)}) custom-call(s32[4,17]{1,0:T(4,128)S(1)} %dynamic-slice_bitcast_fusion.at, bf16[3,512,768]{2,1,0:T(8,128)(2,1)S(1)} %get-tuple-element.339.refs_3_.refs_0_, ...), custom_call_target="tpu_custom_call" | custom-call | bytes 20000000 | tf_op jit(solution)/shard_map/project_backward/pallas_call | solution.py:222
  301.7 1.8 copy-done.10
  303.5 15.6 %feed_backward.3 = (bf16[16,2,48,1536]{3,2,1,0:T(8,128)(2,1)S(1)}, bf16[16,2,48,1536]{3,2,1,0:T(8,128)(2,1)}, f32[2,8,1536]{2,1,0:T(8,128)S(1)}, f32[512,768]{1,0:T(8,128)S(1)}) custom-call(s32[4,17]{1,0:T(4,128)S(1)} %dynamic-slice_bitcast_fusion.at, f32[512,768]{1,0:T(8,128)S(1)} %get-tuple-element.353.refs_0_, ...), custom_call_target="tpu_custom_call" | custom-call | bytes 50000000 | tf_op jit(solution)/shard_map/feed_backward/pallas_call | solution.py:222
  319.2 4.0 add_convert_fusion.9
  325.0 3.8 context_backward.3
  328.8 4.7 collective-permute-done.18
  333.5 2.0 add_convert_fusion.13
  335.6 2.5 add_convert_fusion
  339.9 16.4 %attend_backward.3 = (bf16[3,512,768]{2,1,0:T(8,128)(2,1)S(1)}, f32[1,8,768]{2,1,0:T(8,128)S(1)}) custom-call(s32[1]{0:T(128)} %bitcast.5.core, s32[2]{0:T(128)S(1)} %copy-done.44, bf16[512,2304]{1,0:T(8,128)(2,1)} %copy-done, bf16[512,2304]{1,0:T(8,128)(2,1)} %copy-done, bf16[512,2304]{1,0:T(8,128)(2,1)} %copy-done, ...), custom_call_target="tpu_custom_call" | custom-call | bytes 42500000 | tf_op jit(solution)/shard_map/attend_backward/pallas_call | solution.py:779
  356.9 2.0 collective-permute-start.20
  362.1 3.2 collective-permute-done.20
  367.6 2.4 add_convert_fusion.3
  370.1 5.0 projection_grads.3
  376.7 3.1 collective-permute-done.22
  382.0 2.6 collective-permute-start.28
  384.6 4.1 project_backward.3.refs_2_
  388.7 11.4 %collective-permute-done.23 = bf16[4,2,48,1536]{3,2,1,0:T(8,128)(2,1)S(1)} collective-permute-done((bf16[4,2,48,1536]{3,2,1,0:T(8,128)(2,1)S(1)}, bf16[4,2,48,1536]{3,2,1,0:T(8,128)(2,1)S(1)}, u32[]{:S(2)}, u32[]{:S(2)}) %collective-permute-start.23) | collective-permute-done | bytes 1179680 | tf_op jit(solution)/shard_map/ppermute | solution.py:64
  401.8 1.8 collective-permute-done.24
  411.8 5.4 %collective-permute-done.30 = bf16[4,4,48,384]{3,2,1,0:T(8,128)(2,1)S(1)} collective-permute-done((bf16[4,4,48,384]{3,2,1,0:T(8,128)(2,1)S(1)}, bf16[4,4,48,384]{3,2,1,0:T(8,128)(2,1)S(1)}, u32[]{:S(2)}, u32[]{:S(2)}) %collective-permute-start.30) | collective-permute-done | bytes 589856 | tf_op jit(solution)/shard_map/ppermute | solution.py:64
  418.1 7.9 %collective-permute-done.31 = bf16[2,2,48,1536]{3,2,1,0:T(8,128)(2,1)S(1)} collective-permute-done((bf16[2,2,48,1536]{3,2,1,0:T(8,128)(2,1)S(1)}, bf16[2,2,48,1536]{3,2,1,0:T(8,128)(2,1)S(1)}, u32[]{:S(2)}, u32[]{:S(2)}) %collective-permute-start.31) | collective-permute-done | bytes 589856 | tf_op jit(solution)/shard_map/ppermute | solution.py:64
  428.7 3.1 collective-permute-start.37
  431.8 3.2 join.1
  435.1 7.8 %collective-permute-done.35 = bf16[2,4,48,384]{3,2,1,0:T(8,128)(2,1)S(1)} collective-permute-done((bf16[2,4,48,384]{3,2,1,0:T(8,128)(2,1)S(1)}, bf16[2,4,48,384]{3,2,1,0:T(8,128)(2,1)S(1)}, u32[]{:S(2)}, u32[]{:S(2)}) %collective-permute-start.35) | collective-permute-done | bytes 294944 | tf_op jit(solution)/shard_map/ppermute | solution.py:64
  448.4 1.9 collective-permute-start.47
  462.3 2.7 collective-permute-done.41
  466.3 2.3 collective-permute-start.44
  472.7 2.6 multiply_reduce_fusion.6
  477.2 1.9 multiply_reduce_fusion.1
  480.4 2.4 collective-permute-start.50
  482.8 2.0 collective-permute-start.51
  484.9 3.3 collective-permute-done.51
  489.0 1.8 collective-permute-start.53
  493.5 1.8 collective-permute-done.54
  495.8 2.5 multiply_subtract_fusion
  (307 shorter events, 96.4 us)
Async XLA Ops:
  7.2 157.6 %all-gather.3.cloned.1.call-start = ((), (), s32[]{:S(2)}) async-start(), calls=%async_computation | async-start | bytes 14598144 | tf_op jit(solution)/shard_map/all_gather | solution.py:843
  11.9 9.8 %collective-permute-start = (bf16[1,48,1152]{2,1,0:T(8,128)(2,1)}, bf16[1,48,1152]{2,1,0:T(8,128)(2,1)}, u32[]{:S(2)}, u32[]{:S(2)}) collective-permute-start(bf16[1,48,1152]{2,1,0:T(8,128)(2,1)} %bitcast.31), channel_id=1, source_target_pairs={{0,16},{2,18},{4,20},{6,22},{8,24},{10,26},{12,28},{14,30},{16,0},... | collective-permute-start | bytes 331784 | tf_op jit(solution)/shard_map/ppermute | solution.py:64
  19.2 25.9 %copy-start.61 = (bf16[48,1536]{1,0:T(8,128)(2,1)S(1)}, bf16[48,1536]{1,0:T(8,128)(2,1)}, u32[]{:S(2)}) copy-start(bf16[48,1536]{1,0:T(8,128)(2,1)} %get-tuple-element.503) | copy-start | bytes 442372
  22.7 12.0 %collective-permute-start.1 = (bf16[2,48,1152]{2,1,0:T(8,128)(2,1)S(1)}, bf16[2,48,1152]{2,1,0:T(8,128)(2,1)S(1)}, u32[]{:S(2)}, u32[]{:S(2)}) collective-permute-start(bf16[2,48,1152]{2,1,0:T(8,128)(2,1)S(1)} %pad_maximum_fusion.7), channel_id=1, source_target_pairs={{0,8},{2,10},{4,12},{6,14},{8,0},{10,2},{12,4},{14,6},{16,24},{18,... | collective-permute-start | bytes 663560 | tf_op jit(solution)/shard_map/ppermute | solution.py:64
  34.8 8.4 %collective-permute-start.2 = (bf16[4,48,1152]{2,1,0:T(8,128)(2,1)S(1)}, bf16[4,48,1152]{2,1,0:T(8,128)(2,1)S(1)}, u32[]{:S(2)}, u32[]{:S(2)}) collective-permute-start(bf16[4,48,1152]{2,1,0:T(8,128)(2,1)S(1)} %pad_maximum_fusion.5), channel_id=1, source_target_pairs={{0,2},{2,0},{4,6},{6,4},{8,10},{10,8},{12,14},{14,12},{16,18},{18,... | collective-permute-start | bytes 1327112 | tf_op jit(solution)/shard_map/ppermute | solution.py:64
  44.1 19.7 %collective-permute-start.3 = (bf16[8,48,1152]{2,1,0:T(8,128)(2,1)}, bf16[8,48,1152]{2,1,0:T(8,128)(2,1)}, u32[]{:S(2)}, u32[]{:S(2)}) collective-permute-start(bf16[8,48,1152]{2,1,0:T(8,128)(2,1)} %pad_maximum_fusion.2), channel_id=1, source_target_pairs={{0,4},{2,6},{4,0},{6,2},{8,12},{10,14},{12,8},{14,10},{16,20},{18,... | collective-permute-start | bytes 2654216 | tf_op jit(solution)/shard_map/ppermute | solution.py:64
  45.0 30.3 %collective-permute-start.4 = (bf16[8,48,1152]{2,1,0:T(8,128)(2,1)}, bf16[8,48,1152]{2,1,0:T(8,128)(2,1)S(1)}, u32[]{:S(2)}, u32[]{:S(2)}) collective-permute-start(bf16[8,48,1152]{2,1,0:T(8,128)(2,1)} %pad_maximum_fusion.2), channel_id=1, source_target_pairs={{0,1},{1,0},{2,3},{3,2},{4,5},{5,4},{6,7},{7,6},{8,9},{9,8},{10,11... | collective-permute-start | bytes 2654216 | tf_op jit(solution)/shard_map/ppermute | solution.py:67
  63.8 11.6 %collective-permute-start.5 = (bf16[8,48,1152]{2,1,0:T(8,128)(2,1)}, bf16[8,48,1152]{2,1,0:T(8,128)(2,1)S(1)}, u32[]{:S(2)}, u32[]{:S(2)}) collective-permute-start(bf16[8,48,1152]{2,1,0:T(8,128)(2,1)} %collective-permute-done.3), channel_id=1, source_target_pairs={{0,1},{1,0},{2,3},{3,2},{4,5},{5,4},{6,7},{7,6},{8,9},{9,8},{10,11... | collective-permute-start | bytes 2654216 | tf_op jit(solution)/shard_map/ppermute | solution.py:67
  65.0 26.9 %collective-permute-start.6 = (bf16[1,48,3456]{2,1,0:T(8,128)(2,1)S(1)}, bf16[1,48,3456]{2,1,0:T(8,128)(2,1)S(1)}, u32[]{:S(2)}, u32[]{:S(2)}) collective-permute-start(bf16[1,48,3456]{2,1,0:T(8,128)(2,1)S(1)} %maximum_bitcast_fusion), channel_id=1, source_target_pairs={{0,16},{2,18},{4,20},{6,22},{8,24},{10,26},{12,28},{14,30},{16,0},... | collective-permute-start | bytes 995336 | tf_op jit(solution)/shard_map/ppermute | solution.py:64
  80.0 22.4 %copy-start = (bf16[512,2304]{1,0:T(8,128)(2,1)}, bf16[512,2304]{1,0:T(8,128)(2,1)S(1)}, u32[]{:S(2)}) copy-start(bf16[512,2304]{1,0:T(8,128)(2,1)S(1)} %project.2.refs_0_.refs_1_.refs_2_.refs_3_) | copy-start | bytes 7077892
  92.8 49.2 %collective-permute-start.7 = (bf16[2,48,3456]{2,1,0:T(8,128)(2,1)}, bf16[2,48,3456]{2,1,0:T(8,128)(2,1)}, u32[]{:S(2)}, u32[]{:S(2)}) collective-permute-start(bf16[2,48,3456]{2,1,0:T(8,128)(2,1)} %pad_maximum_fusion.3), channel_id=1, source_target_pairs={{0,8},{2,10},{4,12},{6,14},{8,0},{10,2},{12,4},{14,6},{16,24},{18,... | collective-permute-start | bytes 1990664 | tf_op jit(solution)/shard_map/ppermute | solution.py:64
  143.7 17.8 %collective-permute-start.8 = (bf16[4,48,3456]{2,1,0:T(8,128)(2,1)S(1)}, bf16[4,48,3456]{2,1,0:T(8,128)(2,1)S(1)}, u32[]{:S(2)}, u32[]{:S(2)}) collective-permute-start(bf16[4,48,3456]{2,1,0:T(8,128)(2,1)S(1)} %pad_maximum_fusion.1), channel_id=1, source_target_pairs={{0,2},{2,0},{4,6},{6,4},{8,10},{10,8},{12,14},{14,12},{16,18},{18,... | collective-permute-start | bytes 3981320 | tf_op jit(solution)/shard_map/ppermute | solution.py:64
  163.3 38.9 %collective-permute-start.9 = (bf16[8,48,3456]{2,1,0:T(8,128)(2,1)}, bf16[8,48,3456]{2,1,0:T(8,128)(2,1)}, u32[]{:S(2)}, u32[]{:S(2)}) collective-permute-start(bf16[8,48,3456]{2,1,0:T(8,128)(2,1)} %pad_maximum_fusion), channel_id=1, source_target_pairs={{0,4},{2,6},{4,0},{6,2},{8,12},{10,14},{12,8},{14,10},{16,20},{18,... | collective-permute-start | bytes 7962632 | tf_op jit(solution)/shard_map/ppermute | solution.py:64
  164.8 37.9 %collective-permute-start.10 = (bf16[8,48,3456]{2,1,0:T(8,128)(2,1)}, bf16[8,48,3456]{2,1,0:T(8,128)(2,1)}, u32[]{:S(2)}, u32[]{:S(2)}) collective-permute-start(bf16[8,48,3456]{2,1,0:T(8,128)(2,1)} %pad_maximum_fusion), channel_id=1, source_target_pairs={{0,1},{1,0},{2,3},{3,2},{4,5},{5,4},{6,7},{7,6},{8,9},{9,8},{10,11... | collective-permute-start | bytes 7962632 | tf_op jit(solution)/shard_map/ppermute | solution.py:67
  202.2 6.6 %collective-permute-start.11 = (bf16[8,48,3456]{2,1,0:T(8,128)(2,1)}, bf16[8,48,3456]{2,1,0:T(8,128)(2,1)S(1)}, u32[]{:S(2)}, u32[]{:S(2)}) collective-permute-start(bf16[8,48,3456]{2,1,0:T(8,128)(2,1)} %collective-permute-done.9), channel_id=1, source_target_pairs={{0,1},{1,0},{2,3},{3,2},{4,5},{5,4},{6,7},{7,6},{8,9},{9,8},{10,11... | collective-permute-start | bytes 7962632 | tf_op jit(solution)/shard_map/ppermute | solution.py:67
  250.2 68.9 %copy-start.8 = (bf16[16,2,48,1536]{3,2,1,0:T(8,128)(2,1)}, bf16[16,2,48,1536]{3,2,1,0:T(8,128)(2,1)S(1)}, u32[]{:S(2)}) copy-start(bf16[16,2,48,1536]{3,2,1,0:T(8,128)(2,1)S(1)} %get-tuple-element.435) | copy-start | bytes 14155780
  250.2 8.1 %collective-permute-start.12 = (bf16[16,2,48,1536]{3,2,1,0:T(8,128)(2,1)}, bf16[16,2,48,1536]{3,2,1,0:T(8,128)(2,1)S(1)}, u32[]{:S(2)}, u32[]{:S(2)}) collective-permute-start(bf16[16,2,48,1536]{3,2,1,0:T(8,128)(2,1)} %get-tuple-element.325), channel_id=1, source_target_pairs={{0,1},{1,0},{2,3},{3,2},{4,5},{5,4},{6,7},{7,6},{8,9},{9,8},{10,11... | collective-permute-start | bytes 14155784 | tf_op jit(solution)/shard_map/ppermute | solution.py:67
  261.3 29.2 %collective-permute-start.13 = (bf16[8,2,48,1536]{3,2,1,0:T(8,128)(2,1)}, bf16[8,2,48,1536]{3,2,1,0:T(8,128)(2,1)}, u32[]{:S(2)}, u32[]{:S(2)}) collective-permute-start(bf16[8,2,48,1536]{3,2,1,0:T(8,128)(2,1)} %add_convert_fusion.1), channel_id=1, source_target_pairs={{0,4},{2,6},{4,0},{6,2},{8,12},{10,14},{12,8},{14,10},{16,20},{18,... | collective-permute-start | bytes 7077896 | tf_op jit(solution)/shard_map/ppermute | solution.py:64
  286.9 46.7 %copy-start.13 = (bf16[16,4,48,384]{3,2,1,0:T(8,128)(2,1)}, bf16[16,4,48,384]{3,2,1,0:T(8,128)(2,1)S(1)}, u32[]{:S(2)}) copy-start(bf16[16,4,48,384]{3,2,1,0:T(8,128)(2,1)S(1)} %get-tuple-element.440) | copy-start | bytes 7077892
  293.6 7.2 %collective-permute-start.14 = (bf16[16,4,48,384]{3,2,1,0:T(8,128)(2,1)}, bf16[16,4,48,384]{3,2,1,0:T(8,128)(2,1)S(1)}, u32[]{:S(2)}, u32[]{:S(2)}) collective-permute-start(bf16[16,4,48,384]{3,2,1,0:T(8,128)(2,1)} %get-tuple-element.348), channel_id=1, source_target_pairs={{0,1},{1,0},{2,3},{3,2},{4,5},{5,4},{6,7},{7,6},{8,9},{9,8},{10,11... | collective-permute-start | bytes 7077896 | tf_op jit(solution)/shard_map/ppermute | solution.py:67
  293.6 25.6 %collective-permute-start.15 = (bf16[4,2,48,1536]{3,2,1,0:T(8,128)(2,1)}, bf16[4,2,48,1536]{3,2,1,0:T(8,128)(2,1)}, u32[]{:S(2)}, u32[]{:S(2)}) collective-permute-start(bf16[4,2,48,1536]{3,2,1,0:T(8,128)(2,1)} %add_convert_fusion.5), channel_id=1, source_target_pairs={{0,2},{2,0},{4,6},{6,4},{8,10},{10,8},{12,14},{14,12},{16,18},{18,... | collective-permute-start | bytes 3538952 | tf_op jit(solution)/shard_map/ppermute | solution.py:64
  300.7 22.5 %copy-start.53 = (bf16[16,4,48,384]{3,2,1,0:T(8,128)(2,1)}, bf16[16,4,48,384]{3,2,1,0:T(8,128)(2,1)S(1)}, u32[]{:S(2)}) copy-start(bf16[16,4,48,384]{3,2,1,0:T(8,128)(2,1)S(1)} %collective-permute-done.14) | copy-start | bytes 7077892
  301.1 22.1 %collective-permute-start.16 = (bf16[8,4,48,384]{3,2,1,0:T(8,128)(2,1)S(1)}, bf16[8,4,48,384]{3,2,1,0:T(8,128)(2,1)S(1)}, u32[]{:S(2)}, u32[]{:S(2)}) collective-permute-start(bf16[8,4,48,384]{3,2,1,0:T(8,128)(2,1)S(1)} %add_convert_fusion.4), channel_id=1, source_target_pairs={{0,4},{2,6},{4,0},{6,2},{8,12},{10,14},{12,8},{14,10},{16,20},{18,... | collective-permute-start | bytes 3538952 | tf_op jit(solution)/shard_map/ppermute | solution.py:64
  323.5 12.1 %collective-permute-start.17 = (bf16[16,2,48,1536]{3,2,1,0:T(8,128)(2,1)}, bf16[16,2,48,1536]{3,2,1,0:T(8,128)(2,1)S(1)}, u32[]{:S(2)}, u32[]{:S(2)}) collective-permute-start(bf16[16,2,48,1536]{3,2,1,0:T(8,128)(2,1)} %get-tuple-element.376), channel_id=1, source_target_pairs={{0,1},{1,0},{2,3},{3,2},{4,5},{5,4},{6,7},{7,6},{8,9},{9,8},{10,11... | collective-permute-start | bytes 14155784 | tf_op jit(solution)/shard_map/ppermute | solution.py:67
  323.6 9.9 %collective-permute-start.18 = (bf16[4,4,48,384]{3,2,1,0:T(8,128)(2,1)S(1)}, bf16[4,4,48,384]{3,2,1,0:T(8,128)(2,1)S(1)}, u32[]{:S(2)}, u32[]{:S(2)}) collective-permute-start(bf16[4,4,48,384]{3,2,1,0:T(8,128)(2,1)S(1)} %add_convert_fusion.8), channel_id=1, source_target_pairs={{0,2},{2,0},{4,6},{6,4},{8,10},{10,8},{12,14},{14,12},{16,18},{18,... | collective-permute-start | bytes 1769480 | tf_op jit(solution)/shard_map/ppermute | solution.py:64
  338.4 29.2 %collective-permute-start.21 = (bf16[8,2,48,1536]{3,2,1,0:T(8,128)(2,1)}, bf16[8,2,48,1536]{3,2,1,0:T(8,128)(2,1)}, u32[]{:S(2)}, u32[]{:S(2)}) collective-permute-start(bf16[8,2,48,1536]{3,2,1,0:T(8,128)(2,1)} %add_convert_fusion), channel_id=1, source_target_pairs={{0,4},{2,6},{4,0},{6,2},{8,12},{10,14},{12,8},{14,10},{16,20},{18,... | collective-permute-start | bytes 7077896 | tf_op jit(solution)/shard_map/ppermute | solution.py:64
  339.9 20.6 %collective-permute-start.19 = (bf16[2,2,48,1536]{3,2,1,0:T(8,128)(2,1)}, bf16[2,2,48,1536]{3,2,1,0:T(8,128)(2,1)}, u32[]{:S(2)}, u32[]{:S(2)}) collective-permute-start(bf16[2,2,48,1536]{3,2,1,0:T(8,128)(2,1)} %add_convert_fusion.9), channel_id=1, source_target_pairs={{0,8},{2,10},{4,12},{6,14},{8,0},{10,2},{12,4},{14,6},{16,24},{18,... | collective-permute-start | bytes 1769480 | tf_op jit(solution)/shard_map/ppermute | solution.py:64
  356.9 8.4 %collective-permute-start.20 = (bf16[2,4,48,384]{3,2,1,0:T(8,128)(2,1)}, bf16[2,4,48,384]{3,2,1,0:T(8,128)(2,1)}, u32[]{:S(2)}, u32[]{:S(2)}) collective-permute-start(bf16[2,4,48,384]{3,2,1,0:T(8,128)(2,1)} %add_convert_fusion.13), channel_id=1, source_target_pairs={{0,8},{2,10},{4,12},{6,14},{8,0},{10,2},{12,4},{14,6},{16,24},{18,... | collective-permute-start | bytes 884744 | tf_op jit(solution)/shard_map/ppermute | solution.py:64
  375.2 4.6 collective-permute-start.22
  375.2 24.9 %collective-permute-start.23 = (bf16[4,2,48,1536]{3,2,1,0:T(8,128)(2,1)S(1)}, bf16[4,2,48,1536]{3,2,1,0:T(8,128)(2,1)S(1)}, u32[]{:S(2)}, u32[]{:S(2)}) collective-permute-start(bf16[4,2,48,1536]{3,2,1,0:T(8,128)(2,1)S(1)} %add_convert_fusion.3), channel_id=1, source_target_pairs={{0,2},{2,0},{4,6},{6,4},{8,10},{10,8},{12,14},{14,12},{16,18},{18,... | collective-permute-start | bytes 3538952 | tf_op jit(solution)/shard_map/ppermute | solution.py:64
  380.1 23.6 %collective-permute-start.24 = (bf16[8,4,48,384]{3,2,1,0:T(8,128)(2,1)S(1)}, bf16[8,4,48,384]{3,2,1,0:T(8,128)(2,1)S(1)}, u32[]{:S(2)}, u32[]{:S(2)}) collective-permute-start(bf16[8,4,48,384]{3,2,1,0:T(8,128)(2,1)S(1)} %add_convert_fusion.2), channel_id=1, source_target_pairs={{0,4},{2,6},{4,0},{6,2},{8,12},{10,14},{12,8},{14,10},{16,20},{18,... | collective-permute-start | bytes 3538952 | tf_op jit(solution)/shard_map/ppermute | solution.py:64
  381.6 47.0 %collective-permute-start.26 = (f32[512,768]{1,0:T(8,128)S(1)}, f32[512,768]{1,0:T(8,128)S(1)}, u32[]{:S(2)}, u32[]{:S(2)}) collective-permute-start(f32[512,768]{1,0:T(8,128)S(1)} %copy-done.23), channel_id=1, source_target_pairs={{0,1},{1,0},{2,3},{3,2},{4,5},{5,4},{6,7},{7,6},{8,9},{9,8},{10,11... | collective-permute-start | bytes 4718600 | tf_op jit(solution)/shard_map/ppermute | solution.py:67
  381.6 23.6 %collective-permute-start.27 = (bf16[1,2,48,1536]{3,2,1,0:T(8,128)(2,1)S(1)}, bf16[1,2,48,1536]{3,2,1,0:T(8,128)(2,1)S(1)}, u32[]{:S(2)}, u32[]{:S(2)}) collective-permute-start(bf16[1,2,48,1536]{3,2,1,0:T(8,128)(2,1)S(1)} %add_convert_fusion.12), channel_id=1, source_target_pairs={{0,16},{2,18},{4,20},{6,22},{8,24},{10,26},{12,28},{14,30},{16,0},... | collective-permute-start | bytes 884744 | tf_op jit(solution)/shard_map/ppermute | solution.py:64
  382.0 21.9 %collective-permute-start.28 = (bf16[1,4,48,384]{3,2,1,0:T(8,128)(2,1)S(1)}, bf16[1,4,48,384]{3,2,1,0:T(8,128)(2,1)S(1)}, u32[]{:S(2)}, u32[]{:S(2)}) collective-permute-start(bf16[1,4,48,384]{3,2,1,0:T(8,128)(2,1)S(1)} %add_convert_fusion.15), channel_id=1, source_target_pairs={{0,16},{2,18},{4,20},{6,22},{8,24},{10,26},{12,28},{14,30},{16,0},... | collective-permute-start | bytes 442376 | tf_op jit(solution)/shard_map/ppermute | solution.py:64
  406.8 21.9 %collective-permute-start.29 = (f32[512,768]{1,0:T(8,128)S(1)}, f32[512,768]{1,0:T(8,128)S(1)}, u32[]{:S(2)}, u32[]{:S(2)}) collective-permute-start(f32[512,768]{1,0:T(8,128)S(1)} %project_backward.3.refs_2_), channel_id=1, source_target_pairs={{0,1},{1,0},{2,3},{3,2},{4,5},{5,4},{6,7},{7,6},{8,9},{9,8},{10,11... | collective-permute-start | bytes 4718600 | tf_op jit(solution)/shard_map/ppermute | solution.py:67
  407.3 9.9 %collective-permute-start.30 = (bf16[4,4,48,384]{3,2,1,0:T(8,128)(2,1)S(1)}, bf16[4,4,48,384]{3,2,1,0:T(8,128)(2,1)S(1)}, u32[]{:S(2)}, u32[]{:S(2)}) collective-permute-start(bf16[4,4,48,384]{3,2,1,0:T(8,128)(2,1)S(1)} %add_convert_fusion.6), channel_id=1, source_target_pairs={{0,2},{2,0},{4,6},{6,4},{8,10},{10,8},{12,14},{14,12},{16,18},{18,... | collective-permute-start | bytes 1769480 | tf_op jit(solution)/shard_map/ppermute | solution.py:64
  408.6 17.5 %collective-permute-start.31 = (bf16[2,2,48,1536]{3,2,1,0:T(8,128)(2,1)S(1)}, bf16[2,2,48,1536]{3,2,1,0:T(8,128)(2,1)S(1)}, u32[]{:S(2)}, u32[]{:S(2)}) collective-permute-start(bf16[2,2,48,1536]{3,2,1,0:T(8,128)(2,1)S(1)} %add_convert_fusion.7), channel_id=1, source_target_pairs={{0,8},{2,10},{4,12},{6,14},{8,0},{10,2},{12,4},{14,6},{16,24},{18,... | collective-permute-start | bytes 1769480 | tf_op jit(solution)/shard_map/ppermute | solution.py:64
  408.7 1.7 collective-permute-start.25
  410.5 24.5 %collective-permute-start.32 = (f32[2,8576]{1,0:T(2,128)S(1)}, f32[2,8576]{1,0:T(2,128)S(1)}, u32[]{:S(2)}, u32[]{:S(2)}) collective-permute-start(f32[2,8576]{1,0:T(2,128)S(1)} %add.383), channel_id=1, source_target_pairs={{0,16},{2,18},{4,20},{6,22},{8,24},{10,26},{12,28},{14,30},{16,0},... | collective-permute-start | bytes 205832 | tf_op jit(solution)/shard_map/ppermute | solution.py:64
  417.2 17.8 %collective-permute-start.33 = (f32[2,8576]{1,0:T(2,128)S(1)}, f32[2,8576]{1,0:T(2,128)S(1)}, u32[]{:S(2)}, u32[]{:S(2)}) collective-permute-start(f32[2,8576]{1,0:T(2,128)S(1)} %add.383), channel_id=1, source_target_pairs={{0,8},{2,10},{4,12},{6,14},{8,0},{10,2},{12,4},{14,6},{16,24},{18,... | collective-permute-start | bytes 205832 | tf_op jit(solution)/shard_map/ppermute | solution.py:64
  426.0 9.0 %collective-permute-start.34 = (f32[2,8576]{1,0:T(2,128)S(1)}, f32[2,8576]{1,0:T(2,128)S(1)}, u32[]{:S(2)}, u32[]{:S(2)}) collective-permute-start(f32[2,8576]{1,0:T(2,128)S(1)} %add.383), channel_id=1, source_target_pairs={{0,24},{2,26},{4,28},{6,30},{8,16},{10,18},{12,20},{14,22},{16,8},... | collective-permute-start | bytes 205832 | tf_op jit(solution)/shard_map/ppermute | solution.py:64
  428.7 14.2 %collective-permute-start.35 = (bf16[2,4,48,384]{3,2,1,0:T(8,128)(2,1)S(1)}, bf16[2,4,48,384]{3,2,1,0:T(8,128)(2,1)S(1)}, u32[]{:S(2)}, u32[]{:S(2)}) collective-permute-start(bf16[2,4,48,384]{3,2,1,0:T(8,128)(2,1)S(1)} %add_convert_fusion.11), channel_id=1, source_target_pairs={{0,8},{2,10},{4,12},{6,14},{8,0},{10,2},{12,4},{14,6},{16,24},{18,... | collective-permute-start | bytes 884744 | tf_op jit(solution)/shard_map/ppermute | solution.py:64
  428.7 15.2 %collective-permute-start.37 = (bf16[1,2,48,1536]{3,2,1,0:T(8,128)(2,1)S(1)}, bf16[1,2,48,1536]{3,2,1,0:T(8,128)(2,1)S(1)}, u32[]{:S(2)}, u32[]{:S(2)}) collective-permute-start(bf16[1,2,48,1536]{3,2,1,0:T(8,128)(2,1)S(1)} %add_convert_fusion.10), channel_id=1, source_target_pairs={{0,16},{2,18},{4,20},{6,22},{8,24},{10,26},{12,28},{14,30},{16,0},... | collective-permute-start | bytes 884744 | tf_op jit(solution)/shard_map/ppermute | solution.py:64
  442.9 7.9 %collective-permute-start.36 = (bf16[1,4,48,384]{3,2,1,0:T(8,128)(2,1)S(1)}, bf16[1,4,48,384]{3,2,1,0:T(8,128)(2,1)S(1)}, u32[]{:S(2)}, u32[]{:S(2)}) collective-permute-start(bf16[1,4,48,384]{3,2,1,0:T(8,128)(2,1)S(1)} %add_convert_fusion.14), channel_id=1, source_target_pairs={{0,16},{2,18},{4,20},{6,22},{8,24},{10,26},{12,28},{14,30},{16,0},... | collective-permute-start | bytes 442376 | tf_op jit(solution)/shard_map/ppermute | solution.py:64
  446.1 26.6 %copy-start.50 = (f32[2,48,3,384]{3,1,2,0:T(8,128)S(1)}, f32[2,48,3,384]{3,1,2,0:T(8,128)}, u32[]{:S(2)}) copy-start(f32[2,48,3,384]{3,1,2,0:T(8,128)} %param.22) | copy-start | bytes 1327108
  446.8 12.8 %collective-permute-start.45 = (f32[2,8576]{1,0:T(2,128)S(1)}, f32[2,8576]{1,0:T(2,128)S(1)}, u32[]{:S(2)}, u32[]{:S(2)}) collective-permute-start(f32[2,8576]{1,0:T(2,128)S(1)} %add_add_fusion.1), channel_id=1, source_target_pairs={{0,2},{2,0},{4,6},{6,4},{8,10},{10,8},{12,14},{14,12},{16,18},{18,... | collective-permute-start | bytes 205832 | tf_op jit(solution)/shard_map/ppermute | solution.py:64
  448.0 13.2 %collective-permute-start.46 = (f32[2,8576]{1,0:T(2,128)S(1)}, f32[2,8576]{1,0:T(2,128)}, u32[]{:S(2)}, u32[]{:S(2)}) collective-permute-start(f32[2,8576]{1,0:T(2,128)S(1)} %add_add_fusion.1), channel_id=1, source_target_pairs={{0,4},{2,6},{4,0},{6,2},{8,12},{10,14},{12,8},{14,10},{16,20},{18,... | collective-permute-start | bytes 205832 | tf_op jit(solution)/shard_map/ppermute | solution.py:64
  448.4 12.9 %collective-permute-start.47 = (f32[2,8576]{1,0:T(2,128)S(1)}, f32[2,8576]{1,0:T(2,128)}, u32[]{:S(2)}, u32[]{:S(2)}) collective-permute-start(f32[2,8576]{1,0:T(2,128)S(1)} %add_add_fusion.1), channel_id=1, source_target_pairs={{0,6},{2,4},{4,2},{6,0},{8,14},{10,12},{12,10},{14,8},{16,22},{18,... | collective-permute-start | bytes 205832 | tf_op jit(solution)/shard_map/ppermute | solution.py:64
  452.3 24.8 %copy-start.47 = (f32[2,48,1536]{2,1,0:T(8,128)S(1)}, f32[2,48,1536]{2,1,0:T(8,128)}, u32[]{:S(2)}) copy-start(f32[2,48,1536]{2,1,0:T(8,128)} %param.25) | copy-start | bytes 1769476
  452.3 24.8 %copy-start.48 = (f32[2,48,1536]{2,1,0:T(8,128)S(1)}, f32[2,48,1536]{2,1,0:T(8,128)}, u32[]{:S(2)}) copy-start(f32[2,48,1536]{2,1,0:T(8,128)} %param.24) | copy-start | bytes 1769476
  455.6 1.2 collective-permute-start.38
  456.8 5.4 %collective-permute-start.39 = (f32[8,128]{1,0:T(8,128)S(1)}, f32[8,128]{1,0:T(8,128)S(1)}, u32[]{:S(2)}, u32[]{:S(2)}) collective-permute-start(f32[8,128]{1,0:T(8,128)S(1)} %add.423), channel_id=1, source_target_pairs={{0,16},{2,18},{4,20},{6,22},{8,24},{10,26},{12,28},{14,30},{16,0},... | collective-permute-start | bytes 12296 | tf_op jit(solution)/shard_map/ppermute | solution.py:64
  458.2 4.0 collective-permute-start.40
  459.6 5.4 %collective-permute-start.41 = (f32[8,128]{1,0:T(8,128)S(1)}, f32[8,128]{1,0:T(8,128)S(1)}, u32[]{:S(2)}, u32[]{:S(2)}) collective-permute-start(f32[8,128]{1,0:T(8,128)S(1)} %add.423), channel_id=1, source_target_pairs={{0,24},{2,26},{4,28},{6,30},{8,16},{10,18},{12,20},{14,22},{16,8},... | collective-permute-start | bytes 12296 | tf_op jit(solution)/shard_map/ppermute | solution.py:64
  465.0 4.2 collective-permute-start.42
  465.3 3.8 collective-permute-start.43
  466.3 4.5 collective-permute-start.44
  479.2 1.2 collective-permute-start.48
  480.4 4.5 collective-permute-start.49
  480.4 4.5 collective-permute-start.50
  482.8 5.4 %collective-permute-start.51 = (f32[8,128]{1,0:T(8,128)S(1)}, f32[8,128]{1,0:T(8,128)S(1)}, u32[]{:S(2)}, u32[]{:S(2)}) collective-permute-start(f32[8,128]{1,0:T(8,128)S(1)} %add.452), channel_id=1, source_target_pairs={{0,24},{2,26},{4,28},{6,30},{8,16},{10,18},{12,20},{14,22},{16,8},... | collective-permute-start | bytes 12296 | tf_op jit(solution)/shard_map/ppermute | solution.py:64
  488.2 5.3 %collective-permute-start.52 = (f32[8,128]{1,0:T(8,128)S(1)}, f32[8,128]{1,0:T(8,128)S(1)}, u32[]{:S(2)}, u32[]{:S(2)}) collective-permute-start(f32[8,128]{1,0:T(8,128)S(1)} %add_add_fusion.3), channel_id=1, source_target_pairs={{0,2},{2,0},{4,6},{6,4},{8,10},{10,8},{12,14},{14,12},{16,18},{18,... | collective-permute-start | bytes 12296 | tf_op jit(solution)/shard_map/ppermute | solution.py:64
  489.0 4.5 collective-permute-start.53
  490.8 4.5 collective-permute-start.54
  (67 other events, 410.8 us)
Sparse Core Ops, SparseCore 0:
  11.5 135.7 all-gather.2
